TPU v7x, 32 devices: a whole 2x2x4 slice. The times are simulated.
32 devices in a mesh: tok: 2 (over x), patch: 16 (over z, y, core).
Axes of the slice: x: 2, y: 2, z: 4, core: 2. Of those that a mesh axis runs over, the one named last changes fastest.
Arguments:
- tokens: bfloat16 [16, 1536, 1024], P('patch', 'tok'), may hold values from -6 to 6
- patches: bfloat16 [1024, 1024], P(('tok', 'patch')), may hold values from -6 to 6
- cotangent: bfloat16 [16, 1536, 1024], P('patch', 'tok'), may hold values from -6 to 6
- lengths: int32 [16], replicated, may hold values from 1 to 1536, 18432 in all
- page_of: int32 [16], replicated, may hold values from 0 to 1
- page_counts: int32 [2], replicated, may hold values from 1 to 512, as said below
- self_gain: float32 [1024], replicated, may hold values from 0.5 to 1.5
- self_shift: float32 [1024], replicated, may hold values from -1 to 1
- query_weight: bfloat16 [1024, 1024], replicated, may hold values from -0.1875 to 0.1875
- query_bias: float32 [1024], replicated, may hold values from -1.5 to 1.5
- key_weight: bfloat16 [1024, 1024], replicated, may hold values from -0.1875 to 0.1875
- value_weight: bfloat16 [1024, 1024], replicated, may hold values from -0.1875 to 0.1875
- value_bias: float32 [1024], replicated, may hold values from -1.5 to 1.5
- output_weight: bfloat16 [1024, 1024], replicated, may hold values from -1.5 to 1.5
- output_bias: float32 [1024], replicated, may hold values from -1.5 to 1.5
- cross_gain: float32 [1024], replicated, may hold values from 0.5 to 1.5
- cross_shift: float32 [1024], replicated, may hold values from -1 to 1
- probe_weight: bfloat16 [1024, 1024], replicated, may hold values from -0.1875 to 0.1875
- probe_bias: float32 [1024], replicated, may hold values from -1.5 to 1.5
- source_key: bfloat16 [1024, 1024], replicated, may hold values from -0.1875 to 0.1875
- source_value: bfloat16 [1024, 1024], replicated, may hold values from -0.1875 to 0.1875
- source_bias: float32 [1024], replicated, may hold values from -1.5 to 1.5
- merge_weight: bfloat16 [1024, 1024], replicated, may hold values from -1.5 to 1.5
- merge_bias: float32 [1024], replicated, may hold values from -1.5 to 1.5
- feed_gain: float32 [1024], replicated, may hold values from 0.5 to 1.5
- feed_shift: float32 [1024], replicated, may hold values from -1 to 1
- expand_weight: bfloat16 [1024, 4096], replicated, may hold values from -0.1875 to 0.1875
- expand_bias: float32 [4096], replicated, may hold values from -1.5 to 1.5
- reduce_weight: bfloat16 [4096, 1024], replicated, may hold values from -0.09375 to 0.09375
- reduce_bias: float32 [1024], replicated, may hold values from -1.5 to 1.5
Outputs:
- block_output: bfloat16 [16, 1536, 1024], P('patch', 'tok')
- tokens_grad: float32 [16, 1536, 1024], P('patch', 'tok')
- patches_grad: float32 [1024, 1024], P(('tok', 'patch'))
- self_gain_grad: float32 [1024], P(('tok', 'patch'))
- self_shift_grad: float32 [1024], P(('tok', 'patch'))
- query_weight_grad: float32 [1024, 1024], P(('tok', 'patch'))
- query_bias_grad: float32 [1024], P(('tok', 'patch'))
- key_weight_grad: float32 [1024, 1024], P(('tok', 'patch'))
- value_weight_grad: float32 [1024, 1024], P(('tok', 'patch'))
- value_bias_grad: float32 [1024], P(('tok', 'patch'))
- output_weight_grad: float32 [1024, 1024], P(('tok', 'patch'))
- output_bias_grad: float32 [1024], P(('tok', 'patch'))
- cross_gain_grad: float32 [1024], P(('tok', 'patch'))
- cross_shift_grad: float32 [1024], P(('tok', 'patch'))
- probe_weight_grad: float32 [1024, 1024], P(('tok', 'patch'))
- probe_bias_grad: float32 [1024], P(('tok', 'patch'))
- source_key_grad: float32 [1024, 1024], P(('tok', 'patch'))
- source_value_grad: float32 [1024, 1024], P(('tok', 'patch'))
- source_bias_grad: float32 [1024], P(('tok', 'patch'))
- merge_weight_grad: float32 [1024, 1024], P(('tok', 'patch'))
- merge_bias_grad: float32 [1024], P(('tok', 'patch'))
- feed_gain_grad: float32 [1024], P(('tok', 'patch'))
- feed_shift_grad: float32 [1024], P(('tok', 'patch'))
- expand_weight_grad: float32 [1024, 4096], P(('tok', 'patch'))
- expand_bias_grad: float32 [4096], P(('tok', 'patch'))
- reduce_weight_grad: float32 [4096, 1024], P(('tok', 'patch'))
- reduce_bias_grad: float32 [1024], P(('tok', 'patch'))
Inputs may be any that keep to these rules, and one draw needn't show every extreme that they name: The 16 lengths sum to 18432, and one equals 1536. `page_counts`: one page holds exactly 512 patches.
All inputs are finite; a program needn't handle non-finite values.
Results may differ from a plain program's by a relative error of at most 0.03.
Values may be sent and summed in bfloat16 or wider, within the bound.
No kernel may reach another device: no remote copies, remote signals or barrier semaphores. Data moves between devices by JAX's collectives and lax.ppermute only.
A program may use at most 320 MiB of HBM per device.

v0:
```python
import jax
import jax.numpy as jnp
from jax import lax
from jax.sharding import PartitionSpec as P

HDIM = 64
PAGE_SLOTS = 512


HIGH = lax.Precision.HIGHEST
NEG_FILL = -1e30
EPS_NORM = 1e-05
group_count = 4


def passed_along(value, axis, by):
    count = lax.axis_size(axis)
    pairs = [(i, i + by) for i in range(count) if 0 <= i + by < count]
    return lax.ppermute(value, axis, pairs)


def pick_entry(table, position):
    indices = jnp.arange(table.shape[0], dtype=jnp.int32)
    return jnp.sum(jnp.where(indices == position, table, 0))


def layer_norm(values, gain, shift):
    average = jnp.mean(values, axis=-1, keepdims=True)
    centred = values - average
    spread = jnp.mean(centred * centred, axis=-1, keepdims=True)
    inverse = lax.rsqrt(spread + EPS_NORM)
    normed = centred * inverse
    return (normed * gain + shift, normed, inverse)


def norm_backward(upstream, normed, inverse, gain):
    gain_part = jnp.sum(upstream * normed, axis=0)
    shift_part = jnp.sum(upstream, axis=0)
    scaled = upstream * gain
    centred = scaled - jnp.mean(scaled, axis=-1, keepdims=True)
    centred = centred - normed * jnp.mean(scaled * normed, axis=-1, keepdims=True)
    return (centred * inverse, gain_part, shift_part)


def product(left, right):
    return jnp.dot(left, right, preferred_element_type=jnp.float32)


def product_tn(left, right):
    return lax.dot_general(
        left, right, (((0,), (0,)), ((), ())), preferred_element_type=jnp.float32
    )


def product_nt(left, right):
    return lax.dot_general(
        left, right, (((1,), (1,)), ((), ())), preferred_element_type=jnp.float32
    )


def precise_tn(left, right):
    return lax.dot_general(
        left, right, (((0,), (0,)), ((), ())), precision=HIGH, preferred_element_type=jnp.float32
    )


def precise_nt(left, right):
    return lax.dot_general(
        left, right, (((1,), (1,)), ((), ())), precision=HIGH, preferred_element_type=jnp.float32
    )


def by_groups(matrix):
    row_count, model_width = matrix.shape
    return jnp.transpose(
        matrix.reshape(row_count, group_count, model_width // group_count), (1, 0, 2)
    )


def from_groups(stacked):
    return jnp.transpose(stacked, (1, 0, 2)).reshape(stacked.shape[1], -1)


def split_heads(matrix):
    return matrix.reshape(matrix.shape[0], matrix.shape[1] // HDIM, HDIM)


def group_scores(query, key_rows, allowed):
    scores = jnp.einsum(
        "qhd,khd->hqk",
        split_heads(query),
        split_heads(key_rows),
        preferred_element_type=jnp.float32,
    )
    return jnp.where(allowed[None], scores, NEG_FILL)


def group_forward(query, key_rows, value_rows, allowed):
    scores = group_scores(query, key_rows, allowed)
    row_max = jnp.max(scores, axis=-1, keepdims=True)
    exponent = jnp.exp(scores - row_max)
    row_total = jnp.sum(exponent, axis=-1, keepdims=True)
    soft_weights = (exponent / row_total).astype(jnp.bfloat16)
    mixed_heads = jnp.einsum(
        "hqk,khd->qhd", soft_weights, split_heads(value_rows), preferred_element_type=jnp.float32
    )
    return (mixed_heads.reshape(query.shape[0], -1), (row_max + jnp.log(row_total))[..., 0])


def attend_forward(query, key_rows, value_rows, allowed):

    def one_group(members):
        return group_forward(members[0], members[1], members[2], allowed)

    mixed_heads, log_total = lax.map(
        one_group, (by_groups(query), by_groups(key_rows), by_groups(value_rows))
    )
    return (from_groups(mixed_heads), log_total)


def group_backward(query, key_rows, value_rows, allowed, log_total, upstream):
    scores = group_scores(query, key_rows, allowed)
    soft_weights = jnp.exp(scores - log_total[..., None])
    upstream_heads = split_heads(upstream)
    grad_weights = jnp.einsum(
        "qhd,khd->hqk", upstream_heads, split_heads(value_rows), preferred_element_type=jnp.float32
    )
    grad_values = jnp.einsum(
        "hqk,qhd->khd",
        soft_weights.astype(jnp.bfloat16),
        upstream_heads,
        preferred_element_type=jnp.float32,
    )
    row_inner = jnp.sum(soft_weights * grad_weights, axis=-1, keepdims=True)
    grad_scores = (soft_weights * (grad_weights - row_inner)).astype(jnp.bfloat16)
    grad_query = jnp.einsum(
        "hqk,khd->qhd", grad_scores, split_heads(key_rows), preferred_element_type=jnp.float32
    )
    grad_keys = jnp.einsum(
        "hqk,qhd->khd", grad_scores, split_heads(query), preferred_element_type=jnp.float32
    )
    return (
        grad_query.reshape(query.shape[0], -1),
        grad_keys.reshape(key_rows.shape[0], -1),
        grad_values.reshape(value_rows.shape[0], -1),
    )


def attend_backward(query, key_rows, value_rows, allowed, log_total, upstream):

    def one_group(members):
        return group_backward(members[0], members[1], members[2], allowed, members[3], members[4])

    group_grads = lax.map(
        one_group,
        (
            by_groups(query),
            by_groups(key_rows),
            by_groups(value_rows),
            log_total,
            by_groups(upstream),
        ),
    )
    return (from_groups(group_grads[0]), from_groups(group_grads[1]), from_groups(group_grads[2]))


def exact_gelu(values):
    return jax.nn.gelu(values, approximate=False)


def page_slicer(page_rows_grad, page_start, span):
    page_length = page_rows_grad.shape[0]
    wanted = jnp.arange(span, dtype=jnp.int32)
    offsets = wanted - jnp.asarray(page_start)
    inside = (offsets >= 0) & (offsets < page_length)
    picked = jnp.take(page_rows_grad, jnp.clip(offsets, 0, page_length - 1), axis=0)
    return jnp.where(inside[:, None], picked, jnp.zeros_like(picked))


def local(
    tokens,
    patches,
    cotangent,
    lengths,
    page_of,
    page_counts,
    self_gain,
    self_shift,
    query_weight,
    query_bias,
    key_weight,
    value_weight,
    value_bias,
    output_weight,
    output_bias,
    cross_gain,
    cross_shift,
    probe_weight,
    probe_bias,
    source_key,
    source_value,
    source_bias,
    merge_weight,
    merge_bias,
    feed_gain,
    feed_shift,
    expand_weight,
    expand_bias,
    reduce_weight,
    reduce_bias,
):
    head_scale = HDIM ** (-0.5)
    tok_index = lax.axis_index("tok")
    sequence = lax.axis_index("patch")
    row_count = tokens.shape[1]
    model_width = tokens.shape[2]
    inputs = tokens[0].astype(jnp.float32)
    length = pick_entry(lengths, sequence)
    page_index = pick_entry(page_of, sequence)
    filled = pick_entry(page_counts, page_index)
    page_start = page_index * PAGE_SLOTS
    places = tok_index * row_count + jnp.arange(row_count, dtype=jnp.int32)
    valid_rows = (places < length).astype(jnp.float32)[:, None]
    normed_one, unit_one, inverse_one = layer_norm(inputs, self_gain, self_shift)
    hidden_one = normed_one.astype(jnp.bfloat16)
    query = ((product(hidden_one, query_weight) + query_bias) * head_scale).astype(jnp.bfloat16)
    own_keys = product(hidden_one, key_weight).astype(jnp.bfloat16)
    own_values = (product(hidden_one, value_weight) + value_bias).astype(jnp.bfloat16)
    earlier = passed_along(jnp.concatenate([own_keys, own_values], axis=1), "tok", 1)
    self_keys = jnp.concatenate([earlier[:, :model_width], own_keys], axis=0)
    self_values = jnp.concatenate([earlier[:, model_width:], own_values], axis=0)
    key_places = (tok_index - 1) * row_count + jnp.arange(2 * row_count, dtype=jnp.int32)
    allowed_self = (
        (key_places[None, :] <= places[:, None])
        & (key_places[None, :] >= 0)
        & (key_places[None, :] < length)
    )
    self_out, self_total = attend_forward(query, self_keys, self_values, allowed_self)
    self_mixed = self_out.astype(jnp.bfloat16)
    after_one = inputs + product(self_mixed, output_weight) + output_bias
    normed_two, unit_two, inverse_two = layer_norm(after_one, cross_gain, cross_shift)
    hidden_two = normed_two.astype(jnp.bfloat16)
    probe = ((product(hidden_two, probe_weight) + probe_bias) * head_scale).astype(jnp.bfloat16)
    gathered = lax.all_gather(patches, ("tok", "patch"), axis=0, tiled=True)
    page_rows = lax.dynamic_slice_in_dim(gathered, page_start, PAGE_SLOTS, 0)
    page_keys = product(page_rows, source_key).astype(jnp.bfloat16)
    page_values = (product(page_rows, source_value) + source_bias).astype(jnp.bfloat16)
    slot_index = jnp.arange(PAGE_SLOTS, dtype=jnp.int32)
    allowed_cross = jnp.broadcast_to((slot_index < filled)[None, :], (row_count, PAGE_SLOTS))
    cross_out, cross_total = attend_forward(probe, page_keys, page_values, allowed_cross)
    cross_mixed = cross_out.astype(jnp.bfloat16)
    after_two = after_one + product(cross_mixed, merge_weight) + merge_bias
    normed_three, unit_three, inverse_three = layer_norm(after_two, feed_gain, feed_shift)
    hidden_three = normed_three.astype(jnp.bfloat16)
    pre_act = product(hidden_three, expand_weight) + expand_bias
    activated_full, gelu_pull = jax.vjp(exact_gelu, pre_act)
    activated = activated_full.astype(jnp.bfloat16)
    branch = product(activated, reduce_weight) + reduce_bias
    block_output = (valid_rows * (after_two + branch)).astype(jnp.bfloat16)
    grad_two = valid_rows * cotangent[0].astype(jnp.float32)
    grad_ffn = grad_two.astype(jnp.bfloat16)
    reduce_weight_part = product_tn(activated, grad_ffn)
    reduce_bias_part = jnp.sum(grad_ffn.astype(jnp.float32), axis=0)
    grad_pre = gelu_pull(product_nt(grad_ffn, reduce_weight))[0].astype(jnp.bfloat16)
    expand_weight_part = product_tn(hidden_three, grad_pre)
    expand_bias_part = jnp.sum(grad_pre.astype(jnp.float32), axis=0)
    norm_grad, feed_gain_part, feed_shift_part = norm_backward(
        product_nt(grad_pre, expand_weight), unit_three, inverse_three, feed_gain
    )
    grad_two = grad_two + norm_grad
    grad_merge = grad_two.astype(jnp.bfloat16)
    merge_weight_part = product_tn(cross_mixed, grad_merge)
    merge_bias_part = jnp.sum(grad_merge.astype(jnp.float32), axis=0)
    grad_cross_out = product_nt(grad_merge, merge_weight).astype(jnp.bfloat16)
    probe_raw, page_key_grad, page_value_grad = attend_backward(
        probe, page_keys, page_values, allowed_cross, cross_total, grad_cross_out
    )
    key_float = source_key.astype(jnp.float32)
    value_float = source_value.astype(jnp.float32)
    pair_grads = jnp.concatenate([page_key_grad, page_value_grad], axis=1)
    owner_grads = lax.psum_scatter(
        page_slicer(pair_grads, page_start, patches.shape[0] * lax.axis_size(("tok", "patch"))),
        ("tok", "patch"),
        scatter_dimension=0,
        tiled=True,
    )
    key_grad_rows = owner_grads[:, :model_width]
    value_grad_rows = owner_grads[:, model_width:]
    owned_float = patches.astype(jnp.float32)
    source_key_part = precise_tn(owned_float, key_grad_rows)
    source_value_part = precise_tn(owned_float, value_grad_rows)
    source_bias_part = jnp.sum(value_grad_rows, axis=0)
    patches_grad = precise_nt(key_grad_rows, key_float) + precise_nt(value_grad_rows, value_float)
    probe_grad = probe_raw.astype(jnp.bfloat16)
    probe_weight_part = product_tn(hidden_two, probe_grad) * head_scale
    probe_bias_part = jnp.sum(probe_grad.astype(jnp.float32), axis=0) * head_scale
    norm_grad, cross_gain_part, cross_shift_part = norm_backward(
        product_nt(probe_grad, probe_weight) * head_scale, unit_two, inverse_two, cross_gain
    )
    grad_one = grad_two + norm_grad
    grad_self = grad_one.astype(jnp.bfloat16)
    output_weight_part = product_tn(self_mixed, grad_self)
    output_bias_part = jnp.sum(grad_self.astype(jnp.float32), axis=0)
    grad_self_out = product_nt(grad_self, output_weight).astype(jnp.bfloat16)
    query_raw, keys_raw, values_raw = attend_backward(
        query, self_keys, self_values, allowed_self, self_total, grad_self_out
    )
    returned = passed_along(
        jnp.concatenate([keys_raw[:row_count], values_raw[:row_count]], axis=1).astype(
            jnp.bfloat16
        ),
        "tok",
        -1,
    ).astype(jnp.float32)
    key_grad = (keys_raw[row_count:] + returned[:, :model_width]).astype(jnp.bfloat16)
    value_grad = (values_raw[row_count:] + returned[:, model_width:]).astype(jnp.bfloat16)
    query_grad = query_raw.astype(jnp.bfloat16)
    query_weight_part = product_tn(hidden_one, query_grad) * head_scale
    query_bias_part = jnp.sum(query_grad.astype(jnp.float32), axis=0) * head_scale
    key_weight_part = product_tn(hidden_one, key_grad)
    value_weight_part = product_tn(hidden_one, value_grad)
    value_bias_part = jnp.sum(value_grad.astype(jnp.float32), axis=0)
    upstream_one = (
        product_nt(query_grad, query_weight) * head_scale
        + product_nt(key_grad, key_weight)
        + product_nt(value_grad, value_weight)
    )
    norm_grad, self_gain_part, self_shift_part = norm_backward(
        upstream_one, unit_one, inverse_one, self_gain
    )
    tokens_grad = grad_one + norm_grad
    vectors = jnp.stack(
        [
            self_gain_part,
            self_shift_part,
            query_bias_part,
            value_bias_part,
            output_bias_part,
            cross_gain_part,
            cross_shift_part,
            probe_bias_part,
            source_bias_part,
            merge_bias_part,
            feed_gain_part,
            feed_shift_part,
            reduce_bias_part,
        ],
        axis=1,
    )
    summed = (
        lax.psum_scatter(vectors, ("tok", "patch"), scatter_dimension=0, tiled=True),
        lax.psum_scatter(expand_bias_part, ("tok", "patch"), scatter_dimension=0, tiled=True),
        lax.psum_scatter(query_weight_part, ("tok", "patch"), scatter_dimension=0, tiled=True),
        lax.psum_scatter(key_weight_part, ("tok", "patch"), scatter_dimension=0, tiled=True),
        lax.psum_scatter(value_weight_part, ("tok", "patch"), scatter_dimension=0, tiled=True),
        lax.psum_scatter(output_weight_part, ("tok", "patch"), scatter_dimension=0, tiled=True),
        lax.psum_scatter(probe_weight_part, ("tok", "patch"), scatter_dimension=0, tiled=True),
        lax.psum_scatter(source_key_part, ("tok", "patch"), scatter_dimension=0, tiled=True),
        lax.psum_scatter(source_value_part, ("tok", "patch"), scatter_dimension=0, tiled=True),
        lax.psum_scatter(merge_weight_part, ("tok", "patch"), scatter_dimension=0, tiled=True),
        lax.psum_scatter(expand_weight_part, ("tok", "patch"), scatter_dimension=0, tiled=True),
        lax.psum_scatter(reduce_weight_part, ("tok", "patch"), scatter_dimension=0, tiled=True),
    )
    vector_sums = summed[0]
    return (
        block_output[None],
        tokens_grad[None],
        patches_grad,
        vector_sums[:, 0],
        vector_sums[:, 1],
        summed[2],
        vector_sums[:, 2],
        summed[3],
        summed[4],
        vector_sums[:, 3],
        summed[5],
        vector_sums[:, 4],
        vector_sums[:, 5],
        vector_sums[:, 6],
        summed[6],
        vector_sums[:, 7],
        summed[7],
        summed[8],
        vector_sums[:, 8],
        summed[9],
        vector_sums[:, 9],
        vector_sums[:, 10],
        vector_sums[:, 11],
        summed[10],
        summed[1],
        summed[11],
        vector_sums[:, 12],
    )


def solution(mesh):
    placed = (
        P("patch", "tok", None),
        P(("tok", "patch"), None),
        P("patch", "tok", None),
        P(),
        P(),
        P(),
        P(),
        P(),
        P(),
        P(),
        P(),
        P(),
        P(),
        P(),
        P(),
        P(),
        P(),
        P(),
        P(),
        P(),
        P(),
        P(),
        P(),
        P(),
        P(),
        P(),
        P(),
        P(),
        P(),
        P(),
    )
    return jax.shard_map(
        local,
        mesh=mesh,
        in_specs=placed,
        out_specs=(
            P("patch", "tok", None),
            P("patch", "tok", None),
            P(("tok", "patch"), None),
            P(("tok", "patch")),
            P(("tok", "patch")),
            P(("tok", "patch"), None),
            P(("tok", "patch")),
            P(("tok", "patch"), None),
            P(("tok", "patch"), None),
            P(("tok", "patch")),
            P(("tok", "patch"), None),
            P(("tok", "patch")),
            P(("tok", "patch")),
            P(("tok", "patch")),
            P(("tok", "patch"), None),
            P(("tok", "patch")),
            P(("tok", "patch"), None),
            P(("tok", "patch"), None),
            P(("tok", "patch")),
            P(("tok", "patch"), None),
            P(("tok", "patch")),
            P(("tok", "patch")),
            P(("tok", "patch")),
            P(("tok", "patch"), None),
            P(("tok", "patch")),
            P(("tok", "patch"), None),
            P(("tok", "patch")),
        ),
        check_vma=False,
    )
```

profile of v0, /device:TPU:0, one launch (start us, length us, event | category | flops | bytes accessed | tf_op | source)
XLA Modules:
  0.0 2415.3 jit_solution(12698434246055264076)
XLA Ops:
  42.2 55.2 %collective-permute-done = bf16[768,2048]{1,0:T(8,128)(2,1)} collective-permute-done((bf16[768,2048]{1,0:T(8,128)(2,1)}, bf16[768,2048]{1,0:T(8,128)(2,1)}, u32[]{:S(2)}, u32[]{:S(2)}) %collective-permute-start) | collective-permute-done | bytes 3145760 | tf_op jit(solution)/shard_map/ppermute | solution.py:19
  114.0 93.7 %while.56 = (s32[]{:T(128)}, bf16[4,768,256]{1,2,0:T(8,128)(2,1)}, f32[4,4,768]{2,1,0:T(4,128)}, bf16[4,1536,256]{1,2,0:T(8,128)(2,1)}, bf16[4,768,256]{1,2,0:T(...) while((s32[]{:T(128)}, bf16[4,768,256]{1,2,0:T(8,128)(2,1)}, ...), condition=%wide.region_6.7_spmd.clone, body=%wide.region_3.0_spmd.clone.sunk | while | flops 1253962752 | bytes 73249936 | solution.py:115
  233.8 27.1 %while.57 = (s32[]{:T(128)}, bf16[4,768,256]{1,2,0:T(8,128)(2,1)}, f32[4,4,768]{2,1,0:T(4,128)S(1)}, bf16[4,512,256]{1,2,0:T(8,128)(2,1)S(1)}, bf16[4,768,256]{1...) while((s32[]{:T(128)}, bf16[4,768,256]{1,2,0:T(8,128)(2,1)}, ...), condition=%wide.region_14.15_spmd.clone, body=%wide.region_11.14_spmd.clone.sunk | while | flops 416805888 | bytes 22906976 | solution.py:115
  266.9 38.0 %multiply_convert_fusion.2 = (bf16[768,4096]{1,0:T(8,128)(2,1)}, f32[768,4096]{1,0:T(8,128)}, f32[768,4096]{1,0:T(8,128)}) fusion(f32[4096]{0:T(1024)S(1)} %copy-done.75, bf16[1024,4096]{1,0:T(8,128)(2,1)S(1)} %bitcast.443, f32[768,1024]{1,0:T(8,128)S(1)} %get-tuple-element.536, f32[1024]{0:T(1024)S(1)} %copy-done.37, f32[1024]{0:T(1024)S(1)} %copy-done.33, ...), kind=kOutput, calls=%fused_computation.65 | convolution fusion | flops 6654001152 | bytes 43022336 | tf_op jit(solution)/shard_map/dot_general | solution.py:46
  304.9 21.5 convert_reduce_fusion
  350.3 51.6 %while.58 = (s32[]{:T(128)}, bf16[4,768,256]{1,2,0:T(8,128)(2,1)}, f32[4,512,256]{1,2,0:T(8,128)}, f32[4,512,256]{1,2,0:T(8,128)}, bf16[4,512,256]{1,2,0:T(8,128...) while((s32[]{:T(128)}, bf16[4,768,256]{1,2,0:T(8,128)(2,1)}, ...), condition=%wide.region_21.22_spmd.clone, body=%wide.region_19.21_spmd.clone.sunk | while | flops 1025504256 | bytes 56580736 | solution.py:154
  447.1 244.8 %while.59 = (s32[]{:T(128)}, bf16[4,768,256]{1,2,0:T(8,128)(2,1)}, f32[4,1536,256]{1,2,0:T(8,128)}, f32[4,1536,256]{1,2,0:T(8,128)}, bf16[4,1536,256]{1,2,0:T(8,...) while((s32[]{:T(128)}, bf16[4,768,256]{1,2,0:T(8,128)(2,1)}, ...), condition=%wide.region_26.27_spmd.clone, body=%wide.region_24.26_spmd.clone.sunk | while | flops 3080057856 | bytes 165643424 | solution.py:154
  462.2 16.9 multiply_reduce_fusion.15
  523.7 16.8 multiply_reduce_fusion.15
  584.8 16.8 multiply_reduce_fusion.15
  645.8 16.8 multiply_reduce_fusion.15
  707.5 60.3 %collective-permute-done.1 = bf16[768,2048]{0,1:T(8,128)(2,1)S(1)} collective-permute-done((bf16[768,2048]{0,1:T(8,128)(2,1)S(1)}, bf16[768,2048]{0,1:T(8,128)(2,1)S(1)}, u32[]{:S(2)}, u32[]{:S(2)}) %collective-permute-start.1) | collective-permute-done | bytes 3145760 | tf_op jit(solution)/shard_map/ppermute | solution.py:19
  838.9 13.6 fusion.97
  867.3 40.0 %all-reduce = f32[4096]{0:T(1024)S(1)} all-reduce(f32[4096]{0:T(1024)S(1)} %copy-done.58), channel_id=13, replica_groups=mesh['tok'=2,'patch'=16] {'tok','patch'}, use_global_device_ids=true, to_apply=%region_54.55.clone | all-reduce | flops 4096 | bytes 32768
  936.6 119.1 %reduce-scatter.29.cloned.1.call-done = f32[32,1024]{1,0:T(8,128)} async-done(((f32[1024,1024]{1,0:T(8,128)}), f32[32,1024]{1,0:T(8,128)}) %reduce-scatter.29.cloned.1.call-update) | async-done | bytes 131088 | tf_op jit(solution)/shard_map/reduce_scatter | solution.py:357
  1055.8 140.8 %reduce-scatter.27.cloned.1.call-done = f32[32,1024]{1,0:T(8,128)} async-done(((f32[1024,1024]{1,0:T(8,128)}), f32[32,1024]{1,0:T(8,128)}) %reduce-scatter.27.cloned.1.call-update) | async-done | bytes 131088 | tf_op jit(solution)/shard_map/reduce_scatter | solution.py:356
  1196.6 139.8 %reduce-scatter.21.cloned.1.call-done = f32[32,1024]{1,0:T(8,128)} async-done(((f32[1024,1024]{1,0:T(8,128)}), f32[32,1024]{1,0:T(8,128)}) %reduce-scatter.21.cloned.1.call-update) | async-done | bytes 131088 | tf_op jit(solution)/shard_map/reduce_scatter | solution.py:353
  1336.3 140.2 %reduce-scatter.31.cloned.1.call-done = f32[32,1024]{1,0:T(8,128)} async-done(((f32[1024,1024]{1,0:T(8,128)}), f32[32,1024]{1,0:T(8,128)}) %reduce-scatter.31.cloned.1.call-update) | async-done | bytes 131088 | tf_op jit(solution)/shard_map/reduce_scatter | solution.py:360
  1476.5 140.6 %reduce-scatter.23.cloned.1.call-done = f32[32,1024]{1,0:T(8,128)} async-done(((f32[1024,1024]{1,0:T(8,128)}), f32[32,1024]{1,0:T(8,128)}) %reduce-scatter.23.cloned.1.call-update) | async-done | bytes 131088 | tf_op jit(solution)/shard_map/reduce_scatter | solution.py:354
  1617.1 140.6 %reduce-scatter.25.cloned.1.call-done = f32[32,1024]{1,0:T(8,128)} async-done(((f32[1024,1024]{1,0:T(8,128)}), f32[32,1024]{1,0:T(8,128)}) %reduce-scatter.25.cloned.1.call-update) | async-done | bytes 131088 | tf_op jit(solution)/shard_map/reduce_scatter | solution.py:355
  1757.7 139.8 %reduce-scatter.39.cloned.1.call-done = f32[32,1024]{1,0:T(8,128)} async-done(((f32[1024,1024]{1,0:T(8,128)}), f32[32,1024]{1,0:T(8,128)}) %reduce-scatter.39.cloned.1.call-update) | async-done | bytes 131088
  1897.5 141.0 %reduce-scatter.41.cloned.1.call-done = f32[32,1024]{1,0:T(8,128)} async-done(((f32[1024,1024]{1,0:T(8,128)}), f32[32,1024]{1,0:T(8,128)}) %reduce-scatter.41.cloned.1.call-update) | async-done | bytes 131088
  2038.5 182.6 %reduce-scatter.33.cloned.1.call-done = f32[32,4096]{1,0:T(8,128)} async-done(((f32[1024,4096]{1,0:T(8,128)}), f32[32,4096]{1,0:T(8,128)}) %reduce-scatter.33.cloned.1.call-update) | async-done | bytes 524304 | tf_op jit(solution)/shard_map/reduce_scatter | solution.py:361
  2221.0 187.6 %reduce-scatter.35.cloned.1.call-done = f32[128,1024]{1,0:T(8,128)} async-done(((f32[4096,1024]{1,0:T(8,128)}), f32[128,1024]{1,0:T(8,128)}) %reduce-scatter.35.cloned.1.call-update) | async-done | bytes 524304 | tf_op jit(solution)/shard_map/reduce_scatter | solution.py:362
  (513 shorter events, 629.6 us)
Async XLA Ops:
  7.2 207.5 %copy-start = (bf16[1024,1024]{1,0:T(8,128)(2,1)S(1)}, bf16[1024,1024]{1,0:T(8,128)(2,1)}, u32[]{:S(2)}) copy-start(bf16[1024,1024]{1,0:T(8,128)(2,1)} %param.55) | copy-start | bytes 6291460
  7.2 213.1 %all-gather.2.cloned.1.call-start = ((), (), s32[]{:S(2)}) async-start(), calls=%async_computation.12 | async-start | bytes 2162688 | tf_op jit(solution)/shard_map/all_gather | solution.py:244
  18.9 78.5 %collective-permute-start = (bf16[768,2048]{1,0:T(8,128)(2,1)}, bf16[768,2048]{1,0:T(8,128)(2,1)}, u32[]{:S(2)}, u32[]{:S(2)}) collective-permute-start(bf16[768,2048]{1,0:T(8,128)(2,1)} %pad_maximum_fusion.1), channel_id=1, source_target_pairs={{0,16},{1,17},{2,18},{3,19},{4,20},{5,21},{6,22},{7,23},{8,24},{9,... | collective-permute-start | bytes 9437192 | tf_op jit(solution)/shard_map/ppermute | solution.py:19
  25.4 753.2 %reduce-scatter.19.cloned.1.call-start = ((), (), s32[]{:S(2)}) async-start(), calls=%async_computation.13 | async-start | bytes 8650752 | tf_op jit(solution)/shard_map/reduce_scatter | solution.py:281
  42.2 57.4 %copy-start.14 = (bf16[768,1024]{1,0:T(8,128)(2,1)S(1)}, bf16[768,1024]{1,0:T(8,128)(2,1)}, u32[]{:S(2)}) copy-start(bf16[768,1024]{1,0:T(8,128)(2,1)} %copy-done.13) | copy-start | bytes 4718596
  42.2 57.4 %copy-start.16 = (bf16[768,1024]{1,0:T(8,128)(2,1)S(1)}, bf16[768,1024]{1,0:T(8,128)(2,1)}, u32[]{:S(2)}) copy-start(bf16[768,1024]{1,0:T(8,128)(2,1)} %copy-done.15) | copy-start | bytes 4718596
  233.8 27.1 %copy-start.80 = (f32[1024]{0:T(1024)S(1)}, f32[1024]{0:T(1024)}, u32[]{:S(2)}) copy-start(f32[1024]{0:T(1024)} %param.61) | copy-start | bytes 12292
  266.0 38.9 %copy-start.2 = (f32[768,1024]{1,0:T(8,128)}, f32[768,1024]{1,0:T(8,128)S(1)}, u32[]{:S(2)}) copy-start(f32[768,1024]{1,0:T(8,128)S(1)} %get-tuple-element.536) | copy-start | bytes 9437188
  266.0 73.4 %copy-start.27 = (f32[768]{0:T(1024)}, f32[768]{0:T(1024)S(1)}, u32[]{:S(2)}) copy-start(f32[768]{0:T(1024)S(1)} %broadcast_multiply_fusion.7) | copy-start | bytes 9220
  266.9 72.5 %copy-start.31 = (f32[768]{0:T(1024)}, f32[768]{0:T(1024)S(1)}, u32[]{:S(2)}) copy-start(f32[768]{0:T(1024)S(1)} %add_rsqrt_fusion) | copy-start | bytes 9220
  266.9 38.0 %copy-start.48 = (f32[768]{0:T(1024)S(1)}, f32[768]{0:T(1024)}, u32[]{:S(2)}) copy-start(f32[768]{0:T(1024)} %compare_convert_fusion) | copy-start | bytes 9220
  429.8 497.9 %reduce-scatter.37.cloned.1.call-start = ((), (), s32[]{:S(2)}) async-start(), calls=%async_computation.22 | async-start | bytes 540672
  696.6 71.2 %collective-permute-start.1 = (bf16[768,2048]{0,1:T(8,128)(2,1)S(1)}, bf16[768,2048]{0,1:T(8,128)(2,1)S(1)}, u32[]{:S(2)}, u32[]{:S(2)}) collective-permute-start(bf16[768,2048]{0,1:T(8,128)(2,1)S(1)} %pad_maximum_fusion.4), channel_id=1, source_target_pairs={{16,0},{17,1},{18,2},{19,3},{20,4},{21,5},{22,6},{23,7},{24,8},{25... | collective-permute-start | bytes 9437192 | tf_op jit(solution)/shard_map/ppermute | solution.py:19
  780.8 275.0 %reduce-scatter.29.cloned.1.call-start = ((), (), s32[]{:S(2)}) async-start(), calls=%async_computation.18 | async-start | bytes 4325376 | tf_op jit(solution)/shard_map/reduce_scatter | solution.py:357
  787.5 409.1 %reduce-scatter.27.cloned.1.call-start = ((), (), s32[]{:S(2)}) async-start(), calls=%async_computation.17 | async-start | bytes 4325376 | tf_op jit(solution)/shard_map/reduce_scatter | solution.py:356
  793.6 542.7 %reduce-scatter.21.cloned.1.call-start = ((), (), s32[]{:S(2)}) async-start(), calls=%async_computation.14 | async-start | bytes 4325376 | tf_op jit(solution)/shard_map/reduce_scatter | solution.py:353
  800.4 676.2 %reduce-scatter.31.cloned.1.call-start = ((), (), s32[]{:S(2)}) async-start(), calls=%async_computation.19 | async-start | bytes 4325376 | tf_op jit(solution)/shard_map/reduce_scatter | solution.py:360
  806.5 810.6 %reduce-scatter.23.cloned.1.call-start = ((), (), s32[]{:S(2)}) async-start(), calls=%async_computation.15 | async-start | bytes 4325376 | tf_op jit(solution)/shard_map/reduce_scatter | solution.py:354
  812.6 945.1 %reduce-scatter.25.cloned.1.call-start = ((), (), s32[]{:S(2)}) async-start(), calls=%async_computation.16 | async-start | bytes 4325376 | tf_op jit(solution)/shard_map/reduce_scatter | solution.py:355
  818.7 1078.8 %reduce-scatter.39.cloned.1.call-start = ((), (), s32[]{:S(2)}) async-start(), calls=%async_computation.23 | async-start | bytes 4325376
  828.9 1209.6 %reduce-scatter.41.cloned.1.call-start = ((), (), s32[]{:S(2)}) async-start(), calls=%async_computation.24 | async-start | bytes 4325376
  838.2 1382.8 %reduce-scatter.33.cloned.1.call-start = ((), (), s32[]{:S(2)}) async-start(), calls=%async_computation.20 | async-start | bytes 17301504 | tf_op jit(solution)/shard_map/reduce_scatter | solution.py:361
  852.5 1556.1 %reduce-scatter.35.cloned.1.call-start = ((), (), s32[]{:S(2)}) async-start(), calls=%async_computation.21 | async-start | bytes 17301504 | tf_op jit(solution)/shard_map/reduce_scatter | solution.py:362
  866.6 41.3 %copy-start.85 = (f32[1024]{0:T(1024)S(1)}, f32[1024]{0:T(1024)}, u32[]{:S(2)}) copy-start(f32[1024]{0:T(1024)} %param.67) | copy-start | bytes 12292
  (90 other events, 421.2 us)
Sparse Core Ops, SparseCore 0:
  25.5 58.1 all-gather.1
  429.9 151.2 reduce-scatter.18
  780.9 134.6 reduce-scatter.36
  918.4 137.3 reduce-scatter.28
  1058.6 137.9 reduce-scatter.26
  1199.4 136.9 reduce-scatter.20
  1339.3 137.1 reduce-scatter.30
  1479.5 137.5 reduce-scatter.22
  1620.0 137.5 reduce-scatter.24
  1760.5 136.9 reduce-scatter.38
  1900.5 137.9 reduce-scatter.40
  2041.3 179.6 reduce-scatter.32
  2224.0 184.5 reduce-scatter.34
where the time goes:
time: 2420 us
  waiting for transfers between devices  1590 us (66%)
  matrix products  449 us (19%)
  local copies, waits for them, and re-layouts  168 us (7%)
  other arithmetic  143 us (6%)
  blocking collectives  40 us (2%)
    unnamed x16, waiting for transfers between devices  281 us
    reduce_scatter x1, waiting for transfers between devices, local(): lax.psum_scatter(reduce_weight_part, ('tok', 'patch'), scatter_dimension=...  188 us
    reduce_scatter x1, waiting for transfers between devices, local(): lax.psum_scatter(expand_weight_part, ('tok', 'patch'), scatter_dimension=...  183 us
    reduce_scatter x1, waiting for transfers between devices, local(): lax.psum_scatter(output_weight_part, ('tok', 'patch'), scatter_dimension=...  141 us
    reduce_scatter x1, waiting for transfers between devices, local(): lax.psum_scatter(value_weight_part, ('tok', 'patch'), scatter_dimension=0...  141 us
    reduce_scatter x1, waiting for transfers between devices, local(): lax.psum_scatter(key_weight_part, ('tok', 'patch'), scatter_dimension=0,...  141 us
    reduce_scatter x1, waiting for transfers between devices, local(): lax.psum_scatter(merge_weight_part, ('tok', 'patch'), scatter_dimension=0...  140 us
    reduce_scatter x1, waiting for transfers between devices, local(): lax.psum_scatter(query_weight_part, ('tok', 'patch'), scatter_dimension=0...  140 us
  transfers between devices with their start and end apart: 15, of which 12 were waited for; matrix products, arithmetic and copies ran while one was open for 22% of the time, Pallas kernels for 0%

commit v1 on v0

--- a/solution.py
+++ b/solution.py
@@ -168,13 +168,88 @@
     return jax.nn.gelu(values, approximate=False)
 
 
-def page_slicer(page_rows_grad, page_start, span):
-    page_length = page_rows_grad.shape[0]
-    wanted = jnp.arange(span, dtype=jnp.int32)
-    offsets = wanted - jnp.asarray(page_start)
-    inside = (offsets >= 0) & (offsets < page_length)
-    picked = jnp.take(page_rows_grad, jnp.clip(offsets, 0, page_length - 1), axis=0)
-    return jnp.where(inside[:, None], picked, jnp.zeros_like(picked))
+def other_of(value, axis, flip):
+    pairs = [(i, i ^ flip) for i in range(lax.axis_size(axis))]
+    return lax.ppermute(value, axis, pairs)
+
+
+def digit_axes():
+    patch_bits = lax.axis_size("patch").bit_length() - 1
+    return [("tok", 0)] + [("patch", bit) for bit in reversed(range(patch_bits))]
+
+
+def my_digit(axis, bit):
+    return (lax.axis_index(axis) >> bit) & 1
+
+
+def halve(stacked, place, axis, bit):
+    mine = my_digit(axis, bit)
+    leaving = lax.dynamic_index_in_dim(stacked, 1 - mine, place, keepdims=False)
+    staying = lax.dynamic_index_in_dim(stacked, mine, place, keepdims=False)
+    arrived = other_of(leaving, axis, 1 << bit)
+    total = staying.astype(jnp.float32) + arrived.astype(jnp.float32)
+    return total.astype(stacked.dtype)
+
+
+def halve_all(stacked, order):
+    axes = digit_axes()
+    left = list(axes)
+    for step in order:
+        place = left.index(step)
+        stacked = halve(stacked, place, *step)
+        left.pop(place)
+    return stacked
+
+
+def split_order(first):
+    rest = [step for step in reversed(digit_axes()) if step not in (("patch", 0), ("tok", 0))]
+    if first == "tok":
+        return [("tok", 0)] + rest
+    return rest[:1] + [("tok", 0)] + rest[1:]
+
+
+def scatter_columns(make_half, width, first):
+    half = width // 2
+    core = my_digit("patch", 0)
+    leaving = make_half((1 - core) * half, half, None).astype(jnp.bfloat16)
+    arrived = other_of(leaving, "patch", 1)
+    total = make_half(core * half, half, arrived).astype(jnp.bfloat16)
+    digits = len(digit_axes())
+    rows = total.shape[0] >> digits
+    stacked = total.reshape((2,) * digits + (rows, half))
+    both = halve_all(stacked, split_order(first))
+    own = lax.dynamic_index_in_dim(both, core, 0, keepdims=False)
+    given = lax.dynamic_index_in_dim(both, 1 - core, 0, keepdims=False)
+    taken = other_of(given, "patch", 1)
+    low_half = jnp.where(core == 0, own, taken)
+    high_half = jnp.where(core == 0, taken, own)
+    return jnp.concatenate([low_half, high_half], axis=1).astype(jnp.float32)
+
+
+def scatter_product(left, right, first):
+    def make_half(start, size, added):
+        part = product_tn(left, lax.dynamic_slice_in_dim(right, start, size, 1))
+        return part if added is None else part + added.astype(jnp.float32)
+
+    return scatter_columns(make_half, right.shape[1], first)
+
+
+def scatter_vectors(vectors):
+    digits = len(digit_axes())
+    owners = 1 << digits
+    widths = [vector.shape[0] // owners for vector in vectors]
+    table = jnp.concatenate(
+        [vector.reshape(owners, -1) for vector in vectors], axis=1
+    )
+    spare = -table.shape[1] % 128
+    table = jnp.pad(table, ((0, 0), (0, spare)))
+    stacked = table.reshape((2,) * digits + (table.shape[1],))
+    mine = halve_all(stacked, [("patch", 0)] + split_order("tok"))
+    pieces, start = [], 0
+    for width in widths:
+        pieces.append(mine[start : start + width])
+        start += width
+    return pieces
 
 
 def local(
@@ -209,26 +284,32 @@
     reduce_weight,
     reduce_bias,
 ):
+    bf16, f32 = jnp.bfloat16, jnp.float32
     head_scale = HDIM ** (-0.5)
     tok_index = lax.axis_index("tok")
     sequence = lax.axis_index("patch")
     row_count = tokens.shape[1]
     model_width = tokens.shape[2]
-    inputs = tokens[0].astype(jnp.float32)
+    lead_tokens = passed_along(tokens[0], "tok", 1)
+    gathered = lax.all_gather(patches, ("tok", "patch"), axis=0, tiled=True)
+    inputs = tokens[0].astype(f32)
     length = pick_entry(lengths, sequence)
     page_index = pick_entry(page_of, sequence)
     filled = pick_entry(page_counts, page_index)
     page_start = page_index * PAGE_SLOTS
     places = tok_index * row_count + jnp.arange(row_count, dtype=jnp.int32)
-    valid_rows = (places < length).astype(jnp.float32)[:, None]
+    valid_rows = (places < length).astype(f32)[:, None]
     normed_one, unit_one, inverse_one = layer_norm(inputs, self_gain, self_shift)
-    hidden_one = normed_one.astype(jnp.bfloat16)
-    query = ((product(hidden_one, query_weight) + query_bias) * head_scale).astype(jnp.bfloat16)
-    own_keys = product(hidden_one, key_weight).astype(jnp.bfloat16)
-    own_values = (product(hidden_one, value_weight) + value_bias).astype(jnp.bfloat16)
-    earlier = passed_along(jnp.concatenate([own_keys, own_values], axis=1), "tok", 1)
-    self_keys = jnp.concatenate([earlier[:, :model_width], own_keys], axis=0)
-    self_values = jnp.concatenate([earlier[:, model_width:], own_values], axis=0)
+    hidden_one = normed_one.astype(bf16)
+    query = ((product(hidden_one, query_weight) + query_bias) * head_scale).astype(bf16)
+    own_keys = product(hidden_one, key_weight).astype(bf16)
+    own_values = (product(hidden_one, value_weight) + value_bias).astype(bf16)
+    normed_lead, unit_lead, _ = layer_norm(lead_tokens.astype(f32), self_gain, self_shift)
+    hidden_lead = normed_lead.astype(bf16)
+    lead_keys = product(hidden_lead, key_weight).astype(bf16)
+    lead_values = (product(hidden_lead, value_weight) + value_bias).astype(bf16)
+    self_keys = jnp.concatenate([lead_keys, own_keys], axis=0)
+    self_values = jnp.concatenate([lead_values, own_values], axis=0)
     key_places = (tok_index - 1) * row_count + jnp.arange(2 * row_count, dtype=jnp.int32)
     allowed_self = (
         (key_places[None, :] <= places[:, None])
@@ -236,100 +317,98 @@
         & (key_places[None, :] < length)
     )
     self_out, self_total = attend_forward(query, self_keys, self_values, allowed_self)
-    self_mixed = self_out.astype(jnp.bfloat16)
+    self_mixed = self_out.astype(bf16)
     after_one = inputs + product(self_mixed, output_weight) + output_bias
     normed_two, unit_two, inverse_two = layer_norm(after_one, cross_gain, cross_shift)
-    hidden_two = normed_two.astype(jnp.bfloat16)
-    probe = ((product(hidden_two, probe_weight) + probe_bias) * head_scale).astype(jnp.bfloat16)
-    gathered = lax.all_gather(patches, ("tok", "patch"), axis=0, tiled=True)
+    hidden_two = normed_two.astype(bf16)
+    probe = ((product(hidden_two, probe_weight) + probe_bias) * head_scale).astype(bf16)
     page_rows = lax.dynamic_slice_in_dim(gathered, page_start, PAGE_SLOTS, 0)
-    page_keys = product(page_rows, source_key).astype(jnp.bfloat16)
-    page_values = (product(page_rows, source_value) + source_bias).astype(jnp.bfloat16)
+    page_keys = product(page_rows, source_key).astype(bf16)
+    page_values = (product(page_rows, source_value) + source_bias).astype(bf16)
     slot_index = jnp.arange(PAGE_SLOTS, dtype=jnp.int32)
     allowed_cross = jnp.broadcast_to((slot_index < filled)[None, :], (row_count, PAGE_SLOTS))
     cross_out, cross_total = attend_forward(probe, page_keys, page_values, allowed_cross)
-    cross_mixed = cross_out.astype(jnp.bfloat16)
+    cross_mixed = cross_out.astype(bf16)
     after_two = after_one + product(cross_mixed, merge_weight) + merge_bias
     normed_three, unit_three, inverse_three = layer_norm(after_two, feed_gain, feed_shift)
-    hidden_three = normed_three.astype(jnp.bfloat16)
+    hidden_three = normed_three.astype(bf16)
     pre_act = product(hidden_three, expand_weight) + expand_bias
     activated_full, gelu_pull = jax.vjp(exact_gelu, pre_act)
-    activated = activated_full.astype(jnp.bfloat16)
+    activated = activated_full.astype(bf16)
     branch = product(activated, reduce_weight) + reduce_bias
-    block_output = (valid_rows * (after_two + branch)).astype(jnp.bfloat16)
-    grad_two = valid_rows * cotangent[0].astype(jnp.float32)
-    grad_ffn = grad_two.astype(jnp.bfloat16)
-    reduce_weight_part = product_tn(activated, grad_ffn)
-    reduce_bias_part = jnp.sum(grad_ffn.astype(jnp.float32), axis=0)
-    grad_pre = gelu_pull(product_nt(grad_ffn, reduce_weight))[0].astype(jnp.bfloat16)
-    expand_weight_part = product_tn(hidden_three, grad_pre)
-    expand_bias_part = jnp.sum(grad_pre.astype(jnp.float32), axis=0)
+    block_output = (valid_rows * (after_two + branch)).astype(bf16)
+    grad_two = valid_rows * cotangent[0].astype(f32)
+    grad_ffn = grad_two.astype(bf16)
+    reduce_weight_grad = scatter_product(activated, grad_ffn, "patch")
+    reduce_bias_part = jnp.sum(grad_ffn.astype(f32), axis=0)
+    grad_pre = gelu_pull(product_nt(grad_ffn, reduce_weight))[0].astype(bf16)
+    expand_weight_grad = scatter_product(hidden_three, grad_pre, "tok")
+    expand_bias_part = jnp.sum(grad_pre.astype(f32), axis=0)
     norm_grad, feed_gain_part, feed_shift_part = norm_backward(
         product_nt(grad_pre, expand_weight), unit_three, inverse_three, feed_gain
     )
     grad_two = grad_two + norm_grad
-    grad_merge = grad_two.astype(jnp.bfloat16)
-    merge_weight_part = product_tn(cross_mixed, grad_merge)
-    merge_bias_part = jnp.sum(grad_merge.astype(jnp.float32), axis=0)
-    grad_cross_out = product_nt(grad_merge, merge_weight).astype(jnp.bfloat16)
+    grad_merge = grad_two.astype(bf16)
+    merge_weight_grad = scatter_product(cross_mixed, grad_merge, "patch")
+    merge_bias_part = jnp.sum(grad_merge.astype(f32), axis=0)
+    grad_cross_out = product_nt(grad_merge, merge_weight).astype(bf16)
     probe_raw, page_key_grad, page_value_grad = attend_backward(
         probe, page_keys, page_values, allowed_cross, cross_total, grad_cross_out
     )
-    key_float = source_key.astype(jnp.float32)
-    value_float = source_value.astype(jnp.float32)
-    pair_grads = jnp.concatenate([page_key_grad, page_value_grad], axis=1)
-    owner_grads = lax.psum_scatter(
-        page_slicer(pair_grads, page_start, patches.shape[0] * lax.axis_size(("tok", "patch"))),
-        ("tok", "patch"),
-        scatter_dimension=0,
-        tiled=True,
-    )
-    key_grad_rows = owner_grads[:, :model_width]
-    value_grad_rows = owner_grads[:, model_width:]
-    owned_float = patches.astype(jnp.float32)
-    source_key_part = precise_tn(owned_float, key_grad_rows)
-    source_value_part = precise_tn(owned_float, value_grad_rows)
-    source_bias_part = jnp.sum(value_grad_rows, axis=0)
-    patches_grad = precise_nt(key_grad_rows, key_float) + precise_nt(value_grad_rows, value_float)
-    probe_grad = probe_raw.astype(jnp.bfloat16)
-    probe_weight_part = product_tn(hidden_two, probe_grad) * head_scale
-    probe_bias_part = jnp.sum(probe_grad.astype(jnp.float32), axis=0) * head_scale
+    pair_grads = jnp.concatenate([page_key_grad, page_value_grad], axis=1).astype(bf16)
+    source_grads = scatter_product(page_rows, pair_grads, "tok")
+    source_bias_part = jnp.sum(page_value_grad, axis=0)
+    source_pair = jnp.concatenate([source_key, source_value], axis=1)
+    patch_total = patches.shape[0] * lax.axis_size(("tok", "patch"))
+
+    def patch_half(start, size, added):
+        part = product_nt(pair_grads, lax.dynamic_slice_in_dim(source_pair, start, size, 0))
+        placed = lax.dynamic_update_slice_in_dim(
+            jnp.zeros((patch_total, size), bf16), part.astype(bf16), page_start, 0
+        ).astype(f32)
+        return placed if added is None else placed + added.astype(f32)
+
+    patches_grad = scatter_columns(patch_half, model_width, "patch")
+    probe_grad = probe_raw.astype(bf16)
+    probe_weight_grad = scatter_product(hidden_two, probe_grad, "patch") * head_scale
+    probe_bias_part = jnp.sum(probe_grad.astype(f32), axis=0) * head_scale
     norm_grad, cross_gain_part, cross_shift_part = norm_backward(
         product_nt(probe_grad, probe_weight) * head_scale, unit_two, inverse_two, cross_gain
     )
     grad_one = grad_two + norm_grad
-    grad_self = grad_one.astype(jnp.bfloat16)
-    output_weight_part = product_tn(self_mixed, grad_self)
-    output_bias_part = jnp.sum(grad_self.astype(jnp.float32), axis=0)
-    grad_self_out = product_nt(grad_self, output_weight).astype(jnp.bfloat16)
+    grad_self = grad_one.astype(bf16)
+    output_weight_grad = scatter_product(self_mixed, grad_self, "patch")
+    output_bias_part = jnp.sum(grad_self.astype(f32), axis=0)
+    grad_self_out = product_nt(grad_self, output_weight).astype(bf16)
     query_raw, keys_raw, values_raw = attend_backward(
         query, self_keys, self_values, allowed_self, self_total, grad_self_out
     )
-    returned = passed_along(
-        jnp.concatenate([keys_raw[:row_count], values_raw[:row_count]], axis=1).astype(
-            jnp.bfloat16
-        ),
-        "tok",
-        -1,
-    ).astype(jnp.float32)
-    key_grad = (keys_raw[row_count:] + returned[:, :model_width]).astype(jnp.bfloat16)
-    value_grad = (values_raw[row_count:] + returned[:, model_width:]).astype(jnp.bfloat16)
-    query_grad = query_raw.astype(jnp.bfloat16)
-    query_weight_part = product_tn(hidden_one, query_grad) * head_scale
-    query_bias_part = jnp.sum(query_grad.astype(jnp.float32), axis=0) * head_scale
-    key_weight_part = product_tn(hidden_one, key_grad)
-    value_weight_part = product_tn(hidden_one, value_grad)
-    value_bias_part = jnp.sum(value_grad.astype(jnp.float32), axis=0)
-    upstream_one = (
-        product_nt(query_grad, query_weight) * head_scale
-        + product_nt(key_grad, key_weight)
-        + product_nt(value_grad, value_weight)
-    )
-    norm_grad, self_gain_part, self_shift_part = norm_backward(
-        upstream_one, unit_one, inverse_one, self_gain
-    )
+    key_grad = keys_raw.astype(bf16)
+    value_grad = values_raw.astype(bf16)
+    query_grad = (query_raw * head_scale).astype(bf16)
+    lead_upstream = product_nt(key_grad[:row_count], key_weight) + product_nt(
+        value_grad[:row_count], value_weight
+    )
+    returned = passed_along(lead_upstream.astype(bf16), "tok", -1).astype(f32)
+    own_upstream = (
+        product_nt(query_grad, query_weight)
+        + product_nt(key_grad[row_count:], key_weight)
+        + product_nt(value_grad[row_count:], value_weight)
+    )
+    both_hidden = jnp.concatenate([hidden_lead, hidden_one], axis=0)
+    pair_weight_grad = scatter_product(
+        both_hidden, jnp.concatenate([key_grad, value_grad], axis=1), "tok"
+    )
+    query_weight_grad = scatter_product(hidden_one, query_grad, "patch")
+    query_bias_part = jnp.sum(query_grad.astype(f32), axis=0)
+    value_bias_part = jnp.sum(value_grad.astype(f32), axis=0)
+    self_gain_part = jnp.sum(own_upstream * unit_one, axis=0) + jnp.sum(
+        lead_upstream * unit_lead, axis=0
+    )
+    self_shift_part = jnp.sum(own_upstream, axis=0) + jnp.sum(lead_upstream, axis=0)
+    norm_grad, _, _ = norm_backward(own_upstream + returned, unit_one, inverse_one, self_gain)
     tokens_grad = grad_one + norm_grad
-    vectors = jnp.stack(
+    sums = scatter_vectors(
         [
             self_gain_part,
             self_shift_part,
@@ -343,53 +422,38 @@
             merge_bias_part,
             feed_gain_part,
             feed_shift_part,
+            expand_bias_part,
             reduce_bias_part,
-        ],
-        axis=1,
-    )
-    summed = (
-        lax.psum_scatter(vectors, ("tok", "patch"), scatter_dimension=0, tiled=True),
-        lax.psum_scatter(expand_bias_part, ("tok", "patch"), scatter_dimension=0, tiled=True),
-        lax.psum_scatter(query_weight_part, ("tok", "patch"), scatter_dimension=0, tiled=True),
-        lax.psum_scatter(key_weight_part, ("tok", "patch"), scatter_dimension=0, tiled=True),
-        lax.psum_scatter(value_weight_part, ("tok", "patch"), scatter_dimension=0, tiled=True),
-        lax.psum_scatter(output_weight_part, ("tok", "patch"), scatter_dimension=0, tiled=True),
-        lax.psum_scatter(probe_weight_part, ("tok", "patch"), scatter_dimension=0, tiled=True),
-        lax.psum_scatter(source_key_part, ("tok", "patch"), scatter_dimension=0, tiled=True),
-        lax.psum_scatter(source_value_part, ("tok", "patch"), scatter_dimension=0, tiled=True),
-        lax.psum_scatter(merge_weight_part, ("tok", "patch"), scatter_dimension=0, tiled=True),
-        lax.psum_scatter(expand_weight_part, ("tok", "patch"), scatter_dimension=0, tiled=True),
-        lax.psum_scatter(reduce_weight_part, ("tok", "patch"), scatter_dimension=0, tiled=True),
-    )
-    vector_sums = summed[0]
+        ]
+    )
     return (
         block_output[None],
         tokens_grad[None],
         patches_grad,
-        vector_sums[:, 0],
-        vector_sums[:, 1],
-        summed[2],
-        vector_sums[:, 2],
-        summed[3],
-        summed[4],
-        vector_sums[:, 3],
-        summed[5],
-        vector_sums[:, 4],
-        vector_sums[:, 5],
-        vector_sums[:, 6],
-        summed[6],
-        vector_sums[:, 7],
-        summed[7],
-        summed[8],
-        vector_sums[:, 8],
-        summed[9],
-        vector_sums[:, 9],
-        vector_sums[:, 10],
-        vector_sums[:, 11],
-        summed[10],
-        summed[1],
-        summed[11],
-        vector_sums[:, 12],
+        sums[0],
+        sums[1],
+        query_weight_grad,
+        sums[2],
+        pair_weight_grad[:, :model_width],
+        pair_weight_grad[:, model_width:],
+        sums[3],
+        output_weight_grad,
+        sums[4],
+        sums[5],
+        sums[6],
+        probe_weight_grad,
+        sums[7],
+        source_grads[:, :model_width],
+        source_grads[:, model_width:],
+        sums[8],
+        merge_weight_grad,
+        sums[9],
+        sums[10],
+        sums[11],
+        expand_weight_grad,
+        sums[12],
+        reduce_weight_grad,
+        sums[13],
     )
 
 

time: 2420 us -> 1080 us (0.45)
  waiting for transfers between devices: 1590 us -> 258 us
  starting transfers between devices: 9.63 us -> 64.6 us
  blocking collectives: 40 us -> 0 us
  local copies, waits for them, and re-layouts: 168 us -> 132 us
  other arithmetic: 143 us -> 169 us
    reduce_scatter x9 -> x0, waiting for transfers between devices: 1190 us -> none  [the longest x1 188 us: local(): lax.psum_scatter(reduce_weight_part, ('tok', 'patch'), scatter_dimension=...]
    unnamed x16 -> x1, waiting for transfers between devices: 281 us -> 0.02 us
    ppermute x0 -> x59, waiting for transfers between devices: none -> 225 us  [other_of(): return lax.ppermute(value, axis, pairs)]
    ppermute x2, waiting for transfers between devices: 116 us -> 32.4 us  [passed_along(): return lax.ppermute(value, axis, pairs)]
    ppermute x0 -> x59, starting transfers between devices: none -> 56.9 us  [other_of(): return lax.ppermute(value, axis, pairs)]
    unnamed x1 -> x0, blocking collectives: 40 us -> none
    dot_general x10 -> x12, matrix products: 82.4 us -> 55.4 us  [product(): return jnp.dot(left, right, preferred_element_type=jnp.float32)]
    convert_element_type x2 -> x50, other arithmetic: 1.72 us -> 27.3 us  [the longest x36 9.97 us: halve(): return total.astype(stacked.dtype)]
  transfers between devices with their start and end apart: 15 -> 62, of which waited for: 12 -> 41; matrix products, arithmetic and copies ran while one was open for 22% -> 25% of each run, Pallas kernels for 0% -> 0%
where the time goes in v1:
time: 1080 us; the launch traced here: 1070 us
  matrix products  425 us (39%)
  waiting for transfers between devices  258 us (24%)
  other arithmetic  169 us (16%)
  local copies, waits for them, and re-layouts  132 us (12%)
  starting transfers between devices  64.6 us (6%)
  between operations  17.2 us (2%)
    ppermute x59, waiting for transfers between devices, other_of(): return lax.ppermute(value, axis, pairs)  225 us
    dot_general x12, matrix products, product_nt(): lax.dot_general(left, right, (((1,), (1,)), ((), ())), preferred_element_...  84.7 us
    dot_general x8, matrix products, group_backward(): jnp.einsum('qhd,khd->hqk', upstream_heads, split_heads(value_rows), prefe...  74.6 us
    convert_element_type x8, other arithmetic, group_backward(): (soft_weights * (grad_weights - row_inner)).astype(jnp.bfloat16)  59.4 us
    ppermute x59, starting transfers between devices, other_of(): return lax.ppermute(value, axis, pairs)  56.9 us
    dot_general x16, matrix products, product_tn(): lax.dot_general(left, right, (((0,), (0,)), ((), ())), preferred_element_...  56.3 us
    dot_general x12, matrix products, product(): return jnp.dot(left, right, preferred_element_type=jnp.float32)  55.4 us
    dot_general x16, matrix products, group_scores(): jnp.einsum('qhd,khd->hqk', split_heads(query), split_heads(key_rows), pre...  52.4 us
  transfers between devices with their start and end apart: 62, of which 41 were waited for; matrix products, arithmetic and copies ran while one was open for 25% of the time, Pallas kernels for 0%

profile of v1, /device:TPU:0, one launch (start us, length us, event | category | flops | bytes accessed | tf_op | source)
XLA Modules:
  0.0 1067.7 jit_solution(3349257794527920383)
XLA Ops:
  32.5 16.0 %collective-permute-done = bf16[768,1024]{1,0:T(8,128)(2,1)} collective-permute-done((bf16[768,1024]{1,0:T(8,128)(2,1)}, bf16[768,1024]{1,0:T(8,128)(2,1)}, u32[]{:S(2)}, u32[]{:S(2)}) %collective-permute-start) | collective-permute-done | bytes 1572896 | tf_op jit(solution)/shard_map/ppermute | solution.py:19
  88.0 93.5 %while.60 = (s32[]{:T(128)}, bf16[4,768,256]{1,2,0:T(8,128)(2,1)}, f32[4,4,768]{2,1,0:T(4,128)}, bf16[4,1536,256]{1,2,0:T(8,128)(2,1)}, bf16[4,768,256]{1,2,0:T(...) while((s32[]{:T(128)}, bf16[4,768,256]{1,2,0:T(8,128)(2,1)}, ...), condition=%wide.region_8.9_spmd.clone.clone, body=%wide.region_5.0_spmd.clone.sunk.clone | while | flops 1253962752 | bytes 73249928 | solution.py:115
  206.9 26.9 %while.61 = (s32[]{:T(128)}, bf16[4,768,256]{1,2,0:T(8,128)(2,1)}, f32[4,4,768]{2,1,0:T(4,128)S(1)}, bf16[4,512,256]{1,2,0:T(8,128)(2,1)S(1)}, bf16[4,768,256]{1...) while((s32[]{:T(128)}, bf16[4,768,256]{1,2,0:T(8,128)(2,1)}, ...), condition=%wide.region_16.17_spmd.clone.clone, body=%wide.region_13.16_spmd.clone.sunk.clone | while | flops 416805888 | bytes 22906968 | solution.py:115
  249.9 40.4 %convert_reduce_fusion = (f32[4096]{0:T(1024)}, bf16[768,4096]{1,0:T(8,128)(2,1)}, f32[768,4096]{1,0:T(8,128)}) fusion(f32[768,4096]{1,0:T(8,128)S(1)} %fusion.218, f32[4096]{0:T(1024)S(1)} %copy-done.80, bf16[768,1024]{1,0:T(8,128)(2,1)S(1)} %copy-done.27, bf16[4096,1024]{1,0:T(8,128)(2,1)} %param.66), kind=kOutput, calls=%fused_computation.62 | convolution fusion | flops 6678376448 | bytes 41451520 | tf_op jit(solution)/shard_map/dot_general | solution.py:56
  290.3 12.5 %multiply_reduce_fusion.2 = (f32[1024]{0:T(1024)}, f32[768]{0:T(1024)S(1)}, f32[768]{0:T(1024)S(1)}, f32[1024]{0:T(1024)}, f32[768,1024]{1,0:T(8,128)S(1)}) fusion(f32[768,1024]{1,0:T(8,128)S(1)} %get-tuple-element.500, f32[768]{0:T(1024)S(1)} %add_rsqrt_fusion, f32[768]{0:T(1024)S(1)} %broadcast_multiply_fusion.8, f32[1024]{0:T(1024)S(1)} %copy-done.82, ...), kind=kOutput, calls=%fused_computation.136 | convolution fusion | flops 6449524736 | bytes 20996096 | tf_op jit(solution)/shard_map/dot_general | solution.py:56
  315.1 49.9 %while.62 = (s32[]{:T(128)}, bf16[4,768,256]{1,2,0:T(8,128)(2,1)}, bf16[4,512,256]{1,2,0:T(8,128)(2,1)}, f32[4,512,256]{1,2,0:T(8,128)}, bf16[4,512,256]{1,2,0:T...) while((s32[]{:T(128)}, bf16[4,768,256]{1,2,0:T(8,128)(2,1)}, ...), condition=%wide.region_23.24_spmd.clone.clone, body=%wide.region_21.23_spmd.clone.sunk.clone | while | flops 1025504256 | bytes 55794800 | solution.py:154
  383.7 241.4 %while.63 = (s32[]{:T(128)}, f32[4,768,256]{1,2,0:T(8,128)}, bf16[4,1536,256]{1,2,0:T(8,128)(2,1)}, bf16[4,1536,256]{1,2,0:T(8,128)(2,1)}, bf16[4,1536,256]{1,2,...) while((s32[]{:T(128)}, f32[4,768,256]{1,2,0:T(8,128)}, ...), condition=%wide.region_28.29_spmd.clone.clone, body=%wide.region_26.28_spmd.clone.sunk.clone | while | flops 3080057856 | bytes 162104464 | solution.py:154
  398.3 16.8 %multiply_reduce_fusion.16 = (f32[4,768]{1,0:T(4,128)S(1)}, f32[4,768,1536]{2,1,0:T(8,128)}) fusion(f32[4,768,1536]{2,1,0:T(8,128)} %fusion.410, f32[4,768]{1,0:T(4,128)S(1)} %dynamic-slice_bitcast_fusion.52, pred[768,1536]{1,0:T(8,128)(4,1)S(1)} %and_and_fusion.7, bf16[768,4,64]{0,2,1:T(8,128)(2,1)S(1)} %bitcast.617, ...), kind=kOutput, calls=%fused_computation.45.clone.1.clone | convolution fusion | flops 622851072 | bytes 40132608 | tf_op jit(solution)/shard_map/while/body/eval_jaxpr/qhd,khd->hqk/dot_general | solution.py:125
  415.1 13.1 %multiply_convert_fusion.13 = bf16[4,768,1536]{2,1,0:T(8,128)(2,1)S(1)} fusion(f32[4,768,1536]{2,1,0:T(8,128)} %get-tuple-element.875, f32[4,768,1536]{2,1,0:T(8,128)} %fusion.410, f32[4,768]{1,0:T(4,128)S(1)} %get-tuple-element.876, f32[4,768]{1,0:T(4,128)S(1)} %dynamic-slice_bitcast_fusion.52, pred[768,1536]{1,0:T(8,128)(4,1)S(1)} %and_and_fusion.7), kind=kLoop, calls=%fused_computation.44.clone.1.clone | loop fusion | flops 23592960 | bytes 48390144 | tf_op jit(solution)/shard_map/while/body/eval_jaxpr/convert_element_type | solution.py:135
  458.5 16.8 %multiply_reduce_fusion.16 = (f32[4,768]{1,0:T(4,128)S(1)}, f32[4,768,1536]{2,1,0:T(8,128)}) fusion(f32[4,768,1536]{2,1,0:T(8,128)} %fusion.410, f32[4,768]{1,0:T(4,128)S(1)} %dynamic-slice_bitcast_fusion.52, pred[768,1536]{1,0:T(8,128)(4,1)S(1)} %and_and_fusion.7, bf16[768,4,64]{0,2,1:T(8,128)(2,1)S(1)} %bitcast.617, ...), kind=kOutput, calls=%fused_computation.45.clone.1.clone | convolution fusion | flops 622851072 | bytes 40132608 | tf_op jit(solution)/shard_map/while/body/eval_jaxpr/qhd,khd->hqk/dot_general | solution.py:125
  475.3 13.1 %multiply_convert_fusion.13 = bf16[4,768,1536]{2,1,0:T(8,128)(2,1)S(1)} fusion(f32[4,768,1536]{2,1,0:T(8,128)} %get-tuple-element.875, f32[4,768,1536]{2,1,0:T(8,128)} %fusion.410, f32[4,768]{1,0:T(4,128)S(1)} %get-tuple-element.876, f32[4,768]{1,0:T(4,128)S(1)} %dynamic-slice_bitcast_fusion.52, pred[768,1536]{1,0:T(8,128)(4,1)S(1)} %and_and_fusion.7), kind=kLoop, calls=%fused_computation.44.clone.1.clone | loop fusion | flops 23592960 | bytes 48390144 | tf_op jit(solution)/shard_map/while/body/eval_jaxpr/convert_element_type | solution.py:135
  518.9 16.8 %multiply_reduce_fusion.16 = (f32[4,768]{1,0:T(4,128)S(1)}, f32[4,768,1536]{2,1,0:T(8,128)}) fusion(f32[4,768,1536]{2,1,0:T(8,128)} %fusion.410, f32[4,768]{1,0:T(4,128)S(1)} %dynamic-slice_bitcast_fusion.52, pred[768,1536]{1,0:T(8,128)(4,1)S(1)} %and_and_fusion.7, bf16[768,4,64]{0,2,1:T(8,128)(2,1)S(1)} %bitcast.617, ...), kind=kOutput, calls=%fused_computation.45.clone.1.clone | convolution fusion | flops 622851072 | bytes 40132608 | tf_op jit(solution)/shard_map/while/body/eval_jaxpr/qhd,khd->hqk/dot_general | solution.py:125
  535.6 13.1 %multiply_convert_fusion.13 = bf16[4,768,1536]{2,1,0:T(8,128)(2,1)S(1)} fusion(f32[4,768,1536]{2,1,0:T(8,128)} %get-tuple-element.875, f32[4,768,1536]{2,1,0:T(8,128)} %fusion.410, f32[4,768]{1,0:T(4,128)S(1)} %get-tuple-element.876, f32[4,768]{1,0:T(4,128)S(1)} %dynamic-slice_bitcast_fusion.52, pred[768,1536]{1,0:T(8,128)(4,1)S(1)} %and_and_fusion.7), kind=kLoop, calls=%fused_computation.44.clone.1.clone | loop fusion | flops 23592960 | bytes 48390144 | tf_op jit(solution)/shard_map/while/body/eval_jaxpr/convert_element_type | solution.py:135
  579.1 16.8 %multiply_reduce_fusion.16 = (f32[4,768]{1,0:T(4,128)S(1)}, f32[4,768,1536]{2,1,0:T(8,128)}) fusion(f32[4,768,1536]{2,1,0:T(8,128)} %fusion.410, f32[4,768]{1,0:T(4,128)S(1)} %dynamic-slice_bitcast_fusion.52, pred[768,1536]{1,0:T(8,128)(4,1)S(1)} %and_and_fusion.7, bf16[768,4,64]{0,2,1:T(8,128)(2,1)S(1)} %bitcast.617, ...), kind=kOutput, calls=%fused_computation.45.clone.1.clone | convolution fusion | flops 622851072 | bytes 40132608 | tf_op jit(solution)/shard_map/while/body/eval_jaxpr/qhd,khd->hqk/dot_general | solution.py:125
  595.9 13.1 %multiply_convert_fusion.13 = bf16[4,768,1536]{2,1,0:T(8,128)(2,1)S(1)} fusion(f32[4,768,1536]{2,1,0:T(8,128)} %get-tuple-element.875, f32[4,768,1536]{2,1,0:T(8,128)} %fusion.410, f32[4,768]{1,0:T(4,128)S(1)} %get-tuple-element.876, f32[4,768]{1,0:T(4,128)S(1)} %dynamic-slice_bitcast_fusion.52, pred[768,1536]{1,0:T(8,128)(4,1)S(1)} %and_and_fusion.7), kind=kLoop, calls=%fused_computation.44.clone.1.clone | loop fusion | flops 23592960 | bytes 48390144 | tf_op jit(solution)/shard_map/while/body/eval_jaxpr/convert_element_type | solution.py:135
  661.7 10.2 fusion.82
  727.7 16.4 %collective-permute-done.1 = bf16[768,1024]{1,0:T(8,128)(2,1)S(1)} collective-permute-done((bf16[768,1024]{1,0:T(8,128)(2,1)S(1)}, bf16[768,1024]{1,0:T(8,128)(2,1)S(1)}, u32[]{:S(2)}, u32[]{:S(2)}) %collective-permute-start.1) | collective-permute-done | bytes 1572896 | tf_op jit(solution)/shard_map/ppermute | solution.py:19
  881.8 16.3 %collective-permute-done.38 = bf16[2,2,2,2,32,1024]{5,4,3,2,1,0:T(8,128)(2,1)S(1)} collective-permute-done((bf16[2,2,2,2,32,1024]{5,4,3,2,1,0:T(8,128)(2,1)S(1)}, bf16[2,2,2,2,32,1024]{5,4,3,2,1,0:T(8,128)(2,1)S(1)}, u32[]{:S(2)}, u32[]{:S(2)}) %collective-permute-start.38) | collective-permute-done | bytes 1048608 | tf_op jit(solution)/shard_map/ppermute | solution.py:173
  900.3 19.9 %collective-permute-done.20 = bf16[2,2,2,2,32,1024]{5,4,3,2,1,0:T(8,128)(2,1)S(1)} collective-permute-done((bf16[2,2,2,2,32,1024]{5,4,3,2,1,0:T(8,128)(2,1)S(1)}, bf16[2,2,2,2,32,1024]{5,4,3,2,1,0:T(8,128)(2,1)S(1)}, u32[]{:S(2)}, u32[]{:S(2)}) %collective-permute-start.20) | collective-permute-done | bytes 1048608 | tf_op jit(solution)/shard_map/ppermute | solution.py:173
  924.1 10.2 collective-permute-done.21
  962.8 24.4 %collective-permute-done.56 = bf16[2,2,2,2,128,512]{5,4,3,2,1,0:T(8,128)(2,1)S(1)} collective-permute-done((bf16[2,2,2,2,128,512]{5,4,3,2,1,0:T(8,128)(2,1)S(1)}, bf16[2,2,2,2,128,512]{5,4,3,2,1,0:T(8,128)(2,1)S(1)}, u32[]{:S(2)}, u32[]{:S(2)}) %collective-permute-start.56) | collective-permute-done | bytes 2097184 | tf_op jit(solution)/shard_map/ppermute | solution.py:173
  999.6 17.2 %collective-permute-done.57 = bf16[2,2,2,128,512]{4,3,2,1,0:T(8,128)(2,1)S(1)} collective-permute-done((bf16[2,2,2,128,512]{4,3,2,1,0:T(8,128)(2,1)S(1)}, bf16[2,2,2,128,512]{4,3,2,1,0:T(8,128)(2,1)S(1)}, u32[]{:S(2)}, u32[]{:S(2)}) %collective-permute-start.57) | collective-permute-done | bytes 1048608 | tf_op jit(solution)/shard_map/ppermute | solution.py:173
  1020.5 14.3 %collective-permute-done.58 = bf16[2,2,128,512]{3,2,1,0:T(8,128)(2,1)S(1)} collective-permute-done((bf16[2,2,128,512]{3,2,1,0:T(8,128)(2,1)S(1)}, bf16[2,2,128,512]{3,2,1,0:T(8,128)(2,1)S(1)}, u32[]{:S(2)}, u32[]{:S(2)}) %collective-permute-start.58) | collective-permute-done | bytes 524320 | tf_op jit(solution)/shard_map/ppermute | solution.py:173
  1035.3 10.2 collective-permute-done.52
  (778 shorter events, 721.2 us)
Async XLA Ops:
  7.2 187.5 %all-gather.2.cloned.1.call-start = ((), (), s32[]{:S(2)}) async-start(), calls=%async_computation | async-start | bytes 2162688 | tf_op jit(solution)/shard_map/all_gather | solution.py:294
  7.3 41.3 %collective-permute-start = (bf16[768,1024]{1,0:T(8,128)(2,1)}, bf16[768,1024]{1,0:T(8,128)(2,1)}, u32[]{:S(2)}, u32[]{:S(2)}) collective-permute-start(bf16[768,1024]{1,0:T(8,128)(2,1)} %bitcast.629), channel_id=1, source_target_pairs={{0,16},{1,17},{2,18},{3,19},{4,20},{5,21},{6,22},{7,23},{8,24},{9,... | collective-permute-start | bytes 4718600 | tf_op jit(solution)/shard_map/ppermute | solution.py:19
  646.3 288.4 %collective-permute-start.55 = (bf16[4096,512]{1,0:T(8,128)(2,1)}, bf16[4096,512]{1,0:T(8,128)(2,1)}, u32[]{:S(2)}, u32[]{:S(2)}) collective-permute-start(bf16[4096,512]{1,0:T(8,128)(2,1)} %convolution_convert_fusion), channel_id=1, source_target_pairs={{0,1},{1,0},{2,3},{3,2},{4,5},{5,4},{6,7},{7,6},{8,9},{9,8},{10,11... | collective-permute-start | bytes 12582920 | tf_op jit(solution)/shard_map/ppermute | solution.py:173
  651.5 291.0 %collective-permute-start.49 = (bf16[1024,2048]{1,0:T(8,128)(2,1)}, bf16[1024,2048]{1,0:T(8,128)(2,1)}, u32[]{:S(2)}, u32[]{:S(2)}) collective-permute-start(bf16[1024,2048]{1,0:T(8,128)(2,1)} %convolution_convert_fusion.1), channel_id=1, source_target_pairs={{0,1},{1,0},{2,3},{3,2},{4,5},{5,4},{6,7},{7,6},{8,9},{9,8},{10,11... | collective-permute-start | bytes 12582920 | tf_op jit(solution)/shard_map/ppermute | solution.py:173
  652.0 45.5 %collective-permute-start.43 = (bf16[1024,512]{1,0:T(8,128)(2,1)}, bf16[1024,512]{1,0:T(8,128)(2,1)}, u32[]{:S(2)}, u32[]{:S(2)}) collective-permute-start(bf16[1024,512]{1,0:T(8,128)(2,1)} %convolution_convert_fusion.7), channel_id=1, source_target_pairs={{0,1},{1,0},{2,3},{3,2},{4,5},{5,4},{6,7},{7,6},{8,9},{9,8},{10,11... | collective-permute-start | bytes 3145736 | tf_op jit(solution)/shard_map/ppermute | solution.py:173
  654.0 47.0 %collective-permute-start.31 = (bf16[1024,512]{1,0:T(8,128)(2,1)}, bf16[1024,512]{1,0:T(8,128)(2,1)}, u32[]{:S(2)}, u32[]{:S(2)}) collective-permute-start(bf16[1024,512]{1,0:T(8,128)(2,1)} %convolution_convert_fusion.8), channel_id=1, source_target_pairs={{0,1},{1,0},{2,3},{3,2},{4,5},{5,4},{6,7},{7,6},{8,9},{9,8},{10,11... | collective-permute-start | bytes 3145736 | tf_op jit(solution)/shard_map/ppermute | solution.py:173
  654.6 50.0 %collective-permute-start.25 = (bf16[1024,512]{1,0:T(8,128)(2,1)}, bf16[1024,512]{1,0:T(8,128)(2,1)}, u32[]{:S(2)}, u32[]{:S(2)}) collective-permute-start(bf16[1024,512]{1,0:T(8,128)(2,1)} %convolution_convert_fusion.9), channel_id=1, source_target_pairs={{0,1},{1,0},{2,3},{3,2},{4,5},{5,4},{6,7},{7,6},{8,9},{9,8},{10,11... | collective-permute-start | bytes 3145736 | tf_op jit(solution)/shard_map/ppermute | solution.py:173
  704.8 39.2 %collective-permute-start.1 = (bf16[768,1024]{1,0:T(8,128)(2,1)S(1)}, bf16[768,1024]{1,0:T(8,128)(2,1)S(1)}, u32[]{:S(2)}, u32[]{:S(2)}) collective-permute-start(bf16[768,1024]{1,0:T(8,128)(2,1)S(1)} %copy-done.110), channel_id=1, source_target_pairs={{16,0},{17,1},{18,2},{19,3},{20,4},{21,5},{22,6},{23,7},{24,8},{25... | collective-permute-start | bytes 4718600 | tf_op jit(solution)/shard_map/ppermute | solution.py:19
  713.8 38.0 %collective-permute-start.32 = (bf16[2,2,2,2,32,512]{5,4,3,2,1,0:T(8,128)(2,1)}, bf16[2,2,2,2,32,512]{5,4,3,2,1,0:T(8,128)(2,1)}, u32[]{:S(2)}, u32[]{:S(2)}) collective-permute-start(bf16[2,2,2,2,32,512]{5,4,3,2,1,0:T(8,128)(2,1)} %dynamic-slice_bitcast_fusion.12), channel_id=1, source_target_pairs={{0,2},{1,3},{2,0},{3,1},{4,6},{5,7},{6,4},{7,5},{8,10},{9,11},{10,... | collective-permute-start | bytes 1572872 | tf_op jit(solution)/shard_map/ppermute | solution.py:173
  725.2 28.2 %collective-permute-start.26 = (bf16[2,2,2,2,32,512]{5,4,3,2,1,0:T(8,128)(2,1)}, bf16[2,2,2,2,32,512]{5,4,3,2,1,0:T(8,128)(2,1)}, u32[]{:S(2)}, u32[]{:S(2)}) collective-permute-start(bf16[2,2,2,2,32,512]{5,4,3,2,1,0:T(8,128)(2,1)} %dynamic-slice_bitcast_fusion.13), channel_id=1, source_target_pairs={{0,2},{1,3},{2,0},{3,1},{4,6},{5,7},{6,4},{7,5},{8,10},{9,11},{10,... | collective-permute-start | bytes 1572872 | tf_op jit(solution)/shard_map/ppermute | solution.py:173
  751.8 117.9 %collective-permute-start.37 = (bf16[1024,1024]{1,0:T(8,128)(2,1)}, bf16[1024,1024]{1,0:T(8,128)(2,1)S(1)}, u32[]{:S(2)}, u32[]{:S(2)}) collective-permute-start(bf16[1024,1024]{1,0:T(8,128)(2,1)} %convolution_convert_fusion.2), channel_id=1, source_target_pairs={{0,1},{1,0},{2,3},{3,2},{4,5},{5,4},{6,7},{7,6},{8,9},{9,8},{10,11... | collective-permute-start | bytes 6291464 | tf_op jit(solution)/shard_map/ppermute | solution.py:173
  759.2 31.7 %collective-permute-start.45 = (bf16[2,2,2,32,512]{4,3,2,1,0:T(8,128)(2,1)S(1)}, bf16[2,2,2,32,512]{4,3,2,1,0:T(8,128)(2,1)S(1)}, u32[]{:S(2)}, u32[]{:S(2)}) collective-permute-start(bf16[2,2,2,32,512]{4,3,2,1,0:T(8,128)(2,1)S(1)} %dynamic-slice_bitcast_fusion.19), channel_id=1, source_target_pairs={{0,16},{16,0},{1,17},{17,1},{2,18},{18,2},{3,19},{19,3},{4,20},{20... | collective-permute-start | bytes 786440 | tf_op jit(solution)/shard_map/ppermute | solution.py:173
  805.8 68.3 %collective-permute-start.19 = (bf16[1024,1024]{1,0:T(8,128)(2,1)S(1)}, bf16[1024,1024]{1,0:T(8,128)(2,1)S(1)}, u32[]{:S(2)}, u32[]{:S(2)}) collective-permute-start(bf16[1024,1024]{1,0:T(8,128)(2,1)S(1)} %copy-done.109), channel_id=1, source_target_pairs={{0,1},{1,0},{2,3},{3,2},{4,5},{5,4},{6,7},{7,6},{8,9},{9,8},{10,11... | collective-permute-start | bytes 6291464 | tf_op jit(solution)/shard_map/ppermute | solution.py:173
  871.8 26.3 %collective-permute-start.38 = (bf16[2,2,2,2,32,1024]{5,4,3,2,1,0:T(8,128)(2,1)S(1)}, bf16[2,2,2,2,32,1024]{5,4,3,2,1,0:T(8,128)(2,1)S(1)}, u32[]{:S(2)}, u32[]{:S(2)}) collective-permute-start(bf16[2,2,2,2,32,1024]{5,4,3,2,1,0:T(8,128)(2,1)S(1)} %dynamic-slice_bitcast_fusion.6), channel_id=1, source_target_pairs={{0,16},{16,0},{1,17},{17,1},{2,18},{18,2},{3,19},{19,3},{4,20},{20... | collective-permute-start | bytes 3145736 | tf_op jit(solution)/shard_map/ppermute | solution.py:173
  878.3 41.9 %collective-permute-start.20 = (bf16[2,2,2,2,32,1024]{5,4,3,2,1,0:T(8,128)(2,1)S(1)}, bf16[2,2,2,2,32,1024]{5,4,3,2,1,0:T(8,128)(2,1)S(1)}, u32[]{:S(2)}, u32[]{:S(2)}) collective-permute-start(bf16[2,2,2,2,32,1024]{5,4,3,2,1,0:T(8,128)(2,1)S(1)} %dynamic-slice_bitcast_fusion.7), channel_id=1, source_target_pairs={{0,16},{16,0},{1,17},{17,1},{2,18},{18,2},{3,19},{19,3},{4,20},{20... | collective-permute-start | bytes 3145736 | tf_op jit(solution)/shard_map/ppermute | solution.py:173
  898.6 25.2 %collective-permute-start.39 = (bf16[2,2,2,32,1024]{4,3,2,1,0:T(8,128)(2,1)S(1)}, bf16[2,2,2,32,1024]{4,3,2,1,0:T(8,128)(2,1)S(1)}, u32[]{:S(2)}, u32[]{:S(2)}) collective-permute-start(bf16[2,2,2,32,1024]{4,3,2,1,0:T(8,128)(2,1)S(1)} %dynamic-slice_bitcast_fusion.11), channel_id=1, source_target_pairs={{0,2},{1,3},{2,0},{3,1},{4,6},{5,7},{6,4},{7,5},{8,10},{9,11},{10,... | collective-permute-start | bytes 1572872 | tf_op jit(solution)/shard_map/ppermute | solution.py:173
  924.0 25.6 %collective-permute-start.40 = (bf16[2,2,32,1024]{3,2,1,0:T(8,128)(2,1)S(1)}, bf16[2,2,32,1024]{3,2,1,0:T(8,128)(2,1)S(1)}, u32[]{:S(2)}, u32[]{:S(2)}) collective-permute-start(bf16[2,2,32,1024]{3,2,1,0:T(8,128)(2,1)S(1)} %dynamic-slice_bitcast_fusion.20), channel_id=1, source_target_pairs={{0,4},{1,5},{2,6},{3,7},{4,0},{5,1},{6,2},{7,3},{8,12},{9,13},{10,... | collective-permute-start | bytes 786440 | tf_op jit(solution)/shard_map/ppermute | solution.py:173
  940.7 46.5 %collective-permute-start.56 = (bf16[2,2,2,2,128,512]{5,4,3,2,1,0:T(8,128)(2,1)S(1)}, bf16[2,2,2,2,128,512]{5,4,3,2,1,0:T(8,128)(2,1)S(1)}, u32[]{:S(2)}, u32[]{:S(2)}) collective-permute-start(bf16[2,2,2,2,128,512]{5,4,3,2,1,0:T(8,128)(2,1)S(1)} %dynamic-slice_bitcast_fusion.2), channel_id=1, source_target_pairs={{0,2},{1,3},{2,0},{3,1},{4,6},{5,7},{6,4},{7,5},{8,10},{9,11},{10,... | collective-permute-start | bytes 6291464 | tf_op jit(solution)/shard_map/ppermute | solution.py:173
  948.1 48.6 %collective-permute-start.50 = (bf16[2,2,2,2,32,2048]{5,4,3,2,1,0:T(8,128)(2,1)S(1)}, bf16[2,2,2,2,32,2048]{5,4,3,2,1,0:T(8,128)(2,1)S(1)}, u32[]{:S(2)}, u32[]{:S(2)}) collective-permute-start(bf16[2,2,2,2,32,2048]{5,4,3,2,1,0:T(8,128)(2,1)S(1)} %dynamic-slice_bitcast_fusion.3), channel_id=1, source_target_pairs={{0,16},{16,0},{1,17},{17,1},{2,18},{18,2},{3,19},{19,3},{4,20},{20... | collective-permute-start | bytes 6291464 | tf_op jit(solution)/shard_map/ppermute | solution.py:173
  962.7 36.1 %collective-permute-start.24 = (bf16[32,1024]{1,0:T(8,128)(2,1)S(1)}, bf16[32,1024]{1,0:T(8,128)(2,1)S(1)}, u32[]{:S(2)}, u32[]{:S(2)}) collective-permute-start(bf16[32,1024]{1,0:T(8,128)(2,1)S(1)} %dynamic-slice_bitcast_fusion.39), channel_id=1, source_target_pairs={{0,1},{1,0},{2,3},{3,2},{4,5},{5,4},{6,7},{7,6},{8,9},{9,8},{10,11... | collective-permute-start | bytes 196616 | tf_op jit(solution)/shard_map/ppermute | solution.py:173
  988.0 28.8 %collective-permute-start.57 = (bf16[2,2,2,128,512]{4,3,2,1,0:T(8,128)(2,1)S(1)}, bf16[2,2,2,128,512]{4,3,2,1,0:T(8,128)(2,1)S(1)}, u32[]{:S(2)}, u32[]{:S(2)}) collective-permute-start(bf16[2,2,2,128,512]{4,3,2,1,0:T(8,128)(2,1)S(1)} %dynamic-slice_bitcast_fusion.4), channel_id=1, source_target_pairs={{0,16},{16,0},{1,17},{17,1},{2,18},{18,2},{3,19},{19,3},{4,20},{20... | collective-permute-start | bytes 3145736 | tf_op jit(solution)/shard_map/ppermute | solution.py:173
  997.6 21.1 %collective-permute-start.51 = (bf16[2,2,2,32,2048]{4,3,2,1,0:T(8,128)(2,1)S(1)}, bf16[2,2,2,32,2048]{4,3,2,1,0:T(8,128)(2,1)S(1)}, u32[]{:S(2)}, u32[]{:S(2)}) collective-permute-start(bf16[2,2,2,32,2048]{4,3,2,1,0:T(8,128)(2,1)S(1)} %dynamic-slice_bitcast_fusion.5), channel_id=1, source_target_pairs={{0,2},{1,3},{2,0},{3,1},{4,6},{5,7},{6,4},{7,5},{8,10},{9,11},{10,... | collective-permute-start | bytes 3145736 | tf_op jit(solution)/shard_map/ppermute | solution.py:173
  1019.2 26.4 %collective-permute-start.52 = (bf16[2,2,32,2048]{3,2,1,0:T(8,128)(2,1)S(1)}, bf16[2,2,32,2048]{3,2,1,0:T(8,128)(2,1)S(1)}, u32[]{:S(2)}, u32[]{:S(2)}) collective-permute-start(bf16[2,2,32,2048]{3,2,1,0:T(8,128)(2,1)S(1)} %dynamic-slice_bitcast_fusion.9), channel_id=1, source_target_pairs={{0,4},{1,5},{2,6},{3,7},{4,0},{5,1},{6,2},{7,3},{8,12},{9,13},{10,... | collective-permute-start | bytes 1572872 | tf_op jit(solution)/shard_map/ppermute | solution.py:173
  1035.0 18.6 %collective-permute-start.59 = (bf16[2,128,512]{2,1,0:T(8,128)(2,1)S(1)}, bf16[2,128,512]{2,1,0:T(8,128)(2,1)S(1)}, u32[]{:S(2)}, u32[]{:S(2)}) collective-permute-start(bf16[2,128,512]{2,1,0:T(8,128)(2,1)S(1)} %dynamic-slice_bitcast_fusion.17), channel_id=1, source_target_pairs={{0,8},{1,9},{2,10},{3,11},{4,12},{5,13},{6,14},{7,15},{8,0},{9,1},... | collective-permute-start | bytes 786440 | tf_op jit(solution)/shard_map/ppermute | solution.py:173
  (169 other events, 1680.0 us)
Sparse Core Ops, SparseCore 0:
  13.6 58.1 all-gather.1

commit v2 on v1

v2 whole, which is shorter than its diff:
```python
import jax
import jax.numpy as jnp
from jax import lax
from jax.experimental import pallas as pl
from jax.experimental.pallas import tpu as pltpu
from jax.sharding import PartitionSpec as P

HDIM = 64
PAIR = 2 * HDIM
PAGE_SLOTS = 512
NEG_FILL = -1e30
EPS_NORM = 1e-05
LANES = 128
HIGH = lax.Precision.HIGHEST
MIB = 1 << 20
bf16, f32 = jnp.bfloat16, jnp.float32
Shape = jax.ShapeDtypeStruct


def nn(left, right):
    return lax.dot_general(
        left, right, (((1,), (0,)), ((), ())), preferred_element_type=f32
    )


def nt(left, right, precision=None):
    return lax.dot_general(
        left, right, (((1,), (1,)), ((), ())), precision=precision, preferred_element_type=f32
    )


def tn(left, right):
    return lax.dot_general(
        left, right, (((0,), (0,)), ((), ())), preferred_element_type=f32
    )


def column_sums(values):
    return jnp.sum(values.astype(f32), axis=0, keepdims=True)


def norm_unit(values):
    average = jnp.mean(values, axis=-1, keepdims=True)
    centred = values - average
    spread = jnp.mean(centred * centred, axis=-1, keepdims=True)
    inverse = lax.rsqrt(spread + EPS_NORM)
    return centred * inverse, inverse


def norm_pull(upstream, unit, inverse, gain):
    scaled = upstream * gain
    centred = scaled - jnp.mean(scaled, axis=-1, keepdims=True)
    centred = centred - unit * jnp.mean(scaled * unit, axis=-1, keepdims=True)
    return centred * inverse


def gelu_pair(values):
    share = 0.5 * (1.0 + lax.erf(values * (2.0**-0.5)))
    slope = share + values * (jnp.exp(-0.5 * values * values) * 0.3989422804014327)
    return values * share, slope


def by_core(core, value, rows):
    count, width = value.shape
    split = value.reshape(count // (2 * rows), 2, rows, width)
    first, second = split[:, 0], split[:, 1]
    pair = (jnp.where(core == 0, second, first), jnp.where(core == 0, first, second))
    return [one.reshape(count // 2, width).astype(bf16) for one in pair]


def head_lanes(head):
    lane = lax.broadcasted_iota(jnp.int32, (1, PAIR), 1)
    return (lane >= head * HDIM) & (lane < (head + 1) * HDIM)


def only(value, head):
    return jnp.where(head_lanes(head), value, jnp.zeros_like(value))


def settings(limit=48):
    return pltpu.CompilerParams(
        dimension_semantics=("arbitrary",), vmem_limit_bytes=limit * MIB
    )


def forward_rows(q_ref, parts, out_ref, total_ref, start, count, pair):
    outs, totals = [], []
    for head in range(2):
        query = only(q_ref[pl.ds(start, count), :], head)
        scores = []
        for keys, _, first, rows, mask in parts:
            score = nt(query, keys[pl.ds(first, rows), :])
            if isinstance(mask, str):
                row = lax.broadcasted_iota(jnp.int32, score.shape, 0)
                column = lax.broadcasted_iota(jnp.int32, score.shape, 1)
                score = jnp.where(column <= row, score, NEG_FILL)
            elif mask is not None:
                score = score + mask
            scores.append(score)
        row_max = scores[0].max(-1, keepdims=True)
        for score in scores[1:]:
            row_max = jnp.maximum(row_max, score.max(-1, keepdims=True))
        row_total, out = 0.0, 0.0
        for score, (_, values, first, rows, _) in zip(scores, parts):
            exponent = jnp.exp(score - row_max)
            row_total = row_total + exponent.sum(-1, keepdims=True)
            out = out + nn(exponent.astype(bf16), values[pl.ds(first, rows), :])
        outs.append(out / row_total)
        totals.append(row_max + jnp.log(row_total))
    out_ref[pl.ds(start, count), :] = jnp.where(head_lanes(0), outs[0], outs[1]).astype(bf16)
    lane = lax.broadcasted_iota(jnp.int32, (1, LANES), 1)
    held = total_ref[pl.ds(start, count), :]
    held = jnp.where(lane == 2 * pair, totals[0], held)
    total_ref[pl.ds(start, count), :] = jnp.where(lane == 2 * pair + 1, totals[1], held)


def self_forward(query, lead_keys, lead_values, own_keys, own_values, trailing, count=256):
    rows, width = query.shape

    def body(flag, q_ref, lk, lv, ok, ov, out_ref, total_ref):
        pair = pl.program_id(0)

        @pl.when(pair == 0)
        def _():
            total_ref[...] = jnp.zeros_like(total_ref)

        def go(with_lead):
            for start in range(0, rows, count):
                parts = [(lk, lv, 0, rows, None)] if with_lead else []
                if start:
                    parts.append((ok, ov, 0, start, None))
                parts.append((ok, ov, start, count, "causal"))
                forward_rows(q_ref, parts, out_ref, total_ref, start, count, pair)

        @pl.when(flag[0] == 1)
        def _():
            go(True)

        @pl.when(flag[0] == 0)
        def _():
            go(False)

    block = pl.BlockSpec((rows, PAIR), lambda p, flag: (0, p))
    return pl.pallas_call(
        body,
        out_shape=(Shape((rows, width), bf16), Shape((rows, LANES), f32)),
        grid_spec=pltpu.PrefetchScalarGridSpec(
            num_scalar_prefetch=1,
            grid=(width // PAIR,),
            in_specs=[block] * 5,
            out_specs=[block, pl.BlockSpec((rows, LANES), lambda p, flag: (0, 0))],
        ),
        compiler_params=settings(),
        name="self_forward",
    )(trailing, query, lead_keys, lead_values, own_keys, own_values)


def cross_forward(query, keys, values, filled, count=256):
    rows, width = query.shape
    slots = keys.shape[0]

    def body(filled_ref, q_ref, k_ref, v_ref, out_ref, total_ref):
        pair = pl.program_id(0)

        @pl.when(pair == 0)
        def _():
            total_ref[...] = jnp.zeros_like(total_ref)

        slot = lax.broadcasted_iota(jnp.int32, (1, slots), 1)
        bias = jnp.where(slot < filled_ref[0], 0.0, NEG_FILL)
        for start in range(0, rows, count):
            parts = [(k_ref, v_ref, 0, slots, bias)]
            forward_rows(q_ref, parts, out_ref, total_ref, start, count, pair)

    block = pl.BlockSpec((rows, PAIR), lambda p, f: (0, p))
    page = pl.BlockSpec((slots, PAIR), lambda p, f: (0, p))
    return pl.pallas_call(
        body,
        out_shape=(Shape((rows, width), bf16), Shape((rows, LANES), f32)),
        grid_spec=pltpu.PrefetchScalarGridSpec(
            num_scalar_prefetch=1,
            grid=(width // PAIR,),
            in_specs=[block, page, page],
            out_specs=[block, pl.BlockSpec((rows, LANES), lambda p, f: (0, 0))],
        ),
        compiler_params=settings(),
        name="cross_forward",
    )(filled, query, keys, values)


def row_stats(total_ref, out_ref, grad_ref, pair):
    row = lax.broadcasted_iota(jnp.int32, (8, LANES), 0)
    lane = lax.broadcasted_iota(jnp.int32, (8, LANES), 1)
    choose = ((lane == 2 * pair + row) & (row < 2)).astype(f32)
    totals = nt(choose, total_ref[...], HIGH)
    inner = out_ref[...].astype(f32) * grad_ref[...].astype(f32)
    share = ((lane // HDIM == row) & (row < 2)).astype(f32)
    return totals, nt(share, inner, HIGH)


def backward_keys(q_ref, g_ref, keys, values, first, rows, start, stats, mask, acc, fresh):
    totals, inner = stats
    count = q_ref.shape[0] - start
    key_rows, value_rows = keys[pl.ds(first, rows), :], values[pl.ds(first, rows), :]
    key_grad = jnp.zeros((rows, PAIR), f32)
    value_grad = jnp.zeros((rows, PAIR), f32)
    for head in range(2):
        query = only(q_ref[pl.ds(start, count), :], head)
        upstream = only(g_ref[pl.ds(start, count), :], head)
        score = nt(key_rows, query)
        if isinstance(mask, str):
            row = lax.broadcasted_iota(jnp.int32, score.shape, 0)
            column = lax.broadcasted_iota(jnp.int32, score.shape, 1)
            score = jnp.where(row <= column, score, NEG_FILL)
        elif mask is not None:
            score = score + mask
        soft = jnp.exp(score - totals[head : head + 1, start:])
        grad_soft = nt(value_rows, upstream)
        grad_score = (soft * (grad_soft - inner[head : head + 1, start:])).astype(bf16)
        value_grad = value_grad + nn(soft.astype(bf16), upstream)
        key_grad = key_grad + nn(grad_score, query)
        part = tn(grad_score, only(key_rows, head))
        if fresh and head == 0:
            acc[pl.ds(start, count), :] = part
        else:
            acc[pl.ds(start, count), :] += part
    return key_grad.astype(bf16), value_grad.astype(bf16)


def lead_backward(query, keys, values, out, total, grad, trailing, first, pairs, block=256):
    rows = query.shape[0]

    def body(flag, q_ref, k_ref, v_ref, out_ref, total_ref, g_ref, dq_ref, dk_ref, dv_ref):
        @pl.when(flag[0] == 1)
        def _():
            stats = row_stats(total_ref, out_ref, g_ref, pl.program_id(0) + first)
            for at in range(0, rows, block):
                dk, dv = backward_keys(
                    q_ref, g_ref, k_ref, v_ref, at, block, 0, stats, None, dq_ref, at == 0
                )
                dk_ref[pl.ds(at, block), :] = dk
                dv_ref[pl.ds(at, block), :] = dv

        @pl.when(flag[0] == 0)
        def _():
            for ref in (dq_ref, dk_ref, dv_ref):
                ref[...] = jnp.zeros_like(ref)

    source = pl.BlockSpec((rows, PAIR), lambda p, flag: (0, p + first))
    target = pl.BlockSpec((rows, PAIR), lambda p, flag: (0, p))
    fixed = pl.BlockSpec((rows, LANES), lambda p, flag: (0, 0))
    return pl.pallas_call(
        body,
        out_shape=[Shape((rows, pairs * PAIR), kind) for kind in (f32, bf16, bf16)],
        grid_spec=pltpu.PrefetchScalarGridSpec(
            num_scalar_prefetch=1,
            grid=(pairs,),
            in_specs=[source] * 4 + [fixed, source],
            out_specs=[target] * 3,
        ),
        compiler_params=settings(),
        name="lead_backward",
    )(trailing, query, keys, values, out, total, grad)


def own_backward(query, keys, values, out, total, grad, begun, first, pairs, block=256):
    rows = query.shape[0]

    def body(q_ref, k_ref, v_ref, out_ref, total_ref, g_ref, begun_ref, dq_ref, dk_ref, dv_ref, acc):
        acc[...] = begun_ref[...]
        stats = row_stats(total_ref, out_ref, g_ref, pl.program_id(0) + first)
        for at in range(0, rows, block):
            dk, dv = backward_keys(
                q_ref, g_ref, k_ref, v_ref, at, block, at, stats, "causal", acc, False
            )
            dk_ref[pl.ds(at, block), :] = dk
            dv_ref[pl.ds(at, block), :] = dv
        dq_ref[...] = (acc[...] * (HDIM**-0.5)).astype(bf16)

    source = pl.BlockSpec((rows, PAIR), lambda p: (0, p + first))
    target = pl.BlockSpec((rows, PAIR), lambda p: (0, p))
    fixed = pl.BlockSpec((rows, LANES), lambda p: (0, 0))
    return pl.pallas_call(
        body,
        out_shape=[Shape((rows, pairs * PAIR), bf16)] * 3,
        grid=(pairs,),
        in_specs=[source] * 4 + [fixed, source, target],
        out_specs=[target] * 3,
        scratch_shapes=[pltpu.VMEM((rows, PAIR), f32)],
        compiler_params=settings(),
        name="own_backward",
    )(query, keys, values, out, total, grad, begun)


def cross_backward(query, keys, values, out, total, grad, filled, first, pairs, block=256):
    rows, slots = query.shape[0], keys.shape[0]

    def body(
        filled_ref, q_ref, k_ref, v_ref, out_ref, total_ref, g_ref, dq_ref, dk_ref, dv_ref, acc
    ):
        stats = row_stats(total_ref, out_ref, g_ref, pl.program_id(0) + first)
        for at in range(0, slots, block):
            slot = lax.broadcasted_iota(jnp.int32, (block, 1), 0) + at
            bias = jnp.where(slot < filled_ref[0], 0.0, NEG_FILL)
            dk, dv = backward_keys(
                q_ref, g_ref, k_ref, v_ref, at, block, 0, stats, bias, acc, at == 0
            )
            dk_ref[pl.ds(at, block), :] = dk
            dv_ref[pl.ds(at, block), :] = dv
        dq_ref[...] = (acc[...] * (HDIM**-0.5)).astype(bf16)

    source = pl.BlockSpec((rows, PAIR), lambda p, f: (0, p + first))
    page = pl.BlockSpec((slots, PAIR), lambda p, f: (0, p + first))
    target = pl.BlockSpec((rows, PAIR), lambda p, f: (0, p))
    page_target = pl.BlockSpec((slots, PAIR), lambda p, f: (0, p))
    fixed = pl.BlockSpec((rows, LANES), lambda p, f: (0, 0))
    return pl.pallas_call(
        body,
        out_shape=[Shape((rows, pairs * PAIR), bf16)] + [Shape((slots, pairs * PAIR), bf16)] * 2,
        grid_spec=pltpu.PrefetchScalarGridSpec(
            num_scalar_prefetch=1,
            grid=(pairs,),
            in_specs=[source, page, page, source, fixed, source],
            out_specs=[target, page_target, page_target],
            scratch_shapes=[pltpu.VMEM((rows, PAIR), f32)],
        ),
        compiler_params=settings(),
        name="cross_backward",
    )(filled, query, keys, values, out, total, grad)


def feed_forward(after_one, mixed, merge, cotangent, vectors, expand, bias, reduce, info, owners):
    rows, width = after_one.shape
    hidden = expand.shape[1]
    block, tall = 512, 384
    steps, half = hidden // block, width // 2
    starts = range(0, rows, tall)

    def body(
        info_ref, after_ref, mixed_ref, merge_ref, cot_ref, vec_ref, we_ref, be_ref, wr_ref,
        out_ref, two_ref, cross_ref, rs_ref, ro_ref, es_ref, eo_ref, ms_ref, mo_ref, eb_ref,
        sums_ref, after, h, h_flip, g, branch, up, act, gp,
    ):
        step = pl.program_id(0)
        core, place, length = info_ref[0], info_ref[1], info_ref[2]

        def valid(start):
            row = lax.broadcasted_iota(jnp.int32, (tall, 1), 0) + (start + place)
            return (row < length).astype(f32)

        @pl.when(step == 0)
        def _():
            total = jnp.zeros((1, width), f32)
            for start in starts:
                at = pl.ds(start, tall)
                x = after_ref[at, :] + nn(mixed_ref[at, :], merge_ref[...]) + vec_ref[0:1, :]
                after[at, :] = x
                unit, _ = norm_unit(x)
                low = (unit * vec_ref[1:2, :] + vec_ref[2:3, :]).astype(bf16)
                h[at, :] = low
                h_flip[:, at] = low.T
                grad = (valid(start) * cot_ref[at, :].astype(f32)).astype(bf16)
                g[at, :] = grad
                total = total + column_sums(grad)
                branch[at, :] = jnp.zeros((tall, width), f32)
                up[at, :] = jnp.zeros((tall, width), f32)
            sums_ref[0:1, :] = total

        we, wr = we_ref[...], wr_ref[...]
        for start in starts:
            at = pl.ds(start, tall)
            low, slope = gelu_pair(nn(h[at, :], we) + be_ref[...])
            low = low.astype(bf16)
            act[at, :] = low
            branch[at, :] += nn(low, wr)
            grad = (nt(g[at, :], wr) * slope).astype(bf16)
            gp[at, :] = grad
            up[at, :] += nt(grad, we)
        rs_ref[...], ro_ref[...] = by_core(core, tn(act[...], g[...]), hidden // owners)
        es_ref[...], eo_ref[...] = by_core(core, nn(h_flip[...], gp[...]), width // owners)
        eb_ref[...] = nn(jnp.ones((8, rows), bf16), gp[...])

        @pl.when(step == steps - 1)
        def _():
            gains = jnp.zeros((1, width), f32)
            shifts, merges = gains, gains
            for start in starts:
                at = pl.ds(start, tall)
                x, ok = after[at, :], valid(start)
                out_ref[at, :] = (ok * (x + branch[at, :] + vec_ref[3:4, :])).astype(bf16)
                unit, inverse = norm_unit(x)
                upstream = up[at, :]
                gains = gains + jnp.sum(upstream * unit, axis=0, keepdims=True)
                shifts = shifts + jnp.sum(upstream, axis=0, keepdims=True)
                pulled = norm_pull(upstream, unit, inverse, vec_ref[1:2, :])
                two = ok * cot_ref[at, :].astype(f32) + pulled
                two_ref[at, :] = two
                low = two.astype(bf16)
                g[at, :] = low
                merges = merges + column_sums(low)
                cross_ref[at, :] = nt(low, merge_ref[...]).astype(bf16)
            ms_ref[...], mo_ref[...] = by_core(core, tn(mixed_ref[...], g[...]), width // owners)
            sums_ref[1:2, :], sums_ref[2:3, :], sums_ref[3:4, :] = gains, shifts, merges

    def once(shape):
        return pl.BlockSpec(shape, lambda i, info: (0, 0), pipeline_mode=pl.Buffered(1))

    def fixed(shape):
        return pl.BlockSpec(shape, lambda i, info: (0, 0))

    by_row = pl.BlockSpec((block // 2, width), lambda i, info: (i, 0))
    by_column = pl.BlockSpec((half, block), lambda i, info: (0, i))
    full, low = (rows, width), (rows, width)
    return pl.pallas_call(
        body,
        out_shape=[
            Shape(full, bf16), Shape(full, f32), Shape(full, bf16),
            Shape((hidden // 2, width), bf16), Shape((hidden // 2, width), bf16),
            Shape((half, hidden), bf16), Shape((half, hidden), bf16),
            Shape((half, width), bf16), Shape((half, width), bf16),
            Shape((8, hidden), f32), Shape((8, width), f32),
        ],
        grid_spec=pltpu.PrefetchScalarGridSpec(
            num_scalar_prefetch=1,
            grid=(steps,),
            in_specs=[
                once(full), once(full), once((width, width)), once(full), once((8, width)),
                pl.BlockSpec((width, block), lambda i, info: (0, i)),
                pl.BlockSpec((1, block), lambda i, info: (0, i)),
                pl.BlockSpec((block, width), lambda i, info: (i, 0)),
            ],
            out_specs=[
                fixed(full), fixed(full), fixed(full), by_row, by_row, by_column, by_column,
                fixed((half, width)), fixed((half, width)),
                pl.BlockSpec((8, block), lambda i, info: (0, i)),
                fixed((8, width)),
            ],
            scratch_shapes=[
                pltpu.VMEM(full, f32), pltpu.VMEM(low, bf16), pltpu.VMEM((width, rows), bf16),
                pltpu.VMEM(low, bf16), pltpu.VMEM(full, f32), pltpu.VMEM(full, f32),
                pltpu.VMEM((rows, block), bf16), pltpu.VMEM((rows, block), bf16),
            ],
        ),
        compiler_params=settings(60),
        name="feed_forward",
    )(info, after_one, mixed, merge, cotangent, vectors, expand, bias, reduce)


def streamed(name, body, info, inputs, outs, scratch=()):
    n, m = len(inputs), len(outs)

    def kernel(info_ref, *refs):
        ins, dests = refs[:n], refs[n : n + m]
        held, made = refs[n + m : 2 * n + m], refs[2 * n + m : 2 * n + 2 * m]
        in_sem, out_sem = refs[2 * n + 2 * m : 2 * n + 2 * m + 2]
        rest = refs[2 * n + 2 * m + 2 :]
        loads = [pltpu.make_async_copy(ins[i], held[i], in_sem.at[i]) for i in range(n)]
        for load in loads:
            load.start()
        waited, stores = set(), {}

        def need(i):
            if i not in waited:
                loads[i].wait()
                waited.add(i)
            return held[i]

        def give(i, send=False):
            if send:
                stores[i] = pltpu.make_async_copy(made[i], dests[i], out_sem.at[i])
                stores[i].start()
            return made[i]

        body(info_ref, need, give, *rest)
        for i in range(m):
            stores[i].wait()

    anywhere = pl.BlockSpec(memory_space=pl.ANY)
    return pl.pallas_call(
        kernel,
        out_shape=[Shape(shape, kind) for shape, kind in outs],
        grid_spec=pltpu.PrefetchScalarGridSpec(
            num_scalar_prefetch=1,
            grid=(1,),
            in_specs=[anywhere] * n,
            out_specs=[anywhere] * m,
            scratch_shapes=[pltpu.VMEM(value.shape, value.dtype) for value in inputs]
            + [pltpu.VMEM(shape, kind) for shape, kind in outs]
            + [pltpu.SemaphoreType.DMA((n,)), pltpu.SemaphoreType.DMA((m,))]
            + list(scratch),
        ),
        compiler_params=settings(60),
        name=name,
    )(info, *inputs)


def probe_backward(info, probe_low, probe_high, probe_weight, after_one, two, output_weight, mixed, vectors, owners):
    rows, width = after_one.shape
    half, tall = width // 2, 256

    def body(info_ref, need, give, hidden, low_grad):
        core = info_ref[0]
        left, right = need(0), need(1)
        weight = need(2)
        vec = need(7)
        x_ref, two_ref = need(3), need(4)
        gains = jnp.zeros((1, width), f32)
        shifts, outs = gains, gains
        for start in range(0, rows, tall):
            at = pl.ds(start, tall)
            up = nt(left[at, :], weight[:, :half]) + nt(right[at, :], weight[:, half:])
            unit, inverse = norm_unit(x_ref[at, :])
            hidden[at, :] = (unit * vec[0:1, :] + vec[1:2, :]).astype(bf16)
            gains = gains + jnp.sum(up * unit, axis=0, keepdims=True)
            shifts = shifts + jnp.sum(up, axis=0, keepdims=True)
            one = two_ref[at, :] + norm_pull(up, unit, inverse, vec[0:1, :])
            give(0)[at, :] = one
            low = one.astype(bf16)
            low_grad[at, :] = low
            outs = outs + column_sums(low)
            if start == 0:
                need(5)
            give(1)[at, :] = nt(low, need(5)[...]).astype(bf16)
        give(0, True)
        give(1, True)
        sums = give(4)
        sums[...] = jnp.zeros_like(sums)
        sums[0:1, :], sums[1:2, :], sums[2:3, :] = gains, shifts, outs
        sums[3:4, :half] = column_sums(left[...])
        sums[3:4, half:] = column_sums(right[...])
        give(4, True)
        mixed_ref = need(6)
        columns = (
            (0, half, hidden, left[...]),
            (half, width, hidden, right[...]),
            (width, 2 * width, mixed_ref, low_grad[...]),
        )
        for begin, end, source, grads in columns:
            pair = by_core(core, tn(source[...], grads), width // owners)
            give(2)[:, begin:end], give(3)[:, begin:end] = pair
        give(2, True)
        give(3, True)

    return streamed(
        "probe_backward",
        body,
        info,
        [probe_low, probe_high, probe_weight, after_one, two, output_weight, mixed, vectors],
        [
            ((rows, width), f32), ((rows, width), bf16),
            ((half, 2 * width), bf16), ((half, 2 * width), bf16), ((8, width), f32),
        ],
        [pltpu.VMEM((rows, width), bf16), pltpu.VMEM((rows, width), bf16)],
    )


def page_backward(
    info, key_low, key_high, value_low, value_high, page_rows, key_weight, value_weight, owners,
    patch_total,
):
    slots, width = page_rows.shape
    half = width // 2
    deep = patch_total // 2

    def body(info_ref, need, give):
        core, page = info_ref[0], info_ref[3]
        kl, kh, vl, vh = need(0)[...], need(1)[...], need(2)[...], need(3)[...]
        rows_ref = need(4)
        for i, grads in enumerate((kl, kh, vl, vh)):
            pair = by_core(core, tn(rows_ref[...], grads), width // owners)
            at = pl.ds(i * half, half)
            give(0)[:, at], give(1)[:, at] = pair
        give(0, True)
        give(1, True)
        wk, wv = need(5), need(6)
        total = nt(kl, wk[:, :half]) + nt(kh, wk[:, half:])
        total = total + nt(vl, wv[:, :half]) + nt(vh, wv[:, half:])
        pair = by_core(core, total, patch_total // owners)
        at = pl.ds(pl.multiple_of(page * (slots // 2), slots // 2), slots // 2)
        for which in range(2):
            give(2 + which)[...] = jnp.zeros((deep, width), bf16)
            give(2 + which)[at, :] = pair[which]
            give(2 + which, True)
        sums = give(4)
        sums[...] = jnp.zeros_like(sums)
        sums[0:1, :half] = column_sums(vl)
        sums[0:1, half:] = column_sums(vh)
        give(4, True)

    return streamed(
        "page_backward",
        body,
        info,
        [key_low, key_high, value_low, value_high, page_rows, key_weight, value_weight],
        [
            ((half, 2 * width), bf16), ((half, 2 * width), bf16),
            ((deep, width), bf16), ((deep, width), bf16), ((8, width), f32),
        ],
    )


def lead_upstream(info, keys, values, key_weight, value_weight, lead_tokens, vectors):
    rows, width = lead_tokens.shape
    half, tall = width // 2, 256

    def body(info_ref, need, give, hidden):
        kl, kh, vl, vh = need(0), need(1), need(2), need(3)
        wk, wv = need(4), need(5)
        x_ref, vec = need(6), need(7)
        gains = jnp.zeros((1, width), f32)
        shifts = gains
        for start in range(0, rows, tall):
            at = pl.ds(start, tall)
            up = nt(kl[at, :], wk[:, :half]) + nt(kh[at, :], wk[:, half:])
            up = up + nt(vl[at, :], wv[:, :half]) + nt(vh[at, :], wv[:, half:])
            give(0)[at, :] = up.astype(bf16)
            unit, _ = norm_unit(x_ref[at, :].astype(f32))
            hidden[at, :] = (unit * vec[0:1, :] + vec[1:2, :]).astype(bf16)
            gains = gains + jnp.sum(up * unit, axis=0, keepdims=True)
            shifts = shifts + jnp.sum(up, axis=0, keepdims=True)
        give(0, True)
        sums = give(2)
        sums[...] = jnp.zeros_like(sums)
        sums[0:1, :], sums[1:2, :] = gains, shifts
        sums[2:3, :half], sums[2:3, half:] = column_sums(vl[...]), column_sums(vh[...])
        give(2, True)
        for i, ref in enumerate((kl, kh, vl, vh)):
            give(1)[:, i * half : (i + 1) * half] = tn(hidden[...], ref[...]).astype(bf16)
        give(1, True)

    return streamed(
        "lead_upstream",
        body,
        info,
        [*keys, *values, key_weight, value_weight, lead_tokens, vectors],
        [((rows, width), bf16), ((width, 2 * width), bf16), ((8, width), f32)],
        [pltpu.VMEM((rows, width), bf16)],
    )


def projection_grads(info, hidden, query_grad, key_grad, value_grad, lead_part, high, owners):
    rows, width = hidden.shape
    half = width // 2
    column = half if high else 0

    def body(info_ref, need, give):
        core = info_ref[0]
        h = need(0)
        for i in range(3):
            total = tn(h[...], need(1 + i)[...])
            if i:
                base = (i - 1) * width + column
                total = total + need(4)[:, base : base + half].astype(f32)
            at = pl.ds(i * half, half)
            give(0)[:, at], give(1)[:, at] = by_core(core, total, width // owners)
        give(0, True)
        give(1, True)

    return streamed(
        "projection_grads",
        body,
        info,
        [hidden, query_grad, key_grad, value_grad, lead_part],
        [((half, 3 * half), bf16), ((half, 3 * half), bf16)],
    )


def first_norm_backward(info, queries, keys, values, weights, tokens, one, returned, vectors):
    rows, width = tokens.shape
    half, tall = width // 2, 256

    def body(info_ref, need, give):
        grads = [need(i) for i in range(6)]
        wq, wk, wv = need(6), need(7), need(8)
        x_ref, vec = need(9), need(10)
        one_ref, back_ref = need(11), need(12)
        gains = jnp.zeros((1, width), f32)
        shifts = gains
        for start in range(0, rows, tall):
            at = pl.ds(start, tall)
            up = 0.0
            for i, weight in enumerate((wq, wk, wv)):
                up = up + nt(grads[2 * i][at, :], weight[:, :half])
                up = up + nt(grads[2 * i + 1][at, :], weight[:, half:])
            unit, inverse = norm_unit(x_ref[at, :].astype(f32))
            gains = gains + jnp.sum(up * unit, axis=0, keepdims=True)
            shifts = shifts + jnp.sum(up, axis=0, keepdims=True)
            up = up + back_ref[at, :].astype(f32)
            give(0)[at, :] = one_ref[at, :] + norm_pull(up, unit, inverse, vec[0:1, :])
        give(0, True)
        sums = give(1)
        sums[...] = jnp.zeros_like(sums)
        sums[0:1, :], sums[1:2, :] = gains, shifts
        sums[2:3, :half], sums[2:3, half:] = column_sums(grads[0][...]), column_sums(grads[1][...])
        sums[3:4, :half], sums[3:4, half:] = column_sums(grads[4][...]), column_sums(grads[5][...])
        give(1, True)

    return streamed(
        "first_norm_backward",
        body,
        info,
        [*queries, *keys, *values, *weights, tokens, vectors, one, returned],
        [((rows, width), f32), ((8, width), f32)],
    )


def digit_axes():
    patch_bits = lax.axis_size("patch").bit_length() - 1
    return [("tok", 0)] + [("patch", bit) for bit in reversed(range(patch_bits))]


def my_digit(axis, bit):
    return (lax.axis_index(axis) >> bit) & 1


def tied(*values):
    return lax.optimization_barrier(values)


FIRST_DIGIT = 4


class Sum:
    def __init__(self, sent, kept, tok_first):
        every = digit_axes()
        self.free = every[:-1]
        bits = every[-2:0:-1]
        loose, last = bits[: max(len(bits) - 2, 0)], bits[max(len(bits) - 2, 0) :]
        singles = [every[:1]] + [[one] for one in loose]
        if not tok_first:
            singles = singles[1:] + singles[:1]
        self.stages = singles + [last]
        self.at = 0
        self.terms = [(self.chunks(kept), self.free)]
        self.leaving = [self.chunks(sent)]
        self.hops = [[("patch", 0)]]
        self.mine = None
        self.result = None

    def chunks(self, value):
        count = 1 << len(self.free)
        size = 1
        for n in value.shape[:-1]:
            size *= n
        return value.reshape(count, size // count, value.shape[-1])

    def send(self):
        self.arrived = [hop(value, steps) for value, steps in zip(self.leaving, self.hops)]

    def absorb(self, arrived):
        if self.mine is not None:
            self.result = sum((one[0].astype(f32) for one in arrived), self.mine[0])
            self.leaving = None
            return []
        self.terms += [(self.chunks(one), self.free) for one in arrived]
        digits = self.stages[self.at]
        self.at += 1
        self.free = [one for one in self.free if one not in digits]
        self.hops, jobs = [], []
        last = self.at == len(self.stages)
        for flips in range(0 if last else 1, 1 << len(digits)):
            flipped = [one for i, one in enumerate(digits) if flips >> i & 1]
            choices = []
            for chunk in range(1 << len(self.free)):
                bits = {
                    one: chunk >> (len(self.free) - 1 - i) & 1 for i, one in enumerate(self.free)
                }
                choices.append((bits, flipped))
            jobs.append((self.terms, choices, bf16 if flips else f32))
            if flips:
                self.hops.append(flipped)
        return jobs

    def take(self, made):
        if self.at == len(self.stages):
            self.mine = made[0]
            made = made[1:]
        self.leaving = list(made)


def hop(value, steps):
    axis = steps[0][0]
    flip = sum(1 << bit for _, bit in steps)
    return lax.ppermute(value, axis, [(i, i ^ flip) for i in range(lax.axis_size(axis))])


def added_up(info, jobs):
    digits = digit_axes()
    arrays, known = [], {}
    for terms, _, _ in jobs:
        for value, _ in terms:
            if id(value) not in known:
                known[id(value)] = len(arrays)
                arrays.append(value)
    loads = sum(len(terms) * len(choices) for terms, choices, _ in jobs)

    def body(info_ref, *refs):
        n, m = len(arrays), len(jobs)
        ins, dests = refs[:n], refs[n : n + m]
        held, made = refs[n + m : n + 2 * m], refs[n + 2 * m : n + 3 * m]
        in_sem, out_sem = refs[n + 3 * m], refs[n + 3 * m + 1]
        mine = {one: info_ref[FIRST_DIGIT + i] for i, one in enumerate(digits)}
        copies, count = [], 0
        for job, (terms, choices, _) in enumerate(jobs):
            for t, (value, free) in enumerate(terms):
                for c, (bits, flipped) in enumerate(choices):
                    index = 0
                    for one in free:
                        digit = bits[one] if one in bits else mine[one]
                        digit = 1 - digit if one in flipped else digit
                        index = 2 * index + digit
                    copy = pltpu.make_async_copy(
                        ins[known[id(value)]].at[index], held[job].at[t, c], in_sem.at[count]
                    )
                    copy.start()
                    copies.append((job, copy))
                    count += 1
        stores = []
        for job, (terms, choices, kind) in enumerate(jobs):
            for which, copy in copies:
                if which == job:
                    copy.wait()
            rows = held[job].shape[2]
            slab = min(rows, 16)
            per = rows // slab

            def step(i, _, job=job, terms=terms, kind=kind, slab=slab, per=per):
                chunk, at = i // per, pl.ds(pl.multiple_of(i % per * slab, slab), slab)
                total = held[job][0, chunk, at, :].astype(f32)
                for t in range(1, len(terms)):
                    total = total + held[job][t, chunk, at, :].astype(f32)
                made[job][chunk, at, :] = total.astype(kind)
                return 0

            lax.fori_loop(0, len(choices) * per, step, 0)
            stores.append(pltpu.make_async_copy(made[job], dests[job], out_sem.at[job]))
            stores[-1].start()
        for store in stores:
            store.wait()

    anywhere = pl.BlockSpec(memory_space=pl.ANY)
    shapes = [((len(choices),) + terms[0][0].shape[1:], kind) for terms, choices, kind in jobs]
    held = [
        pltpu.VMEM((len(terms), len(choices)) + terms[0][0].shape[1:], bf16)
        for terms, choices, _ in jobs
    ]
    return pl.pallas_call(
        body,
        out_shape=[Shape(shape, kind) for shape, kind in shapes],
        grid_spec=pltpu.PrefetchScalarGridSpec(
            num_scalar_prefetch=1,
            grid=(1,),
            in_specs=[anywhere] * len(arrays),
            out_specs=[anywhere] * len(jobs),
            scratch_shapes=held
            + [pltpu.VMEM(shape, kind) for shape, kind in shapes]
            + [pltpu.SemaphoreType.DMA((loads,)), pltpu.SemaphoreType.DMA((len(jobs),))],
        ),
        compiler_params=settings(60),
        name="added_up",
    )(info, *arrays)


def advance(info, chain, moving=(), fresh=()):
    moving = [one for one in moving if one.leaving is not None]
    chain, arrived = tied(chain, [one.arrived for one in moving])
    jobs, owners = [], []
    for one, values in zip(moving, arrived):
        new = one.absorb(values)
        owners.append((one, len(new)))
        jobs += new
    if jobs:
        made = added_up(info, jobs)
        for one, count in owners:
            if count:
                one.take(made[:count])
                made = made[count:]
    going = [one for one in moving + list(fresh) if one.leaving is not None]
    chain, leaving = tied(chain, [one.leaving for one in going])
    for one, values in zip(going, leaving):
        one.leaving = values
        one.send()
    return chain


def scatter_vectors(vectors):
    digits = digit_axes()
    owners = 1 << len(digits)
    widths = [vector.shape[0] // owners for vector in vectors]
    table = jnp.concatenate([vector.reshape(owners, -1) for vector in vectors], axis=1)
    table = jnp.pad(table, ((0, 0), (0, -table.shape[1] % 128)))
    mine = table.reshape((2,) * len(digits) + (table.shape[1],))
    left = list(digits)
    for step in digits[::-1]:
        place = left.index(step)
        left.pop(place)
        digit = my_digit(*step)
        keep = lax.dynamic_index_in_dim(mine, digit, place, keepdims=False)
        give = lax.dynamic_index_in_dim(mine, 1 - digit, place, keepdims=False)
        mine = keep + hop(give, [step])
    pieces, start = [], 0
    for width in widths:
        pieces.append(mine[start : start + width])
        start += width
    return pieces


def pick_entry(table, position):
    indices = jnp.arange(table.shape[0], dtype=jnp.int32)
    return jnp.sum(jnp.where(indices == position, table, 0))


def layer_norm(values, gain, shift):
    unit, _ = norm_unit(values)
    return (unit * gain + shift).astype(bf16)


def rows_of(*vectors):
    rows = jnp.stack(vectors, axis=0)
    return jnp.pad(rows, ((0, 8 - len(vectors)), (0, 0)))


def local(
    tokens,
    patches,
    cotangent,
    lengths,
    page_of,
    page_counts,
    self_gain,
    self_shift,
    query_weight,
    query_bias,
    key_weight,
    value_weight,
    value_bias,
    output_weight,
    output_bias,
    cross_gain,
    cross_shift,
    probe_weight,
    probe_bias,
    source_key,
    source_value,
    source_bias,
    merge_weight,
    merge_bias,
    feed_gain,
    feed_shift,
    expand_weight,
    expand_bias,
    reduce_weight,
    reduce_bias,
):
    head_scale = HDIM ** (-0.5)
    tok_index = lax.axis_index("tok").astype(jnp.int32)
    sequence = lax.axis_index("patch")
    core = my_digit("patch", 0).astype(jnp.int32)
    row_count, model_width = tokens.shape[1:]
    lead_tokens = lax.ppermute(tokens[0], "tok", [(0, 1)])
    gathered = lax.all_gather(patches, ("tok", "patch"), axis=0, tiled=True)
    inputs = tokens[0].astype(f32)
    page_index = pick_entry(page_of, sequence)
    filled = pick_entry(page_counts, page_index).reshape(1)
    trailing = tok_index.reshape(1)
    page_start = page_index * PAGE_SLOTS
    digits = [my_digit(*one).astype(jnp.int32) for one in digit_axes()]
    owners = 1 << len(digits)
    info = jnp.stack(
        [core, tok_index * row_count, pick_entry(lengths, sequence), page_index] + digits
    )
    self_vectors = rows_of(self_gain, self_shift)
    cross_vectors = rows_of(cross_gain, cross_shift)
    feed_vectors = rows_of(merge_bias, feed_gain, feed_shift, reduce_bias)

    hidden_one = layer_norm(inputs, self_gain, self_shift)
    query = ((nn(hidden_one, query_weight) + query_bias) * head_scale).astype(bf16)
    own_keys = nn(hidden_one, key_weight).astype(bf16)
    own_values = (nn(hidden_one, value_weight) + value_bias).astype(bf16)
    lead_tokens, query, own_keys, own_values = tied(lead_tokens, query, own_keys, own_values)
    hidden_lead = layer_norm(lead_tokens.astype(f32), self_gain, self_shift)
    lead_keys = nn(hidden_lead, key_weight).astype(bf16)
    lead_values = (nn(hidden_lead, value_weight) + value_bias).astype(bf16)
    self_mixed, self_total = self_forward(
        query, lead_keys, lead_values, own_keys, own_values, trailing
    )
    after_one = inputs + nn(self_mixed, output_weight) + output_bias
    hidden_two = layer_norm(after_one, cross_gain, cross_shift)
    probe = ((nn(hidden_two, probe_weight) + probe_bias) * head_scale).astype(bf16)
    page_rows = lax.dynamic_slice_in_dim(gathered, page_start, PAGE_SLOTS, 0)
    page_keys = nn(page_rows, source_key).astype(bf16)
    page_values = (nn(page_rows, source_value) + source_bias).astype(bf16)
    cross_mixed, cross_total = cross_forward(probe, page_keys, page_values, filled)

    fed = feed_forward(
        after_one, cross_mixed, merge_weight, cotangent[0], feed_vectors, expand_weight,
        expand_bias[None], reduce_weight, info, owners,
    )
    block_output, grad_two, grad_cross_out = fed[:3]
    feed_sums, expand_bias_sums = fed[10], fed[9]
    reduce_sum = Sum(fed[3], fed[4], False)
    expand_sum = Sum(fed[5], fed[6], True)
    merge_sum = Sum(fed[7], fed[8], False)

    half_pairs = model_width // PAIR // 2
    cross_args = (probe, page_keys, page_values, cross_mixed, cross_total)
    grad_cross_out = advance(info, grad_cross_out, [], [expand_sum, reduce_sum, merge_sum])
    low = cross_backward(*cross_args, grad_cross_out, filled, 0, half_pairs)
    low, grad_cross_out = advance(info, (low, grad_cross_out), [expand_sum, reduce_sum, merge_sum])
    high = cross_backward(*cross_args, grad_cross_out, filled, half_pairs, half_pairs)
    patch_total = patches.shape[0] * lax.axis_size(("tok", "patch"))
    paged = page_backward(
        info, low[1], high[1], low[2], high[2], page_rows, source_key, source_value, owners,
        patch_total,
    )
    source_sum = Sum(paged[0], paged[1], True)
    patch_sum = Sum(paged[2], paged[3], False)
    low, high = advance(info, (low, high), [], [source_sum, patch_sum])
    probed = probe_backward(
        info, low[0], high[0], probe_weight, after_one, grad_two, output_weight, self_mixed,
        cross_vectors, owners,
    )
    grad_one, grad_self_out, probe_sums = probed[0], probed[1], probed[4]
    middle_sum = Sum(probed[2], probed[3], False)
    self_args = (query, lead_keys, lead_values, self_mixed, self_total)
    own_args = (query, own_keys, own_values, self_mixed, self_total)
    first = [expand_sum, reduce_sum, merge_sum]
    second = [source_sum, patch_sum]
    grad_self_out = advance(info, grad_self_out, first + second, [middle_sum])
    second = second + [middle_sum]
    lead_low = lead_backward(*self_args, grad_self_out, trailing, 0, half_pairs)
    lead_low, grad_self_out = advance(info, (lead_low, grad_self_out), first + [middle_sum])
    lead_high = lead_backward(*self_args, grad_self_out, trailing, half_pairs, half_pairs)
    led = lead_upstream(
        info, (lead_low[1], lead_high[1]), (lead_low[2], lead_high[2]), key_weight,
        value_weight, lead_tokens, self_vectors,
    )
    led_grad, led_part, lead_sums = led
    led_grad, led_part, grad_self_out = advance(
        info, (led_grad, led_part, grad_self_out), second
    )
    returned = lax.ppermute(led_grad, "tok", [(1, 0)])
    own_low = own_backward(*own_args, grad_self_out, lead_low[0], 0, half_pairs)
    parts = projection_grads(info, hidden_one, *own_low, led_part, False, owners)
    low_sum = Sum(*parts, False)
    own_low, grad_self_out = advance(info, (own_low, grad_self_out), first + second, [low_sum])
    own_high = own_backward(*own_args, grad_self_out, lead_high[0], half_pairs, half_pairs)
    own_high, led_part = advance(info, (own_high, led_part), second + [low_sum])
    parts = projection_grads(info, hidden_one, *own_high, led_part, True, owners)
    high_sum = Sum(*parts, True)
    own_low, own_high = advance(info, (own_low, own_high), [], [high_sum])
    tokens_grad, first_sums = first_norm_backward(
        info, (own_low[0], own_high[0]), (own_low[1], own_high[1]), (own_low[2], own_high[2]),
        (query_weight, key_weight, value_weight), tokens[0], grad_one, returned, self_vectors,
    )
    rest = first + second + [low_sum, high_sum]
    first_sums = advance(info, first_sums, rest)
    sums = scatter_vectors(
        [
            first_sums[0] + lead_sums[0],
            first_sums[1] + lead_sums[1],
            first_sums[2],
            first_sums[3] + lead_sums[2],
            probe_sums[2],
            probe_sums[0],
            probe_sums[1],
            probe_sums[3],
            paged[4][0],
            feed_sums[3],
            feed_sums[1],
            feed_sums[2],
            expand_bias_sums[0],
            feed_sums[0],
        ]
    )
    while any(one.leaving is not None for one in rest):
        advance(info, jnp.zeros((), f32), rest)
    half = model_width // 2
    source_grads = source_sum.result
    projections = [
        jnp.concatenate([one.result[:, i * half : (i + 1) * half] for one in (low_sum, high_sum)], axis=1)
        for i in range(3)
    ]
    return (
        block_output[None],
        tokens_grad[None],
        patch_sum.result,
        sums[0],
        sums[1],
        projections[0],
        sums[2],
        projections[1],
        projections[2],
        sums[3],
        middle_sum.result[:, model_width:],
        sums[4],
        sums[5],
        sums[6],
        middle_sum.result[:, :model_width],
        sums[7],
        source_grads[:, :model_width],
        source_grads[:, model_width:],
        sums[8],
        merge_sum.result,
        sums[9],
        sums[10],
        sums[11],
        expand_sum.result,
        sums[12],
        reduce_sum.result,
        sums[13],
    )


def solution(mesh):
    placed = (
        P("patch", "tok", None),
        P(("tok", "patch"), None),
        P("patch", "tok", None),
        P(),
        P(),
        P(),
        P(),
        P(),
        P(),
        P(),
        P(),
        P(),
        P(),
        P(),
        P(),
        P(),
        P(),
        P(),
        P(),
        P(),
        P(),
        P(),
        P(),
        P(),
        P(),
        P(),
        P(),
        P(),
        P(),
        P(),
    )
    return jax.shard_map(
        local,
        mesh=mesh,
        in_specs=placed,
        out_specs=(
            P("patch", "tok", None),
            P("patch", "tok", None),
            P(("tok", "patch"), None),
            P(("tok", "patch")),
            P(("tok", "patch")),
            P(("tok", "patch"), None),
            P(("tok", "patch")),
            P(("tok", "patch"), None),
            P(("tok", "patch"), None),
            P(("tok", "patch")),
            P(("tok", "patch"), None),
            P(("tok", "patch")),
            P(("tok", "patch")),
            P(("tok", "patch")),
            P(("tok", "patch"), None),
            P(("tok", "patch")),
            P(("tok", "patch"), None),
            P(("tok", "patch"), None),
            P(("tok", "patch")),
            P(("tok", "patch"), None),
            P(("tok", "patch")),
            P(("tok", "patch")),
            P(("tok", "patch")),
            P(("tok", "patch"), None),
            P(("tok", "patch")),
            P(("tok", "patch"), None),
            P(("tok", "patch")),
        ),
        check_vma=False,
    )
```

time: 1080 us -> 693 us (0.64)
  matrix products: 425 us -> 22.5 us
  Pallas kernels: 0 us -> 287 us
  other arithmetic: 169 us -> 24.2 us
  waiting for transfers between devices: 258 us -> 164 us
  local copies, waits for them, and re-layouts: 132 us -> 54.3 us
  starting transfers between devices: 64.6 us -> 115 us
    dot_general x96 -> x9, matrix products: 425 us -> 22.5 us  [nn(): lax.dot_general(left, right, (((1,), (0,)), ((), ())), preferred_element_...]
    pallas_call x0 -> x24, Pallas kernels: none -> 287 us  [the longest x6 71.2 us: streamed(): pl.pallas_call(kernel, out_shape=[Shape(shape, kind) for shape, kind in o...]
    ppermute x61 -> x55, waiting for transfers between devices: 258 us -> 163 us  [the longest x53 139 us: hop(): lax.ppermute(value, axis, [(i, i ^ flip) for i in range(lax.axis_size(axi...]
    convert_element_type x58 -> x1, other arithmetic: 86.8 us -> 0.64 us  [layer_norm(): return (unit * gain + shift).astype(bf16)]
    ppermute x61 -> x55, starting transfers between devices: 64.6 us -> 115 us  [the longest x53 108 us: hop(): lax.ppermute(value, axis, [(i, i ^ flip) for i in range(lax.axis_size(axi...]
    dynamic_slice x44 -> x6, local copies, waits for them, and re-layouts: 49.2 us -> 1.64 us  [the longest x1 1.45 us: local(): page_rows = lax.dynamic_slice_in_dim(gathered, page_start, PAGE_SLOTS, 0)]
    reduce_sum x21 -> x5, other arithmetic: 45.8 us -> 6.33 us  [the longest x2 3.36 us: norm_unit(): average = jnp.mean(values, axis=-1, keepdims=True)]
    dynamic_update_slice x28 -> x0, local copies, waits for them, and re-layouts: 28.6 us -> none  [the longest x16 17.2 us: attend_forward(): lax.map(one_group, (by_groups(query), by_groups(key_rows), by_groups(valu...]
  transfers between devices with their start and end apart: 62 -> 56, of which waited for: 41 -> 14; matrix products, arithmetic and copies ran while one was open for 25% -> 9% of each run, Pallas kernels for 0% -> 23%
where the time goes in v2:
time: 693 us; the launch traced here: 684 us
  Pallas kernels  287 us (41%)
  waiting for transfers between devices  164 us (24%)
  starting transfers between devices  115 us (17%)
  local copies, waits for them, and re-layouts  54.3 us (8%)
  other arithmetic  24.2 us (3%)
  matrix products  22.5 us (3%)
  between operations  16.5 us (2%)
    ppermute x53, waiting for transfers between devices, hop(): lax.ppermute(value, axis, [(i, i ^ flip) for i in range(lax.axis_size(axi...  139 us
    ppermute x53, starting transfers between devices, hop(): lax.ppermute(value, axis, [(i, i ^ flip) for i in range(lax.axis_size(axi...  108 us
    pallas_call x6, Pallas kernels, streamed(): pl.pallas_call(kernel, out_shape=[Shape(shape, kind) for shape, kind in o...  71.2 us
    pallas_call x1, Pallas kernels, feed_forward(): pl.pallas_call(body, out_shape=[Shape(full, bf16), Shape(full, f32), Shap...  62.6 us
    pallas_call x9, Pallas kernels, added_up(): pl.pallas_call(body, out_shape=[Shape(shape, kind) for shape, kind in sha...  45.9 us
    pallas_call x2, Pallas kernels, cross_backward(): pl.pallas_call(body, out_shape=[Shape((rows, pairs * PAIR), bf16)] + [Sha...  32 us
    unnamed x188, local copies, waits for them, and re-layouts  30 us
    pallas_call x2, Pallas kernels, own_backward(): pl.pallas_call(body, out_shape=[Shape((rows, pairs * PAIR), bf16)] * 3, g...  29.3 us
  transfers between devices with their start and end apart: 56, of which 14 were waited for; matrix products, arithmetic and copies ran while one was open for 9% of the time, Pallas kernels for 23%

profile of v2, /device:TPU:0, one launch (start us, length us, event | category | flops | bytes accessed | tf_op | source)
XLA Modules:
  0.0 683.9 jit_solution(7114064475845821015)
XLA Ops:
  30.1 19.0 %collective-permute-done.refs_6_ = bf16[768,1024]{1,0:T(8,128)(2,1)} collective-permute-done((bf16[768,1024]{1,0:T(8,128)(2,1)}, bf16[768,1024]{1,0:T(8,128)(2,1)}, u32[]{:S(2)}, u32[]{:S(2)}) %collective-permute-start) | collective-permute-done | bytes 1572896 | tf_op jit(solution)/shard_map/ppermute | solution.py:960
  61.3 21.2 %self_forward.1 = (bf16[768,1024]{1,0:T(8,128)(2,1)S(1)}, f32[768,128]{1,0:T(8,128)S(1)}) custom-call(s32[1]{0:T(128)} %bitcast.9.flag, bf16[768,1024]{1,0:T(8,128)(2,1)S(1)} %multiply_convert_fusion.1.q_ref, bf16[768,1024]{1,0:T(8,128)(2,1)S(1)} %convolution_convert_fusion.lk.k_ref, bf16[768,1024]{1,0:T(8,128)(2,1)} %add_convert_fusion.1.lv.v_ref, ...), custom_call_target="tpu_custom_call" | custom-call | tf_op jit(solution)/shard_map/self_forward/pallas_call | solution.py:144
  94.3 18.3 %cross_forward.1 = (bf16[768,1024]{1,0:T(8,128)(2,1)S(1)}, f32[768,128]{1,0:T(8,128)S(1)}) custom-call(s32[1]{0:T(128)} %bitcast.10.filled_ref, bf16[768,1024]{1,0:T(8,128)(2,1)S(1)} %multiply_convert_fusion.q_ref, bf16[512,1024]{1,0:T(8,128)(2,1)S(1)} %convolution_convert_fusion.2.k_ref, bf16[512,1024]{1,0:T(8,128)(2,1)S(1)} %add_convert_fusion.3.v_ref), custom_call_target="tpu_custom_call" | custom-call | tf_op jit(solution)/shard_map/cross_forward/pallas_call | solution.py:177
  113.8 62.6 %feed_forward.1 = (bf16[768,1024]{1,0:T(8,128)(2,1)}, f32[768,1024]{1,0:T(8,128)}, bf16[768,1024]{1,0:T(8,128)(2,1)}, bf16[2048,1024]{1,0:T(8,128)(2,1)}, bf16[2...) custom-call(s32[9]{0:T(128)} %stack.61.info_ref, ...), custom_call_target="tpu_custom_call" | custom-call | tf_op jit(solution)/shard_map/feed_forward/pallas_call | solution.py:414
  179.5 15.9 %cross_backward.2 = (bf16[768,512]{1,0:T(8,128)(2,1)S(1)}, bf16[512,512]{1,0:T(8,128)(2,1)S(1)}, bf16[512,512]{1,0:T(8,128)(2,1)S(1)}) custom-call(s32[1]{0:T(128)} %bitcast.10.filled_ref, bf16[768,1024]{1,0:T(8,128)(2,1)S(1)} %multiply_convert_fusion.q_ref, bf16[512,1024]{1,0:T(8,128)(2,1)S(1)} %copy-done.5, bf16[512,1024]{1,0:T(8,128)(2,1)S(1)} %copy-done.8, ...), custom_call_target="tpu_custom_call" | custom-call | tf_op jit(solution)/shard_map/cross_backward/pallas_call | solution.py:317
  207.5 16.1 %cross_backward.3 = (bf16[768,512]{1,0:T(8,128)(2,1)S(1)}, bf16[512,512]{1,0:T(8,128)(2,1)S(1)}, bf16[512,512]{1,0:T(8,128)(2,1)S(1)}) custom-call(s32[1]{0:T(128)} %bitcast.10.filled_ref, bf16[768,1024]{1,0:T(8,128)(2,1)S(1)} %multiply_convert_fusion.q_ref, bf16[512,1024]{1,0:T(8,128)(2,1)S(1)} %copy-done.6, bf16[512,1024]{1,0:T(8,128)(2,1)S(1)} %copy-done.9, ...), custom_call_target="tpu_custom_call" | custom-call | tf_op jit(solution)/shard_map/cross_backward/pallas_call | solution.py:317
  226.1 9.0 %page_backward.1 = (bf16[512,2048]{1,0:T(8,128)(2,1)}, bf16[512,2048]{1,0:T(8,128)(2,1)}, bf16[512,1024]{1,0:T(8,128)(2,1)}, bf16[512,1024]{1,0:T(8,128)(2,1)}, f32[8,1024]{1,0:T(8,128)}) custom-call(s32[9]{0:T(128)} %stack.61.info_ref, bf16[512,512]{1,0:T(8,128)(2,1)} %copy-done.24, bf16[512,512]{1,0:T(8,128)(2,1)} %copy-done.26, ...), custom_call_target="tpu_custom_call" | custom-call | tf_op jit(solution)/shard_map/page_backward/pallas_call | solution.py:479
  235.2 14.1 %collective-permute-start.4 = (bf16[8,32,4096]{2,1,0:T(8,128)(2,1)}, bf16[8,32,4096]{2,1,0:T(8,128)(2,1)}, u32[]{:S(2)}, u32[]{:S(2)}) collective-permute-start(bf16[8,32,4096]{2,1,0:T(8,128)(2,1)} %get-tuple-element.333), channel_id=1, source_target_pairs={{0,16},{16,0},{1,17},{17,1},{2,18},{18,2},{3,19},{19,3},{4,20},{20... | collective-permute-start | bytes 6291464 | tf_op jit(solution)/shard_map/ppermute | solution.py:784
  252.4 17.0 %probe_backward.1 = (f32[768,1024]{1,0:T(8,128)}, bf16[768,1024]{1,0:T(8,128)(2,1)}, bf16[512,2048]{1,0:T(8,128)(2,1)}, bf16[512,2048]{1,0:T(8,128)(2,1)}, f32[8,1024]{1,0:T(8,128)}) custom-call(s32[9]{0:T(128)} %stack.61.info_ref, bf16[768,512]{1,0:T(8,128)(2,1)} %copy-done.22, bf16[768,512]{1,0:T(8,128)(2,1)} %copy-done.23, bf16[1024,1024]{1,0:T(8,128)(2,1)} %refs_2_.1, ...), custom_call_target="tpu_custom_call" | custom-call | tf_op jit(solution)/shard_map/probe_backward/pallas_call | solution.py:479
  269.4 39.0 %collective-permute-done.6.refs_8_.refs_10_ = bf16[8,32,1024]{2,1,0:T(8,128)(2,1)S(1)} collective-permute-done((bf16[8,32,1024]{2,1,0:T(8,128)(2,1)S(1)}, bf16[8,32,1024]{2,1,0:T(8,128)(2,1)S(1)}, u32[]{:S(2)}, u32[]{:S(2)}) %collective-permute-start.6) | collective-permute-done | bytes 524320 | tf_op jit(solution)/shard_map/ppermute | solution.py:784
  325.5 24.4 %collective-permute-done.11.refs_11_ = bf16[4,32,1024]{2,1,0:T(8,128)(2,1)S(1)} collective-permute-done((bf16[4,32,1024]{2,1,0:T(8,128)(2,1)}, bf16[4,32,1024]{2,1,0:T(8,128)(2,1)S(1)}, u32[]{:S(2)}, u32[]{:S(2)}) %collective-permute-start.11) | collective-permute-done | bytes 262176 | tf_op jit(solution)/shard_map/ppermute | solution.py:784
  350.6 8.0 %added_up.11 = (f32[1,32,4096]{2,1,0:T(8,128)}, bf16[1,32,4096]{2,1,0:T(8,128)(2,1)}, bf16[1,32,4096]{2,1,0:T(8,128)(2,1)}, bf16[1,32,4096]{2,1,0:T(8,128)(2,1)}...) custom-call(s32[9]{0:T(128)} %stack.61.info_ref, ...), custom_call_target="tpu_custom_call" | custom-call | tf_op jit(solution)/shard_map/added_up/pallas_call | solution.py:847
  362.7 31.0 %collective-permute-done.14.refs_5_.refs_6_ = bf16[8,32,1024]{2,1,0:T(8,128)(2,1)S(1)} collective-permute-done((bf16[8,32,1024]{2,1,0:T(8,128)(2,1)}, bf16[8,32,1024]{2,1,0:T(8,128)(2,1)S(1)}, u32[]{:S(2)}, u32[]{:S(2)}) %collective-permute-start.14) | collective-permute-done | bytes 524320 | tf_op jit(solution)/shard_map/ppermute | solution.py:784
  403.6 13.7 %lead_upstream.1 = (bf16[768,1024]{1,0:T(8,128)(2,1)}, bf16[1024,2048]{1,0:T(8,128)(2,1)}, f32[8,1024]{1,0:T(8,128)}) custom-call(s32[9]{0:T(128)} %stack.61.info_ref, bf16[768,512]{1,0:T(8,128)(2,1)} %copy-done.18, bf16[768,512]{1,0:T(8,128)(2,1)} %copy-done.20, bf16[768,512]{1,0:T(8,128)(2,1)} %copy-done.19, bf16[768,512]{1,0:T(8,128)(2,1)} %copy-done.21, ...), custom_call_target="tpu_custom_call" | custom-call | tf_op jit(solution)/shard_map/lead_upstream/pallas_call | solution.py:479
  425.8 17.0 %collective-permute-start.27 = (bf16[4,32,2048]{2,1,0:T(8,128)(2,1)}, bf16[4,32,2048]{2,1,0:T(8,128)(2,1)}, u32[]{:S(2)}, u32[]{:S(2)}) collective-permute-start(bf16[4,32,2048]{2,1,0:T(8,128)(2,1)} %get-tuple-element.414), channel_id=1, source_target_pairs={{0,16},{16,0},{1,17},{17,1},{2,18},{18,2},{3,19},{19,3},{4,20},{20... | collective-permute-start | bytes 1572872 | tf_op jit(solution)/shard_map/ppermute | solution.py:784
  447.1 10.6 %collective-permute-start.26 = (bf16[4,32,1024]{2,1,0:T(8,128)(2,1)}, bf16[4,32,1024]{2,1,0:T(8,128)(2,1)}, u32[]{:S(2)}, u32[]{:S(2)}) collective-permute-start(bf16[4,32,1024]{2,1,0:T(8,128)(2,1)} %get-tuple-element.413), channel_id=1, source_target_pairs={{0,16},{16,0},{1,17},{17,1},{2,18},{18,2},{3,19},{19,3},{4,20},{20... | collective-permute-start | bytes 786440 | tf_op jit(solution)/shard_map/ppermute | solution.py:784
  457.7 14.7 %own_backward.2 = (bf16[768,512]{1,0:T(8,128)(2,1)S(1)}, bf16[768,512]{1,0:T(8,128)(2,1)S(1)}, bf16[768,512]{1,0:T(8,128)(2,1)S(1)}) custom-call(bf16[768,1024]{1,0:T(8,128)(2,1)S(1)} %multiply_convert_fusion.1.q_ref, bf16[768,1024]{1,0:T(8,128)(2,1)S(1)} %copy-done.2, bf16[768,1024]{1,0:T(8,128)(2,1)} %add_convert_fusion.2.ov.v_ref, ...), custom_call_target="tpu_custom_call" | custom-call | tf_op jit(solution)/shard_map/own_backward/pallas_call | solution.py:283
  475.1 7.9 %projection_grads.2 = (bf16[512,1536]{1,0:T(8,128)(2,1)}, bf16[512,1536]{1,0:T(8,128)(2,1)}) custom-call(s32[9]{0:T(128)} %stack.61.info_ref, bf16[768,1024]{1,0:T(8,128)(2,1)} %copy-done.31, bf16[768,512]{1,0:T(8,128)(2,1)} %copy-done.10, bf16[768,512]{1,0:T(8,128)(2,1)} %copy-done.11, bf16[768,512]{1,0:T(8,128)(2,1)} %copy-done.12, ...), custom_call_target="tpu_custom_call" | custom-call | tf_op jit(solution)/shard_map/projection_grads/pallas_call | solution.py:479
  488.8 15.3 %collective-permute-start.31 = (bf16[1,32,1024]{2,1,0:T(8,128)(2,1)}, bf16[1,32,1024]{2,1,0:T(8,128)(2,1)}, u32[]{:S(2)}, u32[]{:S(2)}) collective-permute-start(bf16[1,32,1024]{2,1,0:T(8,128)(2,1)} %get-tuple-element.444), channel_id=1, source_target_pairs={{0,4},{1,5},{2,6},{3,7},{4,0},{5,1},{6,2},{7,3},{8,12},{9,13},{10,... | collective-permute-start | bytes 196616 | tf_op jit(solution)/shard_map/ppermute | solution.py:784
  508.7 10.1 %collective-permute-done.32 = bf16[1,32,1024]{2,1,0:T(8,128)(2,1)} collective-permute-done((bf16[1,32,1024]{2,1,0:T(8,128)(2,1)}, bf16[1,32,1024]{2,1,0:T(8,128)(2,1)}, u32[]{:S(2)}, u32[]{:S(2)}) %collective-permute-start.32) | collective-permute-done | bytes 65568 | tf_op jit(solution)/shard_map/ppermute | solution.py:784
  532.4 14.6 %own_backward.3 = (bf16[768,512]{1,0:T(8,128)(2,1)S(1)}, bf16[768,512]{1,0:T(8,128)(2,1)S(1)}, bf16[768,512]{1,0:T(8,128)(2,1)S(1)}) custom-call(bf16[768,1024]{1,0:T(8,128)(2,1)S(1)} %multiply_convert_fusion.1.q_ref, bf16[768,1024]{1,0:T(8,128)(2,1)S(1)} %copy-done.2, bf16[768,1024]{1,0:T(8,128)(2,1)} %add_convert_fusion.2.ov.v_ref, ...), custom_call_target="tpu_custom_call" | custom-call | tf_op jit(solution)/shard_map/own_backward/pallas_call | solution.py:283
  554.9 8.0 %projection_grads.3 = (bf16[512,1536]{1,0:T(8,128)(2,1)}, bf16[512,1536]{1,0:T(8,128)(2,1)}) custom-call(s32[9]{0:T(128)} %stack.61.info_ref, bf16[768,1024]{1,0:T(8,128)(2,1)} %copy-done.31, bf16[768,512]{1,0:T(8,128)(2,1)} %copy-done.13, bf16[768,512]{1,0:T(8,128)(2,1)} %copy-done.14, bf16[768,512]{1,0:T(8,128)(2,1)} %copy-done.15, ...), custom_call_target="tpu_custom_call" | custom-call | tf_op jit(solution)/shard_map/projection_grads/pallas_call | solution.py:479
  584.4 15.7 %first_norm_backward.1 = (f32[768,1024]{1,0:T(8,128)}, f32[8,1024]{1,0:T(8,128)}) custom-call(s32[9]{0:T(128)} %stack.61.info_ref, bf16[768,512]{1,0:T(8,128)(2,1)} %copy-done.10, bf16[768,512]{1,0:T(8,128)(2,1)} %copy-done.13, bf16[768,512]{1,0:T(8,128)(2,1)} %copy-done.11, bf16[768,512]{1,0:T(8,128)(2,1)} %copy-done.14, bf16[768,512]{1,0:T(8,128)(2,1)} %copy-done.12, ...), custom_call_target="tpu_custom_call" | custom-call | tf_op jit(solution)/shard_map/first_norm_backward/pallas_call | solution.py:479
  627.2 14.9 %collective-permute-done.47.refs_6_.refs_2_ = bf16[8,32,1536]{2,1,0:T(8,128)(2,1)S(1)} collective-permute-done((bf16[8,32,1536]{2,1,0:T(8,128)(2,1)S(1)}, bf16[8,32,1536]{2,1,0:T(8,128)(2,1)S(1)}, u32[]{:S(2)}, u32[]{:S(2)}) %collective-permute-start.47) | collective-permute-done | bytes 786464 | tf_op jit(solution)/shard_map/ppermute | solution.py:784
  (377 shorter events, 229.6 us)
Async XLA Ops:
  7.3 81.8 %all-gather.2.cloned.1.call-start = ((), (), s32[]{:S(2)}) async-start(), calls=%async_computation | async-start | bytes 2162688 | tf_op jit(solution)/shard_map/all_gather | solution.py:961
  8.0 41.1 %collective-permute-start = (bf16[768,1024]{1,0:T(8,128)(2,1)}, bf16[768,1024]{1,0:T(8,128)(2,1)}, u32[]{:S(2)}, u32[]{:S(2)}) collective-permute-start(bf16[768,1024]{1,0:T(8,128)(2,1)} %bitcast.101), channel_id=1, source_target_pairs={{0,16},{1,17},{2,18},{3,19},{4,20},{5,21},{6,22},{7,23},{8,24},{9,... | collective-permute-start | bytes 4718600 | tf_op jit(solution)/shard_map/ppermute | solution.py:960
  235.2 73.2 %collective-permute-start.4 = (bf16[8,32,4096]{2,1,0:T(8,128)(2,1)}, bf16[8,32,4096]{2,1,0:T(8,128)(2,1)}, u32[]{:S(2)}, u32[]{:S(2)}) collective-permute-start(bf16[8,32,4096]{2,1,0:T(8,128)(2,1)} %get-tuple-element.333), channel_id=1, source_target_pairs={{0,16},{16,0},{1,17},{17,1},{2,18},{18,2},{3,19},{19,3},{4,20},{20... | collective-permute-start | bytes 6291464 | tf_op jit(solution)/shard_map/ppermute | solution.py:784
  249.2 59.1 %collective-permute-start.5 = (bf16[8,128,1024]{2,1,0:T(8,128)(2,1)}, bf16[8,128,1024]{2,1,0:T(8,128)(2,1)}, u32[]{:S(2)}, u32[]{:S(2)}) collective-permute-start(bf16[8,128,1024]{2,1,0:T(8,128)(2,1)} %get-tuple-element.334), channel_id=1, source_target_pairs={{0,2},{1,3},{2,0},{3,1},{4,6},{5,7},{6,4},{7,5},{8,10},{9,11},{10,... | collective-permute-start | bytes 6291464 | tf_op jit(solution)/shard_map/ppermute | solution.py:784
  250.7 57.6 %collective-permute-start.7 = (bf16[16,32,2048]{2,1,0:T(8,128)(2,1)}, bf16[16,32,2048]{2,1,0:T(8,128)(2,1)}, u32[]{:S(2)}, u32[]{:S(2)}) collective-permute-start(bf16[16,32,2048]{2,1,0:T(8,128)(2,1)} %bitcast.140), channel_id=1, source_target_pairs={{0,1},{1,0},{2,3},{3,2},{4,5},{5,4},{6,7},{7,6},{8,9},{9,8},{10,11... | collective-permute-start | bytes 6291464 | tf_op jit(solution)/shard_map/ppermute | solution.py:784
  250.7 57.6 %collective-permute-start.8 = (bf16[16,32,1024]{2,1,0:T(8,128)(2,1)}, bf16[16,32,1024]{2,1,0:T(8,128)(2,1)S(1)}, u32[]{:S(2)}, u32[]{:S(2)}) collective-permute-start(bf16[16,32,1024]{2,1,0:T(8,128)(2,1)} %bitcast.144), channel_id=1, source_target_pairs={{0,1},{1,0},{2,3},{3,2},{4,5},{5,4},{6,7},{7,6},{8,9},{9,8},{10,11... | collective-permute-start | bytes 3145736 | tf_op jit(solution)/shard_map/ppermute | solution.py:784
  251.3 57.1 %collective-permute-start.6 = (bf16[8,32,1024]{2,1,0:T(8,128)(2,1)S(1)}, bf16[8,32,1024]{2,1,0:T(8,128)(2,1)S(1)}, u32[]{:S(2)}, u32[]{:S(2)}) collective-permute-start(bf16[8,32,1024]{2,1,0:T(8,128)(2,1)S(1)} %copy-done.84), channel_id=1, source_target_pairs={{0,2},{1,3},{2,0},{3,1},{4,6},{5,7},{6,4},{7,5},{8,10},{9,11},{10,... | collective-permute-start | bytes 1572872 | tf_op jit(solution)/shard_map/ppermute | solution.py:784
  316.3 33.5 %collective-permute-start.12 = (bf16[16,32,2048]{2,1,0:T(8,128)(2,1)}, bf16[16,32,2048]{2,1,0:T(8,128)(2,1)}, u32[]{:S(2)}, u32[]{:S(2)}) collective-permute-start(bf16[16,32,2048]{2,1,0:T(8,128)(2,1)} %bitcast.139), channel_id=1, source_target_pairs={{0,1},{1,0},{2,3},{3,2},{4,5},{5,4},{6,7},{7,6},{8,9},{9,8},{10,11... | collective-permute-start | bytes 6291464 | tf_op jit(solution)/shard_map/ppermute | solution.py:784
  316.4 33.4 %collective-permute-start.9 = (bf16[4,32,4096]{2,1,0:T(8,128)(2,1)}, bf16[4,32,4096]{2,1,0:T(8,128)(2,1)}, u32[]{:S(2)}, u32[]{:S(2)}) collective-permute-start(bf16[4,32,4096]{2,1,0:T(8,128)(2,1)} %get-tuple-element.356), channel_id=1, source_target_pairs={{0,2},{1,3},{2,0},{3,1},{4,6},{5,7},{6,4},{7,5},{8,10},{9,11},{10,... | collective-permute-start | bytes 3145736 | tf_op jit(solution)/shard_map/ppermute | solution.py:784
  318.0 31.8 %collective-permute-start.10 = (bf16[4,128,1024]{2,1,0:T(8,128)(2,1)}, bf16[4,128,1024]{2,1,0:T(8,128)(2,1)}, u32[]{:S(2)}, u32[]{:S(2)}) collective-permute-start(bf16[4,128,1024]{2,1,0:T(8,128)(2,1)} %get-tuple-element.357), channel_id=1, source_target_pairs={{0,16},{16,0},{1,17},{17,1},{2,18},{18,2},{3,19},{19,3},{4,20},{20... | collective-permute-start | bytes 3145736 | tf_op jit(solution)/shard_map/ppermute | solution.py:784
  318.4 31.5 %collective-permute-start.11 = (bf16[4,32,1024]{2,1,0:T(8,128)(2,1)}, bf16[4,32,1024]{2,1,0:T(8,128)(2,1)S(1)}, u32[]{:S(2)}, u32[]{:S(2)}) collective-permute-start(bf16[4,32,1024]{2,1,0:T(8,128)(2,1)} %get-tuple-element.358), channel_id=1, source_target_pairs={{0,16},{16,0},{1,17},{17,1},{2,18},{18,2},{3,19},{19,3},{4,20},{20... | collective-permute-start | bytes 786440 | tf_op jit(solution)/shard_map/ppermute | solution.py:784
  320.0 76.3 %collective-permute-start.13 = (bf16[8,32,2048]{2,1,0:T(8,128)(2,1)}, bf16[8,32,2048]{2,1,0:T(8,128)(2,1)}, u32[]{:S(2)}, u32[]{:S(2)}) collective-permute-start(bf16[8,32,2048]{2,1,0:T(8,128)(2,1)} %get-tuple-element.386), channel_id=1, source_target_pairs={{0,16},{16,0},{1,17},{17,1},{2,18},{18,2},{3,19},{19,3},{4,20},{20... | collective-permute-start | bytes 3145736 | tf_op jit(solution)/shard_map/ppermute | solution.py:784
  358.6 58.7 %collective-permute-start.15 = (bf16[8,32,2048]{2,1,0:T(8,128)(2,1)}, bf16[8,32,2048]{2,1,0:T(8,128)(2,1)}, u32[]{:S(2)}, u32[]{:S(2)}) collective-permute-start(bf16[8,32,2048]{2,1,0:T(8,128)(2,1)} %get-tuple-element.388), channel_id=1, source_target_pairs={{0,2},{1,3},{2,0},{3,1},{4,6},{5,7},{6,4},{7,5},{8,10},{9,11},{10,... | collective-permute-start | bytes 3145736 | tf_op jit(solution)/shard_map/ppermute | solution.py:784
  359.2 34.6 %collective-permute-start.14 = (bf16[8,32,1024]{2,1,0:T(8,128)(2,1)}, bf16[8,32,1024]{2,1,0:T(8,128)(2,1)S(1)}, u32[]{:S(2)}, u32[]{:S(2)}) collective-permute-start(bf16[8,32,1024]{2,1,0:T(8,128)(2,1)} %get-tuple-element.387), channel_id=1, source_target_pairs={{0,2},{1,3},{2,0},{3,1},{4,6},{5,7},{6,4},{7,5},{8,10},{9,11},{10,... | collective-permute-start | bytes 1572872 | tf_op jit(solution)/shard_map/ppermute | solution.py:784
  360.7 65.1 %collective-permute-start.16 = (bf16[1,32,4096]{2,1,0:T(8,128)(2,1)}, bf16[1,32,4096]{2,1,0:T(8,128)(2,1)}, u32[]{:S(2)}, u32[]{:S(2)}) collective-permute-start(bf16[1,32,4096]{2,1,0:T(8,128)(2,1)} %get-tuple-element.403), channel_id=1, source_target_pairs={{0,4},{1,5},{2,6},{3,7},{4,0},{5,1},{6,2},{7,3},{8,12},{9,13},{10,... | collective-permute-start | bytes 786440 | tf_op jit(solution)/shard_map/ppermute | solution.py:784
  362.3 61.2 %collective-permute-start.22 = (bf16[1,32,1024]{2,1,0:T(8,128)(2,1)}, bf16[1,32,1024]{2,1,0:T(8,128)(2,1)}, u32[]{:S(2)}, u32[]{:S(2)}) collective-permute-start(bf16[1,32,1024]{2,1,0:T(8,128)(2,1)} %get-tuple-element.409), channel_id=1, source_target_pairs={{0,4},{1,5},{2,6},{3,7},{4,0},{5,1},{6,2},{7,3},{8,12},{9,13},{10,... | collective-permute-start | bytes 196616 | tf_op jit(solution)/shard_map/ppermute | solution.py:784
  425.3 57.7 %collective-permute-start.25 = (bf16[4,32,2048]{2,1,0:T(8,128)(2,1)}, bf16[4,32,2048]{2,1,0:T(8,128)(2,1)S(1)}, u32[]{:S(2)}, u32[]{:S(2)}) collective-permute-start(bf16[4,32,2048]{2,1,0:T(8,128)(2,1)} %get-tuple-element.412), channel_id=1, source_target_pairs={{0,2},{1,3},{2,0},{3,1},{4,6},{5,7},{6,4},{7,5},{8,10},{9,11},{10,... | collective-permute-start | bytes 1572872 | tf_op jit(solution)/shard_map/ppermute | solution.py:784
  425.8 57.2 %collective-permute-start.27 = (bf16[4,32,2048]{2,1,0:T(8,128)(2,1)}, bf16[4,32,2048]{2,1,0:T(8,128)(2,1)}, u32[]{:S(2)}, u32[]{:S(2)}) collective-permute-start(bf16[4,32,2048]{2,1,0:T(8,128)(2,1)} %get-tuple-element.414), channel_id=1, source_target_pairs={{0,16},{16,0},{1,17},{17,1},{2,18},{18,2},{3,19},{19,3},{4,20},{20... | collective-permute-start | bytes 1572872 | tf_op jit(solution)/shard_map/ppermute | solution.py:784
  442.8 40.2 %collective-permute-start.20 = (bf16[1,128,1024]{2,1,0:T(8,128)(2,1)}, bf16[1,128,1024]{2,1,0:T(8,128)(2,1)}, u32[]{:S(2)}, u32[]{:S(2)}) collective-permute-start(bf16[1,128,1024]{2,1,0:T(8,128)(2,1)} %get-tuple-element.407), channel_id=1, source_target_pairs={{0,8},{1,9},{2,10},{3,11},{4,12},{5,13},{6,14},{7,15},{8,0},{9,1},... | collective-permute-start | bytes 786440 | tf_op jit(solution)/shard_map/ppermute | solution.py:784
  445.4 37.6 %collective-permute-start.21 = (bf16[1,128,1024]{2,1,0:T(8,128)(2,1)}, bf16[1,128,1024]{2,1,0:T(8,128)(2,1)}, u32[]{:S(2)}, u32[]{:S(2)}) collective-permute-start(bf16[1,128,1024]{2,1,0:T(8,128)(2,1)} %get-tuple-element.408), channel_id=1, source_target_pairs={{0,12},{1,13},{2,14},{3,15},{4,8},{5,9},{6,10},{7,11},{8,4},{9,5},... | collective-permute-start | bytes 786440 | tf_op jit(solution)/shard_map/ppermute | solution.py:784
  447.1 36.0 %collective-permute-start.26 = (bf16[4,32,1024]{2,1,0:T(8,128)(2,1)}, bf16[4,32,1024]{2,1,0:T(8,128)(2,1)}, u32[]{:S(2)}, u32[]{:S(2)}) collective-permute-start(bf16[4,32,1024]{2,1,0:T(8,128)(2,1)} %get-tuple-element.413), channel_id=1, source_target_pairs={{0,16},{16,0},{1,17},{17,1},{2,18},{18,2},{3,19},{19,3},{4,20},{20... | collective-permute-start | bytes 786440 | tf_op jit(solution)/shard_map/ppermute | solution.py:784
  488.7 62.4 %collective-permute-start.37 = (bf16[16,32,1536]{2,1,0:T(8,128)(2,1)}, bf16[16,32,1536]{2,1,0:T(8,128)(2,1)}, u32[]{:S(2)}, u32[]{:S(2)}) collective-permute-start(bf16[16,32,1536]{2,1,0:T(8,128)(2,1)} %bitcast.142), channel_id=1, source_target_pairs={{0,1},{1,0},{2,3},{3,2},{4,5},{5,4},{6,7},{7,6},{8,9},{9,8},{10,11... | collective-permute-start | bytes 4718600 | tf_op jit(solution)/shard_map/ppermute | solution.py:784
  549.7 34.7 %collective-permute-start.38 = (bf16[768,1024]{1,0:T(8,128)(2,1)}, bf16[768,1024]{1,0:T(8,128)(2,1)}, u32[]{:S(2)}, u32[]{:S(2)}) collective-permute-start(bf16[768,1024]{1,0:T(8,128)(2,1)} %get-tuple-element.475), channel_id=1, source_target_pairs={{16,0},{17,1},{18,2},{19,3},{20,4},{21,5},{22,6},{23,7},{24,8},{25... | collective-permute-start | bytes 4718600 | tf_op jit(solution)/shard_map/ppermute | solution.py:1042
  562.9 37.3 %collective-permute-start.40 = (bf16[16,32,1536]{2,1,0:T(8,128)(2,1)}, bf16[16,32,1536]{2,1,0:T(8,128)(2,1)S(1)}, u32[]{:S(2)}, u32[]{:S(2)}) collective-permute-start(bf16[16,32,1536]{2,1,0:T(8,128)(2,1)} %bitcast.143), channel_id=1, source_target_pairs={{0,1},{1,0},{2,3},{3,2},{4,5},{5,4},{6,7},{7,6},{8,9},{9,8},{10,11... | collective-permute-start | bytes 4718600 | tf_op jit(solution)/shard_map/ppermute | solution.py:784
  (124 other events, 1130.9 us)
Sparse Core Ops, SparseCore 0:
  11.0 60.5 all-gather.1

commit v3 on v2

v3 whole, which is shorter than its diff:
```python
import jax
import jax.numpy as jnp
from jax import lax
from jax.experimental import pallas as pl
from jax.experimental.pallas import tpu as pltpu
from jax.sharding import PartitionSpec as P

HDIM = 64
PAIR = 2 * HDIM
PAGE_SLOTS = 512
NEG_FILL = -1e30
EPS_NORM = 1e-05
LANES = 128
PIECE = 512
HIGH = lax.Precision.HIGHEST
MIB = 1 << 20
bf16, f32 = jnp.bfloat16, jnp.float32
Shape = pltpu.HBM


def nn(left, right):
    return lax.dot_general(
        left, right, (((1,), (0,)), ((), ())), preferred_element_type=f32
    )


def nt(left, right, precision=None):
    return lax.dot_general(
        left, right, (((1,), (1,)), ((), ())), precision=precision, preferred_element_type=f32
    )


def tn(left, right):
    return lax.dot_general(
        left, right, (((0,), (0,)), ((), ())), preferred_element_type=f32
    )


def column_sums(values):
    return jnp.sum(values.astype(f32), axis=0, keepdims=True)


def norm_unit(values):
    average = jnp.mean(values, axis=-1, keepdims=True)
    centred = values - average
    spread = jnp.mean(centred * centred, axis=-1, keepdims=True)
    inverse = lax.rsqrt(spread + EPS_NORM)
    return centred * inverse, inverse


def norm_pull(upstream, unit, inverse, gain):
    scaled = upstream * gain
    centred = scaled - jnp.mean(scaled, axis=-1, keepdims=True)
    centred = centred - unit * jnp.mean(scaled * unit, axis=-1, keepdims=True)
    return centred * inverse


def gelu_pair(values):
    share = 0.5 * (1.0 + lax.erf(values * (2.0**-0.5)))
    slope = share + values * (jnp.exp(-0.5 * values * values) * 0.3989422804014327)
    return values * share, slope


def by_core(core, value, each, fine):
    count, width = value.shape
    split = value.reshape(count // (2 * each), 2, each, width)
    found = []
    for own in range(2):
        one = jnp.where((core == 0) == (own == 0), split[:, 1], split[:, 0])
        one = one.reshape(count // (2 * each), each // fine, fine, width)
        columns = [one[..., at : at + PIECE] for at in range(0, width, PIECE)]
        one = columns[0] if len(columns) == 1 else jnp.concatenate(columns, axis=1)
        found.append(one.astype(bf16))
    return found


def head_lanes(head):
    lane = lax.broadcasted_iota(jnp.int32, (1, PAIR), 1)
    return (lane >= head * HDIM) & (lane < (head + 1) * HDIM)


def only(value, head):
    return jnp.where(head_lanes(head), value, jnp.zeros_like(value))


TINY = pl.CostEstimate(flops=1, bytes_accessed=1, transcendentals=0)


def settings(limit=48):
    return pltpu.CompilerParams(
        dimension_semantics=("arbitrary",), vmem_limit_bytes=limit * MIB
    )


def scores_of(key_rows, query, start, mask):
    score = nt(key_rows, query[start:])
    if isinstance(mask, str):
        rows = score.shape[0]
        row = lax.broadcasted_iota(jnp.int32, (rows, rows), 0)
        column = lax.broadcasted_iota(jnp.int32, (rows, rows), 1)
        corner = jnp.where(row <= column, score[:, :rows], NEG_FILL)
        if score.shape[1] == rows:
            return corner
        return jnp.concatenate([corner, score[:, rows:]], axis=1)
    return score if mask is None else score + mask


def from_start(whole, start, part, combine):
    if whole is None:
        return part
    if start == 0:
        return combine(whole, part)
    return jnp.concatenate([whole[:, :start], combine(whole[:, start:], part)], axis=1)


def forward_pair(q_ref, k_ref, v_ref, blocks, begun, out_ref, total_ref):
    values = v_ref[...].T
    outs = []
    for head in range(2):
        lanes = slice(head * HDIM, (head + 1) * HDIM)
        query = only(q_ref[...], head)
        earlier = None if begun is None else begun[1][0, head : head + 1, :]
        row_max, scores = earlier, []
        for first, rows, start, mask in blocks:
            score = scores_of(k_ref[pl.ds(first, rows), :], query, start, mask)
            row_max = from_start(row_max, start, score.max(0, keepdims=True), jnp.maximum)
            scores.append(score)
        total, out = None, None
        if begun is not None:
            total = jnp.exp(earlier - row_max)
            out = begun[0][lanes] * total
        for score, (first, rows, start, _) in zip(scores, blocks):
            exponent = jnp.exp(score - row_max[:, start:])
            total = from_start(total, start, exponent.sum(0, keepdims=True), jnp.add)
            part = nn(values[lanes, first : first + rows], exponent.astype(bf16))
            out = from_start(out, start, part, jnp.add)
        outs.append(out / total)
        total_ref[0, head : head + 1, :] = row_max + jnp.log(total)
    out_ref[...] = jnp.concatenate(outs, axis=0).T.astype(bf16)


def backward_pair(q_ref, k_ref, v_ref, out_ref, total_ref, g_ref, blocks, acc, fresh, dk_ref, dv_ref):
    queries, upstreams, keys = q_ref[...].T, g_ref[...].T, k_ref[...].T
    product = upstreams.astype(f32) * out_ref[...].T.astype(f32)
    for first, rows, start, mask in blocks:
        key_rows, value_rows = k_ref[pl.ds(first, rows), :], v_ref[pl.ds(first, rows), :]
        key_grads, value_grads = [], []
        for head in range(2):
            lanes = slice(head * HDIM, (head + 1) * HDIM)
            inner = product[lanes, start:].sum(0, keepdims=True)
            score = scores_of(key_rows, only(q_ref[...], head), start, mask)
            soft = jnp.exp(score - total_ref[0, head : head + 1, start:])
            grad_soft = nt(value_rows, only(g_ref[...], head)[start:])
            grad_score = (soft * (grad_soft - inner)).astype(bf16)
            value_grads.append(nt(upstreams[lanes, start:], soft.astype(bf16)))
            key_grads.append(nt(queries[lanes, start:], grad_score))
            part = nn(keys[lanes, first : first + rows], grad_score)
            if fresh and first == 0:
                acc[lanes, start:] = part
            else:
                acc[lanes, start:] += part
        dk_ref[pl.ds(first, rows), :] = jnp.concatenate(key_grads, axis=0).T.astype(bf16)
        dv_ref[pl.ds(first, rows), :] = jnp.concatenate(value_grads, axis=0).T.astype(bf16)


def causal_blocks(rows, size=256):
    return [(at, size, at, "causal") for at in range(0, rows, size)]


def totals_shape(rows, width):
    return (width // PAIR, 2, rows)


def own_forward(query, keys, values):
    rows, width = query.shape

    def body(q_ref, k_ref, v_ref, out_ref, total_ref):
        forward_pair(q_ref, k_ref, v_ref, causal_blocks(rows), None, out_ref, total_ref)

    block = pl.BlockSpec((rows, PAIR), lambda p: (0, p))
    total = pl.BlockSpec((1, 2, rows), lambda p: (p, 0, 0))
    return pl.pallas_call(
        body,
        out_shape=(Shape((rows, width), bf16), Shape(totals_shape(rows, width), f32)),
        grid=(width // PAIR,),
        in_specs=[block] * 3,
        out_specs=[block, total],
        cost_estimate=TINY,
        compiler_params=settings(),
        name="own_forward",
    )(query, keys, values)


def lead_forward(query, keys, values, begun, begun_total, trailing):
    rows, width = query.shape

    def body(flag, q_ref, k_ref, v_ref, begun_ref, old_ref, out_ref, total_ref):
        @pl.when(flag[0] == 1)
        def _():
            begun = (begun_ref[...].T.astype(f32), old_ref)
            blocks = [(0, rows, 0, None)]
            forward_pair(q_ref, k_ref, v_ref, blocks, begun, out_ref, total_ref)

        @pl.when(flag[0] == 0)
        def _():
            out_ref[...] = begun_ref[...]
            total_ref[...] = old_ref[...]

    block = pl.BlockSpec((rows, PAIR), lambda p, flag: (0, p))
    total = pl.BlockSpec((1, 2, rows), lambda p, flag: (p, 0, 0))
    return pl.pallas_call(
        body,
        out_shape=(Shape((rows, width), bf16), Shape(totals_shape(rows, width), f32)),
        grid_spec=pltpu.PrefetchScalarGridSpec(
            num_scalar_prefetch=1,
            grid=(width // PAIR,),
            in_specs=[block] * 4 + [total],
            out_specs=[block, total],
        ),
        cost_estimate=TINY,
        compiler_params=settings(),
        name="lead_forward",
    )(trailing, query, keys, values, begun, begun_total)


def slot_bias(filled_ref, slots):
    slot = lax.broadcasted_iota(jnp.int32, (slots, 1), 0)
    return jnp.where(slot < filled_ref[0], 0.0, NEG_FILL)


def cross_forward(query, keys, values, filled):
    rows, width = query.shape
    slots = keys.shape[0]

    def body(filled_ref, q_ref, k_ref, v_ref, out_ref, total_ref):
        blocks = [(0, slots, 0, slot_bias(filled_ref, slots))]
        forward_pair(q_ref, k_ref, v_ref, blocks, None, out_ref, total_ref)

    block = pl.BlockSpec((rows, PAIR), lambda p, f: (0, p))
    page = pl.BlockSpec((slots, PAIR), lambda p, f: (0, p))
    total = pl.BlockSpec((1, 2, rows), lambda p, f: (p, 0, 0))
    return pl.pallas_call(
        body,
        out_shape=(Shape((rows, width), bf16), Shape(totals_shape(rows, width), f32)),
        grid_spec=pltpu.PrefetchScalarGridSpec(
            num_scalar_prefetch=1,
            grid=(width // PAIR,),
            in_specs=[block, page, page],
            out_specs=[block, total],
        ),
        cost_estimate=TINY,
        compiler_params=settings(),
        name="cross_forward",
    )(filled, query, keys, values)


def lead_backward(query, keys, values, out, total, grad, trailing, first, pairs, size=384):
    rows = query.shape[0]

    def body(flag, q_ref, k_ref, v_ref, out_ref, total_ref, g_ref, dq_ref, dk_ref, dv_ref):
        @pl.when(flag[0] == 1)
        def _():
            blocks = [(at, size, 0, None) for at in range(0, rows, size)]
            backward_pair(
                q_ref, k_ref, v_ref, out_ref, total_ref, g_ref, blocks, dq_ref, True, dk_ref, dv_ref
            )

        @pl.when(flag[0] == 0)
        def _():
            for ref in (dq_ref, dk_ref, dv_ref):
                ref[...] = jnp.zeros_like(ref)

    source = pl.BlockSpec((rows, PAIR), lambda p, flag: (0, p + first))
    target = pl.BlockSpec((rows, PAIR), lambda p, flag: (0, p))
    totals = pl.BlockSpec((1, 2, rows), lambda p, flag: (p + first, 0, 0))
    return pl.pallas_call(
        body,
        out_shape=[Shape((pairs * PAIR, rows), f32)] + [Shape((rows, pairs * PAIR), bf16)] * 2,
        grid_spec=pltpu.PrefetchScalarGridSpec(
            num_scalar_prefetch=1,
            grid=(pairs,),
            in_specs=[source] * 4 + [totals, source],
            out_specs=[pl.BlockSpec((PAIR, rows), lambda p, flag: (p, 0)), target, target],
        ),
        cost_estimate=TINY,
        compiler_params=settings(),
        name="lead_backward",
    )(trailing, query, keys, values, out, total, grad)


def own_backward(query, keys, values, out, total, grad, begun, first, pairs):
    rows = query.shape[0]

    def body(q_ref, k_ref, v_ref, out_ref, total_ref, g_ref, begun_ref, dq_ref, dk_ref, dv_ref, acc):
        acc[...] = begun_ref[...]
        backward_pair(
            q_ref, k_ref, v_ref, out_ref, total_ref, g_ref, causal_blocks(rows), acc, False,
            dk_ref, dv_ref,
        )
        dq_ref[...] = (acc[...] * (HDIM**-0.5)).T.astype(bf16)

    source = pl.BlockSpec((rows, PAIR), lambda p: (0, p + first))
    target = pl.BlockSpec((rows, PAIR), lambda p: (0, p))
    totals = pl.BlockSpec((1, 2, rows), lambda p: (p + first, 0, 0))
    return pl.pallas_call(
        body,
        out_shape=[Shape((rows, pairs * PAIR), bf16)] * 3,
        grid=(pairs,),
        in_specs=[source] * 4 + [totals, source, pl.BlockSpec((PAIR, rows), lambda p: (p, 0))],
        out_specs=[target] * 3,
        scratch_shapes=[pltpu.VMEM((PAIR, rows), f32)],
        cost_estimate=TINY,
        compiler_params=settings(),
        name="own_backward",
    )(query, keys, values, out, total, grad, begun)


def cross_backward(query, keys, values, out, total, grad, filled, first, pairs):
    rows, slots = query.shape[0], keys.shape[0]

    def body(
        filled_ref, q_ref, k_ref, v_ref, out_ref, total_ref, g_ref, dq_ref, dk_ref, dv_ref, acc
    ):
        blocks = [(0, slots, 0, slot_bias(filled_ref, slots))]
        backward_pair(
            q_ref, k_ref, v_ref, out_ref, total_ref, g_ref, blocks, acc, True, dk_ref, dv_ref
        )
        dq_ref[...] = (acc[...] * (HDIM**-0.5)).T.astype(bf16)

    source = pl.BlockSpec((rows, PAIR), lambda p, f: (0, p + first))
    page = pl.BlockSpec((slots, PAIR), lambda p, f: (0, p + first))
    target = pl.BlockSpec((rows, PAIR), lambda p, f: (0, p))
    page_target = pl.BlockSpec((slots, PAIR), lambda p, f: (0, p))
    totals = pl.BlockSpec((1, 2, rows), lambda p, f: (p + first, 0, 0))
    return pl.pallas_call(
        body,
        out_shape=[Shape((rows, pairs * PAIR), bf16)] + [Shape((slots, pairs * PAIR), bf16)] * 2,
        grid_spec=pltpu.PrefetchScalarGridSpec(
            num_scalar_prefetch=1,
            grid=(pairs,),
            in_specs=[source, page, page, source, totals, source],
            out_specs=[target, page_target, page_target],
            scratch_shapes=[pltpu.VMEM((PAIR, rows), f32)],
        ),
        cost_estimate=TINY,
        compiler_params=settings(),
        name="cross_backward",
    )(filled, query, keys, values, out, total, grad)


def feed_forward(after_one, mixed, merge, cotangent, vectors, expand, bias, reduce, info, owners):
    rows, width = after_one.shape
    hidden = expand.shape[1]
    block, tall = PIECE, 384
    steps, fine, others = hidden // block, width // owners, owners // 2
    tall_pieces = hidden // owners // fine * (width // PIECE)
    starts = range(0, rows, tall)

    def body(
        info_ref, after_ref, mixed_ref, merge_ref, cot_ref, vec_ref, we_ref, be_ref, wr_ref,
        out_ref, two_ref, cross_ref, rs_ref, ro_ref, es_ref, eo_ref, ms_ref, mo_ref, eb_ref,
        sums_ref, after, h, h_flip, g, branch, up, act, gp,
    ):
        step = pl.program_id(0)
        core, place, length = info_ref[0], info_ref[1], info_ref[2]

        def valid(start):
            row = lax.broadcasted_iota(jnp.int32, (tall, 1), 0) + (start + place)
            return (row < length).astype(f32)

        @pl.when(step == 0)
        def _():
            total = jnp.zeros((1, width), f32)
            for start in starts:
                at = pl.ds(start, tall)
                x = after_ref[at, :] + nn(mixed_ref[at, :], merge_ref[...]) + vec_ref[0:1, :]
                after[at, :] = x
                unit, _ = norm_unit(x)
                low = (unit * vec_ref[1:2, :] + vec_ref[2:3, :]).astype(bf16)
                h[at, :] = low
                h_flip[:, at] = low.T
                grad = (valid(start) * cot_ref[at, :].astype(f32)).astype(bf16)
                g[at, :] = grad
                total = total + column_sums(grad)
                branch[at, :] = jnp.zeros((tall, width), f32)
                up[at, :] = jnp.zeros((tall, width), f32)
            sums_ref[0:1, :] = total

        we, wr = we_ref[...], wr_ref[...]
        for start in starts:
            at = pl.ds(start, tall)
            low, slope = gelu_pair(nn(h[at, :], we) + be_ref[...])
            low = low.astype(bf16)
            act[at, :] = low
            branch[at, :] += nn(low, wr)
            grad = (nt(g[at, :], wr) * slope).astype(bf16)
            gp[at, :] = grad
            up[at, :] += nt(grad, we)
        rs_ref[...], ro_ref[...] = by_core(core, tn(act[...], g[...]), hidden // owners, fine)
        es_ref[...], eo_ref[...] = by_core(core, nn(h_flip[...], gp[...]), fine, fine)
        eb_ref[...] = nn(jnp.ones((8, rows), bf16), gp[...])

        @pl.when(step == steps - 1)
        def _():
            gains = jnp.zeros((1, width), f32)
            shifts, merges = gains, gains
            for start in starts:
                at = pl.ds(start, tall)
                x, ok = after[at, :], valid(start)
                out_ref[at, :] = (ok * (x + branch[at, :] + vec_ref[3:4, :])).astype(bf16)
                unit, inverse = norm_unit(x)
                upstream = up[at, :]
                gains = gains + jnp.sum(upstream * unit, axis=0, keepdims=True)
                shifts = shifts + jnp.sum(upstream, axis=0, keepdims=True)
                pulled = norm_pull(upstream, unit, inverse, vec_ref[1:2, :])
                two = ok * cot_ref[at, :].astype(f32) + pulled
                two_ref[at, :] = two
                low = two.astype(bf16)
                g[at, :] = low
                merges = merges + column_sums(low)
                cross_ref[at, :] = nt(low, merge_ref[...]).astype(bf16)
            ms_ref[...], mo_ref[...] = by_core(core, tn(mixed_ref[...], g[...]), fine, fine)
            sums_ref[1:2, :], sums_ref[2:3, :], sums_ref[3:4, :] = gains, shifts, merges

    def once(shape):
        return pl.BlockSpec(shape, lambda i, info: (0, 0), pipeline_mode=pl.Buffered(1))

    def fixed(shape):
        return pl.BlockSpec(shape, lambda i, info: (0,) * len(shape))

    rows_each = others // steps
    by_row = pl.BlockSpec((rows_each, tall_pieces, fine, PIECE), lambda i, info: (i, 0, 0, 0))
    by_column = pl.BlockSpec((others, 1, fine, PIECE), lambda i, info: (0, i, 0, 0))
    merged = (others, width // PIECE, fine, PIECE)
    full, low = (rows, width), (rows, width)
    return pl.pallas_call(
        body,
        out_shape=[
            Shape(full, bf16), Shape(full, f32), Shape(full, bf16),
            *[Shape((others, tall_pieces, fine, PIECE), bf16)] * 2,
            *[Shape((others, steps, fine, PIECE), bf16)] * 2,
            *[Shape(merged, bf16)] * 2,
            Shape((8, hidden), f32), Shape((8, width), f32),
        ],
        grid_spec=pltpu.PrefetchScalarGridSpec(
            num_scalar_prefetch=1,
            grid=(steps,),
            in_specs=[
                once(full), once(full), once((width, width)), once(full), once((8, width)),
                pl.BlockSpec((width, block), lambda i, info: (0, i)),
                pl.BlockSpec((1, block), lambda i, info: (0, i)),
                pl.BlockSpec((block, width), lambda i, info: (i, 0)),
            ],
            out_specs=[
                fixed(full), fixed(full), fixed(full), by_row, by_row, by_column, by_column,
                fixed(merged), fixed(merged),
                pl.BlockSpec((8, block), lambda i, info: (0, i)),
                fixed((8, width)),
            ],
            scratch_shapes=[
                pltpu.VMEM(full, f32), pltpu.VMEM(low, bf16), pltpu.VMEM((width, rows), bf16),
                pltpu.VMEM(low, bf16), pltpu.VMEM(full, f32), pltpu.VMEM(full, f32),
                pltpu.VMEM((rows, block), bf16), pltpu.VMEM((rows, block), bf16),
            ],
        ),
        cost_estimate=TINY,
        compiler_params=settings(60),
        name="feed_forward",
    )(info, after_one, mixed, merge, cotangent, vectors, expand, bias, reduce)


def streamed(name, body, info, inputs, outs, scratch=()):
    n, m = len(inputs), len(outs)

    def kernel(info_ref, *refs):
        ins, dests = refs[:n], refs[n : n + m]
        held, made = refs[n + m : 2 * n + m], refs[2 * n + m : 2 * n + 2 * m]
        in_sem, out_sem = refs[2 * n + 2 * m : 2 * n + 2 * m + 2]
        rest = refs[2 * n + 2 * m + 2 :]
        loads = [pltpu.make_async_copy(ins[i], held[i], in_sem.at[i]) for i in range(n)]
        for load in loads:
            load.start()
        waited, stores = set(), {}

        def need(i):
            if i not in waited:
                loads[i].wait()
                waited.add(i)
            return held[i]

        def give(i, send=False):
            if send:
                stores[i] = pltpu.make_async_copy(made[i], dests[i], out_sem.at[i])
                stores[i].start()
            return made[i]

        body(info_ref, need, give, *rest)
        for i in range(m):
            stores[i].wait()

    anywhere = pl.BlockSpec(memory_space=pltpu.HBM)
    return pl.pallas_call(
        kernel,
        out_shape=[Shape(shape, kind) for shape, kind in outs],
        grid_spec=pltpu.PrefetchScalarGridSpec(
            num_scalar_prefetch=1,
            grid=(1,),
            in_specs=[anywhere] * n,
            out_specs=[anywhere] * m,
            scratch_shapes=[pltpu.VMEM(value.shape, value.dtype) for value in inputs]
            + [pltpu.VMEM(shape, kind) for shape, kind in outs]
            + [pltpu.SemaphoreType.DMA((n,)), pltpu.SemaphoreType.DMA((m,))]
            + list(scratch),
        ),
        cost_estimate=TINY,
        compiler_params=settings(60),
        name=name,
    )(info, *inputs)


def probe_backward(info, probe_low, probe_high, probe_weight, after_one, two, output_weight, mixed, vectors, owners):
    rows, width = after_one.shape
    half, tall, fine = width // 2, 256, width // owners

    def body(info_ref, need, give, hidden, low_grad):
        core = info_ref[0]
        left, right = need(0), need(1)
        weight = need(2)
        vec = need(7)
        x_ref, two_ref = need(3), need(4)
        gains = jnp.zeros((1, width), f32)
        shifts, outs = gains, gains
        for start in range(0, rows, tall):
            at = pl.ds(start, tall)
            up = nt(left[at, :], weight[:, :half]) + nt(right[at, :], weight[:, half:])
            unit, inverse = norm_unit(x_ref[at, :])
            hidden[at, :] = (unit * vec[0:1, :] + vec[1:2, :]).astype(bf16)
            gains = gains + jnp.sum(up * unit, axis=0, keepdims=True)
            shifts = shifts + jnp.sum(up, axis=0, keepdims=True)
            one = two_ref[at, :] + norm_pull(up, unit, inverse, vec[0:1, :])
            give(0)[at, :] = one
            low = one.astype(bf16)
            low_grad[at, :] = low
            outs = outs + column_sums(low)
            if start == 0:
                need(5)
            give(1)[at, :] = nt(low, need(5)[...]).astype(bf16)
        give(0, True)
        give(1, True)
        sums = give(4)
        sums[...] = jnp.zeros_like(sums)
        sums[0:1, :], sums[1:2, :], sums[2:3, :] = gains, shifts, outs
        sums[3:4, :half] = column_sums(left[...])
        sums[3:4, half:] = column_sums(right[...])
        give(4, True)
        mixed_ref = need(6)
        columns = (
            (0, 1, hidden, left[...]),
            (1, 2, hidden, right[...]),
            (2, 4, mixed_ref, low_grad[...]),
        )
        for begin, end, source, grads in columns:
            pair = by_core(core, tn(source[...], grads), fine, fine)
            give(2)[:, begin:end], give(3)[:, begin:end] = pair
        give(2, True)
        give(3, True)

    return streamed(
        "probe_backward",
        body,
        info,
        [probe_low, probe_high, probe_weight, after_one, two, output_weight, mixed, vectors],
        [
            ((rows, width), f32), ((rows, width), bf16),
            ((owners // 2, 4, fine, PIECE), bf16), ((owners // 2, 4, fine, PIECE), bf16),
            ((8, width), f32),
        ],
        [pltpu.VMEM((rows, width), bf16), pltpu.VMEM((rows, width), bf16)],
    )


def page_backward(
    info, key_low, key_high, value_low, value_high, page_rows, key_weight, value_weight, owners,
    patch_total,
):
    slots, width = page_rows.shape
    half, fine = width // 2, width // owners
    patch_shape = (owners // 2, patch_total // owners // fine * (width // PIECE), fine, PIECE)

    def body(info_ref, need, give):
        core, page = info_ref[0], info_ref[3]
        kl, kh, vl, vh = need(0)[...], need(1)[...], need(2)[...], need(3)[...]
        rows_ref = need(4)
        for i, grads in enumerate((kl, kh, vl, vh)):
            pair = by_core(core, tn(rows_ref[...], grads), fine, fine)
            give(0)[:, i : i + 1], give(1)[:, i : i + 1] = pair
        give(0, True)
        give(1, True)
        wk, wv = need(5), need(6)
        total = nt(kl, wk[:, :half]) + nt(kh, wk[:, half:])
        total = total + nt(vl, wv[:, :half]) + nt(vh, wv[:, half:])
        pair = by_core(core, total, patch_total // owners, fine)
        each = pair[0].shape[0]
        at = pl.ds(pl.multiple_of(page * each, each), each)
        for which in range(2):
            give(2 + which)[...] = jnp.zeros(patch_shape, bf16)
            give(2 + which)[at] = pair[which]
            give(2 + which, True)
        sums = give(4)
        sums[...] = jnp.zeros_like(sums)
        sums[0:1, :half] = column_sums(vl)
        sums[0:1, half:] = column_sums(vh)
        give(4, True)

    return streamed(
        "page_backward",
        body,
        info,
        [key_low, key_high, value_low, value_high, page_rows, key_weight, value_weight],
        [
            ((owners // 2, 4, fine, PIECE), bf16), ((owners // 2, 4, fine, PIECE), bf16),
            (patch_shape, bf16), (patch_shape, bf16), ((8, width), f32),
        ],
    )


def lead_upstream(info, keys, values, key_weight, value_weight, lead_tokens, vectors):
    rows, width = lead_tokens.shape
    half, tall = width // 2, 256

    def body(info_ref, need, give, hidden):
        kl, kh, vl, vh = need(0), need(1), need(2), need(3)
        wk, wv = need(4), need(5)
        x_ref, vec = need(6), need(7)
        gains = jnp.zeros((1, width), f32)
        shifts = gains
        for start in range(0, rows, tall):
            at = pl.ds(start, tall)
            up = nt(kl[at, :], wk[:, :half]) + nt(kh[at, :], wk[:, half:])
            up = up + nt(vl[at, :], wv[:, :half]) + nt(vh[at, :], wv[:, half:])
            give(0)[at, :] = up.astype(bf16)
            unit, _ = norm_unit(x_ref[at, :].astype(f32))
            hidden[at, :] = (unit * vec[0:1, :] + vec[1:2, :]).astype(bf16)
            gains = gains + jnp.sum(up * unit, axis=0, keepdims=True)
            shifts = shifts + jnp.sum(up, axis=0, keepdims=True)
        give(0, True)
        sums = give(2)
        sums[...] = jnp.zeros_like(sums)
        sums[0:1, :], sums[1:2, :] = gains, shifts
        sums[2:3, :half], sums[2:3, half:] = column_sums(vl[...]), column_sums(vh[...])
        give(2, True)
        for i, ref in enumerate((kl, kh, vl, vh)):
            give(1)[:, i * half : (i + 1) * half] = tn(hidden[...], ref[...]).astype(bf16)
        give(1, True)

    return streamed(
        "lead_upstream",
        body,
        info,
        [*keys, *values, key_weight, value_weight, lead_tokens, vectors],
        [((rows, width), bf16), ((width, 2 * width), bf16), ((8, width), f32)],
        [pltpu.VMEM((rows, width), bf16)],
    )


def projection_grads(info, hidden, query_grad, key_grad, value_grad, lead_part, high, owners):
    rows, width = hidden.shape
    half, fine = width // 2, width // owners
    column = half if high else 0

    def body(info_ref, need, give):
        core = info_ref[0]
        h = need(0)
        for i in range(3):
            total = tn(h[...], need(1 + i)[...])
            if i:
                base = (i - 1) * width + column
                total = total + need(4)[:, base : base + half].astype(f32)
            pair = by_core(core, total, fine, fine)
            give(0)[:, i : i + 1], give(1)[:, i : i + 1] = pair
        give(0, True)
        give(1, True)

    return streamed(
        "projection_grads",
        body,
        info,
        [hidden, query_grad, key_grad, value_grad, lead_part],
        [((owners // 2, 3, fine, PIECE), bf16)] * 2,
    )


def first_norm_backward(info, queries, keys, values, weights, tokens, one, returned, vectors, first, count, held):
    rows, width = tokens.shape
    half, tall = width // 2, count // 2
    n = 0 if held is None else 1

    def body(info_ref, *refs):
        grads = refs[:6]
        wq, wk, wv, x_ref, vec, one_ref, back_ref = refs[6:13]
        out_ref, sums = refs[13 + n :]
        gains = jnp.zeros((1, width), f32)
        shifts = gains
        for start in range(0, count, tall):
            at = pl.ds(start, tall)
            up = 0.0
            for i, weight in enumerate((wq, wk, wv)):
                up = up + nt(grads[2 * i][at, :], weight[:, :half])
                up = up + nt(grads[2 * i + 1][at, :], weight[:, half:])
            unit, inverse = norm_unit(x_ref[at, :].astype(f32))
            gains = gains + jnp.sum(up * unit, axis=0, keepdims=True)
            shifts = shifts + jnp.sum(up, axis=0, keepdims=True)
            up = up + back_ref[at, :].astype(f32)
            out_ref[at, :] = one_ref[at, :] + norm_pull(up, unit, inverse, vec[0:1, :])
        sums[...] = jnp.zeros_like(sums)
        sums[0:1, :], sums[1:2, :] = gains, shifts
        sums[2:3, :half], sums[2:3, half:] = column_sums(grads[0][...]), column_sums(grads[1][...])
        sums[3:4, :half], sums[3:4, half:] = column_sums(grads[4][...]), column_sums(grads[5][...])

    block = first // count
    narrow = pl.BlockSpec((count, half), lambda i, info: (block, 0))
    wide = pl.BlockSpec((count, width), lambda i, info: (block, 0))
    whole = pl.BlockSpec((width, width), lambda i, info: (0, 0))
    eight = pl.BlockSpec((8, width), lambda i, info: (0, 0))
    return pl.pallas_call(
        body,
        out_shape=[Shape((rows, width), f32), Shape((8, width), f32)],
        grid_spec=pltpu.PrefetchScalarGridSpec(
            num_scalar_prefetch=1,
            grid=(1,),
            in_specs=[narrow] * 6 + [whole] * 3 + [wide, eight, wide, wide]
            + [pl.BlockSpec(memory_space=pltpu.HBM)] * n,
            out_specs=[wide, eight],
        ),
        input_output_aliases={14: 0} if n else {},
        cost_estimate=TINY,
        compiler_params=settings(),
        name="first_norm_backward",
    )(
        info, *queries, *keys, *values, *weights, tokens, vectors, one, returned,
        *([] if held is None else [held]),
    )


def digit_axes():
    patch_bits = lax.axis_size("patch").bit_length() - 1
    return [("tok", 0)] + [("patch", bit) for bit in reversed(range(patch_bits))]


def my_digit(axis, bit):
    return (lax.axis_index(axis) >> bit) & 1


def tied(*values):
    return lax.optimization_barrier(values)


FIRST_DIGIT = 4


class Part:
    def __init__(self, kept, tok_first, shape, start=0, pieces=None):
        self.tok_first, self.shape = tok_first, shape
        self.pieces = pieces or kept.shape[1]
        self.terms = [(kept, owner_digits(), start)]


def owner_digits():
    return digit_axes()[:-1]


def stages_of(tok_first):
    every = digit_axes()
    bits = every[-2:0:-1]
    loose, last = bits[: max(len(bits) - 2, 0)], bits[max(len(bits) - 2, 0) :]
    singles = [[one] for one in loose]
    return ([every[:1]] + singles if tok_first else singles + [every[:1]]) + [last]


class Sum:
    def __init__(self, *sent):
        self.parts = [part for _, parts in sent for part in parts]
        self.at = 0
        self.leaving = [array for array, _ in sent]
        self.hops = [[("patch", 0)]] * len(sent)
        self.groups = [parts for _, parts in sent]
        self.mine = self.results = None

    def send(self):
        self.arrived = [hop(value, steps) for value, steps in zip(self.leaving, self.hops)]

    def free(self, part, at):
        settled = [one for stage in stages_of(part.tok_first)[:at] for one in stage]
        return [one for one in owner_digits() if one not in settled]

    def absorb(self, arrived):
        if self.mine is not None:
            self.results = finished([part for part in self.parts], self.mine, arrived)
            self.leaving = None
            return []
        for value, group in zip(arrived, self.groups):
            start = 0
            for part in group:
                part.terms = part.terms + [(value, self.free(part, self.at), start)]
                start += part.pieces
        stages = [stages_of(part.tok_first) for part in self.parts]
        last = self.at == len(stages[0]) - 1
        ways = [stage[self.at] for stage in stages]
        self.at += 1
        jobs, self.hops, self.groups = [], [], []
        for digits in [way for i, way in enumerate(ways) if way not in ways[:i]]:
            group = [part for part, way in zip(self.parts, ways) if way == digits]
            free = self.free(group[0], self.at)
            for flips in range(0 if last else 1, 1 << len(digits)):
                flipped = [one for i, one in enumerate(digits) if flips >> i & 1]
                choices = []
                for chunk in range(1 << len(free)):
                    bits = {one: chunk >> (len(free) - 1 - i) & 1 for i, one in enumerate(free)}
                    choices.append((bits, flipped))
                terms = [(part.terms, part.pieces) for part in group]
                jobs.append((terms, choices, bf16 if flips else f32))
                if flips:
                    self.hops.append(flipped)
                    self.groups.append(group)
        return jobs

    def take(self, made):
        if self.at == len(stages_of(True)):
            self.mine = made[0]
            made = made[1:]
        self.leaving = list(made)


def hop(value, steps):
    axis = steps[0][0]
    flip = sum(1 << bit for _, bit in steps)
    return lax.ppermute(value, axis, [(i, i ^ flip) for i in range(lax.axis_size(axis))])


def finished(parts, mine, arrived):
    def body(mine_ref, *refs):
        came, outs = refs[: len(arrived)], refs[len(arrived) :]
        piece = 0
        for part, out in zip(parts, outs):
            fine = mine_ref.shape[2]
            tall = out.shape[0] // fine
            for p in range(part.pieces):
                total = mine_ref[0, piece]
                for ref in came:
                    total = total + ref[0, piece].astype(f32)
                row, column = p % tall * fine, p // tall * PIECE
                out[row : row + fine, column : column + PIECE] = total
                piece += 1

    return pl.pallas_call(
        body,
        out_shape=[Shape(part.shape, f32) for part in parts],
        cost_estimate=TINY,
        compiler_params=pltpu.CompilerParams(vmem_limit_bytes=40 * MIB),
        name="finished",
    )(mine, *arrived)


def added_up(info, jobs):
    digits = digit_axes()
    arrays, known = [], {}
    for parts, _, _ in jobs:
        for terms, _ in parts:
            for value, _, _ in terms:
                if id(value) not in known:
                    known[id(value)] = len(arrays)
                    arrays.append(value)
    fine = arrays[0].shape[2]
    units = [(job, part) for job in range(len(jobs)) for part in range(len(jobs[job][0]))]
    loads = sum(len(jobs[job][0][part][0]) * len(jobs[job][1]) for job, part in units)

    def body(info_ref, *refs):
        n, m, k = len(arrays), len(jobs), len(units)
        ins, dests = refs[:n], refs[n : n + m]
        held, made = refs[n + m : n + m + k], refs[n + m + k : n + 2 * m + k]
        in_sem, out_sem = refs[n + 2 * m + k :]
        mine = {one: info_ref[FIRST_DIGIT + i] for i, one in enumerate(digits)}
        copies, count = [], 0
        for unit, (job, part) in enumerate(units):
            terms, pieces = jobs[job][0][part]
            copies.append([])
            for t, (value, free, start) in enumerate(terms):
                for c, (bits, flipped) in enumerate(jobs[job][1]):
                    index = 0
                    for one in free:
                        digit = bits[one] if one in bits else mine[one]
                        digit = 1 - digit if one in flipped else digit
                        index = 2 * index + digit
                    copy = pltpu.make_async_copy(
                        ins[known[id(value)]].at[index, pl.ds(start, pieces)],
                        held[unit].at[t, c],
                        in_sem.at[count],
                    )
                    copy.start()
                    copies[-1].append(copy)
                    count += 1
        offsets = [0] * m
        left = [len(jobs[job][0]) for job in range(m)]
        stores = []
        for unit, (job, part) in enumerate(units):
            terms, pieces = jobs[job][0][part]
            for copy in copies[unit]:
                copy.wait()
            offset = offsets[job]

            batch = max(one for one in range(1, 9) if pieces % one == 0)
            per = pieces // batch

            def step(i, _, unit=unit, job=job, count=len(terms), per=per, batch=batch, offset=offset):
                chunk = i // per
                for p in range(batch):
                    piece = i % per * batch + p
                    total = held[unit][0, chunk, piece].astype(f32)
                    for t in range(1, count):
                        total = total + held[unit][t, chunk, piece].astype(f32)
                    made[job][chunk, offset + piece] = total.astype(jobs[job][2])
                return 0

            lax.fori_loop(0, len(jobs[job][1]) * per, step, 0)
            offsets[job] += pieces
            left[job] -= 1
            if not left[job]:
                stores.append(pltpu.make_async_copy(made[job], dests[job], out_sem.at[job]))
                stores[-1].start()
        for store in stores:
            store.wait()

    anywhere = pl.BlockSpec(memory_space=pltpu.HBM)
    shapes = [
        ((len(choices), sum(pieces for _, pieces in parts), fine, PIECE), kind)
        for parts, choices, kind in jobs
    ]
    held = [
        pltpu.VMEM(
            (len(jobs[job][0][part][0]), len(jobs[job][1]), jobs[job][0][part][1], fine, PIECE), bf16
        )
        for job, part in units
    ]
    return pl.pallas_call(
        body,
        out_shape=[Shape(shape, kind) for shape, kind in shapes],
        grid_spec=pltpu.PrefetchScalarGridSpec(
            num_scalar_prefetch=1,
            grid=(1,),
            in_specs=[anywhere] * len(arrays),
            out_specs=[anywhere] * len(jobs),
            scratch_shapes=held
            + [pltpu.VMEM(shape, kind) for shape, kind in shapes]
            + [pltpu.SemaphoreType.DMA((loads,)), pltpu.SemaphoreType.DMA((len(jobs),))],
        ),
        cost_estimate=TINY,
        compiler_params=settings(60),
        name="added_up",
    )(info, *arrays)


def advance(info, chain, moving=(), fresh=()):
    moving = [one for one in moving if one.leaving is not None]
    chain, arrived = tied(chain, [one.arrived for one in moving])
    jobs, owners = [], []
    for one, values in zip(moving, arrived):
        new = one.absorb(values)
        owners.append((one, len(new)))
        jobs += new
    if jobs:
        made = added_up(info, jobs)
        for one, count in owners:
            if count:
                one.take(made[:count])
                made = made[count:]
    going = [one for one in moving + list(fresh) if one.leaving is not None]
    chain, leaving = tied(chain, [one.leaving for one in going])
    for one, values in zip(going, leaving):
        one.leaving = values
        one.send()
    return chain


def vector_table(feed, expand_bias, probe, page, lead, first_low, first_high):
    width = feed.shape[1]

    def body(feed_ref, bias_ref, probe_ref, page_ref, lead_ref, low_ref, high_ref, out):
        rows = [
            low_ref[0:1, :] + high_ref[0:1, :] + lead_ref[0:1, :],
            low_ref[1:2, :] + high_ref[1:2, :] + lead_ref[1:2, :],
            low_ref[2:3, :] + high_ref[2:3, :],
            low_ref[3:4, :] + high_ref[3:4, :] + lead_ref[2:3, :],
            probe_ref[2:3, :],
            probe_ref[0:1, :],
            probe_ref[1:2, :],
            probe_ref[3:4, :],
            page_ref[0:1, :],
            feed_ref[3:4, :],
            feed_ref[1:2, :],
            feed_ref[2:3, :],
            feed_ref[0:1, :],
        ]
        out[...] = jnp.zeros_like(out)
        for i, row in enumerate(rows):
            out[i : i + 1, :] = row
        out[16 : 16 + bias_ref.shape[0], :] = bias_ref[...]

    return pl.pallas_call(
        body,
        out_shape=jax.ShapeDtypeStruct((24, width), f32),
        cost_estimate=TINY,
        name="vector_table",
    )(feed, expand_bias, probe, page, lead, first_low, first_high)


def scatter_rows(table, width, first, last):
    digits = digit_axes()
    fine = width >> len(digits)
    for axis, bit in digits[first:last]:
        half = table.shape[1] // 2
        if half % LANES:
            table = table + hop(table, [(axis, bit)])
        else:
            digit = my_digit(axis, bit)
            keep = lax.dynamic_slice_in_dim(table, digit * half, half, 1)
            give = lax.dynamic_slice_in_dim(table, (1 - digit) * half, half, 1)
            table = keep + hop(give, [(axis, bit)])
    if last < len(digits):
        return table
    inside = 0
    for axis, bit in digits[(table.shape[1] // fine).bit_length() * -1 + 1 :]:
        inside = 2 * inside + my_digit(axis, bit)
    return lax.dynamic_slice_in_dim(table, inside * fine, fine, 1)


def pick_entry(table, position):
    indices = jnp.arange(table.shape[0], dtype=jnp.int32)
    return jnp.sum(jnp.where(indices == position, table, 0))


def layer_norm(values, gain, shift):
    unit, _ = norm_unit(values)
    return (unit * gain + shift).astype(bf16)


def rows_of(*vectors):
    rows = jnp.stack(vectors, axis=0)
    return jnp.pad(rows, ((0, 8 - len(vectors)), (0, 0)))


def local(
    tokens,
    patches,
    cotangent,
    lengths,
    page_of,
    page_counts,
    self_gain,
    self_shift,
    query_weight,
    query_bias,
    key_weight,
    value_weight,
    value_bias,
    output_weight,
    output_bias,
    cross_gain,
    cross_shift,
    probe_weight,
    probe_bias,
    source_key,
    source_value,
    source_bias,
    merge_weight,
    merge_bias,
    feed_gain,
    feed_shift,
    expand_weight,
    expand_bias,
    reduce_weight,
    reduce_bias,
):
    head_scale = HDIM ** (-0.5)
    tok_index = lax.axis_index("tok").astype(jnp.int32)
    sequence = lax.axis_index("patch")
    core = my_digit("patch", 0).astype(jnp.int32)
    row_count, model_width = tokens.shape[1:]
    lead_tokens = lax.ppermute(tokens[0], "tok", [(0, 1)])
    gathered = lax.all_gather(patches, ("tok", "patch"), axis=0, tiled=True)
    inputs = tokens[0].astype(f32)
    page_index = pick_entry(page_of, sequence)
    filled = pick_entry(page_counts, page_index).reshape(1)
    trailing = tok_index.reshape(1)
    page_start = page_index * PAGE_SLOTS
    digits = [my_digit(*one).astype(jnp.int32) for one in digit_axes()]
    owners = 1 << len(digits)
    info = jnp.stack(
        [core, tok_index * row_count, pick_entry(lengths, sequence), page_index] + digits
    )
    self_vectors = rows_of(self_gain, self_shift)
    cross_vectors = rows_of(cross_gain, cross_shift)
    feed_vectors = rows_of(merge_bias, feed_gain, feed_shift, reduce_bias)

    hidden_one = layer_norm(inputs, self_gain, self_shift)
    query = ((nn(hidden_one, query_weight) + query_bias) * head_scale).astype(bf16)
    own_keys = nn(hidden_one, key_weight).astype(bf16)
    own_values = (nn(hidden_one, value_weight) + value_bias).astype(bf16)
    own_mixed, own_total = own_forward(query, own_keys, own_values)
    lead_tokens, own_mixed = tied(lead_tokens, own_mixed)
    hidden_lead = layer_norm(lead_tokens.astype(f32), self_gain, self_shift)
    lead_keys = nn(hidden_lead, key_weight).astype(bf16)
    lead_values = (nn(hidden_lead, value_weight) + value_bias).astype(bf16)
    self_mixed, self_total = lead_forward(
        query, lead_keys, lead_values, own_mixed, own_total, trailing
    )
    after_one = inputs + nn(self_mixed, output_weight) + output_bias
    hidden_two = layer_norm(after_one, cross_gain, cross_shift)
    probe = ((nn(hidden_two, probe_weight) + probe_bias) * head_scale).astype(bf16)
    page_rows = lax.dynamic_slice_in_dim(gathered, page_start, PAGE_SLOTS, 0)
    page_keys = nn(page_rows, source_key).astype(bf16)
    page_values = (nn(page_rows, source_value) + source_bias).astype(bf16)
    cross_mixed, cross_total = cross_forward(probe, page_keys, page_values, filled)

    fed = feed_forward(
        after_one, cross_mixed, merge_weight, cotangent[0], feed_vectors, expand_weight,
        expand_bias[None], reduce_weight, info, owners,
    )
    block_output, grad_two, grad_cross_out = fed[:3]
    feed_sums, expand_bias_sums = fed[10], fed[9]
    fine, model = model_width // owners, (model_width // owners, model_width)
    half_model = (fine, model_width // 2)
    first = Sum(
        (fed[5], [Part(fed[6], True, (fine, expand_weight.shape[1]))]),
        (fed[3], [Part(fed[4], False, (expand_weight.shape[1] // owners, model_width))]),
        (fed[7], [Part(fed[8], False, model)]),
    )

    half_pairs = model_width // PAIR // 2
    cross_args = (probe, page_keys, page_values, cross_mixed, cross_total)
    grad_cross_out = advance(info, grad_cross_out, [], [first])
    low = cross_backward(*cross_args, grad_cross_out, filled, 0, half_pairs)
    low, grad_cross_out = advance(info, (low, grad_cross_out), [first])
    high = cross_backward(*cross_args, grad_cross_out, filled, half_pairs, half_pairs)
    patch_total = patches.shape[0] * lax.axis_size(("tok", "patch"))
    paged = page_backward(
        info, low[1], high[1], low[2], high[2], page_rows, source_key, source_value, owners,
        patch_total,
    )
    probed = probe_backward(
        info, low[0], high[0], probe_weight, after_one, grad_two, output_weight, self_mixed,
        cross_vectors, owners,
    )
    grad_one, grad_self_out, probe_sums = probed[0], probed[1], probed[4]
    second = Sum(
        (paged[0], [Part(paged[1], True, (fine, 2 * model_width))]),
        (paged[2], [Part(paged[3], False, (patches.shape[0], model_width))]),
        (probed[2], [Part(probed[3], False, (fine, 2 * model_width))]),
    )
    self_args = (query, lead_keys, lead_values, self_mixed, self_total)
    own_args = (query, own_keys, own_values, self_mixed, self_total)
    grad_self_out = advance(info, grad_self_out, [first], [second])
    lead_low = lead_backward(*self_args, grad_self_out, trailing, 0, half_pairs)
    lead_low, grad_self_out = advance(info, (lead_low, grad_self_out), [first, second])
    lead_high = lead_backward(*self_args, grad_self_out, trailing, half_pairs, half_pairs)
    led_grad, led_part, lead_sums = lead_upstream(
        info, (lead_low[1], lead_high[1]), (lead_low[2], lead_high[2]), key_weight,
        value_weight, lead_tokens, self_vectors,
    )
    led_grad, led_part, grad_self_out = advance(
        info, (led_grad, led_part, grad_self_out), [first, second]
    )
    own_low = own_backward(*own_args, grad_self_out, lead_low[0], 0, half_pairs)
    own_low, led_grad = advance(info, (own_low, led_grad), [second])
    returned = lax.ppermute(led_grad, "tok", [(1, 0)])
    parts = projection_grads(info, hidden_one, *own_low, led_part, False, owners)
    third = Sum((parts[0], [Part(parts[1], i == 1, half_model, i, 1) for i in range(3)]))
    own_low, grad_self_out = advance(info, (own_low, grad_self_out), [], [third])
    own_high = own_backward(*own_args, grad_self_out, lead_high[0], half_pairs, half_pairs)
    own_high, led_part = advance(info, (own_high, led_part), [second, third])
    parts = projection_grads(info, hidden_one, *own_high, led_part, True, owners)
    fourth = Sum((parts[0], [Part(parts[1], i != 1, half_model, i, 1) for i in range(3)]))
    own_low, own_high, returned = advance(
        info, (own_low, own_high, returned), [third], [fourth]
    )
    first_norm = (
        info, (own_low[0], own_high[0]), (own_low[1], own_high[1]), (own_low[2], own_high[2]),
        (query_weight, key_weight, value_weight), tokens[0], grad_one, returned, self_vectors,
    )
    top = first_norm_backward(*first_norm, 0, row_count // 2, None)
    top = advance(info, top, [third, fourth])
    rest = first_norm_backward(*first_norm, row_count // 2, row_count // 2, top[0])
    tokens_grad = rest[0]
    top_sums, rest_sums = advance(info, (top[1], rest[1]), [third, fourth])
    bias_rows = expand_bias_sums[0].reshape(owners, -1, fine)
    bias_rows = jnp.transpose(bias_rows, (1, 0, 2)).reshape(-1, model_width)
    table = vector_table(
        feed_sums, bias_rows, probe_sums, paged[4], lead_sums, top_sums, rest_sums
    )
    table = scatter_rows(table, model_width, 0, 3)
    table = advance(info, table, [third, fourth])
    sums = scatter_rows(table, model_width, 3, len(digits))
    totals = [first, second, third, fourth]
    while any(one.leaving is not None for one in totals):
        sums = advance(info, sums, totals)
    expand_grad, reduce_grad, merge_grad = first.results
    source_grads, patches_grad, middle_grads = second.results
    projections = [
        jnp.concatenate([one.results[i] for one in (third, fourth)], axis=1) for i in range(3)
    ]
    return (
        block_output[None],
        tokens_grad[None],
        patches_grad,
        sums[0],
        sums[1],
        projections[0],
        sums[2],
        projections[1],
        projections[2],
        sums[3],
        middle_grads[:, model_width:],
        sums[4],
        sums[5],
        sums[6],
        middle_grads[:, :model_width],
        sums[7],
        source_grads[:, :model_width],
        source_grads[:, model_width:],
        sums[8],
        merge_grad,
        sums[9],
        sums[10],
        sums[11],
        expand_grad,
        sums[16 : 16 + expand_bias.shape[0] // model_width].reshape(-1),
        reduce_grad,
        sums[12],
    )


def solution(mesh):
    placed = (
        P("patch", "tok", None),
        P(("tok", "patch"), None),
        P("patch", "tok", None),
        P(),
        P(),
        P(),
        P(),
        P(),
        P(),
        P(),
        P(),
        P(),
        P(),
        P(),
        P(),
        P(),
        P(),
        P(),
        P(),
        P(),
        P(),
        P(),
        P(),
        P(),
        P(),
        P(),
        P(),
        P(),
        P(),
        P(),
    )
    return jax.shard_map(
        local,
        mesh=mesh,
        in_specs=placed,
        out_specs=(
            P("patch", "tok", None),
            P("patch", "tok", None),
            P(("tok", "patch"), None),
            P(("tok", "patch")),
            P(("tok", "patch")),
            P(("tok", "patch"), None),
            P(("tok", "patch")),
            P(("tok", "patch"), None),
            P(("tok", "patch"), None),
            P(("tok", "patch")),
            P(("tok", "patch"), None),
            P(("tok", "patch")),
            P(("tok", "patch")),
            P(("tok", "patch")),
            P(("tok", "patch"), None),
            P(("tok", "patch")),
            P(("tok", "patch"), None),
            P(("tok", "patch"), None),
            P(("tok", "patch")),
            P(("tok", "patch"), None),
            P(("tok", "patch")),
            P(("tok", "patch")),
            P(("tok", "patch")),
            P(("tok", "patch"), None),
            P(("tok", "patch")),
            P(("tok", "patch"), None),
            P(("tok", "patch")),
        ),
        check_vma=False,
    )
```

time: 693 us -> 569 us (0.82)
  waiting for transfers between devices: 164 us -> 75.8 us
  starting transfers between devices: 115 us -> 99.6 us
  local copies, waits for them, and re-layouts: 54.3 us -> 44.9 us
  other arithmetic: 24.2 us -> 16.3 us
    ppermute x53 -> x41, waiting for transfers between devices: 139 us -> 69 us  [hop(): lax.ppermute(value, axis, [(i, i ^ flip) for i in range(lax.axis_size(axi...]
    pallas_call x4 -> x12, Pallas kernels: 46.3 us -> 72.4 us  [the longest x2 20.8 us: first_norm_backward(): pl.pallas_call(body, out_shape=[Shape((rows, width), f32), Shape((8, widt...]
    pallas_call x6 -> x5, Pallas kernels: 71.2 us -> 54.6 us  [streamed(): pl.pallas_call(kernel, out_shape=[Shape(shape, kind) for shape, kind in o...]
    ppermute x53 -> x41, starting transfers between devices: 108 us -> 92.2 us  [hop(): lax.ppermute(value, axis, [(i, i ^ flip) for i in range(lax.axis_size(axi...]
    ppermute x1, waiting for transfers between devices: 19 us -> 6.15 us  [local(): lead_tokens = lax.ppermute(tokens[0], 'tok', [(0, 1)])]
    add x14 -> x5, other arithmetic: 11.4 us -> 0.89 us  [the longest x3 0.81 us: scatter_rows(): table = keep + hop(give, [(axis, bit)])]
    another operation x10 -> x2, local copies, waits for them, and re-layouts: 11.7 us -> 2.2 us  [local(): bias_rows = expand_bias_sums[0].reshape(owners, -1, fine)]
    pallas_call x2, Pallas kernels: 32 us -> 24 us  [cross_backward(): pl.pallas_call(body, out_shape=[Shape((rows, pairs * PAIR), bf16)] + [Sha...]
  transfers between devices with their start and end apart: 56 -> 44, of which waited for: 14 -> 13; matrix products, arithmetic and copies ran while one was open for 9% -> 7% of each run, Pallas kernels for 23% -> 28%
where the time goes in v3:
time: 569 us; the launch traced here: 561 us
  Pallas kernels  287 us (50%)
  starting transfers between devices  99.6 us (18%)
  waiting for transfers between devices  75.8 us (13%)
  local copies, waits for them, and re-layouts  44.9 us (8%)
  matrix products  21.6 us (4%)
  other arithmetic  16.3 us (3%)
  between operations  16.1 us (3%)
    ppermute x41, starting transfers between devices, hop(): lax.ppermute(value, axis, [(i, i ^ flip) for i in range(lax.axis_size(axi...  92.2 us
    ppermute x41, waiting for transfers between devices, hop(): lax.ppermute(value, axis, [(i, i ^ flip) for i in range(lax.axis_size(axi...  69 us
    pallas_call x1, Pallas kernels, feed_forward(): pl.pallas_call(body, out_shape=[Shape(full, bf16), Shape(full, f32), Shap...  62.8 us
    pallas_call x5, Pallas kernels, streamed(): pl.pallas_call(kernel, out_shape=[Shape(shape, kind) for shape, kind in o...  54.6 us
    pallas_call x10, Pallas kernels, added_up(): pl.pallas_call(body, out_shape=[Shape(shape, kind) for shape, kind in sha...  47.6 us
    unnamed x160, local copies, waits for them, and re-layouts  33.4 us
    pallas_call x2, Pallas kernels, own_backward(): pl.pallas_call(body, out_shape=[Shape((rows, pairs * PAIR), bf16)] * 3, g...  25.7 us
    pallas_call x2, Pallas kernels, cross_backward(): pl.pallas_call(body, out_shape=[Shape((rows, pairs * PAIR), bf16)] + [Sha...  24 us
  transfers between devices with their start and end apart: 44, of which 13 were waited for; matrix products, arithmetic and copies ran while one was open for 7% of the time, Pallas kernels for 28%

profile of v3, /device:TPU:0, one launch (start us, length us, event | category | flops | bytes accessed | tf_op | source)
XLA Modules:
  0.0 561.4 jit_solution(7088674930686326193)
XLA Ops:
  24.7 13.9 %own_forward.1 = (bf16[768,1024]{1,0:T(8,128)(2,1)}, f32[8,2,768]{2,1,0:T(2,128)}) custom-call(bf16[768,1024]{1,0:T(8,128)(2,1)S(1)} %multiply_convert_fusion.1.q_ref, bf16[768,1024]{1,0:T(8,128)(2,1)S(1)} %convolution_convert_fusion.1.k_ref, bf16[768,1024]{1,0:T(8,128)(2,1)S(1)} %add_convert_fusion.2.v_ref), custom_call_target="tpu_custom_call" | custom-call | flops 1 | bytes 1 | tf_op jit(solution)/shard_map/own_forward/pallas_call | solution.py:182
  60.2 6.9 %lead_forward.1 = (bf16[768,1024]{1,0:T(8,128)(2,1)}, f32[8,2,768]{2,1,0:T(2,128)}) custom-call(s32[1]{0:T(128)} %bitcast.9.flag, bf16[768,1024]{1,0:T(8,128)(2,1)S(1)} %multiply_convert_fusion.1.q_ref, bf16[768,1024]{1,0:T(8,128)(2,1)S(1)} %convolution_convert_fusion.k_ref, bf16[768,1024]{1,0:T(8,128)(2,1)S(1)} %add_convert_fusion.1.v_ref, ...), custom_call_target="tpu_custom_call" | custom-call | flops 1 | bytes 1 | tf_op jit(solution)/shard_map/lead_forward/pallas_call | solution.py:211
  82.0 14.5 %cross_forward.1 = (bf16[768,1024]{1,0:T(8,128)(2,1)}, f32[8,2,768]{2,1,0:T(2,128)}) custom-call(s32[1]{0:T(128)} %bitcast.10.filled_ref, bf16[768,1024]{1,0:T(8,128)(2,1)S(1)} %copy-done.5, bf16[512,1024]{1,0:T(8,128)(2,1)S(1)} %convolution_convert_fusion.2.k_ref, bf16[512,1024]{1,0:T(8,128)(2,1)S(1)} %add_convert_fusion.3.v_ref), custom_call_target="tpu_custom_call" | custom-call | flops 1 | bytes 1 | tf_op jit(solution)/shard_map/cross_forward/pallas_call | solution.py:242
  96.5 62.8 %feed_forward.1 = (bf16[768,1024]{1,0:T(8,128)(2,1)}, f32[768,1024]{1,0:T(8,128)}, bf16[768,1024]{1,0:T(8,128)(2,1)}, bf16[16,8,32,512]{3,2,1,0:T(8,128)(2,1)}, ...) custom-call(s32[9]{0:T(128)} %stack.61.info_ref, ...), custom_call_target="tpu_custom_call" | custom-call | flops 1 | bytes 1 | tf_op jit(solution)/shard_map/feed_forward/pallas_call | solution.py:436
  165.3 12.0 %cross_backward.2 = (bf16[768,512]{1,0:T(8,128)(2,1)}, bf16[512,512]{1,0:T(8,128)(2,1)}, bf16[512,512]{1,0:T(8,128)(2,1)}) custom-call(s32[1]{0:T(128)} %bitcast.10.filled_ref, bf16[768,1024]{1,0:T(8,128)(2,1)S(1)} %copy-done.6, bf16[512,1024]{1,0:T(8,128)(2,1)S(1)} %copy-done.15, bf16[512,1024]{1,0:T(8,128)(2,1)S(1)} %copy-done.18, ...), custom_call_target="tpu_custom_call" | custom-call | flops 1 | bytes 1 | tf_op jit(solution)/shard_map/cross_backward/pallas_call | solution.py:335
  177.2 6.7 %added_up.10 = (bf16[8,8,32,512]{3,2,1,0:T(8,128)(2,1)}, bf16[8,10,32,512]{3,2,1,0:T(8,128)(2,1)}) custom-call(s32[9]{0:T(128)} %stack.61.info_ref, bf16[16,8,32,512]{3,2,1,0:T(8,128)(2,1)} %get-tuple-element.299.refs_0_, bf16[16,8,32,512]{3,2,1,0:T(8,128)(2,1)} %collective-permute-done.1.refs_1_, ...), custom_call_target="tpu_custom_call" | custom-call | flops 1 | bytes 1 | tf_op jit(solution)/shard_map/added_up/pallas_call | solution.py:944
  185.5 20.7 %collective-permute-start.4 = (bf16[8,8,32,512]{3,2,1,0:T(8,128)(2,1)}, bf16[8,8,32,512]{3,2,1,0:T(8,128)(2,1)}, u32[]{:S(2)}, u32[]{:S(2)}) collective-permute-start(bf16[8,8,32,512]{3,2,1,0:T(8,128)(2,1)} %get-tuple-element.312), channel_id=1, source_target_pairs={{0,16},{16,0},{1,17},{17,1},{2,18},{18,2},{3,19},{19,3},{4,20},{20... | collective-permute-start | bytes 6291464 | tf_op jit(solution)/shard_map/ppermute | solution.py:837
  212.1 12.1 %cross_backward.3 = (bf16[768,512]{1,0:T(8,128)(2,1)}, bf16[512,512]{1,0:T(8,128)(2,1)}, bf16[512,512]{1,0:T(8,128)(2,1)}) custom-call(s32[1]{0:T(128)} %bitcast.10.filled_ref, bf16[768,1024]{1,0:T(8,128)(2,1)S(1)} %copy-done.7, bf16[512,1024]{1,0:T(8,128)(2,1)S(1)} %copy-done.16, bf16[512,1024]{1,0:T(8,128)(2,1)S(1)} %copy-done.19, ...), custom_call_target="tpu_custom_call" | custom-call | flops 1 | bytes 1 | tf_op jit(solution)/shard_map/cross_backward/pallas_call | solution.py:335
  224.2 16.4 %probe_backward.1 = (f32[768,1024]{1,0:T(8,128)}, bf16[768,1024]{1,0:T(8,128)(2,1)}, bf16[16,4,32,512]{3,2,1,0:T(8,128)(2,1)}, bf16[16,4,32,512]{3,2,1,0:T(8,128)(2,1)}, f32[8,1024]{1,0:T(8,128)}) custom-call(s32[9]{0:T(128)} %stack.61.info_ref, bf16[768,512]{1,0:T(8,128)(2,1)} %get-tuple-element.307.refs_0_, bf16[768,512]{1,0:T(8,128)(2,1)} %get-tuple-element.309.refs_1_, ...), custom_call_target="tpu_custom_call" | custom-call | flops 1 | bytes 1 | tf_op jit(solution)/shard_map/probe_backward/pallas_call | solution.py:502
  240.5 8.9 %page_backward.1 = (bf16[16,4,32,512]{3,2,1,0:T(8,128)(2,1)}, bf16[16,4,32,512]{3,2,1,0:T(8,128)(2,1)}, bf16[16,2,32,512]{3,2,1,0:T(8,128)(2,1)}, bf16[16,2,32,512]{3,2,1,0:T(8,128)(2,1)}, f32[8,1024]{1,0:T(8,128)}) custom-call(s32[9]{0:T(128)} %stack.61.info_ref, bf16[512,512]{1,0:T(8,128)(2,1)} %get-tuple-element.319.refs_0_, ...), custom_call_target="tpu_custom_call" | custom-call | flops 1 | bytes 1 | tf_op jit(solution)/shard_map/page_backward/pallas_call | solution.py:502
  258.5 11.7 %collective-permute-start.7 = (bf16[4,10,32,512]{3,2,1,0:T(8,128)(2,1)}, bf16[4,10,32,512]{3,2,1,0:T(8,128)(2,1)}, u32[]{:S(2)}, u32[]{:S(2)}) collective-permute-start(bf16[4,10,32,512]{3,2,1,0:T(8,128)(2,1)} %get-tuple-element.331), channel_id=1, source_target_pairs={{0,16},{16,0},{1,17},{17,1},{2,18},{18,2},{3,19},{19,3},{4,20},{20... | collective-permute-start | bytes 3932168 | tf_op jit(solution)/shard_map/ppermute | solution.py:837
  279.0 16.4 %collective-permute-done.6.refs_3_ = bf16[4,8,32,512]{3,2,1,0:T(8,128)(2,1)} collective-permute-done((bf16[4,8,32,512]{3,2,1,0:T(8,128)(2,1)}, bf16[4,8,32,512]{3,2,1,0:T(8,128)(2,1)}, u32[]{:S(2)}, u32[]{:S(2)}) %collective-permute-start.6) | collective-permute-done | bytes 1048608 | tf_op jit(solution)/shard_map/ppermute | solution.py:837
  299.6 9.2 %added_up.12 = (f32[1,18,32,512]{3,2,1,0:T(8,128)}, bf16[1,18,32,512]{3,2,1,0:T(8,128)(2,1)}, bf16[1,18,32,512]{3,2,1,0:T(8,128)(2,1)}, bf16[1,18,32,512]{3,2,1,...) custom-call(s32[9]{0:T(128)} %stack.61.info_ref, ...), custom_call_target="tpu_custom_call" | custom-call | flops 1 | bytes 1 | tf_op jit(solution)/shard_map/added_up/pallas_call | solution.py:944
  324.5 13.7 %lead_upstream.1 = (bf16[768,1024]{1,0:T(8,128)(2,1)}, bf16[1024,2048]{1,0:T(8,128)(2,1)}, f32[8,1024]{1,0:T(8,128)}) custom-call(s32[9]{0:T(128)} %stack.61.info_ref, bf16[768,512]{1,0:T(8,128)(2,1)} %get-tuple-element.352.refs_0_, bf16[768,512]{1,0:T(8,128)(2,1)} %get-tuple-element.354.refs_1_, bf16[768,512]{1,0:T(8,128)(2,1)} %get-tuple-element.355.refs_2_, ...), custom_call_target="tpu_custom_call" | custom-call | flops 1 | bytes 1 | tf_op jit(solution)/shard_map/lead_upstream/pallas_call | solution.py:502
  338.2 18.3 %collective-permute-done.12.refs_1_ = bf16[1,18,32,512]{3,2,1,0:T(8,128)(2,1)} collective-permute-done((bf16[1,18,32,512]{3,2,1,0:T(8,128)(2,1)}, bf16[1,18,32,512]{3,2,1,0:T(8,128)(2,1)}, u32[]{:S(2)}, u32[]{:S(2)}) %collective-permute-start.12) | collective-permute-done | bytes 589856 | tf_op jit(solution)/shard_map/ppermute | solution.py:837
  363.1 12.7 %own_backward.2 = (bf16[768,512]{1,0:T(8,128)(2,1)}, bf16[768,512]{1,0:T(8,128)(2,1)}, bf16[768,512]{1,0:T(8,128)(2,1)}) custom-call(bf16[768,1024]{1,0:T(8,128)(2,1)S(1)} %multiply_convert_fusion.1.q_ref, bf16[768,1024]{1,0:T(8,128)(2,1)S(1)} %convolution_convert_fusion.1.k_ref, bf16[768,1024]{1,0:T(8,128)(2,1)S(1)} %copy-done.1, ...), custom_call_target="tpu_custom_call" | custom-call | flops 1 | bytes 1 | tf_op jit(solution)/shard_map/own_backward/pallas_call | solution.py:305
  381.4 7.9 %projection_grads.2 = (bf16[16,3,32,512]{3,2,1,0:T(8,128)(2,1)}, bf16[16,3,32,512]{3,2,1,0:T(8,128)(2,1)}) custom-call(s32[9]{0:T(128)} %stack.61.info_ref, bf16[768,1024]{1,0:T(8,128)(2,1)} %copy-done.49, bf16[768,512]{1,0:T(8,128)(2,1)} %get-tuple-element.436.refs_1_.refs_0_, bf16[768,512]{1,0:T(8,128)(2,1)} %get-tuple-element.438.refs_2_, ...), custom_call_target="tpu_custom_call" | custom-call | flops 1 | bytes 1 | tf_op jit(solution)/shard_map/projection_grads/pallas_call | solution.py:502
  390.6 12.2 %collective-permute-start.18 = (bf16[1,10,32,512]{3,2,1,0:T(8,128)(2,1)}, bf16[1,10,32,512]{3,2,1,0:T(8,128)(2,1)S(1)}, u32[]{:S(2)}, u32[]{:S(2)}) collective-permute-start(bf16[1,10,32,512]{3,2,1,0:T(8,128)(2,1)} %get-tuple-element.405), channel_id=1, source_target_pairs={{0,4},{1,5},{2,6},{3,7},{4,0},{5,1},{6,2},{7,3},{8,12},{9,13},{10,... | collective-permute-start | bytes 983048 | tf_op jit(solution)/shard_map/ppermute | solution.py:837
  406.8 13.0 %own_backward.3 = (bf16[768,512]{1,0:T(8,128)(2,1)}, bf16[768,512]{1,0:T(8,128)(2,1)}, bf16[768,512]{1,0:T(8,128)(2,1)}) custom-call(bf16[768,1024]{1,0:T(8,128)(2,1)S(1)} %multiply_convert_fusion.1.q_ref, bf16[768,1024]{1,0:T(8,128)(2,1)S(1)} %convolution_convert_fusion.1.k_ref, bf16[768,1024]{1,0:T(8,128)(2,1)S(1)} %copy-done.2, ...), custom_call_target="tpu_custom_call" | custom-call | flops 1 | bytes 1 | tf_op jit(solution)/shard_map/own_backward/pallas_call | solution.py:305
  419.7 8.9 %collective-permute-done.19.refs_1_ = bf16[1,10,32,512]{3,2,1,0:T(8,128)(2,1)S(1)} collective-permute-done((bf16[1,10,32,512]{3,2,1,0:T(8,128)(2,1)}, bf16[1,10,32,512]{3,2,1,0:T(8,128)(2,1)S(1)}, u32[]{:S(2)}, u32[]{:S(2)}) %collective-permute-start.19) | collective-permute-done | bytes 327712 | tf_op jit(solution)/shard_map/ppermute | solution.py:837
  436.9 7.8 %projection_grads.3 = (bf16[16,3,32,512]{3,2,1,0:T(8,128)(2,1)}, bf16[16,3,32,512]{3,2,1,0:T(8,128)(2,1)}) custom-call(s32[9]{0:T(128)} %stack.61.info_ref, bf16[768,1024]{1,0:T(8,128)(2,1)} %copy-done.49, bf16[768,512]{1,0:T(8,128)(2,1)} %get-tuple-element.437.refs_1_, bf16[768,512]{1,0:T(8,128)(2,1)} %get-tuple-element.439.refs_2_.refs_3_, ...), custom_call_target="tpu_custom_call" | custom-call | flops 1 | bytes 1 | tf_op jit(solution)/shard_map/projection_grads/pallas_call | solution.py:502
  454.6 10.4 %first_norm_backward.2 = (f32[768,1024]{1,0:T(8,128)}, f32[8,1024]{1,0:T(8,128)}) custom-call(s32[9]{0:T(128)S(1)} %copy-done.39, bf16[768,512]{1,0:T(8,128)(2,1)S(1)} %copy-done.20, bf16[768,512]{1,0:T(8,128)(2,1)S(1)} %copy-done.23, bf16[768,512]{1,0:T(8,128)(2,1)S(1)} %copy-done.21, bf16[768,512]{1,0:T(8,128)(2,1)S(1)} %copy-done.24, ...), custom_call_target="tpu_custom_call" | custom-call | flops 1 | bytes 1 | tf_op jit(solution)/shard_map/first_norm_backward/pallas_call | solution.py:725
  472.6 7.5 %collective-permute-start.28 = (bf16[1,3,32,512]{3,2,1,0:T(8,128)(2,1)}, bf16[1,3,32,512]{3,2,1,0:T(8,128)(2,1)}, u32[]{:S(2)}, u32[]{:S(2)}) collective-permute-start(bf16[1,3,32,512]{3,2,1,0:T(8,128)(2,1)} %get-tuple-element.474), channel_id=1, source_target_pairs={{0,4},{1,5},{2,6},{3,7},{4,0},{5,1},{6,2},{7,3},{8,12},{9,13},{10,... | collective-permute-start | bytes 294920 | tf_op jit(solution)/shard_map/ppermute | solution.py:837
  489.5 10.4 %first_norm_backward.3 = (f32[768,1024]{1,0:T(8,128)}, f32[8,1024]{1,0:T(8,128)}) custom-call(s32[9]{0:T(128)S(1)} %copy-done.40, bf16[768,512]{1,0:T(8,128)(2,1)S(1)} %copy-done.20, bf16[768,512]{1,0:T(8,128)(2,1)S(1)} %copy-done.23, bf16[768,512]{1,0:T(8,128)(2,1)S(1)} %copy-done.21, ...), custom_call_target="tpu_custom_call", output_to_operand_aliasing={{0}: (14, {})} | custom-call | flops 1 | bytes 1 | tf_op jit(solution)/shard_map/first_norm_backward/pallas_call | solution.py:725
  (305 shorter events, 210.4 us)
Async XLA Ops:
  7.3 69.0 %all-gather.2.cloned.1.call-start = ((), (), s32[]{:S(2)}) async-start(), calls=%async_computation | async-start | bytes 2162688 | tf_op jit(solution)/shard_map/all_gather | solution.py:1089
  8.0 41.1 %collective-permute-start = (bf16[768,1024]{1,0:T(8,128)(2,1)}, bf16[768,1024]{1,0:T(8,128)(2,1)}, u32[]{:S(2)}, u32[]{:S(2)}) collective-permute-start(bf16[768,1024]{1,0:T(8,128)(2,1)} %bitcast.71), channel_id=1, source_target_pairs={{0,16},{1,17},{2,18},{3,19},{4,20},{5,21},{6,22},{7,23},{8,24},{9,... | collective-permute-start | bytes 4718600 | tf_op jit(solution)/shard_map/ppermute | solution.py:1088
  183.9 68.5 %collective-permute-start.5 = (bf16[8,10,32,512]{3,2,1,0:T(8,128)(2,1)}, bf16[8,10,32,512]{3,2,1,0:T(8,128)(2,1)}, u32[]{:S(2)}, u32[]{:S(2)}) collective-permute-start(bf16[8,10,32,512]{3,2,1,0:T(8,128)(2,1)} %get-tuple-element.313), channel_id=1, source_target_pairs={{0,2},{1,3},{2,0},{3,1},{4,6},{5,7},{6,4},{7,5},{8,10},{9,11},{10,... | collective-permute-start | bytes 7864328 | tf_op jit(solution)/shard_map/ppermute | solution.py:837
  185.5 66.9 %collective-permute-start.4 = (bf16[8,8,32,512]{3,2,1,0:T(8,128)(2,1)}, bf16[8,8,32,512]{3,2,1,0:T(8,128)(2,1)}, u32[]{:S(2)}, u32[]{:S(2)}) collective-permute-start(bf16[8,8,32,512]{3,2,1,0:T(8,128)(2,1)} %get-tuple-element.312), channel_id=1, source_target_pairs={{0,16},{16,0},{1,17},{17,1},{2,18},{18,2},{3,19},{19,3},{4,20},{20... | collective-permute-start | bytes 6291464 | tf_op jit(solution)/shard_map/ppermute | solution.py:837
  257.9 41.6 %collective-permute-start.8 = (bf16[16,4,32,512]{3,2,1,0:T(8,128)(2,1)}, bf16[16,4,32,512]{3,2,1,0:T(8,128)(2,1)}, u32[]{:S(2)}, u32[]{:S(2)}) collective-permute-start(bf16[16,4,32,512]{3,2,1,0:T(8,128)(2,1)} %get-tuple-element.332), channel_id=1, source_target_pairs={{0,1},{1,0},{2,3},{3,2},{4,5},{5,4},{6,7},{7,6},{8,9},{9,8},{10,11... | collective-permute-start | bytes 6291464 | tf_op jit(solution)/shard_map/ppermute | solution.py:837
  258.0 41.6 %collective-permute-start.10 = (bf16[16,4,32,512]{3,2,1,0:T(8,128)(2,1)}, bf16[16,4,32,512]{3,2,1,0:T(8,128)(2,1)}, u32[]{:S(2)}, u32[]{:S(2)}) collective-permute-start(bf16[16,4,32,512]{3,2,1,0:T(8,128)(2,1)} %get-tuple-element.334), channel_id=1, source_target_pairs={{0,1},{1,0},{2,3},{3,2},{4,5},{5,4},{6,7},{7,6},{8,9},{9,8},{10,11... | collective-permute-start | bytes 6291464 | tf_op jit(solution)/shard_map/ppermute | solution.py:837
  258.5 41.1 %collective-permute-start.7 = (bf16[4,10,32,512]{3,2,1,0:T(8,128)(2,1)}, bf16[4,10,32,512]{3,2,1,0:T(8,128)(2,1)}, u32[]{:S(2)}, u32[]{:S(2)}) collective-permute-start(bf16[4,10,32,512]{3,2,1,0:T(8,128)(2,1)} %get-tuple-element.331), channel_id=1, source_target_pairs={{0,16},{16,0},{1,17},{17,1},{2,18},{18,2},{3,19},{19,3},{4,20},{20... | collective-permute-start | bytes 3932168 | tf_op jit(solution)/shard_map/ppermute | solution.py:837
  270.3 25.2 %collective-permute-start.6 = (bf16[4,8,32,512]{3,2,1,0:T(8,128)(2,1)}, bf16[4,8,32,512]{3,2,1,0:T(8,128)(2,1)}, u32[]{:S(2)}, u32[]{:S(2)}) collective-permute-start(bf16[4,8,32,512]{3,2,1,0:T(8,128)(2,1)} %get-tuple-element.330), channel_id=1, source_target_pairs={{0,2},{1,3},{2,0},{3,1},{4,6},{5,7},{6,4},{7,5},{8,10},{9,11},{10,... | collective-permute-start | bytes 3145736 | tf_op jit(solution)/shard_map/ppermute | solution.py:837
  271.8 23.7 %collective-permute-start.9 = (bf16[16,2,32,512]{3,2,1,0:T(8,128)(2,1)}, bf16[16,2,32,512]{3,2,1,0:T(8,128)(2,1)}, u32[]{:S(2)}, u32[]{:S(2)}) collective-permute-start(bf16[16,2,32,512]{3,2,1,0:T(8,128)(2,1)} %get-tuple-element.333), channel_id=1, source_target_pairs={{0,1},{1,0},{2,3},{3,2},{4,5},{5,4},{6,7},{7,6},{8,9},{9,8},{10,11... | collective-permute-start | bytes 3145736 | tf_op jit(solution)/shard_map/ppermute | solution.py:837
  308.8 47.7 %collective-permute-start.15 = (bf16[8,6,32,512]{3,2,1,0:T(8,128)(2,1)}, bf16[8,6,32,512]{3,2,1,0:T(8,128)(2,1)}, u32[]{:S(2)}, u32[]{:S(2)}) collective-permute-start(bf16[8,6,32,512]{3,2,1,0:T(8,128)(2,1)} %get-tuple-element.363), channel_id=1, source_target_pairs={{0,2},{1,3},{2,0},{3,1},{4,6},{5,7},{6,4},{7,5},{8,10},{9,11},{10,... | collective-permute-start | bytes 4718600 | tf_op jit(solution)/shard_map/ppermute | solution.py:837
  310.4 46.1 %collective-permute-start.14 = (bf16[8,4,32,512]{3,2,1,0:T(8,128)(2,1)}, bf16[8,4,32,512]{3,2,1,0:T(8,128)(2,1)}, u32[]{:S(2)}, u32[]{:S(2)}) collective-permute-start(bf16[8,4,32,512]{3,2,1,0:T(8,128)(2,1)} %get-tuple-element.362), channel_id=1, source_target_pairs={{0,16},{16,0},{1,17},{17,1},{2,18},{18,2},{3,19},{19,3},{4,20},{20... | collective-permute-start | bytes 3145736 | tf_op jit(solution)/shard_map/ppermute | solution.py:837
  312.2 26.0 %collective-permute-start.11 = (bf16[1,18,32,512]{3,2,1,0:T(8,128)(2,1)}, bf16[1,18,32,512]{3,2,1,0:T(8,128)(2,1)}, u32[]{:S(2)}, u32[]{:S(2)}) collective-permute-start(bf16[1,18,32,512]{3,2,1,0:T(8,128)(2,1)} %get-tuple-element.359), channel_id=1, source_target_pairs={{0,4},{1,5},{2,6},{3,7},{4,0},{5,1},{6,2},{7,3},{8,12},{9,13},{10,... | collective-permute-start | bytes 1769480 | tf_op jit(solution)/shard_map/ppermute | solution.py:837
  313.7 42.8 %collective-permute-start.12 = (bf16[1,18,32,512]{3,2,1,0:T(8,128)(2,1)}, bf16[1,18,32,512]{3,2,1,0:T(8,128)(2,1)}, u32[]{:S(2)}, u32[]{:S(2)}) collective-permute-start(bf16[1,18,32,512]{3,2,1,0:T(8,128)(2,1)} %get-tuple-element.360), channel_id=1, source_target_pairs={{0,8},{1,9},{2,10},{3,11},{4,12},{5,13},{6,14},{7,15},{8,0},{9,1},... | collective-permute-start | bytes 1769480 | tf_op jit(solution)/shard_map/ppermute | solution.py:837
  316.3 40.2 %collective-permute-start.13 = (bf16[1,18,32,512]{3,2,1,0:T(8,128)(2,1)}, bf16[1,18,32,512]{3,2,1,0:T(8,128)(2,1)}, u32[]{:S(2)}, u32[]{:S(2)}) collective-permute-start(bf16[1,18,32,512]{3,2,1,0:T(8,128)(2,1)} %get-tuple-element.361), channel_id=1, source_target_pairs={{0,12},{1,13},{2,14},{3,15},{4,8},{5,9},{6,10},{7,11},{8,4},{9,5},... | collective-permute-start | bytes 1769480 | tf_op jit(solution)/shard_map/ppermute | solution.py:837
  389.3 40.1 %collective-permute-start.21 = (bf16[16,3,32,512]{3,2,1,0:T(8,128)(2,1)}, bf16[16,3,32,512]{3,2,1,0:T(8,128)(2,1)}, u32[]{:S(2)}, u32[]{:S(2)}) collective-permute-start(bf16[16,3,32,512]{3,2,1,0:T(8,128)(2,1)} %get-tuple-element.408), channel_id=1, source_target_pairs={{0,1},{1,0},{2,3},{3,2},{4,5},{5,4},{6,7},{7,6},{8,9},{9,8},{10,11... | collective-permute-start | bytes 4718600 | tf_op jit(solution)/shard_map/ppermute | solution.py:837
  389.3 55.5 %collective-permute-start.22 = (bf16[768,1024]{1,0:T(8,128)(2,1)}, bf16[768,1024]{1,0:T(8,128)(2,1)}, u32[]{:S(2)}, u32[]{:S(2)}) collective-permute-start(bf16[768,1024]{1,0:T(8,128)(2,1)} %get-tuple-element.420), channel_id=1, source_target_pairs={{16,0},{17,1},{18,2},{19,3},{20,4},{21,5},{22,6},{23,7},{24,8},{25... | collective-permute-start | bytes 4718600 | tf_op jit(solution)/shard_map/ppermute | solution.py:1174
  390.6 29.1 %collective-permute-start.18 = (bf16[1,10,32,512]{3,2,1,0:T(8,128)(2,1)}, bf16[1,10,32,512]{3,2,1,0:T(8,128)(2,1)S(1)}, u32[]{:S(2)}, u32[]{:S(2)}) collective-permute-start(bf16[1,10,32,512]{3,2,1,0:T(8,128)(2,1)} %get-tuple-element.405), channel_id=1, source_target_pairs={{0,4},{1,5},{2,6},{3,7},{4,0},{5,1},{6,2},{7,3},{8,12},{9,13},{10,... | collective-permute-start | bytes 983048 | tf_op jit(solution)/shard_map/ppermute | solution.py:837
  402.9 25.8 %collective-permute-start.19 = (bf16[1,10,32,512]{3,2,1,0:T(8,128)(2,1)}, bf16[1,10,32,512]{3,2,1,0:T(8,128)(2,1)S(1)}, u32[]{:S(2)}, u32[]{:S(2)}) collective-permute-start(bf16[1,10,32,512]{3,2,1,0:T(8,128)(2,1)} %get-tuple-element.406), channel_id=1, source_target_pairs={{0,8},{1,9},{2,10},{3,11},{4,12},{5,13},{6,14},{7,15},{8,0},{9,1},... | collective-permute-start | bytes 983048 | tf_op jit(solution)/shard_map/ppermute | solution.py:837
  404.0 24.7 %collective-permute-start.20 = (bf16[1,10,32,512]{3,2,1,0:T(8,128)(2,1)}, bf16[1,10,32,512]{3,2,1,0:T(8,128)(2,1)S(1)}, u32[]{:S(2)}, u32[]{:S(2)}) collective-permute-start(bf16[1,10,32,512]{3,2,1,0:T(8,128)(2,1)} %get-tuple-element.407), channel_id=1, source_target_pairs={{0,12},{1,13},{2,14},{3,15},{4,8},{5,9},{6,10},{7,11},{8,4},{9,5},... | collective-permute-start | bytes 983048 | tf_op jit(solution)/shard_map/ppermute | solution.py:837
  470.9 29.0 %collective-permute-start.31 = (bf16[8,2,32,512]{3,2,1,0:T(8,128)(2,1)}, bf16[8,2,32,512]{3,2,1,0:T(8,128)(2,1)}, u32[]{:S(2)}, u32[]{:S(2)}) collective-permute-start(bf16[8,2,32,512]{3,2,1,0:T(8,128)(2,1)} %get-tuple-element.477), channel_id=1, source_target_pairs={{0,16},{16,0},{1,17},{17,1},{2,18},{18,2},{3,19},{19,3},{4,20},{20... | collective-permute-start | bytes 1572872 | tf_op jit(solution)/shard_map/ppermute | solution.py:837
  471.1 28.8 %collective-permute-start.32 = (bf16[8,1,32,512]{3,2,1,0:T(8,128)(2,1)}, bf16[8,1,32,512]{3,2,1,0:T(8,128)(2,1)}, u32[]{:S(2)}, u32[]{:S(2)}) collective-permute-start(bf16[8,1,32,512]{3,2,1,0:T(8,128)(2,1)} %get-tuple-element.478), channel_id=1, source_target_pairs={{0,2},{1,3},{2,0},{3,1},{4,6},{5,7},{6,4},{7,5},{8,10},{9,11},{10,... | collective-permute-start | bytes 786440 | tf_op jit(solution)/shard_map/ppermute | solution.py:837
  472.6 27.3 %collective-permute-start.28 = (bf16[1,3,32,512]{3,2,1,0:T(8,128)(2,1)}, bf16[1,3,32,512]{3,2,1,0:T(8,128)(2,1)}, u32[]{:S(2)}, u32[]{:S(2)}) collective-permute-start(bf16[1,3,32,512]{3,2,1,0:T(8,128)(2,1)} %get-tuple-element.474), channel_id=1, source_target_pairs={{0,4},{1,5},{2,6},{3,7},{4,0},{5,1},{6,2},{7,3},{8,12},{9,13},{10,... | collective-permute-start | bytes 294920 | tf_op jit(solution)/shard_map/ppermute | solution.py:837
  480.1 19.8 %collective-permute-start.29 = (bf16[1,3,32,512]{3,2,1,0:T(8,128)(2,1)}, bf16[1,3,32,512]{3,2,1,0:T(8,128)(2,1)}, u32[]{:S(2)}, u32[]{:S(2)}) collective-permute-start(bf16[1,3,32,512]{3,2,1,0:T(8,128)(2,1)} %get-tuple-element.475), channel_id=1, source_target_pairs={{0,8},{1,9},{2,10},{3,11},{4,12},{5,13},{6,14},{7,15},{8,0},{9,1},... | collective-permute-start | bytes 294920 | tf_op jit(solution)/shard_map/ppermute | solution.py:837
  481.1 18.8 %collective-permute-start.30 = (bf16[1,3,32,512]{3,2,1,0:T(8,128)(2,1)}, bf16[1,3,32,512]{3,2,1,0:T(8,128)(2,1)}, u32[]{:S(2)}, u32[]{:S(2)}) collective-permute-start(bf16[1,3,32,512]{3,2,1,0:T(8,128)(2,1)} %get-tuple-element.476), channel_id=1, source_target_pairs={{0,12},{1,13},{2,14},{3,15},{4,8},{5,9},{6,10},{7,11},{8,4},{9,5},... | collective-permute-start | bytes 294920 | tf_op jit(solution)/shard_map/ppermute | solution.py:837
  (100 other events, 735.5 us)
Sparse Core Ops, SparseCore 0:
  11.0 60.4 all-gather.1

commit v4 on v3

--- a/solution.py
+++ b/solution.py
@@ -90,6 +90,10 @@
     return pltpu.CompilerParams(
         dimension_semantics=("arbitrary",), vmem_limit_bytes=limit * MIB
     )
+
+
+def in_hbm(*values):
+    return [pltpu.with_memory_space_constraint(value, pltpu.HBM) for value in values]
 
 
 def scores_of(key_rows, query, start, mask):
@@ -188,7 +192,7 @@
         cost_estimate=TINY,
         compiler_params=settings(),
         name="own_forward",
-    )(query, keys, values)
+    )(*in_hbm(query, keys, values))
 
 
 def lead_forward(query, keys, values, begun, begun_total, trailing):
@@ -220,7 +224,7 @@
         cost_estimate=TINY,
         compiler_params=settings(),
         name="lead_forward",
-    )(trailing, query, keys, values, begun, begun_total)
+    )(trailing, *in_hbm(query, keys, values, begun, begun_total))
 
 
 def slot_bias(filled_ref, slots):
@@ -251,7 +255,7 @@
         cost_estimate=TINY,
         compiler_params=settings(),
         name="cross_forward",
-    )(filled, query, keys, values)
+    )(filled, *in_hbm(query, keys, values))
 
 
 def lead_backward(query, keys, values, out, total, grad, trailing, first, pairs, size=384):
@@ -285,7 +289,7 @@
         cost_estimate=TINY,
         compiler_params=settings(),
         name="lead_backward",
-    )(trailing, query, keys, values, out, total, grad)
+    )(trailing, *in_hbm(query, keys, values, out, total, grad))
 
 
 def own_backward(query, keys, values, out, total, grad, begun, first, pairs):
@@ -312,7 +316,7 @@
         cost_estimate=TINY,
         compiler_params=settings(),
         name="own_backward",
-    )(query, keys, values, out, total, grad, begun)
+    )(*in_hbm(query, keys, values, out, total, grad, begun))
 
 
 def cross_backward(query, keys, values, out, total, grad, filled, first, pairs):
@@ -345,22 +349,29 @@
         cost_estimate=TINY,
         compiler_params=settings(),
         name="cross_backward",
-    )(filled, query, keys, values, out, total, grad)
-
-
-def feed_forward(after_one, mixed, merge, cotangent, vectors, expand, bias, reduce, info, owners):
-    rows, width = after_one.shape
+    )(filled, *in_hbm(query, keys, values, out, total, grad))
+
+
+def feed_forward(start_from, mixed, merge, cotangent, vectors, expand, bias, reduce, info, owners, begun):
+    rows, width = start_from.shape
     hidden = expand.shape[1]
     block, tall = PIECE, 384
-    steps, fine, others = hidden // block, width // owners, owners // 2
-    tall_pieces = hidden // owners // fine * (width // PIECE)
+    steps, fine, others = hidden // block // 2, width // owners, owners // 2
     starts = range(0, rows, tall)
-
-    def body(
-        info_ref, after_ref, mixed_ref, merge_ref, cot_ref, vec_ref, we_ref, be_ref, wr_ref,
-        out_ref, two_ref, cross_ref, rs_ref, ro_ref, es_ref, eo_ref, ms_ref, mo_ref, eb_ref,
-        sums_ref, after, h, h_flip, g, branch, up, act, gp,
-    ):
+    final = begun is not None
+
+    def body(info_ref, *refs):
+        from_ref, mixed_ref, merge_ref, cot_ref, vec_ref, we_ref, be_ref, wr_ref = refs[:8]
+        refs = refs[8:]
+        if final:
+            old_refs, refs = refs[:2], refs[2:]
+            out_ref, two_ref, cross_ref, ms_ref, mo_ref = refs[:5]
+            refs = refs[5:]
+        else:
+            new_refs, refs = refs[:3], refs[3:]
+        rs_ref, ro_ref, es_ref, eo_ref, eb_ref, sums_ref = refs[:6]
+        h, h_flip, g, branch, up, act, gp, sems = refs[6:14]
+        after = from_ref if final else refs[14]
         step = pl.program_id(0)
         core, place, length = info_ref[0], info_ref[1], info_ref[2]
 
@@ -368,13 +379,26 @@
             row = lax.broadcasted_iota(jnp.int32, (tall, 1), 0) + (start + place)
             return (row < length).astype(f32)
 
+        def copy(i):
+            inside = (branch, up, after)[i]
+            if final:
+                return pltpu.make_async_copy(old_refs[i], inside, sems.at[i])
+            return pltpu.make_async_copy(inside, new_refs[i], sems.at[i])
+
         @pl.when(step == 0)
         def _():
+            if final:
+                copy(0).start()
+                copy(1).start()
             total = jnp.zeros((1, width), f32)
             for start in starts:
                 at = pl.ds(start, tall)
-                x = after_ref[at, :] + nn(mixed_ref[at, :], merge_ref[...]) + vec_ref[0:1, :]
-                after[at, :] = x
+                x = from_ref[at, :]
+                if not final:
+                    x = x + nn(mixed_ref[at, :], merge_ref[...]) + vec_ref[0:1, :]
+                    after[at, :] = x
+                    branch[at, :] = jnp.zeros((tall, width), f32)
+                    up[at, :] = jnp.zeros((tall, width), f32)
                 unit, _ = norm_unit(x)
                 low = (unit * vec_ref[1:2, :] + vec_ref[2:3, :]).astype(bf16)
                 h[at, :] = low
@@ -382,9 +406,13 @@
                 grad = (valid(start) * cot_ref[at, :].astype(f32)).astype(bf16)
                 g[at, :] = grad
                 total = total + column_sums(grad)
-                branch[at, :] = jnp.zeros((tall, width), f32)
-                up[at, :] = jnp.zeros((tall, width), f32)
+            sums_ref[...] = jnp.zeros_like(sums_ref)
             sums_ref[0:1, :] = total
+            if final:
+                copy(0).wait()
+                copy(1).wait()
+            else:
+                copy(2).start()
 
         we, wr = we_ref[...], wr_ref[...]
         for start in starts:
@@ -396,12 +424,26 @@
             grad = (nt(g[at, :], wr) * slope).astype(bf16)
             gp[at, :] = grad
             up[at, :] += nt(grad, we)
-        rs_ref[...], ro_ref[...] = by_core(core, tn(act[...], g[...]), hidden // owners, fine)
+        if not final:
+            @pl.when(step == steps - 1)
+            def _():
+                copy(0).start()
+                copy(1).start()
+
+        each = hidden // owners // fine
+        for ref, one in zip(
+            (rs_ref, ro_ref), by_core(core, tn(act[...], g[...]), hidden // owners, fine)
+        ):
+            ref[0], ref[1] = one[:, :each], one[:, each:]
         es_ref[...], eo_ref[...] = by_core(core, nn(h_flip[...], gp[...]), fine, fine)
         eb_ref[...] = nn(jnp.ones((8, rows), bf16), gp[...])
 
         @pl.when(step == steps - 1)
         def _():
+            if not final:
+                for i in range(3):
+                    copy(i).wait()
+                return
             gains = jnp.zeros((1, width), f32)
             shifts, merges = gains, gains
             for start in starts:
@@ -422,51 +464,62 @@
             ms_ref[...], mo_ref[...] = by_core(core, tn(mixed_ref[...], g[...]), fine, fine)
             sums_ref[1:2, :], sums_ref[2:3, :], sums_ref[3:4, :] = gains, shifts, merges
 
+    base = steps if final else 0
+
     def once(shape):
         return pl.BlockSpec(shape, lambda i, info: (0, 0), pipeline_mode=pl.Buffered(1))
 
     def fixed(shape):
         return pl.BlockSpec(shape, lambda i, info: (0,) * len(shape))
 
-    rows_each = others // steps
-    by_row = pl.BlockSpec((rows_each, tall_pieces, fine, PIECE), lambda i, info: (i, 0, 0, 0))
+    each = hidden // owners // fine
+    pairs = others // 2 // steps
+    by_row = pl.BlockSpec((2, pairs, each, fine, PIECE), lambda i, info: (0, i, 0, 0, 0))
     by_column = pl.BlockSpec((others, 1, fine, PIECE), lambda i, info: (0, i, 0, 0))
     merged = (others, width // PIECE, fine, PIECE)
-    full, low = (rows, width), (rows, width)
+    hbm = pl.BlockSpec(memory_space=pltpu.HBM)
+    full = (rows, width)
+    shared_shapes = [
+        *[Shape((2, others // 2, each, fine, PIECE), bf16)] * 2,
+        *[Shape((others, steps, fine, PIECE), bf16)] * 2,
+        Shape((8, hidden // 2), f32), Shape((8, width), f32),
+    ]
+    shared_specs = [
+        by_row, by_row, by_column, by_column,
+        pl.BlockSpec((8, block), lambda i, info: (0, i)), fixed((8, width)),
+    ]
+    if final:
+        shapes = [Shape(full, bf16), Shape(full, f32), Shape(full, bf16), Shape(merged, bf16), Shape(merged, bf16)]
+        specs = [fixed(full)] * 3 + [fixed(merged)] * 2
+    else:
+        shapes, specs = [Shape(full, f32)] * 3, [hbm] * 3
     return pl.pallas_call(
         body,
-        out_shape=[
-            Shape(full, bf16), Shape(full, f32), Shape(full, bf16),
-            *[Shape((others, tall_pieces, fine, PIECE), bf16)] * 2,
-            *[Shape((others, steps, fine, PIECE), bf16)] * 2,
-            *[Shape(merged, bf16)] * 2,
-            Shape((8, hidden), f32), Shape((8, width), f32),
-        ],
+        out_shape=shapes + shared_shapes,
         grid_spec=pltpu.PrefetchScalarGridSpec(
             num_scalar_prefetch=1,
             grid=(steps,),
             in_specs=[
                 once(full), once(full), once((width, width)), once(full), once((8, width)),
-                pl.BlockSpec((width, block), lambda i, info: (0, i)),
-                pl.BlockSpec((1, block), lambda i, info: (0, i)),
-                pl.BlockSpec((block, width), lambda i, info: (i, 0)),
-            ],
-            out_specs=[
-                fixed(full), fixed(full), fixed(full), by_row, by_row, by_column, by_column,
-                fixed(merged), fixed(merged),
-                pl.BlockSpec((8, block), lambda i, info: (0, i)),
-                fixed((8, width)),
-            ],
+                pl.BlockSpec((width, block), lambda i, info: (0, base + i)),
+                pl.BlockSpec((1, block), lambda i, info: (0, base + i)),
+                pl.BlockSpec((block, width), lambda i, info: (base + i, 0)),
+            ] + ([hbm] * 2 if final else []),
+            out_specs=specs + shared_specs,
             scratch_shapes=[
-                pltpu.VMEM(full, f32), pltpu.VMEM(low, bf16), pltpu.VMEM((width, rows), bf16),
-                pltpu.VMEM(low, bf16), pltpu.VMEM(full, f32), pltpu.VMEM(full, f32),
+                pltpu.VMEM(full, bf16), pltpu.VMEM((width, rows), bf16), pltpu.VMEM(full, bf16),
+                pltpu.VMEM(full, f32), pltpu.VMEM(full, f32),
                 pltpu.VMEM((rows, block), bf16), pltpu.VMEM((rows, block), bf16),
-            ],
+                pltpu.SemaphoreType.DMA((3,)),
+            ] + ([] if final else [pltpu.VMEM(full, f32)]),
         ),
         cost_estimate=TINY,
         compiler_params=settings(60),
         name="feed_forward",
-    )(info, after_one, mixed, merge, cotangent, vectors, expand, bias, reduce)
+    )(
+        info, *in_hbm(start_from, mixed, merge, cotangent), vectors,
+        *in_hbm(expand), bias, *in_hbm(reduce), *(begun if final else ()),
+    )
 
 
 def streamed(name, body, info, inputs, outs, scratch=()):
@@ -585,7 +638,7 @@
 ):
     slots, width = page_rows.shape
     half, fine = width // 2, width // owners
-    patch_shape = (owners // 2, patch_total // owners // fine * (width // PIECE), fine, PIECE)
+    pieces = patch_total // owners // fine * (width // PIECE)
 
     def body(info_ref, need, give):
         core, page = info_ref[0], info_ref[3]
@@ -594,8 +647,6 @@
         for i, grads in enumerate((kl, kh, vl, vh)):
             pair = by_core(core, tn(rows_ref[...], grads), fine, fine)
             give(0)[:, i : i + 1], give(1)[:, i : i + 1] = pair
-        give(0, True)
-        give(1, True)
         wk, wv = need(5), need(6)
         total = nt(kl, wk[:, :half]) + nt(kh, wk[:, half:])
         total = total + nt(vl, wv[:, :half]) + nt(vh, wv[:, half:])
@@ -603,14 +654,14 @@
         each = pair[0].shape[0]
         at = pl.ds(pl.multiple_of(page * each, each), each)
         for which in range(2):
-            give(2 + which)[...] = jnp.zeros(patch_shape, bf16)
-            give(2 + which)[at] = pair[which]
-            give(2 + which, True)
-        sums = give(4)
+            give(which)[:, 4:] = jnp.zeros((owners // 2, pieces, fine, PIECE), bf16)
+            give(which)[at, 4:] = pair[which]
+            give(which, True)
+        sums = give(2)
         sums[...] = jnp.zeros_like(sums)
         sums[0:1, :half] = column_sums(vl)
         sums[0:1, half:] = column_sums(vh)
-        give(4, True)
+        give(2, True)
 
     return streamed(
         "page_backward",
@@ -618,8 +669,7 @@
         info,
         [key_low, key_high, value_low, value_high, page_rows, key_weight, value_weight],
         [
-            ((owners // 2, 4, fine, PIECE), bf16), ((owners // 2, 4, fine, PIECE), bf16),
-            (patch_shape, bf16), (patch_shape, bf16), ((8, width), f32),
+            *[((owners // 2, 4 + pieces, fine, PIECE), bf16)] * 2, ((8, width), f32),
         ],
     )
 
@@ -690,18 +740,17 @@
     )
 
 
-def first_norm_backward(info, queries, keys, values, weights, tokens, one, returned, vectors, first, count, held):
+def first_norm_backward(info, queries, keys, values, weights, tokens, one, returned, vectors):
     rows, width = tokens.shape
-    half, tall = width // 2, count // 2
-    n = 0 if held is None else 1
+    half, tall = width // 2, 384
 
     def body(info_ref, *refs):
         grads = refs[:6]
         wq, wk, wv, x_ref, vec, one_ref, back_ref = refs[6:13]
-        out_ref, sums = refs[13 + n :]
+        out_ref, sums = refs[13:]
         gains = jnp.zeros((1, width), f32)
         shifts = gains
-        for start in range(0, count, tall):
+        for start in range(0, rows, tall):
             at = pl.ds(start, tall)
             up = 0.0
             for i, weight in enumerate((wq, wk, wv)):
@@ -717,9 +766,8 @@
         sums[2:3, :half], sums[2:3, half:] = column_sums(grads[0][...]), column_sums(grads[1][...])
         sums[3:4, :half], sums[3:4, half:] = column_sums(grads[4][...]), column_sums(grads[5][...])
 
-    block = first // count
-    narrow = pl.BlockSpec((count, half), lambda i, info: (block, 0))
-    wide = pl.BlockSpec((count, width), lambda i, info: (block, 0))
+    narrow = pl.BlockSpec((rows, half), lambda i, info: (0, 0))
+    wide = pl.BlockSpec((rows, width), lambda i, info: (0, 0))
     whole = pl.BlockSpec((width, width), lambda i, info: (0, 0))
     eight = pl.BlockSpec((8, width), lambda i, info: (0, 0))
     return pl.pallas_call(
@@ -728,18 +776,13 @@
         grid_spec=pltpu.PrefetchScalarGridSpec(
             num_scalar_prefetch=1,
             grid=(1,),
-            in_specs=[narrow] * 6 + [whole] * 3 + [wide, eight, wide, wide]
-            + [pl.BlockSpec(memory_space=pltpu.HBM)] * n,
+            in_specs=[narrow] * 6 + [whole] * 3 + [wide, eight, wide, wide],
             out_specs=[wide, eight],
         ),
-        input_output_aliases={14: 0} if n else {},
         cost_estimate=TINY,
         compiler_params=settings(),
         name="first_norm_backward",
-    )(
-        info, *queries, *keys, *values, *weights, tokens, vectors, one, returned,
-        *([] if held is None else [held]),
-    )
+    )(info, *in_hbm(*queries, *keys, *values, *weights, tokens), vectors, *in_hbm(one, returned))
 
 
 def digit_axes():
@@ -759,8 +802,8 @@
 
 
 class Part:
-    def __init__(self, kept, tok_first, shape, start=0, pieces=None):
-        self.tok_first, self.shape = tok_first, shape
+    def __init__(self, kept, tok_first, place, start=0, pieces=None):
+        self.tok_first, self.place = tok_first, place
         self.pieces = pieces or kept.shape[1]
         self.terms = [(kept, owner_digits(), start)]
 
@@ -769,33 +812,35 @@
     return digit_axes()[:-1]
 
 
-def stages_of(tok_first):
+def stages_of(tok_first, direct):
     every = digit_axes()
     bits = every[-2:0:-1]
     loose, last = bits[: max(len(bits) - 2, 0)], bits[max(len(bits) - 2, 0) :]
     singles = [[one] for one in loose]
-    return ([every[:1]] + singles if tok_first else singles + [every[:1]]) + [last]
+    ends = [last] if direct else [[one] for one in last]
+    return ([every[:1]] + singles if tok_first else singles + [every[:1]]) + ends
 
 
 class Sum:
-    def __init__(self, *sent):
+    def __init__(self, direct, *sent):
+        self.direct = direct
         self.parts = [part for _, parts in sent for part in parts]
         self.at = 0
         self.leaving = [array for array, _ in sent]
         self.hops = [[("patch", 0)]] * len(sent)
         self.groups = [parts for _, parts in sent]
-        self.mine = self.results = None
+        self.mine = self.came = None
 
     def send(self):
         self.arrived = [hop(value, steps) for value, steps in zip(self.leaving, self.hops)]
 
     def free(self, part, at):
-        settled = [one for stage in stages_of(part.tok_first)[:at] for one in stage]
+        settled = [one for stage in stages_of(part.tok_first, self.direct)[:at] for one in stage]
         return [one for one in owner_digits() if one not in settled]
 
     def absorb(self, arrived):
         if self.mine is not None:
-            self.results = finished([part for part in self.parts], self.mine, arrived)
+            self.came = arrived
             self.leaving = None
             return []
         for value, group in zip(arrived, self.groups):
@@ -803,7 +848,7 @@
             for part in group:
                 part.terms = part.terms + [(value, self.free(part, self.at), start)]
                 start += part.pieces
-        stages = [stages_of(part.tok_first) for part in self.parts]
+        stages = [stages_of(part.tok_first, self.direct) for part in self.parts]
         last = self.at == len(stages[0]) - 1
         ways = [stage[self.at] for stage in stages]
         self.at += 1
@@ -825,7 +870,7 @@
         return jobs
 
     def take(self, made):
-        if self.at == len(stages_of(True)):
+        if self.at == len(stages_of(True, self.direct)):
             self.mine = made[0]
             made = made[1:]
         self.leaving = list(made)
@@ -837,28 +882,34 @@
     return lax.ppermute(value, axis, [(i, i ^ flip) for i in range(lax.axis_size(axis))])
 
 
-def finished(parts, mine, arrived):
-    def body(mine_ref, *refs):
-        came, outs = refs[: len(arrived)], refs[len(arrived) :]
-        piece = 0
-        for part, out in zip(parts, outs):
-            fine = mine_ref.shape[2]
-            tall = out.shape[0] // fine
-            for p in range(part.pieces):
-                total = mine_ref[0, piece]
-                for ref in came:
-                    total = total + ref[0, piece].astype(f32)
-                row, column = p % tall * fine, p // tall * PIECE
-                out[row : row + fine, column : column + PIECE] = total
-                piece += 1
+def finished(shapes, *totals):
+    arrays = [one for total in totals for one in [total.mine, *total.came]]
+
+    def body(*refs):
+        refs, outs = list(refs[: len(arrays)]), refs[len(arrays) :]
+        for total in totals:
+            mine_ref, *came = refs[: 1 + len(total.came)]
+            refs = refs[1 + len(total.came) :]
+            piece = 0
+            for part in total.parts:
+                out, at_column = part.place
+                fine = mine_ref.shape[2]
+                tall = shapes[out][0] // fine
+                for p in range(part.pieces):
+                    sum_here = mine_ref[0, piece]
+                    for ref in came:
+                        sum_here = sum_here + ref[0, piece].astype(f32)
+                    row, column = p % tall * fine, at_column + p // tall * PIECE
+                    outs[out][row : row + fine, column : column + PIECE] = sum_here
+                    piece += 1
 
     return pl.pallas_call(
         body,
-        out_shape=[Shape(part.shape, f32) for part in parts],
+        out_shape=[Shape(shape, f32) for shape in shapes],
         cost_estimate=TINY,
         compiler_params=pltpu.CompilerParams(vmem_limit_bytes=40 * MIB),
         name="finished",
-    )(mine, *arrived)
+    )(*arrays)
 
 
 def added_up(info, jobs):
@@ -948,7 +999,7 @@
             num_scalar_prefetch=1,
             grid=(1,),
             in_specs=[anywhere] * len(arrays),
-            out_specs=[anywhere] * len(jobs),
+            out_specs=[pl.BlockSpec(memory_space=pltpu.HBM)] * len(jobs),
             scratch_shapes=held
             + [pltpu.VMEM(shape, kind) for shape, kind in shapes]
             + [pltpu.SemaphoreType.DMA((loads,)), pltpu.SemaphoreType.DMA((len(jobs),))],
@@ -981,15 +1032,15 @@
     return chain
 
 
-def vector_table(feed, expand_bias, probe, page, lead, first_low, first_high):
+def vector_table(feed, expand_bias, probe, page, lead, first):
     width = feed.shape[1]
 
-    def body(feed_ref, bias_ref, probe_ref, page_ref, lead_ref, low_ref, high_ref, out):
+    def body(feed_ref, bias_ref, probe_ref, page_ref, lead_ref, first_ref, out):
         rows = [
-            low_ref[0:1, :] + high_ref[0:1, :] + lead_ref[0:1, :],
-            low_ref[1:2, :] + high_ref[1:2, :] + lead_ref[1:2, :],
-            low_ref[2:3, :] + high_ref[2:3, :],
-            low_ref[3:4, :] + high_ref[3:4, :] + lead_ref[2:3, :],
+            first_ref[0:1, :] + lead_ref[0:1, :],
+            first_ref[1:2, :] + lead_ref[1:2, :],
+            first_ref[2:3, :],
+            first_ref[3:4, :] + lead_ref[2:3, :],
             probe_ref[2:3, :],
             probe_ref[0:1, :],
             probe_ref[1:2, :],
@@ -1010,7 +1061,7 @@
         out_shape=jax.ShapeDtypeStruct((24, width), f32),
         cost_estimate=TINY,
         name="vector_table",
-    )(feed, expand_bias, probe, page, lead, first_low, first_high)
+    )(feed, expand_bias, probe, page, lead, first)
 
 
 def scatter_rows(table, width, first, last):
@@ -1121,25 +1172,41 @@
     page_values = (nn(page_rows, source_value) + source_bias).astype(bf16)
     cross_mixed, cross_total = cross_forward(probe, page_keys, page_values, filled)
 
-    fed = feed_forward(
-        after_one, cross_mixed, merge_weight, cotangent[0], feed_vectors, expand_weight,
-        expand_bias[None], reduce_weight, info, owners,
-    )
-    block_output, grad_two, grad_cross_out = fed[:3]
-    feed_sums, expand_bias_sums = fed[10], fed[9]
-    fine, model = model_width // owners, (model_width // owners, model_width)
-    half_model = (fine, model_width // 2)
+    feed_args = (
+        cross_mixed, merge_weight, cotangent[0], feed_vectors, expand_weight, expand_bias[None],
+        reduce_weight, info, owners,
+    )
+    branch, upstream, after_two, *fed = feed_forward(after_one, *feed_args, None)
+    fine = model_width // owners
+    deep = expand_weight.shape[1] // 2
+
+    def by_owner(value):
+        return value.reshape((-1,) + value.shape[2:])
+
     first = Sum(
-        (fed[5], [Part(fed[6], True, (fine, expand_weight.shape[1]))]),
-        (fed[3], [Part(fed[4], False, (expand_weight.shape[1] // owners, model_width))]),
-        (fed[7], [Part(fed[8], False, model)]),
-    )
+        False,
+        (fed[2], [Part(fed[3], True, (0, 0))]),
+        (by_owner(fed[0]), [Part(by_owner(fed[1]), False, (1, 0))]),
+    )
+    low_bias, low_sums = fed[4:]
+    after_two, branch, upstream = advance(info, (after_two, branch, upstream), [], [first])
+    block_output, grad_two, grad_cross_out, *fed = feed_forward(
+        after_two, *feed_args, (branch, upstream)
+    )
+    second = Sum(
+        False,
+        (fed[4], [Part(fed[5], True, (0, deep))]),
+        (by_owner(fed[2]), [Part(by_owner(fed[3]), False, (2, 0))]),
+        (fed[0], [Part(fed[1], False, (3, 0))]),
+    )
+    expand_bias_sums = jnp.concatenate([low_bias[0], fed[6][0]])
+    feed_sums = fed[7]
 
     half_pairs = model_width // PAIR // 2
     cross_args = (probe, page_keys, page_values, cross_mixed, cross_total)
-    grad_cross_out = advance(info, grad_cross_out, [], [first])
+    grad_cross_out = advance(info, grad_cross_out, [first], [second])
     low = cross_backward(*cross_args, grad_cross_out, filled, 0, half_pairs)
-    low, grad_cross_out = advance(info, (low, grad_cross_out), [first])
+    low, grad_cross_out = advance(info, (low, grad_cross_out), [first, second])
     high = cross_backward(*cross_args, grad_cross_out, filled, half_pairs, half_pairs)
     patch_total = patches.shape[0] * lax.axis_size(("tok", "patch"))
     paged = page_backward(
@@ -1151,62 +1218,73 @@
         cross_vectors, owners,
     )
     grad_one, grad_self_out, probe_sums = probed[0], probed[1], probed[4]
-    second = Sum(
-        (paged[0], [Part(paged[1], True, (fine, 2 * model_width))]),
-        (paged[2], [Part(paged[3], False, (patches.shape[0], model_width))]),
-        (probed[2], [Part(probed[3], False, (fine, 2 * model_width))]),
+    third = Sum(
+        False,
+        (
+            paged[0],
+            [Part(paged[1], True, (0, 0), 0, 4), Part(paged[1], False, (1, 0), 4, paged[1].shape[1] - 4)],
+        ),
+        (probed[2], [Part(probed[3], False, (2, 0))]),
     )
     self_args = (query, lead_keys, lead_values, self_mixed, self_total)
     own_args = (query, own_keys, own_values, self_mixed, self_total)
-    grad_self_out = advance(info, grad_self_out, [first], [second])
+    grad_self_out = advance(info, grad_self_out, [first, second], [third])
     lead_low = lead_backward(*self_args, grad_self_out, trailing, 0, half_pairs)
-    lead_low, grad_self_out = advance(info, (lead_low, grad_self_out), [first, second])
+    lead_low, grad_self_out = advance(info, (lead_low, grad_self_out), [first, second, third])
     lead_high = lead_backward(*self_args, grad_self_out, trailing, half_pairs, half_pairs)
     led_grad, led_part, lead_sums = lead_upstream(
         info, (lead_low[1], lead_high[1]), (lead_low[2], lead_high[2]), key_weight,
         value_weight, lead_tokens, self_vectors,
     )
     led_grad, led_part, grad_self_out = advance(
-        info, (led_grad, led_part, grad_self_out), [first, second]
-    )
+        info, (led_grad, led_part, grad_self_out), [first, second, third]
+    )
+    returned = lax.ppermute(led_grad, "tok", [(1, 0)])
     own_low = own_backward(*own_args, grad_self_out, lead_low[0], 0, half_pairs)
-    own_low, led_grad = advance(info, (own_low, led_grad), [second])
-    returned = lax.ppermute(led_grad, "tok", [(1, 0)])
+    own_low, grad_self_out = advance(info, (own_low, grad_self_out), [second, third])
     parts = projection_grads(info, hidden_one, *own_low, led_part, False, owners)
-    third = Sum((parts[0], [Part(parts[1], i == 1, half_model, i, 1) for i in range(3)]))
-    own_low, grad_self_out = advance(info, (own_low, grad_self_out), [], [third])
+    half = model_width // 2
+    fourth = Sum(True, (parts[0], [Part(parts[1], i == 1, (i, 0), i, 1) for i in range(3)]))
+    own_low, grad_self_out = advance(info, (own_low, grad_self_out), [], [fourth])
     own_high = own_backward(*own_args, grad_self_out, lead_high[0], half_pairs, half_pairs)
-    own_high, led_part = advance(info, (own_high, led_part), [second, third])
-    parts = projection_grads(info, hidden_one, *own_high, led_part, True, owners)
-    fourth = Sum((parts[0], [Part(parts[1], i != 1, half_model, i, 1) for i in range(3)]))
     own_low, own_high, returned = advance(
-        info, (own_low, own_high, returned), [third], [fourth]
-    )
-    first_norm = (
+        info, (own_low, own_high, returned), [third, fourth]
+    )
+    tokens_grad, first_sums = first_norm_backward(
         info, (own_low[0], own_high[0]), (own_low[1], own_high[1]), (own_low[2], own_high[2]),
         (query_weight, key_weight, value_weight), tokens[0], grad_one, returned, self_vectors,
     )
-    top = first_norm_backward(*first_norm, 0, row_count // 2, None)
-    top = advance(info, top, [third, fourth])
-    rest = first_norm_backward(*first_norm, row_count // 2, row_count // 2, top[0])
-    tokens_grad = rest[0]
-    top_sums, rest_sums = advance(info, (top[1], rest[1]), [third, fourth])
-    bias_rows = expand_bias_sums[0].reshape(owners, -1, fine)
+    first_sums, own_high, led_part = advance(
+        info, (first_sums, own_high, led_part), [third, fourth]
+    )
+    parts = projection_grads(info, hidden_one, *own_high, led_part, True, owners)
+    bias_rows = expand_bias_sums.reshape(owners, -1, fine)
     bias_rows = jnp.transpose(bias_rows, (1, 0, 2)).reshape(-1, model_width)
-    table = vector_table(
-        feed_sums, bias_rows, probe_sums, paged[4], lead_sums, top_sums, rest_sums
-    )
-    table = scatter_rows(table, model_width, 0, 3)
-    table = advance(info, table, [third, fourth])
+    table = vector_table(feed_sums, bias_rows, probe_sums, paged[2], lead_sums, first_sums)
+    table = scatter_rows(table, model_width, 0, 1)
+    fifth = Sum(True, (parts[0], [Part(parts[1], i != 1, (i, half), i, 1) for i in range(3)]))
+    table = advance(info, table, [fourth], [fifth])
+    table = scatter_rows(table, model_width, 1, 3)
+    table = advance(info, table, [fourth, fifth])
     sums = scatter_rows(table, model_width, 3, len(digits))
-    totals = [first, second, third, fourth]
+    totals = [first, second, third, fourth, fifth]
     while any(one.leaving is not None for one in totals):
         sums = advance(info, sums, totals)
-    expand_grad, reduce_grad, merge_grad = first.results
-    source_grads, patches_grad, middle_grads = second.results
-    projections = [
-        jnp.concatenate([one.results[i] for one in (third, fourth)], axis=1) for i in range(3)
-    ]
+    tall = expand_weight.shape[1] // owners
+    model, half_reduce = (fine, model_width), (tall, half)
+    expand_grad, reduce_low, reduce_high, merge_grad = finished(
+        [(fine, expand_weight.shape[1]), half_reduce, half_reduce, model], first, second
+    )
+    is_first = tok_index == 0
+    given = jnp.where(is_first, reduce_high, reduce_low).astype(bf16)
+    taken = hop(given, [("tok", 0)]).astype(f32)
+    reduce_grad = jnp.concatenate(
+        [jnp.where(is_first, reduce_low, taken), jnp.where(is_first, taken, reduce_high)], axis=1
+    )
+    source_grads, patches_grad, middle_grads = finished(
+        [(fine, 2 * model_width), (patches.shape[0], model_width), (fine, 2 * model_width)], third
+    )
+    projections = finished([model] * 3, fourth, fifth)
     return (
         block_output[None],
         tokens_grad[None],

time: 569 us -> 535 us (0.940)
  starting transfers between devices: 99.6 us -> 76.6 us
  local copies, waits for them, and re-layouts: 44.9 us -> 30.5 us
  Pallas kernels: 287 us -> 297 us
  other arithmetic: 16.3 us -> 9.02 us
    ppermute x41 -> x47, starting transfers between devices: 92.2 us -> 70.3 us  [hop(): lax.ppermute(value, axis, [(i, i ^ flip) for i in range(lax.axis_size(axi...]
    unnamed x160 -> x144, local copies, waits for them, and re-layouts: 33.4 us -> 20.1 us
    pallas_call x5, Pallas kernels: 68.7 us -> 75.7 us  [the longest x2 72.9 us: feed_forward(): pl.pallas_call(body, out_shape=shapes + shared_shapes, grid_spec=pltpu.Pr...]
    pallas_call x10 -> x12, Pallas kernels: 47.6 us -> 53.5 us  [added_up(): pl.pallas_call(body, out_shape=[Shape(shape, kind) for shape, kind in sha...]
    pallas_call x2 -> x1, Pallas kernels: 20.8 us -> 15.5 us  [first_norm_backward(): pl.pallas_call(body, out_shape=[Shape((rows, width), f32), Shape((8, widt...]
    ppermute x41 -> x47, waiting for transfers between devices: 69 us -> 66.8 us  [hop(): lax.ppermute(value, axis, [(i, i ^ flip) for i in range(lax.axis_size(axi...]
  transfers between devices with their start and end apart: 44 -> 50, of which waited for: 13 -> 19; matrix products, arithmetic and copies ran while one was open for 7% -> 7% of each run, Pallas kernels for 28% -> 37%
where the time goes in v4:
time: 535 us; the launch traced here: 529 us
  Pallas kernels  297 us (56%)
  starting transfers between devices  76.6 us (14%)
  waiting for transfers between devices  73.6 us (14%)
  local copies, waits for them, and re-layouts  30.5 us (6%)
  matrix products  26 us (5%)
  between operations  15.9 us (3%)
  other arithmetic  9.02 us (2%)
    pallas_call x2, Pallas kernels, feed_forward(): pl.pallas_call(body, out_shape=shapes + shared_shapes, grid_spec=pltpu.Pr...  72.9 us
    ppermute x47, starting transfers between devices, hop(): lax.ppermute(value, axis, [(i, i ^ flip) for i in range(lax.axis_size(axi...  70.3 us
    ppermute x47, waiting for transfers between devices, hop(): lax.ppermute(value, axis, [(i, i ^ flip) for i in range(lax.axis_size(axi...  66.8 us
    pallas_call x5, Pallas kernels, streamed(): pl.pallas_call(kernel, out_shape=[Shape(shape, kind) for shape, kind in o...  56.1 us
    pallas_call x12, Pallas kernels, added_up(): pl.pallas_call(body, out_shape=[Shape(shape, kind) for shape, kind in sha...  53.5 us
    dot_general x9, matrix products, nn(): lax.dot_general(left, right, (((1,), (0,)), ((), ())), preferred_element_...  26 us
    pallas_call x2, Pallas kernels, own_backward(): pl.pallas_call(body, out_shape=[Shape((rows, pairs * PAIR), bf16)] * 3, g...  25.2 us
    pallas_call x2, Pallas kernels, cross_backward(): pl.pallas_call(body, out_shape=[Shape((rows, pairs * PAIR), bf16)] + [Sha...  23.7 us
  transfers between devices with their start and end apart: 50, of which 19 were waited for; matrix products, arithmetic and copies ran while one was open for 7% of the time, Pallas kernels for 37%

profile of v4, /device:TPU:0, one launch (start us, length us, event | category | flops | bytes accessed | tf_op | source)
XLA Modules:
  0.0 528.5 jit_solution(3383807085942918506)
XLA Ops:
  26.8 14.3 %own_forward.1 = (bf16[768,1024]{1,0:T(8,128)(2,1)}, f32[8,2,768]{2,1,0:T(2,128)}) custom-call(bf16[768,1024]{1,0:T(8,128)(2,1)} %multiply_convert_fusion.1.q_ref, bf16[768,1024]{1,0:T(8,128)(2,1)} %convolution_convert_fusion.1.k_ref, bf16[768,1024]{1,0:T(8,128)(2,1)} %add_convert_fusion.2.v_ref), custom_call_target="tpu_custom_call" | custom-call | flops 1 | bytes 1 | tf_op jit(solution)/shard_map/own_forward/pallas_call | solution.py:186
  56.1 7.2 %lead_forward.1 = (bf16[768,1024]{1,0:T(8,128)(2,1)}, f32[8,2,768]{2,1,0:T(2,128)}) custom-call(s32[1]{0:T(128)} %bitcast.9.flag, bf16[768,1024]{1,0:T(8,128)(2,1)} %multiply_convert_fusion.1.q_ref, bf16[768,1024]{1,0:T(8,128)(2,1)} %convolution_convert_fusion.k_ref, bf16[768,1024]{1,0:T(8,128)(2,1)} %add_convert_fusion.1.v_ref, ...), custom_call_target="tpu_custom_call" | custom-call | flops 1 | bytes 1 | tf_op jit(solution)/shard_map/lead_forward/pallas_call | solution.py:215
  79.1 14.7 %cross_forward.1 = (bf16[768,1024]{1,0:T(8,128)(2,1)}, f32[8,2,768]{2,1,0:T(2,128)}) custom-call(s32[1]{0:T(128)} %bitcast.10.filled_ref, bf16[768,1024]{1,0:T(8,128)(2,1)} %multiply_convert_fusion.q_ref, bf16[512,1024]{1,0:T(8,128)(2,1)} %convolution_convert_fusion.2.k_ref, bf16[512,1024]{1,0:T(8,128)(2,1)} %add_convert_fusion.3.v_ref), custom_call_target="tpu_custom_call" | custom-call | flops 1 | bytes 1 | tf_op jit(solution)/shard_map/cross_forward/pallas_call | solution.py:246
  93.8 33.2 %feed_forward.2 = (f32[768,1024]{1,0:T(8,128)}, f32[768,1024]{1,0:T(8,128)}, f32[768,1024]{1,0:T(8,128)}, bf16[2,8,4,32,512]{4,3,2,1,0:T(8,128)(2,1)}, bf16[2,8,...) custom-call(s32[9]{0:T(128)} %stack.61.info_ref, ...), custom_call_target="tpu_custom_call" | custom-call | flops 1 | bytes 1 | tf_op jit(solution)/shard_map/feed_forward/pallas_call | solution.py:496
  127.5 39.7 %feed_forward.3 = (bf16[768,1024]{1,0:T(8,128)(2,1)}, f32[768,1024]{1,0:T(8,128)}, bf16[768,1024]{1,0:T(8,128)(2,1)}, bf16[16,2,32,512]{3,2,1,0:T(8,128)(2,1)}, ...) custom-call(s32[9]{0:T(128)} %stack.61.info_ref, ...), custom_call_target="tpu_custom_call" | custom-call | flops 1 | bytes 1 | tf_op jit(solution)/shard_map/feed_forward/pallas_call | solution.py:496
  173.8 18.9 %collective-permute-start.3 = (bf16[8,4,32,512]{3,2,1,0:T(8,128)(2,1)}, bf16[8,4,32,512]{3,2,1,0:T(8,128)(2,1)S(1)}, u32[]{:S(2)}, u32[]{:S(2)}) collective-permute-start(bf16[8,4,32,512]{3,2,1,0:T(8,128)(2,1)} %get-tuple-element.335), channel_id=1, source_target_pairs={{0,16},{16,0},{1,17},{17,1},{2,18},{18,2},{3,19},{19,3},{4,20},{20... | collective-permute-start | bytes 3145736 | tf_op jit(solution)/shard_map/ppermute | solution.py:882
  194.2 11.8 %cross_backward.2 = (bf16[768,512]{1,0:T(8,128)(2,1)}, bf16[512,512]{1,0:T(8,128)(2,1)}, bf16[512,512]{1,0:T(8,128)(2,1)}) custom-call(s32[1]{0:T(128)} %bitcast.10.filled_ref, bf16[768,1024]{1,0:T(8,128)(2,1)} %multiply_convert_fusion.q_ref, bf16[512,1024]{1,0:T(8,128)(2,1)} %convolution_convert_fusion.2.k_ref, bf16[512,1024]{1,0:T(8,128)(2,1)} %add_convert_fusion.3.v_ref, ...), custom_call_target="tpu_custom_call" | custom-call | flops 1 | bytes 1 | tf_op jit(solution)/shard_map/cross_backward/pallas_call | solution.py:339
  206.0 10.3 %collective-permute-done.3.refs_2_ = bf16[8,4,32,512]{3,2,1,0:T(8,128)(2,1)S(1)} collective-permute-done((bf16[8,4,32,512]{3,2,1,0:T(8,128)(2,1)}, bf16[8,4,32,512]{3,2,1,0:T(8,128)(2,1)S(1)}, u32[]{:S(2)}, u32[]{:S(2)}) %collective-permute-start.3) | collective-permute-done | bytes 1048608 | tf_op jit(solution)/shard_map/ppermute | solution.py:882
  219.8 6.7 %added_up.13 = (bf16[4,4,32,512]{3,2,1,0:T(8,128)(2,1)}, bf16[4,4,32,512]{3,2,1,0:T(8,128)(2,1)}, bf16[8,4,32,512]{3,2,1,0:T(8,128)(2,1)}, bf16[8,6,32,512]{3,2,1,0:T(8,128)(2,1)}) custom-call(s32[9]{0:T(128)} %stack.61.info_ref, bf16[16,4,32,512]{3,2,1,0:T(8,128)(2,1)} %get-tuple-element.322.refs_0_, bf16[16,4,32,512]{3,2,1,0:T(8,128)(2,1)} %copy-done.8, ...), custom_call_target="tpu_custom_call" | custom-call | flops 1 | bytes 1 | tf_op jit(solution)/shard_map/added_up/pallas_call | solution.py:995
  231.2 11.9 %cross_backward.3 = (bf16[768,512]{1,0:T(8,128)(2,1)}, bf16[512,512]{1,0:T(8,128)(2,1)}, bf16[512,512]{1,0:T(8,128)(2,1)}) custom-call(s32[1]{0:T(128)} %bitcast.10.filled_ref, bf16[768,1024]{1,0:T(8,128)(2,1)} %multiply_convert_fusion.q_ref, bf16[512,1024]{1,0:T(8,128)(2,1)} %convolution_convert_fusion.2.k_ref, bf16[512,1024]{1,0:T(8,128)(2,1)} %add_convert_fusion.3.v_ref, ...), custom_call_target="tpu_custom_call" | custom-call | flops 1 | bytes 1 | tf_op jit(solution)/shard_map/cross_backward/pallas_call | solution.py:339
  243.1 16.4 %probe_backward.1 = (f32[768,1024]{1,0:T(8,128)}, bf16[768,1024]{1,0:T(8,128)(2,1)}, bf16[16,4,32,512]{3,2,1,0:T(8,128)(2,1)}, bf16[16,4,32,512]{3,2,1,0:T(8,128)(2,1)}, f32[8,1024]{1,0:T(8,128)}) custom-call(s32[9]{0:T(128)} %stack.61.info_ref, bf16[768,512]{1,0:T(8,128)(2,1)} %get-tuple-element.356.refs_0_, bf16[768,512]{1,0:T(8,128)(2,1)} %get-tuple-element.358.refs_1_, ...), custom_call_target="tpu_custom_call" | custom-call | flops 1 | bytes 1 | tf_op jit(solution)/shard_map/probe_backward/pallas_call | solution.py:555
  259.5 10.3 %page_backward.1 = (bf16[16,6,32,512]{3,2,1,0:T(8,128)(2,1)}, bf16[16,6,32,512]{3,2,1,0:T(8,128)(2,1)}, f32[8,1024]{1,0:T(8,128)}) custom-call(s32[9]{0:T(128)} %stack.61.info_ref, bf16[512,512]{1,0:T(8,128)(2,1)} %get-tuple-element.373.refs_0_, bf16[512,512]{1,0:T(8,128)(2,1)} %get-tuple-element.374.refs_1_, bf16[512,512]{1,0:T(8,128)(2,1)} %get-tuple-element.375.refs_2_, ...), custom_call_target="tpu_custom_call" | custom-call | flops 1 | bytes 1 | tf_op jit(solution)/shard_map/page_backward/pallas_call | solution.py:555
  289.3 6.2 %collective-permute-done.12.refs_4_ = bf16[2,8,32,512]{3,2,1,0:T(8,128)(2,1)S(1)} collective-permute-done((bf16[2,8,32,512]{3,2,1,0:T(8,128)(2,1)}, bf16[2,8,32,512]{3,2,1,0:T(8,128)(2,1)S(1)}, u32[]{:S(2)}, u32[]{:S(2)}) %collective-permute-start.12) | collective-permute-done | bytes 524320 | tf_op jit(solution)/shard_map/ppermute | solution.py:882
  303.5 7.5 %added_up.15 = (f32[1,8,32,512]{3,2,1,0:T(8,128)}, bf16[1,8,32,512]{3,2,1,0:T(8,128)(2,1)}, bf16[2,10,32,512]{3,2,1,0:T(8,128)(2,1)}, bf16[8,4,32,512]{3,2,1,0:T(8,128)(2,1)}, bf16[8,6,32,512]{3,2,1,0:T(8,128)(2,1)}) custom-call(s32[9]{0:T(128)} %stack.61.info_ref, bf16[16,4,32,512]{3,2,1,0:T(8,128)(2,1)} %get-tuple-element.322.refs_0_, ...), custom_call_target="tpu_custom_call" | custom-call | flops 1 | bytes 1 | tf_op jit(solution)/shard_map/added_up/pallas_call | solution.py:995
  323.3 13.6 %lead_upstream.1 = (bf16[768,1024]{1,0:T(8,128)(2,1)}, bf16[1024,2048]{1,0:T(8,128)(2,1)}, f32[8,1024]{1,0:T(8,128)}) custom-call(s32[9]{0:T(128)} %stack.61.info_ref, bf16[768,512]{1,0:T(8,128)(2,1)} %get-tuple-element.403.refs_0_, bf16[768,512]{1,0:T(8,128)(2,1)} %get-tuple-element.405.refs_1_, bf16[768,512]{1,0:T(8,128)(2,1)} %get-tuple-element.406.refs_2_, ...), custom_call_target="tpu_custom_call" | custom-call | flops 1 | bytes 1 | tf_op jit(solution)/shard_map/lead_upstream/pallas_call | solution.py:555
  336.9 9.9 %collective-permute-done.20.refs_14_.refs_4_.refs_5_ = bf16[8,6,32,512]{3,2,1,0:T(8,128)(2,1)S(1)} collective-permute-done((bf16[8,6,32,512]{3,2,1,0:T(8,128)(2,1)}, bf16[8,6,32,512]{3,2,1,0:T(8,128)(2,1)S(1)}, u32[]{:S(2)}, u32[]{:S(2)}) %collective-permute-start.20) | collective-permute-done | bytes 1572896 | tf_op jit(solution)/shard_map/ppermute | solution.py:882
  347.9 5.8 %added_up.16 = (f32[1,10,32,512]{3,2,1,0:T(8,128)}, bf16[1,10,32,512]{3,2,1,0:T(8,128)(2,1)}, bf16[4,4,32,512]{3,2,1,0:T(8,128)(2,1)}, bf16[4,6,32,512]{3,2,1,0:T(8,128)(2,1)}) custom-call(s32[9]{0:T(128)} %stack.61.info_ref, bf16[16,4,32,512]{3,2,1,0:T(8,128)(2,1)} %get-tuple-element.346.refs_6_.refs_8_.refs_9_.refs_0_, bf16[16,4,32,512]{3,2,1,0:T(8,128)(2,1)} %copy-done.9, ...), custom_call_target="tpu_custom_call" | custom-call | flops 1 | bytes 1 | tf_op jit(solution)/shard_map/added_up/pallas_call | solution.py:995
  360.2 12.7 %own_backward.2 = (bf16[768,512]{1,0:T(8,128)(2,1)}, bf16[768,512]{1,0:T(8,128)(2,1)}, bf16[768,512]{1,0:T(8,128)(2,1)}) custom-call(bf16[768,1024]{1,0:T(8,128)(2,1)} %multiply_convert_fusion.1.q_ref, bf16[768,1024]{1,0:T(8,128)(2,1)} %convolution_convert_fusion.1.k_ref, bf16[768,1024]{1,0:T(8,128)(2,1)} %add_convert_fusion.2.v_ref, ...), custom_call_target="tpu_custom_call" | custom-call | flops 1 | bytes 1 | tf_op jit(solution)/shard_map/own_backward/pallas_call | solution.py:309
  379.4 8.0 %projection_grads.2 = (bf16[16,3,32,512]{3,2,1,0:T(8,128)(2,1)}, bf16[16,3,32,512]{3,2,1,0:T(8,128)(2,1)}) custom-call(s32[9]{0:T(128)} %stack.61.info_ref, bf16[768,1024]{1,0:T(8,128)(2,1)} %copy-done.15, bf16[768,512]{1,0:T(8,128)(2,1)} %get-tuple-element.471.refs_1_.refs_0_, bf16[768,512]{1,0:T(8,128)(2,1)} %get-tuple-element.473.refs_2_, ...), custom_call_target="tpu_custom_call" | custom-call | flops 1 | bytes 1 | tf_op jit(solution)/shard_map/projection_grads/pallas_call | solution.py:555
  388.8 12.5 %own_backward.3 = (bf16[768,512]{1,0:T(8,128)(2,1)}, bf16[768,512]{1,0:T(8,128)(2,1)}, bf16[768,512]{1,0:T(8,128)(2,1)}) custom-call(bf16[768,1024]{1,0:T(8,128)(2,1)} %multiply_convert_fusion.1.q_ref, bf16[768,1024]{1,0:T(8,128)(2,1)} %convolution_convert_fusion.1.k_ref, bf16[768,1024]{1,0:T(8,128)(2,1)} %add_convert_fusion.2.v_ref, ...), custom_call_target="tpu_custom_call" | custom-call | flops 1 | bytes 1 | tf_op jit(solution)/shard_map/own_backward/pallas_call | solution.py:309
  418.5 15.5 %first_norm_backward.1 = (f32[768,1024]{1,0:T(8,128)}, f32[8,1024]{1,0:T(8,128)}) custom-call(s32[9]{0:T(128)S(1)} %copy-done.4, bf16[768,512]{1,0:T(8,128)(2,1)} %get-tuple-element.471.refs_1_.refs_0_, bf16[768,512]{1,0:T(8,128)(2,1)} %get-tuple-element.511.refs_1_, bf16[768,512]{1,0:T(8,128)(2,1)} %get-tuple-element.473.refs_2_, ...), custom_call_target="tpu_custom_call" | custom-call | flops 1 | bytes 1 | tf_op jit(solution)/shard_map/first_norm_backward/pallas_call | solution.py:773
  442.6 7.8 %projection_grads.3 = (bf16[16,3,32,512]{3,2,1,0:T(8,128)(2,1)}, bf16[16,3,32,512]{3,2,1,0:T(8,128)(2,1)}) custom-call(s32[9]{0:T(128)} %stack.61.info_ref, bf16[768,1024]{1,0:T(8,128)(2,1)} %copy-done.15, bf16[768,512]{1,0:T(8,128)(2,1)} %get-tuple-element.511.refs_1_, bf16[768,512]{1,0:T(8,128)(2,1)} %get-tuple-element.512.refs_3_.refs_2_, ...), custom_call_target="tpu_custom_call" | custom-call | flops 1 | bytes 1 | tf_op jit(solution)/shard_map/projection_grads/pallas_call | solution.py:555
  467.7 5.3 %collective-permute-done.36.refs_2_ = bf16[1,3,32,512]{3,2,1,0:T(8,128)(2,1)S(1)} collective-permute-done((bf16[1,3,32,512]{3,2,1,0:T(8,128)(2,1)}, bf16[1,3,32,512]{3,2,1,0:T(8,128)(2,1)S(1)}, u32[]{:S(2)}, u32[]{:S(2)}) %collective-permute-start.36) | collective-permute-done | bytes 98336 | tf_op jit(solution)/shard_map/ppermute | solution.py:882
  482.4 7.9 %collective-permute-done.48 = bf16[128,512]{1,0:T(8,128)(2,1)S(1)} collective-permute-done((bf16[128,512]{1,0:T(8,128)(2,1)S(1)}, bf16[128,512]{1,0:T(8,128)(2,1)S(1)}, u32[]{:S(2)}, u32[]{:S(2)}) %collective-permute-start.48) | collective-permute-done | bytes 131104 | tf_op jit(solution)/shard_map/ppermute | solution.py:882
  (306 shorter events, 204.5 us)
Async XLA Ops:
  7.3 65.3 %all-gather.2.cloned.1.call-start = ((), (), s32[]{:S(2)}) async-start(), calls=%async_computation | async-start | bytes 2162688 | tf_op jit(solution)/shard_map/all_gather | solution.py:1140
  8.0 41.1 %collective-permute-start = (bf16[768,1024]{1,0:T(8,128)(2,1)}, bf16[768,1024]{1,0:T(8,128)(2,1)S(1)}, u32[]{:S(2)}, u32[]{:S(2)}) collective-permute-start(bf16[768,1024]{1,0:T(8,128)(2,1)} %bitcast.82), channel_id=1, source_target_pairs={{0,16},{1,17},{2,18},{3,19},{4,20},{5,21},{6,22},{7,23},{8,24},{9,... | collective-permute-start | bytes 4718600 | tf_op jit(solution)/shard_map/ppermute | solution.py:1139
  127.0 40.3 %collective-permute-start.1 = (bf16[16,4,32,512]{3,2,1,0:T(8,128)(2,1)}, bf16[16,4,32,512]{3,2,1,0:T(8,128)(2,1)S(1)}, u32[]{:S(2)}, u32[]{:S(2)}) collective-permute-start(bf16[16,4,32,512]{3,2,1,0:T(8,128)(2,1)} %get-tuple-element.319), channel_id=1, source_target_pairs={{0,1},{1,0},{2,3},{3,2},{4,5},{5,4},{6,7},{7,6},{8,9},{9,8},{10,11... | collective-permute-start | bytes 6291464 | tf_op jit(solution)/shard_map/ppermute | solution.py:882
  127.0 40.2 %collective-permute-start.2 = (bf16[16,4,32,512]{3,2,1,0:T(8,128)(2,1)}, bf16[16,4,32,512]{3,2,1,0:T(8,128)(2,1)}, u32[]{:S(2)}, u32[]{:S(2)}) collective-permute-start(bf16[16,4,32,512]{3,2,1,0:T(8,128)(2,1)} %bitcast.98), channel_id=1, source_target_pairs={{0,1},{1,0},{2,3},{3,2},{4,5},{5,4},{6,7},{7,6},{8,9},{9,8},{10,11... | collective-permute-start | bytes 6291464 | tf_op jit(solution)/shard_map/ppermute | solution.py:882
  173.2 44.6 %collective-permute-start.5 = (bf16[16,4,32,512]{3,2,1,0:T(8,128)(2,1)}, bf16[16,4,32,512]{3,2,1,0:T(8,128)(2,1)S(1)}, u32[]{:S(2)}, u32[]{:S(2)}) collective-permute-start(bf16[16,4,32,512]{3,2,1,0:T(8,128)(2,1)} %get-tuple-element.337), channel_id=1, source_target_pairs={{0,1},{1,0},{2,3},{3,2},{4,5},{5,4},{6,7},{7,6},{8,9},{9,8},{10,11... | collective-permute-start | bytes 6291464 | tf_op jit(solution)/shard_map/ppermute | solution.py:882
  173.4 44.4 %collective-permute-start.6 = (bf16[16,4,32,512]{3,2,1,0:T(8,128)(2,1)}, bf16[16,4,32,512]{3,2,1,0:T(8,128)(2,1)}, u32[]{:S(2)}, u32[]{:S(2)}) collective-permute-start(bf16[16,4,32,512]{3,2,1,0:T(8,128)(2,1)} %bitcast.97), channel_id=1, source_target_pairs={{0,1},{1,0},{2,3},{3,2},{4,5},{5,4},{6,7},{7,6},{8,9},{9,8},{10,11... | collective-permute-start | bytes 6291464 | tf_op jit(solution)/shard_map/ppermute | solution.py:882
  173.8 42.5 %collective-permute-start.3 = (bf16[8,4,32,512]{3,2,1,0:T(8,128)(2,1)}, bf16[8,4,32,512]{3,2,1,0:T(8,128)(2,1)S(1)}, u32[]{:S(2)}, u32[]{:S(2)}) collective-permute-start(bf16[8,4,32,512]{3,2,1,0:T(8,128)(2,1)} %get-tuple-element.335), channel_id=1, source_target_pairs={{0,16},{16,0},{1,17},{17,1},{2,18},{18,2},{3,19},{19,3},{4,20},{20... | collective-permute-start | bytes 3145736 | tf_op jit(solution)/shard_map/ppermute | solution.py:882
  192.7 25.1 %collective-permute-start.4 = (bf16[8,4,32,512]{3,2,1,0:T(8,128)(2,1)}, bf16[8,4,32,512]{3,2,1,0:T(8,128)(2,1)S(1)}, u32[]{:S(2)}, u32[]{:S(2)}) collective-permute-start(bf16[8,4,32,512]{3,2,1,0:T(8,128)(2,1)} %get-tuple-element.336), channel_id=1, source_target_pairs={{0,2},{1,3},{2,0},{3,1},{4,6},{5,7},{6,4},{7,5},{8,10},{9,11},{10,... | collective-permute-start | bytes 3145736 | tf_op jit(solution)/shard_map/ppermute | solution.py:882
  194.2 23.6 %collective-permute-start.7 = (bf16[16,2,32,512]{3,2,1,0:T(8,128)(2,1)}, bf16[16,2,32,512]{3,2,1,0:T(8,128)(2,1)S(1)}, u32[]{:S(2)}, u32[]{:S(2)}) collective-permute-start(bf16[16,2,32,512]{3,2,1,0:T(8,128)(2,1)} %get-tuple-element.339), channel_id=1, source_target_pairs={{0,1},{1,0},{2,3},{3,2},{4,5},{5,4},{6,7},{7,6},{8,9},{9,8},{10,11... | collective-permute-start | bytes 3145736 | tf_op jit(solution)/shard_map/ppermute | solution.py:882
  226.5 46.8 %collective-permute-start.11 = (bf16[8,6,32,512]{3,2,1,0:T(8,128)(2,1)}, bf16[8,6,32,512]{3,2,1,0:T(8,128)(2,1)S(1)}, u32[]{:S(2)}, u32[]{:S(2)}) collective-permute-start(bf16[8,6,32,512]{3,2,1,0:T(8,128)(2,1)} %get-tuple-element.364), channel_id=1, source_target_pairs={{0,2},{1,3},{2,0},{3,1},{4,6},{5,7},{6,4},{7,5},{8,10},{9,11},{10,... | collective-permute-start | bytes 4718600 | tf_op jit(solution)/shard_map/ppermute | solution.py:882
  228.1 45.2 %collective-permute-start.10 = (bf16[8,4,32,512]{3,2,1,0:T(8,128)(2,1)}, bf16[8,4,32,512]{3,2,1,0:T(8,128)(2,1)S(1)}, u32[]{:S(2)}, u32[]{:S(2)}) collective-permute-start(bf16[8,4,32,512]{3,2,1,0:T(8,128)(2,1)} %get-tuple-element.363), channel_id=1, source_target_pairs={{0,16},{16,0},{1,17},{17,1},{2,18},{18,2},{3,19},{19,3},{4,20},{20... | collective-permute-start | bytes 3145736 | tf_op jit(solution)/shard_map/ppermute | solution.py:882
  228.7 44.5 %collective-permute-start.8 = (bf16[4,4,32,512]{3,2,1,0:T(8,128)(2,1)}, bf16[4,4,32,512]{3,2,1,0:T(8,128)(2,1)S(1)}, u32[]{:S(2)}, u32[]{:S(2)}) collective-permute-start(bf16[4,4,32,512]{3,2,1,0:T(8,128)(2,1)} %get-tuple-element.361), channel_id=1, source_target_pairs={{0,2},{1,3},{2,0},{3,1},{4,6},{5,7},{6,4},{7,5},{8,10},{9,11},{10,... | collective-permute-start | bytes 1572872 | tf_op jit(solution)/shard_map/ppermute | solution.py:882
  229.2 44.0 %collective-permute-start.9 = (bf16[4,4,32,512]{3,2,1,0:T(8,128)(2,1)}, bf16[4,4,32,512]{3,2,1,0:T(8,128)(2,1)S(1)}, u32[]{:S(2)}, u32[]{:S(2)}) collective-permute-start(bf16[4,4,32,512]{3,2,1,0:T(8,128)(2,1)} %get-tuple-element.362), channel_id=1, source_target_pairs={{0,16},{16,0},{1,17},{17,1},{2,18},{18,2},{3,19},{19,3},{4,20},{20... | collective-permute-start | bytes 1572872 | tf_op jit(solution)/shard_map/ppermute | solution.py:882
  280.1 20.3 %collective-permute-start.15 = (bf16[16,6,32,512]{3,2,1,0:T(8,128)(2,1)}, bf16[16,6,32,512]{3,2,1,0:T(8,128)(2,1)S(1)}, u32[]{:S(2)}, u32[]{:S(2)}) collective-permute-start(bf16[16,6,32,512]{3,2,1,0:T(8,128)(2,1)} %get-tuple-element.386), channel_id=1, source_target_pairs={{0,1},{1,0},{2,3},{3,2},{4,5},{5,4},{6,7},{7,6},{8,9},{9,8},{10,11... | collective-permute-start | bytes 9437192 | tf_op jit(solution)/shard_map/ppermute | solution.py:882
  280.2 20.2 %collective-permute-start.16 = (bf16[16,4,32,512]{3,2,1,0:T(8,128)(2,1)}, bf16[16,4,32,512]{3,2,1,0:T(8,128)(2,1)S(1)}, u32[]{:S(2)}, u32[]{:S(2)}) collective-permute-start(bf16[16,4,32,512]{3,2,1,0:T(8,128)(2,1)} %get-tuple-element.387), channel_id=1, source_target_pairs={{0,1},{1,0},{2,3},{3,2},{4,5},{5,4},{6,7},{7,6},{8,9},{9,8},{10,11... | collective-permute-start | bytes 6291464 | tf_op jit(solution)/shard_map/ppermute | solution.py:882
  311.0 35.8 %collective-permute-start.20 = (bf16[8,6,32,512]{3,2,1,0:T(8,128)(2,1)}, bf16[8,6,32,512]{3,2,1,0:T(8,128)(2,1)S(1)}, u32[]{:S(2)}, u32[]{:S(2)}) collective-permute-start(bf16[8,6,32,512]{3,2,1,0:T(8,128)(2,1)} %get-tuple-element.413), channel_id=1, source_target_pairs={{0,2},{1,3},{2,0},{3,1},{4,6},{5,7},{6,4},{7,5},{8,10},{9,11},{10,... | collective-permute-start | bytes 4718600 | tf_op jit(solution)/shard_map/ppermute | solution.py:882
  312.6 24.3 %collective-permute-start.19 = (bf16[8,4,32,512]{3,2,1,0:T(8,128)(2,1)}, bf16[8,4,32,512]{3,2,1,0:T(8,128)(2,1)S(1)}, u32[]{:S(2)}, u32[]{:S(2)}) collective-permute-start(bf16[8,4,32,512]{3,2,1,0:T(8,128)(2,1)} %get-tuple-element.412), channel_id=1, source_target_pairs={{0,16},{16,0},{1,17},{17,1},{2,18},{18,2},{3,19},{19,3},{4,20},{20... | collective-permute-start | bytes 3145736 | tf_op jit(solution)/shard_map/ppermute | solution.py:882
  313.5 23.4 %collective-permute-start.18 = (bf16[2,10,32,512]{3,2,1,0:T(8,128)(2,1)}, bf16[2,10,32,512]{3,2,1,0:T(8,128)(2,1)S(1)}, u32[]{:S(2)}, u32[]{:S(2)}) collective-permute-start(bf16[2,10,32,512]{3,2,1,0:T(8,128)(2,1)} %get-tuple-element.411), channel_id=1, source_target_pairs={{0,4},{1,5},{2,6},{3,7},{4,0},{5,1},{6,2},{7,3},{8,12},{9,13},{10,... | collective-permute-start | bytes 1966088 | tf_op jit(solution)/shard_map/ppermute | solution.py:882
  315.1 21.8 %collective-permute-start.17 = (bf16[1,8,32,512]{3,2,1,0:T(8,128)(2,1)}, bf16[1,8,32,512]{3,2,1,0:T(8,128)(2,1)S(1)}, u32[]{:S(2)}, u32[]{:S(2)}) collective-permute-start(bf16[1,8,32,512]{3,2,1,0:T(8,128)(2,1)} %get-tuple-element.410), channel_id=1, source_target_pairs={{0,8},{1,9},{2,10},{3,11},{4,12},{5,13},{6,14},{7,15},{8,0},{9,1},... | collective-permute-start | bytes 786440 | tf_op jit(solution)/shard_map/ppermute | solution.py:882
  353.8 21.1 %collective-permute-start.23 = (bf16[4,6,32,512]{3,2,1,0:T(8,128)(2,1)}, bf16[4,6,32,512]{3,2,1,0:T(8,128)(2,1)S(1)}, u32[]{:S(2)}, u32[]{:S(2)}) collective-permute-start(bf16[4,6,32,512]{3,2,1,0:T(8,128)(2,1)} %get-tuple-element.430), channel_id=1, source_target_pairs={{0,16},{16,0},{1,17},{17,1},{2,18},{18,2},{3,19},{19,3},{4,20},{20... | collective-permute-start | bytes 2359304 | tf_op jit(solution)/shard_map/ppermute | solution.py:882
  358.9 47.1 %collective-permute-start.24 = (bf16[768,1024]{1,0:T(8,128)(2,1)}, bf16[768,1024]{1,0:T(8,128)(2,1)}, u32[]{:S(2)}, u32[]{:S(2)}) collective-permute-start(bf16[768,1024]{1,0:T(8,128)(2,1)} %get-tuple-element.455), channel_id=1, source_target_pairs={{16,0},{17,1},{18,2},{19,3},{20,4},{21,5},{22,6},{23,7},{24,8},{25... | collective-permute-start | bytes 4718600 | tf_op jit(solution)/shard_map/ppermute | solution.py:1242
  412.1 21.9 %collective-permute-start.28 = (bf16[8,2,32,512]{3,2,1,0:T(8,128)(2,1)}, bf16[8,2,32,512]{3,2,1,0:T(8,128)(2,1)S(1)}, u32[]{:S(2)}, u32[]{:S(2)}) collective-permute-start(bf16[8,2,32,512]{3,2,1,0:T(8,128)(2,1)} %get-tuple-element.483), channel_id=1, source_target_pairs={{0,2},{1,3},{2,0},{3,1},{4,6},{5,7},{6,4},{7,5},{8,10},{9,11},{10,... | collective-permute-start | bytes 1572872 | tf_op jit(solution)/shard_map/ppermute | solution.py:882
  413.2 20.7 %collective-permute-start.29 = (bf16[8,1,32,512]{3,2,1,0:T(8,128)(2,1)}, bf16[8,1,32,512]{3,2,1,0:T(8,128)(2,1)S(1)}, u32[]{:S(2)}, u32[]{:S(2)}) collective-permute-start(bf16[8,1,32,512]{3,2,1,0:T(8,128)(2,1)} %get-tuple-element.484), channel_id=1, source_target_pairs={{0,16},{16,0},{1,17},{17,1},{2,18},{18,2},{3,19},{19,3},{4,20},{20... | collective-permute-start | bytes 786440 | tf_op jit(solution)/shard_map/ppermute | solution.py:882
  413.4 20.5 %collective-permute-start.27 = (bf16[1,10,32,512]{3,2,1,0:T(8,128)(2,1)}, bf16[1,10,32,512]{3,2,1,0:T(8,128)(2,1)S(1)}, u32[]{:S(2)}, u32[]{:S(2)}) collective-permute-start(bf16[1,10,32,512]{3,2,1,0:T(8,128)(2,1)} %get-tuple-element.482), channel_id=1, source_target_pairs={{0,8},{1,9},{2,10},{3,11},{4,12},{5,13},{6,14},{7,15},{8,0},{9,1},... | collective-permute-start | bytes 983048 | tf_op jit(solution)/shard_map/ppermute | solution.py:882
  (98 other events, 663.0 us)
Sparse Core Ops, SparseCore 0:
  11.0 60.5 all-gather.1

commit v5 on v4

--- a/solution.py
+++ b/solution.py
@@ -124,20 +124,23 @@
         lanes = slice(head * HDIM, (head + 1) * HDIM)
         query = only(q_ref[...], head)
         earlier = None if begun is None else begun[1][0, head : head + 1, :]
-        row_max, scores = earlier, []
+        row_max, scores = None, []
         for first, rows, start, mask in blocks:
             score = scores_of(k_ref[pl.ds(first, rows), :], query, start, mask)
             row_max = from_start(row_max, start, score.max(0, keepdims=True), jnp.maximum)
             scores.append(score)
+        if begun is not None:
+            row_max = jnp.maximum(row_max, earlier)
         total, out = None, None
-        if begun is not None:
-            total = jnp.exp(earlier - row_max)
-            out = begun[0][lanes] * total
         for score, (first, rows, start, _) in zip(scores, blocks):
             exponent = jnp.exp(score - row_max[:, start:])
             total = from_start(total, start, exponent.sum(0, keepdims=True), jnp.add)
             part = nn(values[lanes, first : first + rows], exponent.astype(bf16))
             out = from_start(out, start, part, jnp.add)
+        if begun is not None:
+            share = jnp.exp(earlier - row_max)
+            total = total + share
+            out = out + begun[0][lanes] * share
         outs.append(out / total)
         total_ref[0, head : head + 1, :] = row_max + jnp.log(total)
     out_ref[...] = jnp.concatenate(outs, axis=0).T.astype(bf16)
@@ -801,6 +804,87 @@
 FIRST_DIGIT = 4
 
 
+class Gather:
+    def __init__(self, block):
+        every = digit_axes()
+        self.order = every[-2:0:-1] + every[:1] + every[-1:]
+        self.held, self.at = block[None], 0
+        self.arrived = hop(self.held, self.order[:1])
+
+    def step(self, chain):
+        chain, arrived = tied(chain, self.arrived)
+        self.held = jnp.concatenate([self.held, arrived], axis=0)
+        self.at += 1
+        if self.at < len(self.order):
+            chain, self.held = tied(chain, self.held)
+            self.arrived = hop(self.held, self.order[self.at : self.at + 1])
+        return chain
+
+    def rest(self, chain):
+        while self.at < len(self.order):
+            chain = self.step(chain)
+        return chain
+
+    def places(self, first, count):
+        digits = digit_axes()
+        device = first + jnp.arange(count, dtype=jnp.int32)
+        place = jnp.zeros((count,), jnp.int32)
+        for i, one in enumerate(self.order):
+            theirs = (device >> (len(digits) - 1 - digits.index(one))) & 1
+            place = place | ((theirs ^ my_digit(*one)) << i)
+        return place.astype(jnp.int32)
+
+
+def page_forward(places, blocks, key_weight, value_weight, value_bias):
+    count, (each, width) = places.shape[0], blocks.shape[1:]
+    slots = count * each
+
+    def body(place_ref, blocks_ref, wk_ref, wv_ref, bias_ref, rows_out, k_out, v_out, rows, wk, wv, k, v, sems):
+        copies = [
+            pltpu.make_async_copy(
+                blocks_ref.at[place_ref[i]], rows.at[pl.ds(i * each, each)], sems.at[i]
+            )
+            for i in range(count)
+        ]
+        copies.append(pltpu.make_async_copy(wk_ref, wk, sems.at[count]))
+        copies.append(pltpu.make_async_copy(wv_ref, wv, sems.at[count + 1]))
+        for copy in copies:
+            copy.start()
+        for copy in copies[:-1]:
+            copy.wait()
+        stores = [pltpu.make_async_copy(rows, rows_out, sems.at[count + 2])]
+        stores[0].start()
+        k[...] = nn(rows[...], wk[...]).astype(bf16)
+        stores.append(pltpu.make_async_copy(k, k_out, sems.at[count + 3]))
+        stores[1].start()
+        copies[-1].wait()
+        v[...] = (nn(rows[...], wv[...]) + bias_ref[...]).astype(bf16)
+        stores.append(pltpu.make_async_copy(v, v_out, sems.at[count + 4]))
+        stores[2].start()
+        for store in stores:
+            store.wait()
+
+    hbm = pl.BlockSpec(memory_space=pltpu.HBM)
+    return pl.pallas_call(
+        body,
+        out_shape=[Shape((slots, width), bf16)] * 3,
+        grid_spec=pltpu.PrefetchScalarGridSpec(
+            num_scalar_prefetch=1,
+            grid=(1,),
+            in_specs=[hbm] * 3 + [pl.BlockSpec((1, width), lambda i, places: (0, 0))],
+            out_specs=[hbm] * 3,
+            scratch_shapes=[
+                pltpu.VMEM((slots, width), bf16), pltpu.VMEM((width, width), bf16),
+                pltpu.VMEM((width, width), bf16), pltpu.VMEM((slots, width), bf16),
+                pltpu.VMEM((slots, width), bf16), pltpu.SemaphoreType.DMA((count + 5,)),
+            ],
+        ),
+        cost_estimate=TINY,
+        compiler_params=settings(),
+        name="page_forward",
+    )(places, blocks, key_weight, value_weight, value_bias)
+
+
 class Part:
     def __init__(self, kept, tok_first, place, start=0, pieces=None):
         self.tok_first, self.place = tok_first, place
@@ -1137,7 +1221,6 @@
     core = my_digit("patch", 0).astype(jnp.int32)
     row_count, model_width = tokens.shape[1:]
     lead_tokens = lax.ppermute(tokens[0], "tok", [(0, 1)])
-    gathered = lax.all_gather(patches, ("tok", "patch"), axis=0, tiled=True)
     inputs = tokens[0].astype(f32)
     page_index = pick_entry(page_of, sequence)
     filled = pick_entry(page_counts, page_index).reshape(1)
@@ -1156,20 +1239,26 @@
     query = ((nn(hidden_one, query_weight) + query_bias) * head_scale).astype(bf16)
     own_keys = nn(hidden_one, key_weight).astype(bf16)
     own_values = (nn(hidden_one, value_weight) + value_bias).astype(bf16)
+    gather = Gather(patches)
+    query = gather.step(query)
+    own_values = gather.step(own_values)
     own_mixed, own_total = own_forward(query, own_keys, own_values)
-    lead_tokens, own_mixed = tied(lead_tokens, own_mixed)
+    lead_tokens, own_mixed = gather.step((lead_tokens, own_mixed))
     hidden_lead = layer_norm(lead_tokens.astype(f32), self_gain, self_shift)
     lead_keys = nn(hidden_lead, key_weight).astype(bf16)
     lead_values = (nn(hidden_lead, value_weight) + value_bias).astype(bf16)
     self_mixed, self_total = lead_forward(
         query, lead_keys, lead_values, own_mixed, own_total, trailing
     )
+    self_mixed = gather.step(self_mixed)
     after_one = inputs + nn(self_mixed, output_weight) + output_bias
     hidden_two = layer_norm(after_one, cross_gain, cross_shift)
     probe = ((nn(hidden_two, probe_weight) + probe_bias) * head_scale).astype(bf16)
-    page_rows = lax.dynamic_slice_in_dim(gathered, page_start, PAGE_SLOTS, 0)
-    page_keys = nn(page_rows, source_key).astype(bf16)
-    page_values = (nn(page_rows, source_value) + source_bias).astype(bf16)
+    probe = gather.rest(probe)
+    page_rows, page_keys, page_values = page_forward(
+        gather.places(page_start // patches.shape[0], PAGE_SLOTS // patches.shape[0]),
+        gather.held, source_key, source_value, source_bias[None],
+    )
     cross_mixed, cross_total = cross_forward(probe, page_keys, page_values, filled)
 
     feed_args = (
@@ -1206,8 +1295,9 @@
     cross_args = (probe, page_keys, page_values, cross_mixed, cross_total)
     grad_cross_out = advance(info, grad_cross_out, [first], [second])
     low = cross_backward(*cross_args, grad_cross_out, filled, 0, half_pairs)
-    low, grad_cross_out = advance(info, (low, grad_cross_out), [first, second])
+    low, grad_cross_out = tied(low, grad_cross_out)
     high = cross_backward(*cross_args, grad_cross_out, filled, half_pairs, half_pairs)
+    low, high = advance(info, (low, high), [first, second])
     patch_total = patches.shape[0] * lax.axis_size(("tok", "patch"))
     paged = page_backward(
         info, low[1], high[1], low[2], high[2], page_rows, source_key, source_value, owners,
@@ -1244,7 +1334,7 @@
     own_low, grad_self_out = advance(info, (own_low, grad_self_out), [second, third])
     parts = projection_grads(info, hidden_one, *own_low, led_part, False, owners)
     half = model_width // 2
-    fourth = Sum(True, (parts[0], [Part(parts[1], i == 1, (i, 0), i, 1) for i in range(3)]))
+    fourth = Sum(False, (parts[0], [Part(parts[1], i == 1, (i, 0), i, 1) for i in range(3)]))
     own_low, grad_self_out = advance(info, (own_low, grad_self_out), [], [fourth])
     own_high = own_backward(*own_args, grad_self_out, lead_high[0], half_pairs, half_pairs)
     own_low, own_high, returned = advance(
@@ -1263,10 +1353,14 @@
     table = vector_table(feed_sums, bias_rows, probe_sums, paged[2], lead_sums, first_sums)
     table = scatter_rows(table, model_width, 0, 1)
     fifth = Sum(True, (parts[0], [Part(parts[1], i != 1, (i, half), i, 1) for i in range(3)]))
-    table = advance(info, table, [fourth], [fifth])
-    table = scatter_rows(table, model_width, 1, 3)
+    table = advance(info, table, [], [fifth])
+    table = scatter_rows(table, model_width, 1, 2)
     table = advance(info, table, [fourth, fifth])
-    sums = scatter_rows(table, model_width, 3, len(digits))
+    table = scatter_rows(table, model_width, 2, 3)
+    table = advance(info, table, [fourth, fifth])
+    table = scatter_rows(table, model_width, 3, len(digits) - 1)
+    table = advance(info, table, [fourth, fifth])
+    sums = scatter_rows(table, model_width, len(digits) - 1, len(digits))
     totals = [first, second, third, fourth, fifth]
     while any(one.leaving is not None for one in totals):
         sums = advance(info, sums, totals)

time: 535 us -> 517 us (0.966)
  starting transfers between devices: 76.6 us -> 62.9 us
  between operations: 15.9 us -> 2.48 us
    ppermute x47 -> x51, starting transfers between devices: 70.3 us -> 57.1 us  [hop(): lax.ppermute(value, axis, [(i, i ^ flip) for i in range(lax.axis_size(axi...]
    ppermute x47 -> x51, waiting for transfers between devices: 66.8 us -> 75.9 us  [hop(): lax.ppermute(value, axis, [(i, i ^ flip) for i in range(lax.axis_size(axi...]
    pallas_call x0 -> x1, Pallas kernels: none -> 6.84 us  [page_forward(): pl.pallas_call(body, out_shape=[Shape((slots, width), bf16)] * 3, grid_sp...]
    dot_general x9 -> x7, matrix products: 26 us -> 23 us  [nn(): lax.dot_general(left, right, (((1,), (0,)), ((), ())), preferred_element_...]
    pallas_call x12 -> x11, Pallas kernels: 53.5 us -> 51.7 us  [added_up(): pl.pallas_call(body, out_shape=[Shape(shape, kind) for shape, kind in sha...]
    unnamed x144 -> x148, local copies, waits for them, and re-layouts: 20.1 us -> 21.3 us
  transfers between devices with their start and end apart: 50 -> 53, of which waited for: 19 -> 20; matrix products, arithmetic and copies ran while one was open for 7% -> 8% of each run, Pallas kernels for 37% -> 39%
where the time goes in v5:
time: 517 us; the launch traced here: 510 us
  Pallas kernels  301 us (58%)
  waiting for transfers between devices  77.2 us (15%)
  starting transfers between devices  62.9 us (12%)
  local copies, waits for them, and re-layouts  30.2 us (6%)
  matrix products  23 us (4%)
  other arithmetic  13.3 us (3%)
    ppermute x51, waiting for transfers between devices, hop(): lax.ppermute(value, axis, [(i, i ^ flip) for i in range(lax.axis_size(axi...  75.9 us
    pallas_call x2, Pallas kernels, feed_forward(): pl.pallas_call(body, out_shape=shapes + shared_shapes, grid_spec=pltpu.Pr...  72.3 us
    ppermute x51, starting transfers between devices, hop(): lax.ppermute(value, axis, [(i, i ^ flip) for i in range(lax.axis_size(axi...  57.1 us
    pallas_call x5, Pallas kernels, streamed(): pl.pallas_call(kernel, out_shape=[Shape(shape, kind) for shape, kind in o...  56.5 us
    pallas_call x11, Pallas kernels, added_up(): pl.pallas_call(body, out_shape=[Shape(shape, kind) for shape, kind in sha...  51.7 us
    pallas_call x2, Pallas kernels, own_backward(): pl.pallas_call(body, out_shape=[Shape((rows, pairs * PAIR), bf16)] * 3, g...  25.4 us
    pallas_call x2, Pallas kernels, cross_backward(): pl.pallas_call(body, out_shape=[Shape((rows, pairs * PAIR), bf16)] + [Sha...  23.7 us
    dot_general x7, matrix products, nn(): lax.dot_general(left, right, (((1,), (0,)), ((), ())), preferred_element_...  23 us
  transfers between devices with their start and end apart: 53, of which 20 were waited for; matrix products, arithmetic and copies ran while one was open for 8% of the time, Pallas kernels for 39%

profile of v5, /device:TPU:0, one launch (start us, length us, event | category | flops | bytes accessed | tf_op | source)
XLA Modules:
  0.0 510.3 jit_solution(12475236535201602634)
XLA Ops:
  30.2 14.0 %own_forward.1 = (bf16[768,1024]{1,0:T(8,128)(2,1)}, f32[8,2,768]{2,1,0:T(2,128)}) custom-call(bf16[768,1024]{1,0:T(8,128)(2,1)} %multiply_convert_fusion.1.q_ref, bf16[768,1024]{1,0:T(8,128)(2,1)} %convolution_convert_fusion.1.k_ref, bf16[768,1024]{1,0:T(8,128)(2,1)} %add_convert_fusion.2.v_ref), custom_call_target="tpu_custom_call" | custom-call | flops 1 | bytes 1 | tf_op jit(solution)/shard_map/own_forward/pallas_call | solution.py:189
  57.1 7.0 %lead_forward.1 = (bf16[768,1024]{1,0:T(8,128)(2,1)}, f32[8,2,768]{2,1,0:T(2,128)}) custom-call(s32[1]{0:T(128)} %bitcast.9.flag, bf16[768,1024]{1,0:T(8,128)(2,1)} %multiply_convert_fusion.1.q_ref, bf16[768,1024]{1,0:T(8,128)(2,1)} %convolution_convert_fusion.k_ref, bf16[768,1024]{1,0:T(8,128)(2,1)} %add_convert_fusion.1.v_ref, ...), custom_call_target="tpu_custom_call" | custom-call | flops 1 | bytes 1 | tf_op jit(solution)/shard_map/lead_forward/pallas_call | solution.py:218
  75.0 6.8 %page_forward.1 = (bf16[512,1024]{1,0:T(8,128)(2,1)}, bf16[512,1024]{1,0:T(8,128)(2,1)}, bf16[512,1024]{1,0:T(8,128)(2,1)}) custom-call(s32[16]{0:T(128)S(1)} %shift-left_or_fusion.place_ref, bf16[32,32,1024]{2,1,0:T(8,128)(2,1)S(1)} %pad_maximum_fusion.blocks_ref, bf16[1024,1024]{1,0:T(8,128)(2,1)S(1)} %copy-done, bf16[1024,1024]{1,0:T(8,128)(2,1)} %refs_6_.2, ...), custom_call_target="tpu_custom_call" | custom-call | flops 1 | bytes 1 | tf_op jit(solution)/shard_map/page_forward/pallas_call | solution.py:868
  81.8 14.8 %cross_forward.1 = (bf16[768,1024]{1,0:T(8,128)(2,1)}, f32[8,2,768]{2,1,0:T(2,128)}) custom-call(s32[1]{0:T(128)} %bitcast.11.filled_ref, bf16[768,1024]{1,0:T(8,128)(2,1)} %multiply_convert_fusion.q_ref, bf16[512,1024]{1,0:T(8,128)(2,1)} %get-tuple-element.346.k_ref, bf16[512,1024]{1,0:T(8,128)(2,1)} %get-tuple-element.347.v_ref), custom_call_target="tpu_custom_call" | custom-call | flops 1 | bytes 1 | tf_op jit(solution)/shard_map/cross_forward/pallas_call | solution.py:249
  96.6 32.9 %feed_forward.2 = (f32[768,1024]{1,0:T(8,128)}, f32[768,1024]{1,0:T(8,128)}, f32[768,1024]{1,0:T(8,128)}, bf16[2,8,4,32,512]{4,3,2,1,0:T(8,128)(2,1)}, bf16[2,8,...) custom-call(s32[9]{0:T(128)} %stack.61.info_ref, ...), custom_call_target="tpu_custom_call" | custom-call | flops 1 | bytes 1 | tf_op jit(solution)/shard_map/feed_forward/pallas_call | solution.py:499
  130.1 39.4 %feed_forward.3 = (bf16[768,1024]{1,0:T(8,128)(2,1)}, f32[768,1024]{1,0:T(8,128)}, bf16[768,1024]{1,0:T(8,128)(2,1)}, bf16[16,2,32,512]{3,2,1,0:T(8,128)(2,1)}, ...) custom-call(s32[9]{0:T(128)} %stack.61.info_ref, ...), custom_call_target="tpu_custom_call" | custom-call | flops 1 | bytes 1 | tf_op jit(solution)/shard_map/feed_forward/pallas_call | solution.py:499
  175.8 13.9 %collective-permute-start.8 = (bf16[8,4,32,512]{3,2,1,0:T(8,128)(2,1)}, bf16[8,4,32,512]{3,2,1,0:T(8,128)(2,1)S(1)}, u32[]{:S(2)}, u32[]{:S(2)}) collective-permute-start(bf16[8,4,32,512]{3,2,1,0:T(8,128)(2,1)} %get-tuple-element.387), channel_id=1, source_target_pairs={{0,16},{16,0},{1,17},{17,1},{2,18},{18,2},{3,19},{19,3},{4,20},{20... | collective-permute-start | bytes 3145736 | tf_op jit(solution)/shard_map/ppermute | solution.py:966
  190.2 11.8 %cross_backward.2 = (bf16[768,512]{1,0:T(8,128)(2,1)}, bf16[512,512]{1,0:T(8,128)(2,1)}, bf16[512,512]{1,0:T(8,128)(2,1)}) custom-call(s32[1]{0:T(128)} %bitcast.11.filled_ref, bf16[768,1024]{1,0:T(8,128)(2,1)} %multiply_convert_fusion.q_ref, bf16[512,1024]{1,0:T(8,128)(2,1)} %get-tuple-element.346.k_ref, bf16[512,1024]{1,0:T(8,128)(2,1)} %get-tuple-element.347.v_ref, ...), custom_call_target="tpu_custom_call" | custom-call | flops 1 | bytes 1 | tf_op jit(solution)/shard_map/cross_backward/pallas_call | solution.py:342
  202.0 11.9 %cross_backward.3 = (bf16[768,512]{1,0:T(8,128)(2,1)}, bf16[512,512]{1,0:T(8,128)(2,1)}, bf16[512,512]{1,0:T(8,128)(2,1)}) custom-call(s32[1]{0:T(128)} %bitcast.11.filled_ref, bf16[768,1024]{1,0:T(8,128)(2,1)} %multiply_convert_fusion.q_ref, bf16[512,1024]{1,0:T(8,128)(2,1)} %get-tuple-element.346.k_ref, bf16[512,1024]{1,0:T(8,128)(2,1)} %get-tuple-element.347.v_ref, ...), custom_call_target="tpu_custom_call" | custom-call | flops 1 | bytes 1 | tf_op jit(solution)/shard_map/cross_backward/pallas_call | solution.py:342
  216.7 7.1 %added_up.12 = (bf16[4,4,32,512]{3,2,1,0:T(8,128)(2,1)}, bf16[4,4,32,512]{3,2,1,0:T(8,128)(2,1)}, bf16[8,4,32,512]{3,2,1,0:T(8,128)(2,1)}, bf16[8,6,32,512]{3,2,1,0:T(8,128)(2,1)}) custom-call(s32[9]{0:T(128)} %stack.61.info_ref, bf16[16,4,32,512]{3,2,1,0:T(8,128)(2,1)} %get-tuple-element.367.refs_0_, bf16[16,4,32,512]{3,2,1,0:T(8,128)(2,1)} %copy-done.11, ...), custom_call_target="tpu_custom_call" | custom-call | flops 1 | bytes 1 | tf_op jit(solution)/shard_map/added_up/pallas_call | solution.py:1079
  228.6 16.4 %probe_backward.1 = (f32[768,1024]{1,0:T(8,128)}, bf16[768,1024]{1,0:T(8,128)(2,1)}, bf16[16,4,32,512]{3,2,1,0:T(8,128)(2,1)}, bf16[16,4,32,512]{3,2,1,0:T(8,128)(2,1)}, f32[8,1024]{1,0:T(8,128)}) custom-call(s32[9]{0:T(128)} %stack.61.info_ref, bf16[768,512]{1,0:T(8,128)(2,1)} %get-tuple-element.410.refs_0_, bf16[768,512]{1,0:T(8,128)(2,1)} %get-tuple-element.411.refs_1_, ...), custom_call_target="tpu_custom_call" | custom-call | flops 1 | bytes 1 | tf_op jit(solution)/shard_map/probe_backward/pallas_call | solution.py:558
  245.0 10.4 %page_backward.1 = (bf16[16,6,32,512]{3,2,1,0:T(8,128)(2,1)}, bf16[16,6,32,512]{3,2,1,0:T(8,128)(2,1)}, f32[8,1024]{1,0:T(8,128)}) custom-call(s32[9]{0:T(128)} %stack.61.info_ref, bf16[512,512]{1,0:T(8,128)(2,1)} %get-tuple-element.426.refs_0_, bf16[512,512]{1,0:T(8,128)(2,1)} %get-tuple-element.427.refs_1_, bf16[512,512]{1,0:T(8,128)(2,1)} %get-tuple-element.428.refs_2_, ...), custom_call_target="tpu_custom_call" | custom-call | flops 1 | bytes 1 | tf_op jit(solution)/shard_map/page_backward/pallas_call | solution.py:558
  255.4 16.1 %collective-permute-done.13.refs_3_ = bf16[4,4,32,512]{3,2,1,0:T(8,128)(2,1)S(1)} collective-permute-done((bf16[4,4,32,512]{3,2,1,0:T(8,128)(2,1)}, bf16[4,4,32,512]{3,2,1,0:T(8,128)(2,1)S(1)}, u32[]{:S(2)}, u32[]{:S(2)}) %collective-permute-start.13) | collective-permute-done | bytes 524320 | tf_op jit(solution)/shard_map/ppermute | solution.py:966
  285.8 7.4 %collective-permute-done.17.refs_4_ = bf16[2,8,32,512]{3,2,1,0:T(8,128)(2,1)S(1)} collective-permute-done((bf16[2,8,32,512]{3,2,1,0:T(8,128)(2,1)}, bf16[2,8,32,512]{3,2,1,0:T(8,128)(2,1)S(1)}, u32[]{:S(2)}, u32[]{:S(2)}) %collective-permute-start.17) | collective-permute-done | bytes 524320 | tf_op jit(solution)/shard_map/ppermute | solution.py:966
  293.4 5.3 %collective-permute-done.19.refs_16_.refs_8_ = bf16[4,6,32,512]{3,2,1,0:T(8,128)(2,1)S(1)} collective-permute-done((bf16[4,6,32,512]{3,2,1,0:T(8,128)(2,1)}, bf16[4,6,32,512]{3,2,1,0:T(8,128)(2,1)S(1)}, u32[]{:S(2)}, u32[]{:S(2)}) %collective-permute-start.19) | collective-permute-done | bytes 786464 | tf_op jit(solution)/shard_map/ppermute | solution.py:966
  301.8 7.5 %added_up.14 = (f32[1,8,32,512]{3,2,1,0:T(8,128)}, bf16[1,8,32,512]{3,2,1,0:T(8,128)(2,1)}, bf16[2,10,32,512]{3,2,1,0:T(8,128)(2,1)}, bf16[8,4,32,512]{3,2,1,0:T(8,128)(2,1)}, bf16[8,6,32,512]{3,2,1,0:T(8,128)(2,1)}) custom-call(s32[9]{0:T(128)} %stack.61.info_ref, bf16[16,4,32,512]{3,2,1,0:T(8,128)(2,1)} %get-tuple-element.367.refs_0_, ...), custom_call_target="tpu_custom_call" | custom-call | flops 1 | bytes 1 | tf_op jit(solution)/shard_map/added_up/pallas_call | solution.py:1079
  318.1 13.6 %lead_upstream.1 = (bf16[768,1024]{1,0:T(8,128)(2,1)}, bf16[1024,2048]{1,0:T(8,128)(2,1)}, f32[8,1024]{1,0:T(8,128)}) custom-call(s32[9]{0:T(128)} %stack.61.info_ref, bf16[768,512]{1,0:T(8,128)(2,1)} %get-tuple-element.457.refs_0_, bf16[768,512]{1,0:T(8,128)(2,1)} %get-tuple-element.459.refs_1_, bf16[768,512]{1,0:T(8,128)(2,1)} %get-tuple-element.460.refs_2_, ...), custom_call_target="tpu_custom_call" | custom-call | flops 1 | bytes 1 | tf_op jit(solution)/shard_map/lead_upstream/pallas_call | solution.py:558
  335.1 10.0 %collective-permute-done.25.refs_14_.refs_4_.refs_5_ = bf16[8,6,32,512]{3,2,1,0:T(8,128)(2,1)S(1)} collective-permute-done((bf16[8,6,32,512]{3,2,1,0:T(8,128)(2,1)}, bf16[8,6,32,512]{3,2,1,0:T(8,128)(2,1)S(1)}, u32[]{:S(2)}, u32[]{:S(2)}) %collective-permute-start.25) | collective-permute-done | bytes 1572896 | tf_op jit(solution)/shard_map/ppermute | solution.py:966
  346.2 5.9 %added_up.15 = (f32[1,10,32,512]{3,2,1,0:T(8,128)}, bf16[1,10,32,512]{3,2,1,0:T(8,128)(2,1)}, bf16[4,4,32,512]{3,2,1,0:T(8,128)(2,1)}, bf16[4,6,32,512]{3,2,1,0:T(8,128)(2,1)}) custom-call(s32[9]{0:T(128)} %stack.61.info_ref, bf16[16,4,32,512]{3,2,1,0:T(8,128)(2,1)} %get-tuple-element.400.refs_6_.refs_8_.refs_9_.refs_0_, ...), custom_call_target="tpu_custom_call" | custom-call | flops 1 | bytes 1 | tf_op jit(solution)/shard_map/added_up/pallas_call | solution.py:1079
  355.9 12.9 %own_backward.2 = (bf16[768,512]{1,0:T(8,128)(2,1)}, bf16[768,512]{1,0:T(8,128)(2,1)}, bf16[768,512]{1,0:T(8,128)(2,1)}) custom-call(bf16[768,1024]{1,0:T(8,128)(2,1)} %multiply_convert_fusion.1.q_ref, bf16[768,1024]{1,0:T(8,128)(2,1)} %convolution_convert_fusion.1.k_ref, bf16[768,1024]{1,0:T(8,128)(2,1)} %add_convert_fusion.2.v_ref, ...), custom_call_target="tpu_custom_call" | custom-call | flops 1 | bytes 1 | tf_op jit(solution)/shard_map/own_backward/pallas_call | solution.py:312
  377.4 8.0 %projection_grads.2 = (bf16[16,3,32,512]{3,2,1,0:T(8,128)(2,1)}, bf16[16,3,32,512]{3,2,1,0:T(8,128)(2,1)}) custom-call(s32[9]{0:T(128)} %stack.61.info_ref, bf16[768,1024]{1,0:T(8,128)(2,1)} %copy-done.19, bf16[768,512]{1,0:T(8,128)(2,1)} %get-tuple-element.525.refs_1_.refs_0_, bf16[768,512]{1,0:T(8,128)(2,1)} %get-tuple-element.527.refs_2_, ...), custom_call_target="tpu_custom_call" | custom-call | flops 1 | bytes 1 | tf_op jit(solution)/shard_map/projection_grads/pallas_call | solution.py:558
  386.1 12.5 %own_backward.3 = (bf16[768,512]{1,0:T(8,128)(2,1)}, bf16[768,512]{1,0:T(8,128)(2,1)}, bf16[768,512]{1,0:T(8,128)(2,1)}) custom-call(bf16[768,1024]{1,0:T(8,128)(2,1)} %multiply_convert_fusion.1.q_ref, bf16[768,1024]{1,0:T(8,128)(2,1)} %convolution_convert_fusion.1.k_ref, bf16[768,1024]{1,0:T(8,128)(2,1)} %add_convert_fusion.2.v_ref, ...), custom_call_target="tpu_custom_call" | custom-call | flops 1 | bytes 1 | tf_op jit(solution)/shard_map/own_backward/pallas_call | solution.py:312
  414.6 15.4 %first_norm_backward.1 = (f32[768,1024]{1,0:T(8,128)}, f32[8,1024]{1,0:T(8,128)}) custom-call(s32[9]{0:T(128)S(1)} %copy-done.5, bf16[768,512]{1,0:T(8,128)(2,1)} %get-tuple-element.525.refs_1_.refs_0_, bf16[768,512]{1,0:T(8,128)(2,1)} %get-tuple-element.557.refs_1_, bf16[768,512]{1,0:T(8,128)(2,1)} %get-tuple-element.527.refs_2_, ...), custom_call_target="tpu_custom_call" | custom-call | flops 1 | bytes 1 | tf_op jit(solution)/shard_map/first_norm_backward/pallas_call | solution.py:776
  438.1 8.0 %projection_grads.3 = (bf16[16,3,32,512]{3,2,1,0:T(8,128)(2,1)}, bf16[16,3,32,512]{3,2,1,0:T(8,128)(2,1)}) custom-call(s32[9]{0:T(128)} %stack.61.info_ref, bf16[768,1024]{1,0:T(8,128)(2,1)} %copy-done.19, bf16[768,512]{1,0:T(8,128)(2,1)} %get-tuple-element.557.refs_1_, bf16[768,512]{1,0:T(8,128)(2,1)} %get-tuple-element.558.refs_3_.refs_2_, ...), custom_call_target="tpu_custom_call" | custom-call | flops 1 | bytes 1 | tf_op jit(solution)/shard_map/projection_grads/pallas_call | solution.py:558
  (318 shorter events, 198.8 us)
Async XLA Ops:
  3.7 40.4 %collective-permute-start.1 = (bf16[768,1024]{1,0:T(8,128)(2,1)}, bf16[768,1024]{1,0:T(8,128)(2,1)}, u32[]{:S(2)}, u32[]{:S(2)}) collective-permute-start(bf16[768,1024]{1,0:T(8,128)(2,1)} %bitcast.81), channel_id=1, source_target_pairs={{0,16},{1,17},{2,18},{3,19},{4,20},{5,21},{6,22},{7,23},{8,24},{9,... | collective-permute-start | bytes 4718600 | tf_op jit(solution)/shard_map/ppermute | solution.py:1223
  23.7 20.5 %collective-permute-start.3 = (bf16[4,32,1024]{2,1,0:T(8,128)(2,1)S(1)}, bf16[4,32,1024]{2,1,0:T(8,128)(2,1)S(1)}, u32[]{:S(2)}, u32[]{:S(2)}) collective-permute-start(bf16[4,32,1024]{2,1,0:T(8,128)(2,1)S(1)} %pad_maximum_fusion.4), channel_id=1, source_target_pairs={{0,8},{1,9},{2,10},{3,11},{4,12},{5,13},{6,14},{7,15},{8,0},{9,1},... | collective-permute-start | bytes 786440 | tf_op jit(solution)/shard_map/ppermute | solution.py:966
  129.5 40.0 %collective-permute-start.6 = (bf16[16,4,32,512]{3,2,1,0:T(8,128)(2,1)}, bf16[16,4,32,512]{3,2,1,0:T(8,128)(2,1)S(1)}, u32[]{:S(2)}, u32[]{:S(2)}) collective-permute-start(bf16[16,4,32,512]{3,2,1,0:T(8,128)(2,1)} %get-tuple-element.364), channel_id=1, source_target_pairs={{0,1},{1,0},{2,3},{3,2},{4,5},{5,4},{6,7},{7,6},{8,9},{9,8},{10,11... | collective-permute-start | bytes 6291464 | tf_op jit(solution)/shard_map/ppermute | solution.py:966
  129.6 40.0 %collective-permute-start.7 = (bf16[16,4,32,512]{3,2,1,0:T(8,128)(2,1)}, bf16[16,4,32,512]{3,2,1,0:T(8,128)(2,1)}, u32[]{:S(2)}, u32[]{:S(2)}) collective-permute-start(bf16[16,4,32,512]{3,2,1,0:T(8,128)(2,1)} %bitcast.99), channel_id=1, source_target_pairs={{0,1},{1,0},{2,3},{3,2},{4,5},{5,4},{6,7},{7,6},{8,9},{9,8},{10,11... | collective-permute-start | bytes 6291464 | tf_op jit(solution)/shard_map/ppermute | solution.py:966
  175.2 39.5 %collective-permute-start.10 = (bf16[16,4,32,512]{3,2,1,0:T(8,128)(2,1)}, bf16[16,4,32,512]{3,2,1,0:T(8,128)(2,1)S(1)}, u32[]{:S(2)}, u32[]{:S(2)}) collective-permute-start(bf16[16,4,32,512]{3,2,1,0:T(8,128)(2,1)} %get-tuple-element.389), channel_id=1, source_target_pairs={{0,1},{1,0},{2,3},{3,2},{4,5},{5,4},{6,7},{7,6},{8,9},{9,8},{10,11... | collective-permute-start | bytes 6291464 | tf_op jit(solution)/shard_map/ppermute | solution.py:966
  175.4 39.5 %collective-permute-start.11 = (bf16[16,4,32,512]{3,2,1,0:T(8,128)(2,1)}, bf16[16,4,32,512]{3,2,1,0:T(8,128)(2,1)}, u32[]{:S(2)}, u32[]{:S(2)}) collective-permute-start(bf16[16,4,32,512]{3,2,1,0:T(8,128)(2,1)} %bitcast.98), channel_id=1, source_target_pairs={{0,1},{1,0},{2,3},{3,2},{4,5},{5,4},{6,7},{7,6},{8,9},{9,8},{10,11... | collective-permute-start | bytes 6291464 | tf_op jit(solution)/shard_map/ppermute | solution.py:966
  175.8 38.0 %collective-permute-start.8 = (bf16[8,4,32,512]{3,2,1,0:T(8,128)(2,1)}, bf16[8,4,32,512]{3,2,1,0:T(8,128)(2,1)S(1)}, u32[]{:S(2)}, u32[]{:S(2)}) collective-permute-start(bf16[8,4,32,512]{3,2,1,0:T(8,128)(2,1)} %get-tuple-element.387), channel_id=1, source_target_pairs={{0,16},{16,0},{1,17},{17,1},{2,18},{18,2},{3,19},{19,3},{4,20},{20... | collective-permute-start | bytes 3145736 | tf_op jit(solution)/shard_map/ppermute | solution.py:966
  189.7 25.1 %collective-permute-start.9 = (bf16[8,4,32,512]{3,2,1,0:T(8,128)(2,1)}, bf16[8,4,32,512]{3,2,1,0:T(8,128)(2,1)S(1)}, u32[]{:S(2)}, u32[]{:S(2)}) collective-permute-start(bf16[8,4,32,512]{3,2,1,0:T(8,128)(2,1)} %get-tuple-element.388), channel_id=1, source_target_pairs={{0,2},{1,3},{2,0},{3,1},{4,6},{5,7},{6,4},{7,5},{8,10},{9,11},{10,... | collective-permute-start | bytes 3145736 | tf_op jit(solution)/shard_map/ppermute | solution.py:966
  190.2 24.6 %collective-permute-start.12 = (bf16[16,2,32,512]{3,2,1,0:T(8,128)(2,1)}, bf16[16,2,32,512]{3,2,1,0:T(8,128)(2,1)S(1)}, u32[]{:S(2)}, u32[]{:S(2)}) collective-permute-start(bf16[16,2,32,512]{3,2,1,0:T(8,128)(2,1)} %get-tuple-element.391), channel_id=1, source_target_pairs={{0,1},{1,0},{2,3},{3,2},{4,5},{5,4},{6,7},{7,6},{8,9},{9,8},{10,11... | collective-permute-start | bytes 3145736 | tf_op jit(solution)/shard_map/ppermute | solution.py:966
  223.8 47.8 %collective-permute-start.16 = (bf16[8,6,32,512]{3,2,1,0:T(8,128)(2,1)}, bf16[8,6,32,512]{3,2,1,0:T(8,128)(2,1)S(1)}, u32[]{:S(2)}, u32[]{:S(2)}) collective-permute-start(bf16[8,6,32,512]{3,2,1,0:T(8,128)(2,1)} %get-tuple-element.417), channel_id=1, source_target_pairs={{0,2},{1,3},{2,0},{3,1},{4,6},{5,7},{6,4},{7,5},{8,10},{9,11},{10,... | collective-permute-start | bytes 4718600 | tf_op jit(solution)/shard_map/ppermute | solution.py:966
  224.8 46.7 %collective-permute-start.15 = (bf16[8,4,32,512]{3,2,1,0:T(8,128)(2,1)}, bf16[8,4,32,512]{3,2,1,0:T(8,128)(2,1)S(1)}, u32[]{:S(2)}, u32[]{:S(2)}) collective-permute-start(bf16[8,4,32,512]{3,2,1,0:T(8,128)(2,1)} %get-tuple-element.416), channel_id=1, source_target_pairs={{0,16},{16,0},{1,17},{17,1},{2,18},{18,2},{3,19},{19,3},{4,20},{20... | collective-permute-start | bytes 3145736 | tf_op jit(solution)/shard_map/ppermute | solution.py:966
  225.0 46.6 %collective-permute-start.13 = (bf16[4,4,32,512]{3,2,1,0:T(8,128)(2,1)}, bf16[4,4,32,512]{3,2,1,0:T(8,128)(2,1)S(1)}, u32[]{:S(2)}, u32[]{:S(2)}) collective-permute-start(bf16[4,4,32,512]{3,2,1,0:T(8,128)(2,1)} %get-tuple-element.414), channel_id=1, source_target_pairs={{0,2},{1,3},{2,0},{3,1},{4,6},{5,7},{6,4},{7,5},{8,10},{9,11},{10,... | collective-permute-start | bytes 1572872 | tf_op jit(solution)/shard_map/ppermute | solution.py:966
  226.5 45.0 %collective-permute-start.14 = (bf16[4,4,32,512]{3,2,1,0:T(8,128)(2,1)}, bf16[4,4,32,512]{3,2,1,0:T(8,128)(2,1)S(1)}, u32[]{:S(2)}, u32[]{:S(2)}) collective-permute-start(bf16[4,4,32,512]{3,2,1,0:T(8,128)(2,1)} %get-tuple-element.415), channel_id=1, source_target_pairs={{0,16},{16,0},{1,17},{17,1},{2,18},{18,2},{3,19},{19,3},{4,20},{20... | collective-permute-start | bytes 1572872 | tf_op jit(solution)/shard_map/ppermute | solution.py:966
  278.4 20.3 %collective-permute-start.20 = (bf16[16,6,32,512]{3,2,1,0:T(8,128)(2,1)}, bf16[16,6,32,512]{3,2,1,0:T(8,128)(2,1)S(1)}, u32[]{:S(2)}, u32[]{:S(2)}) collective-permute-start(bf16[16,6,32,512]{3,2,1,0:T(8,128)(2,1)} %get-tuple-element.440), channel_id=1, source_target_pairs={{0,1},{1,0},{2,3},{3,2},{4,5},{5,4},{6,7},{7,6},{8,9},{9,8},{10,11... | collective-permute-start | bytes 9437192 | tf_op jit(solution)/shard_map/ppermute | solution.py:966
  278.5 20.2 %collective-permute-start.21 = (bf16[16,4,32,512]{3,2,1,0:T(8,128)(2,1)}, bf16[16,4,32,512]{3,2,1,0:T(8,128)(2,1)S(1)}, u32[]{:S(2)}, u32[]{:S(2)}) collective-permute-start(bf16[16,4,32,512]{3,2,1,0:T(8,128)(2,1)} %get-tuple-element.441), channel_id=1, source_target_pairs={{0,1},{1,0},{2,3},{3,2},{4,5},{5,4},{6,7},{7,6},{8,9},{9,8},{10,11... | collective-permute-start | bytes 6291464 | tf_op jit(solution)/shard_map/ppermute | solution.py:966
  279.0 19.7 %collective-permute-start.19 = (bf16[4,6,32,512]{3,2,1,0:T(8,128)(2,1)}, bf16[4,6,32,512]{3,2,1,0:T(8,128)(2,1)S(1)}, u32[]{:S(2)}, u32[]{:S(2)}) collective-permute-start(bf16[4,6,32,512]{3,2,1,0:T(8,128)(2,1)} %get-tuple-element.439), channel_id=1, source_target_pairs={{0,16},{16,0},{1,17},{17,1},{2,18},{18,2},{3,19},{19,3},{4,20},{20... | collective-permute-start | bytes 2359304 | tf_op jit(solution)/shard_map/ppermute | solution.py:966
  309.3 35.8 %collective-permute-start.25 = (bf16[8,6,32,512]{3,2,1,0:T(8,128)(2,1)}, bf16[8,6,32,512]{3,2,1,0:T(8,128)(2,1)S(1)}, u32[]{:S(2)}, u32[]{:S(2)}) collective-permute-start(bf16[8,6,32,512]{3,2,1,0:T(8,128)(2,1)} %get-tuple-element.467), channel_id=1, source_target_pairs={{0,2},{1,3},{2,0},{3,1},{4,6},{5,7},{6,4},{7,5},{8,10},{9,11},{10,... | collective-permute-start | bytes 4718600 | tf_op jit(solution)/shard_map/ppermute | solution.py:966
  310.9 24.2 %collective-permute-start.24 = (bf16[8,4,32,512]{3,2,1,0:T(8,128)(2,1)}, bf16[8,4,32,512]{3,2,1,0:T(8,128)(2,1)S(1)}, u32[]{:S(2)}, u32[]{:S(2)}) collective-permute-start(bf16[8,4,32,512]{3,2,1,0:T(8,128)(2,1)} %get-tuple-element.466), channel_id=1, source_target_pairs={{0,16},{16,0},{1,17},{17,1},{2,18},{18,2},{3,19},{19,3},{4,20},{20... | collective-permute-start | bytes 3145736 | tf_op jit(solution)/shard_map/ppermute | solution.py:966
  311.2 21.5 %collective-permute-start.23 = (bf16[2,10,32,512]{3,2,1,0:T(8,128)(2,1)}, bf16[2,10,32,512]{3,2,1,0:T(8,128)(2,1)S(1)}, u32[]{:S(2)}, u32[]{:S(2)}) collective-permute-start(bf16[2,10,32,512]{3,2,1,0:T(8,128)(2,1)} %get-tuple-element.465), channel_id=1, source_target_pairs={{0,4},{1,5},{2,6},{3,7},{4,0},{5,1},{6,2},{7,3},{8,12},{9,13},{10,... | collective-permute-start | bytes 1966088 | tf_op jit(solution)/shard_map/ppermute | solution.py:966
  311.8 19.9 %collective-permute-start.22 = (bf16[1,8,32,512]{3,2,1,0:T(8,128)(2,1)}, bf16[1,8,32,512]{3,2,1,0:T(8,128)(2,1)S(1)}, u32[]{:S(2)}, u32[]{:S(2)}) collective-permute-start(bf16[1,8,32,512]{3,2,1,0:T(8,128)(2,1)} %get-tuple-element.464), channel_id=1, source_target_pairs={{0,8},{1,9},{2,10},{3,11},{4,12},{5,13},{6,14},{7,15},{8,0},{9,1},... | collective-permute-start | bytes 786440 | tf_op jit(solution)/shard_map/ppermute | solution.py:966
  352.1 20.8 %collective-permute-start.28 = (bf16[4,6,32,512]{3,2,1,0:T(8,128)(2,1)}, bf16[4,6,32,512]{3,2,1,0:T(8,128)(2,1)S(1)}, u32[]{:S(2)}, u32[]{:S(2)}) collective-permute-start(bf16[4,6,32,512]{3,2,1,0:T(8,128)(2,1)} %get-tuple-element.484), channel_id=1, source_target_pairs={{0,16},{16,0},{1,17},{17,1},{2,18},{18,2},{3,19},{19,3},{4,20},{20... | collective-permute-start | bytes 2359304 | tf_op jit(solution)/shard_map/ppermute | solution.py:966
  354.6 49.3 %collective-permute-start.29 = (bf16[768,1024]{1,0:T(8,128)(2,1)}, bf16[768,1024]{1,0:T(8,128)(2,1)}, u32[]{:S(2)}, u32[]{:S(2)}) collective-permute-start(bf16[768,1024]{1,0:T(8,128)(2,1)} %get-tuple-element.509), channel_id=1, source_target_pairs={{16,0},{17,1},{18,2},{19,3},{20,4},{21,5},{22,6},{23,7},{24,8},{25... | collective-permute-start | bytes 4718600 | tf_op jit(solution)/shard_map/ppermute | solution.py:1332
  385.4 18.6 %collective-permute-start.31 = (bf16[16,3,32,512]{3,2,1,0:T(8,128)(2,1)}, bf16[16,3,32,512]{3,2,1,0:T(8,128)(2,1)S(1)}, u32[]{:S(2)}, u32[]{:S(2)}) collective-permute-start(bf16[16,3,32,512]{3,2,1,0:T(8,128)(2,1)} %get-tuple-element.511), channel_id=1, source_target_pairs={{0,1},{1,0},{2,3},{3,2},{4,5},{5,4},{6,7},{7,6},{8,9},{9,8},{10,11... | collective-permute-start | bytes 4718600 | tf_op jit(solution)/shard_map/ppermute | solution.py:966
  410.0 20.1 %collective-permute-start.33 = (bf16[8,2,32,512]{3,2,1,0:T(8,128)(2,1)}, bf16[8,2,32,512]{3,2,1,0:T(8,128)(2,1)S(1)}, u32[]{:S(2)}, u32[]{:S(2)}) collective-permute-start(bf16[8,2,32,512]{3,2,1,0:T(8,128)(2,1)} %get-tuple-element.537), channel_id=1, source_target_pairs={{0,2},{1,3},{2,0},{3,1},{4,6},{5,7},{6,4},{7,5},{8,10},{9,11},{10,... | collective-permute-start | bytes 1572872 | tf_op jit(solution)/shard_map/ppermute | solution.py:966
  (103 other events, 675.9 us)

commit v6 on v5

--- a/solution.py
+++ b/solution.py
@@ -530,9 +530,9 @@
 
     def kernel(info_ref, *refs):
         ins, dests = refs[:n], refs[n : n + m]
-        held, made = refs[n + m : 2 * n + m], refs[2 * n + m : 2 * n + 2 * m]
-        in_sem, out_sem = refs[2 * n + 2 * m : 2 * n + 2 * m + 2]
-        rest = refs[2 * n + 2 * m + 2 :]
+        refs = refs[n + m :]
+        held, made, refs = refs[:n], refs[n : n + m], refs[n + m :]
+        in_sem, out_sem, *rest = refs
         loads = [pltpu.make_async_copy(ins[i], held[i], in_sem.at[i]) for i in range(n)]
         for load in loads:
             load.start()
@@ -572,6 +572,53 @@
         compiler_params=settings(60),
         name=name,
     )(info, *inputs)
+
+
+def norm_project(name, info, tokens, weights, ways, vectors, keep):
+    rows, width = tokens.shape
+    n = len(weights)
+
+    def body(info_ref, need, give):
+        vec = need(1)
+        for start in range(0, rows, 256):
+            at = pl.ds(start, 256)
+            unit, _ = norm_unit(need(0)[at, :].astype(f32))
+            low = (unit * vec[0:1, :] + vec[1:2, :]).astype(bf16)
+            if keep:
+                give(n)[at, :] = low
+            for i, (row, factor) in enumerate(ways):
+                made = nn(low, need(2 + i)[...])
+                if row is not None:
+                    made = made + vec[row : row + 1, :]
+                give(i)[at, :] = (made * factor).astype(bf16)
+        for i in range(n + keep):
+            give(i, True)
+
+    return streamed(
+        name, body, info, [tokens, vectors, *weights], [((rows, width), bf16)] * (n + keep),
+    )
+
+
+def output_project(info, mixed, tokens, output_weight, probe_weight, vectors):
+    rows, width = tokens.shape
+
+    def body(info_ref, need, give):
+        vec = need(2)
+        for start in range(0, rows, 256):
+            at = pl.ds(start, 256)
+            x = need(1)[at, :].astype(f32) + nn(need(0)[at, :], need(3)[...]) + vec[0:1, :]
+            give(0)[at, :] = x
+            unit, _ = norm_unit(x)
+            low = (unit * vec[1:2, :] + vec[2:3, :]).astype(bf16)
+            made = nn(low, need(4)[...]) + vec[3:4, :]
+            give(1)[at, :] = (made * (HDIM**-0.5)).astype(bf16)
+        give(0, True)
+        give(1, True)
+
+    return streamed(
+        "output_project", body, info, [mixed, tokens, vectors, output_weight, probe_weight],
+        [((rows, width), f32), ((rows, width), bf16)],
+    )
 
 
 def probe_backward(info, probe_low, probe_high, probe_weight, after_one, two, output_weight, mixed, vectors, owners):
@@ -745,47 +792,37 @@
 
 def first_norm_backward(info, queries, keys, values, weights, tokens, one, returned, vectors):
     rows, width = tokens.shape
-    half, tall = width // 2, 384
-
-    def body(info_ref, *refs):
-        grads = refs[:6]
-        wq, wk, wv, x_ref, vec, one_ref, back_ref = refs[6:13]
-        out_ref, sums = refs[13:]
+    half, tall = width // 2, 256
+
+    def body(info_ref, need, give):
+        grads = [need(i) for i in range(6)]
+        vec = need(10)
         gains = jnp.zeros((1, width), f32)
         shifts = gains
         for start in range(0, rows, tall):
             at = pl.ds(start, tall)
             up = 0.0
-            for i, weight in enumerate((wq, wk, wv)):
-                up = up + nt(grads[2 * i][at, :], weight[:, :half])
-                up = up + nt(grads[2 * i + 1][at, :], weight[:, half:])
-            unit, inverse = norm_unit(x_ref[at, :].astype(f32))
+            for i in range(3):
+                up = up + nt(grads[2 * i][at, :], need(6 + i)[:, :half])
+                up = up + nt(grads[2 * i + 1][at, :], need(6 + i)[:, half:])
+            unit, inverse = norm_unit(need(9)[at, :].astype(f32))
             gains = gains + jnp.sum(up * unit, axis=0, keepdims=True)
             shifts = shifts + jnp.sum(up, axis=0, keepdims=True)
-            up = up + back_ref[at, :].astype(f32)
-            out_ref[at, :] = one_ref[at, :] + norm_pull(up, unit, inverse, vec[0:1, :])
+            up = up + need(12)[at, :].astype(f32)
+            give(0)[at, :] = need(11)[at, :] + norm_pull(up, unit, inverse, vec[0:1, :])
+        give(0, True)
+        sums = give(1)
         sums[...] = jnp.zeros_like(sums)
         sums[0:1, :], sums[1:2, :] = gains, shifts
         sums[2:3, :half], sums[2:3, half:] = column_sums(grads[0][...]), column_sums(grads[1][...])
         sums[3:4, :half], sums[3:4, half:] = column_sums(grads[4][...]), column_sums(grads[5][...])
-
-    narrow = pl.BlockSpec((rows, half), lambda i, info: (0, 0))
-    wide = pl.BlockSpec((rows, width), lambda i, info: (0, 0))
-    whole = pl.BlockSpec((width, width), lambda i, info: (0, 0))
-    eight = pl.BlockSpec((8, width), lambda i, info: (0, 0))
-    return pl.pallas_call(
-        body,
-        out_shape=[Shape((rows, width), f32), Shape((8, width), f32)],
-        grid_spec=pltpu.PrefetchScalarGridSpec(
-            num_scalar_prefetch=1,
-            grid=(1,),
-            in_specs=[narrow] * 6 + [whole] * 3 + [wide, eight, wide, wide],
-            out_specs=[wide, eight],
-        ),
-        cost_estimate=TINY,
-        compiler_params=settings(),
-        name="first_norm_backward",
-    )(info, *in_hbm(*queries, *keys, *values, *weights, tokens), vectors, *in_hbm(one, returned))
+        give(1, True)
+
+    return streamed(
+        "first_norm_backward", body, info,
+        [*queries, *keys, *values, *weights, tokens, vectors, one, returned],
+        [((rows, width), f32), ((8, width), f32)],
+    )
 
 
 def digit_axes():
@@ -808,20 +845,21 @@
     def __init__(self, block):
         every = digit_axes()
         self.order = every[-2:0:-1] + every[:1] + every[-1:]
-        self.held, self.at = block[None], 0
-        self.arrived = hop(self.held, self.order[:1])
+        self.held, self.at = block[None], 2
+        one, two = self.order[:2]
+        self.arrived = [hop(self.held, steps) for steps in ([one], [two], [one, two])]
 
     def step(self, chain):
         chain, arrived = tied(chain, self.arrived)
-        self.held = jnp.concatenate([self.held, arrived], axis=0)
-        self.at += 1
+        self.held = jnp.concatenate([self.held, *arrived], axis=0)
         if self.at < len(self.order):
             chain, self.held = tied(chain, self.held)
-            self.arrived = hop(self.held, self.order[self.at : self.at + 1])
+            self.arrived = [hop(self.held, self.order[self.at : self.at + 1])]
+        self.at += 1
         return chain
 
     def rest(self, chain):
-        while self.at < len(self.order):
+        while self.at <= len(self.order):
             chain = self.step(chain)
         return chain
 
@@ -1171,11 +1209,6 @@
 def pick_entry(table, position):
     indices = jnp.arange(table.shape[0], dtype=jnp.int32)
     return jnp.sum(jnp.where(indices == position, table, 0))
-
-
-def layer_norm(values, gain, shift):
-    unit, _ = norm_unit(values)
-    return (unit * gain + shift).astype(bf16)
 
 
 def rows_of(*vectors):
@@ -1221,7 +1254,6 @@
     core = my_digit("patch", 0).astype(jnp.int32)
     row_count, model_width = tokens.shape[1:]
     lead_tokens = lax.ppermute(tokens[0], "tok", [(0, 1)])
-    inputs = tokens[0].astype(f32)
     page_index = pick_entry(page_of, sequence)
     filled = pick_entry(page_counts, page_index).reshape(1)
     trailing = tok_index.reshape(1)
@@ -1231,29 +1263,31 @@
     info = jnp.stack(
         [core, tok_index * row_count, pick_entry(lengths, sequence), page_index] + digits
     )
-    self_vectors = rows_of(self_gain, self_shift)
+    self_vectors = rows_of(self_gain, self_shift, query_bias, value_bias)
     cross_vectors = rows_of(cross_gain, cross_shift)
+    output_vectors = rows_of(output_bias, cross_gain, cross_shift, probe_bias)
     feed_vectors = rows_of(merge_bias, feed_gain, feed_shift, reduce_bias)
 
-    hidden_one = layer_norm(inputs, self_gain, self_shift)
-    query = ((nn(hidden_one, query_weight) + query_bias) * head_scale).astype(bf16)
-    own_keys = nn(hidden_one, key_weight).astype(bf16)
-    own_values = (nn(hidden_one, value_weight) + value_bias).astype(bf16)
     gather = Gather(patches)
+    nothing = jnp.zeros((1,), jnp.int32)
+    query, own_keys, own_values, hidden_one = norm_project(
+        "own_project", nothing, tokens[0], [query_weight, key_weight, value_weight],
+        [(2, head_scale), (None, 1.0), (3, 1.0)], self_vectors, True,
+    )
     query = gather.step(query)
-    own_values = gather.step(own_values)
     own_mixed, own_total = own_forward(query, own_keys, own_values)
     lead_tokens, own_mixed = gather.step((lead_tokens, own_mixed))
-    hidden_lead = layer_norm(lead_tokens.astype(f32), self_gain, self_shift)
-    lead_keys = nn(hidden_lead, key_weight).astype(bf16)
-    lead_values = (nn(hidden_lead, value_weight) + value_bias).astype(bf16)
+    lead_keys, lead_values = norm_project(
+        "lead_project", nothing, lead_tokens, [key_weight, value_weight],
+        [(None, 1.0), (3, 1.0)], self_vectors, False,
+    )
     self_mixed, self_total = lead_forward(
         query, lead_keys, lead_values, own_mixed, own_total, trailing
     )
     self_mixed = gather.step(self_mixed)
-    after_one = inputs + nn(self_mixed, output_weight) + output_bias
-    hidden_two = layer_norm(after_one, cross_gain, cross_shift)
-    probe = ((nn(hidden_two, probe_weight) + probe_bias) * head_scale).astype(bf16)
+    after_one, probe = output_project(
+        nothing, self_mixed, tokens[0], output_weight, probe_weight, output_vectors
+    )
     probe = gather.rest(probe)
     page_rows, page_keys, page_values = page_forward(
         gather.places(page_start // patches.shape[0], PAGE_SLOTS // patches.shape[0]),
@@ -1295,9 +1329,9 @@
     cross_args = (probe, page_keys, page_values, cross_mixed, cross_total)
     grad_cross_out = advance(info, grad_cross_out, [first], [second])
     low = cross_backward(*cross_args, grad_cross_out, filled, 0, half_pairs)
-    low, grad_cross_out = tied(low, grad_cross_out)
+    low, grad_cross_out = advance(info, (low, grad_cross_out), [second])
     high = cross_backward(*cross_args, grad_cross_out, filled, half_pairs, half_pairs)
-    low, high = advance(info, (low, high), [first, second])
+    low, high = advance(info, (low, high), [first])
     patch_total = patches.shape[0] * lax.axis_size(("tok", "patch"))
     paged = page_backward(
         info, low[1], high[1], low[2], high[2], page_rows, source_key, source_value, owners,
@@ -1353,7 +1387,7 @@
     table = vector_table(feed_sums, bias_rows, probe_sums, paged[2], lead_sums, first_sums)
     table = scatter_rows(table, model_width, 0, 1)
     fifth = Sum(True, (parts[0], [Part(parts[1], i != 1, (i, half), i, 1) for i in range(3)]))
-    table = advance(info, table, [], [fifth])
+    table = advance(info, table, [fourth], [fifth])
     table = scatter_rows(table, model_width, 1, 2)
     table = advance(info, table, [fourth, fifth])
     table = scatter_rows(table, model_width, 2, 3)

time: 517 us -> 507 us (0.981)
  Pallas kernels: 301 us -> 329 us
  matrix products: 23 us -> 0 us
  waiting for transfers between devices: 77.2 us -> 58 us
  starting transfers between devices: 62.9 us -> 76.4 us
  other arithmetic: 13.3 us -> 6.94 us
    pallas_call x5 -> x9, Pallas kernels: 56.5 us -> 96 us  [streamed(): pl.pallas_call(kernel, out_shape=[Shape(shape, kind) for shape, kind in o...]
    dot_general x7 -> x0, matrix products: 23 us -> none  [nn(): lax.dot_general(left, right, (((1,), (0,)), ((), ())), preferred_element_...]
    ppermute x51 -> x52, waiting for transfers between devices: 75.9 us -> 53.8 us  [hop(): lax.ppermute(value, axis, [(i, i ^ flip) for i in range(lax.axis_size(axi...]
    pallas_call x1 -> x0, Pallas kernels: 15.4 us -> none  [first_norm_backward(): pl.pallas_call(body, out_shape=[Shape((rows, width), f32), Shape((8, widt...]
    ppermute x51 -> x52, starting transfers between devices: 57.1 us -> 70.1 us  [hop(): lax.ppermute(value, axis, [(i, i ^ flip) for i in range(lax.axis_size(axi...]
    reduce_sum x5 -> x0, other arithmetic: 6.46 us -> none  [the longest x2 3.5 us: norm_unit(): average = jnp.mean(values, axis=-1, keepdims=True)]
    pallas_call x11 -> x13, Pallas kernels: 51.7 us -> 55.8 us  [added_up(): pl.pallas_call(body, out_shape=[Shape(shape, kind) for shape, kind in sha...]
    unnamed x148 -> x108, local copies, waits for them, and re-layouts: 21.3 us -> 18.8 us
  transfers between devices with their start and end apart: 53 -> 54, of which waited for: 20 -> 17; matrix products, arithmetic and copies ran while one was open for 8% -> 3% of each run, Pallas kernels for 39% -> 47%
where the time goes in v6:
time: 507 us; the launch traced here: 500 us
  Pallas kernels  329 us (65%)
  starting transfers between devices  76.4 us (15%)
  waiting for transfers between devices  58 us (11%)
  local copies, waits for them, and re-layouts  27.6 us (5%)
  other arithmetic  6.94 us (1%)
    pallas_call x9, Pallas kernels, streamed(): pl.pallas_call(kernel, out_shape=[Shape(shape, kind) for shape, kind in o...  96 us
    pallas_call x2, Pallas kernels, feed_forward(): pl.pallas_call(body, out_shape=shapes + shared_shapes, grid_spec=pltpu.Pr...  72.3 us
    ppermute x52, starting transfers between devices, hop(): lax.ppermute(value, axis, [(i, i ^ flip) for i in range(lax.axis_size(axi...  70.1 us
    pallas_call x13, Pallas kernels, added_up(): pl.pallas_call(body, out_shape=[Shape(shape, kind) for shape, kind in sha...  55.8 us
    ppermute x52, waiting for transfers between devices, hop(): lax.ppermute(value, axis, [(i, i ^ flip) for i in range(lax.axis_size(axi...  53.8 us
    pallas_call x2, Pallas kernels, own_backward(): pl.pallas_call(body, out_shape=[Shape((rows, pairs * PAIR), bf16)] * 3, g...  25.4 us
    pallas_call x2, Pallas kernels, cross_backward(): pl.pallas_call(body, out_shape=[Shape((rows, pairs * PAIR), bf16)] + [Sha...  23.6 us
    unnamed x108, local copies, waits for them, and re-layouts  18.8 us
  transfers between devices with their start and end apart: 54, of which 17 were waited for; matrix products, arithmetic and copies ran while one was open for 3% of the time, Pallas kernels for 47%

profile of v6, /device:TPU:0, one launch (start us, length us, event | category | flops | bytes accessed | tf_op | source)
XLA Modules:
  0.0 500.3 jit_solution(15685311821161534114)
XLA Ops:
  10.6 9.4 %own_project.1 = (bf16[768,1024]{1,0:T(8,128)(2,1)}, bf16[768,1024]{1,0:T(8,128)(2,1)}, bf16[768,1024]{1,0:T(8,128)(2,1)}, bf16[768,1024]{1,0:T(8,128)(2,1)}) custom-call(s32[1]{0:T(128)} %constant.18.clone.1.info_ref, bf16[768,1024]{1,0:T(8,128)(2,1)} %bitcast.71, f32[8,1024]{1,0:T(8,128)} %select_maximum_fusion.7.refs_1_.refs_7_.refs_10_, ...), custom_call_target="tpu_custom_call" | custom-call | flops 1 | bytes 1 | tf_op jit(solution)/shard_map/own_project/pallas_call | solution.py:558
  22.7 14.0 %own_forward.1 = (bf16[768,1024]{1,0:T(8,128)(2,1)}, f32[8,2,768]{2,1,0:T(2,128)}) custom-call(bf16[768,1024]{1,0:T(8,128)(2,1)} %get-tuple-element.338.q_ref, bf16[768,1024]{1,0:T(8,128)(2,1)} %get-tuple-element.339.k_ref, bf16[768,1024]{1,0:T(8,128)(2,1)} %get-tuple-element.340.v_ref), custom_call_target="tpu_custom_call" | custom-call | flops 1 | bytes 1 | tf_op jit(solution)/shard_map/own_forward/pallas_call | solution.py:189
  42.0 6.9 %lead_project.1 = (bf16[768,1024]{1,0:T(8,128)(2,1)}, bf16[768,1024]{1,0:T(8,128)(2,1)}) custom-call(s32[1]{0:T(128)} %constant.18.clone.1.info_ref, bf16[768,1024]{1,0:T(8,128)(2,1)} %copy-done.17, f32[8,1024]{1,0:T(8,128)} %select_maximum_fusion.7.refs_1_.refs_7_.refs_10_, bf16[1024,1024]{1,0:T(8,128)(2,1)} %refs_7_.5, bf16[1024,1024]{1,0:T(8,128)(2,1)} %refs_8_.1), custom_call_target="tpu_custom_call" | custom-call | flops 1 | bytes 1 | tf_op jit(solution)/shard_map/lead_project/pallas_call | solution.py:558
  48.9 6.5 %lead_forward.1 = (bf16[768,1024]{1,0:T(8,128)(2,1)}, f32[8,2,768]{2,1,0:T(2,128)}) custom-call(s32[1]{0:T(128)} %bitcast.8.flag, bf16[768,1024]{1,0:T(8,128)(2,1)} %get-tuple-element.338.q_ref, bf16[768,1024]{1,0:T(8,128)(2,1)} %get-tuple-element.347.k_ref, bf16[768,1024]{1,0:T(8,128)(2,1)} %get-tuple-element.348.v_ref, ...), custom_call_target="tpu_custom_call" | custom-call | flops 1 | bytes 1 | tf_op jit(solution)/shard_map/lead_forward/pallas_call | solution.py:218
  62.0 8.6 %output_project.1 = (f32[768,1024]{1,0:T(8,128)}, bf16[768,1024]{1,0:T(8,128)(2,1)}) custom-call(s32[1]{0:T(128)} %constant.18.clone.1.info_ref, bf16[768,1024]{1,0:T(8,128)(2,1)} %get-tuple-element.355.refs_0_.refs_6_.out_ref, bf16[768,1024]{1,0:T(8,128)(2,1)} %bitcast.72, f32[8,1024]{1,0:T(8,128)} %get-tuple-element.659.refs_2_, ...), custom_call_target="tpu_custom_call" | custom-call | flops 1 | bytes 1 | tf_op jit(solution)/shard_map/output_project/pallas_call | solution.py:558
  72.2 6.8 %page_forward.1 = (bf16[512,1024]{1,0:T(8,128)(2,1)}, bf16[512,1024]{1,0:T(8,128)(2,1)}, bf16[512,1024]{1,0:T(8,128)(2,1)}) custom-call(s32[16]{0:T(128)S(1)} %shift-left_or_fusion.place_ref, bf16[32,32,1024]{2,1,0:T(8,128)(2,1)S(1)} %pad_maximum_fusion.blocks_ref, bf16[1024,1024]{1,0:T(8,128)(2,1)S(1)} %copy-done, bf16[1024,1024]{1,0:T(8,128)(2,1)} %refs_6_.2, ...), custom_call_target="tpu_custom_call" | custom-call | flops 1 | bytes 1 | tf_op jit(solution)/shard_map/page_forward/pallas_call | solution.py:906
  79.0 14.7 %cross_forward.1 = (bf16[768,1024]{1,0:T(8,128)(2,1)}, f32[8,2,768]{2,1,0:T(2,128)}) custom-call(s32[1]{0:T(128)} %bitcast.19.filled_ref, bf16[768,1024]{1,0:T(8,128)(2,1)} %get-tuple-element.359.q_ref, bf16[512,1024]{1,0:T(8,128)(2,1)} %get-tuple-element.361.k_ref, bf16[512,1024]{1,0:T(8,128)(2,1)} %get-tuple-element.362.v_ref), custom_call_target="tpu_custom_call" | custom-call | flops 1 | bytes 1 | tf_op jit(solution)/shard_map/cross_forward/pallas_call | solution.py:249
  93.8 32.9 %feed_forward.2 = (f32[768,1024]{1,0:T(8,128)}, f32[768,1024]{1,0:T(8,128)}, f32[768,1024]{1,0:T(8,128)}, bf16[2,8,4,32,512]{4,3,2,1,0:T(8,128)(2,1)}, bf16[2,8,...) custom-call(s32[9]{0:T(128)} %stack.86.info_ref, ...), custom_call_target="tpu_custom_call" | custom-call | flops 1 | bytes 1 | tf_op jit(solution)/shard_map/feed_forward/pallas_call | solution.py:499
  127.2 39.5 %feed_forward.3 = (bf16[768,1024]{1,0:T(8,128)(2,1)}, f32[768,1024]{1,0:T(8,128)}, bf16[768,1024]{1,0:T(8,128)(2,1)}, bf16[16,2,32,512]{3,2,1,0:T(8,128)(2,1)}, ...) custom-call(s32[9]{0:T(128)} %stack.86.info_ref, ...), custom_call_target="tpu_custom_call" | custom-call | flops 1 | bytes 1 | tf_op jit(solution)/shard_map/feed_forward/pallas_call | solution.py:499
  173.2 13.4 %collective-permute-start.12 = (bf16[8,4,32,512]{3,2,1,0:T(8,128)(2,1)}, bf16[8,4,32,512]{3,2,1,0:T(8,128)(2,1)}, u32[]{:S(2)}, u32[]{:S(2)}) collective-permute-start(bf16[8,4,32,512]{3,2,1,0:T(8,128)(2,1)} %get-tuple-element.417), channel_id=1, source_target_pairs={{0,16},{16,0},{1,17},{17,1},{2,18},{18,2},{3,19},{19,3},{4,20},{20... | collective-permute-start | bytes 3145736 | tf_op jit(solution)/shard_map/ppermute | solution.py:1004
  188.1 11.8 %cross_backward.2 = (bf16[768,512]{1,0:T(8,128)(2,1)}, bf16[512,512]{1,0:T(8,128)(2,1)}, bf16[512,512]{1,0:T(8,128)(2,1)}) custom-call(s32[1]{0:T(128)} %bitcast.19.filled_ref, bf16[768,1024]{1,0:T(8,128)(2,1)} %get-tuple-element.359.q_ref, bf16[512,1024]{1,0:T(8,128)(2,1)} %get-tuple-element.361.k_ref, bf16[512,1024]{1,0:T(8,128)(2,1)} %get-tuple-element.362.v_ref, ...), custom_call_target="tpu_custom_call" | custom-call | flops 1 | bytes 1 | tf_op jit(solution)/shard_map/cross_backward/pallas_call | solution.py:342
  207.0 11.8 %cross_backward.3 = (bf16[768,512]{1,0:T(8,128)(2,1)}, bf16[512,512]{1,0:T(8,128)(2,1)}, bf16[512,512]{1,0:T(8,128)(2,1)}) custom-call(s32[1]{0:T(128)} %bitcast.19.filled_ref, bf16[768,1024]{1,0:T(8,128)(2,1)} %get-tuple-element.359.q_ref, bf16[512,1024]{1,0:T(8,128)(2,1)} %get-tuple-element.361.k_ref, bf16[512,1024]{1,0:T(8,128)(2,1)} %get-tuple-element.362.v_ref, ...), custom_call_target="tpu_custom_call" | custom-call | flops 1 | bytes 1 | tf_op jit(solution)/shard_map/cross_backward/pallas_call | solution.py:342
  226.7 16.4 %probe_backward.1 = (f32[768,1024]{1,0:T(8,128)}, bf16[768,1024]{1,0:T(8,128)(2,1)}, bf16[16,4,32,512]{3,2,1,0:T(8,128)(2,1)}, bf16[16,4,32,512]{3,2,1,0:T(8,128)(2,1)}, f32[8,1024]{1,0:T(8,128)}) custom-call(s32[9]{0:T(128)} %stack.86.info_ref, bf16[768,512]{1,0:T(8,128)(2,1)} %get-tuple-element.429.refs_0_, bf16[768,512]{1,0:T(8,128)(2,1)} %get-tuple-element.430.refs_1_, ...), custom_call_target="tpu_custom_call" | custom-call | flops 1 | bytes 1 | tf_op jit(solution)/shard_map/probe_backward/pallas_call | solution.py:558
  243.2 10.4 %page_backward.1 = (bf16[16,6,32,512]{3,2,1,0:T(8,128)(2,1)}, bf16[16,6,32,512]{3,2,1,0:T(8,128)(2,1)}, f32[8,1024]{1,0:T(8,128)}) custom-call(s32[9]{0:T(128)} %stack.86.info_ref, bf16[512,512]{1,0:T(8,128)(2,1)} %get-tuple-element.445.refs_0_, bf16[512,512]{1,0:T(8,128)(2,1)} %get-tuple-element.446.refs_1_, bf16[512,512]{1,0:T(8,128)(2,1)} %get-tuple-element.447.refs_2_, ...), custom_call_target="tpu_custom_call" | custom-call | flops 1 | bytes 1 | tf_op jit(solution)/shard_map/page_backward/pallas_call | solution.py:558
  272.4 6.1 %collective-permute-done.18.refs_4_ = bf16[2,8,32,512]{3,2,1,0:T(8,128)(2,1)S(1)} collective-permute-done((bf16[2,8,32,512]{3,2,1,0:T(8,128)(2,1)}, bf16[2,8,32,512]{3,2,1,0:T(8,128)(2,1)S(1)}, u32[]{:S(2)}, u32[]{:S(2)}) %collective-permute-start.18) | collective-permute-done | bytes 524320 | tf_op jit(solution)/shard_map/ppermute | solution.py:1004
  287.2 7.5 %added_up.17 = (f32[1,8,32,512]{3,2,1,0:T(8,128)}, bf16[1,8,32,512]{3,2,1,0:T(8,128)(2,1)}, bf16[2,10,32,512]{3,2,1,0:T(8,128)(2,1)}, bf16[8,4,32,512]{3,2,1,0:T(8,128)(2,1)}, bf16[8,6,32,512]{3,2,1,0:T(8,128)(2,1)}) custom-call(s32[9]{0:T(128)} %stack.86.info_ref, bf16[16,4,32,512]{3,2,1,0:T(8,128)(2,1)} %get-tuple-element.382.refs_0_, ...), custom_call_target="tpu_custom_call" | custom-call | flops 1 | bytes 1 | tf_op jit(solution)/shard_map/added_up/pallas_call | solution.py:1117
  305.5 13.6 %lead_upstream.1 = (bf16[768,1024]{1,0:T(8,128)(2,1)}, bf16[1024,2048]{1,0:T(8,128)(2,1)}, f32[8,1024]{1,0:T(8,128)}) custom-call(s32[9]{0:T(128)} %stack.86.info_ref, bf16[768,512]{1,0:T(8,128)(2,1)} %get-tuple-element.476.refs_0_, bf16[768,512]{1,0:T(8,128)(2,1)} %get-tuple-element.478.refs_1_, bf16[768,512]{1,0:T(8,128)(2,1)} %get-tuple-element.479.refs_2_, ...), custom_call_target="tpu_custom_call" | custom-call | flops 1 | bytes 1 | tf_op jit(solution)/shard_map/lead_upstream/pallas_call | solution.py:558
  320.6 10.0 %collective-permute-done.26.refs_14_.refs_4_.refs_5_ = bf16[8,6,32,512]{3,2,1,0:T(8,128)(2,1)S(1)} collective-permute-done((bf16[8,6,32,512]{3,2,1,0:T(8,128)(2,1)}, bf16[8,6,32,512]{3,2,1,0:T(8,128)(2,1)S(1)}, u32[]{:S(2)}, u32[]{:S(2)}) %collective-permute-start.26) | collective-permute-done | bytes 1572896 | tf_op jit(solution)/shard_map/ppermute | solution.py:1004
  343.3 12.9 %own_backward.2 = (bf16[768,512]{1,0:T(8,128)(2,1)}, bf16[768,512]{1,0:T(8,128)(2,1)}, bf16[768,512]{1,0:T(8,128)(2,1)}) custom-call(bf16[768,1024]{1,0:T(8,128)(2,1)} %get-tuple-element.338.q_ref, bf16[768,1024]{1,0:T(8,128)(2,1)} %get-tuple-element.339.k_ref, bf16[768,1024]{1,0:T(8,128)(2,1)} %get-tuple-element.340.v_ref, ...), custom_call_target="tpu_custom_call" | custom-call | flops 1 | bytes 1 | tf_op jit(solution)/shard_map/own_backward/pallas_call | solution.py:312
  362.9 8.0 %projection_grads.2 = (bf16[16,3,32,512]{3,2,1,0:T(8,128)(2,1)}, bf16[16,3,32,512]{3,2,1,0:T(8,128)(2,1)}) custom-call(s32[9]{0:T(128)} %stack.86.info_ref, bf16[768,1024]{1,0:T(8,128)(2,1)} %get-tuple-element.518.refs_0_, bf16[768,512]{1,0:T(8,128)(2,1)} %get-tuple-element.545.refs_1_.refs_0_, bf16[768,512]{1,0:T(8,128)(2,1)} %get-tuple-element.547.refs_2_, ...), custom_call_target="tpu_custom_call" | custom-call | flops 1 | bytes 1 | tf_op jit(solution)/shard_map/projection_grads/pallas_call | solution.py:558
  372.6 12.5 %own_backward.3 = (bf16[768,512]{1,0:T(8,128)(2,1)}, bf16[768,512]{1,0:T(8,128)(2,1)}, bf16[768,512]{1,0:T(8,128)(2,1)}) custom-call(bf16[768,1024]{1,0:T(8,128)(2,1)} %get-tuple-element.338.q_ref, bf16[768,1024]{1,0:T(8,128)(2,1)} %get-tuple-element.339.k_ref, bf16[768,1024]{1,0:T(8,128)(2,1)} %get-tuple-element.340.v_ref, ...), custom_call_target="tpu_custom_call" | custom-call | flops 1 | bytes 1 | tf_op jit(solution)/shard_map/own_backward/pallas_call | solution.py:312
  402.1 14.9 %first_norm_backward.1 = (f32[768,1024]{1,0:T(8,128)}, f32[8,1024]{1,0:T(8,128)}) custom-call(s32[9]{0:T(128)} %stack.86.info_ref, bf16[768,512]{1,0:T(8,128)(2,1)} %get-tuple-element.545.refs_1_.refs_0_, bf16[768,512]{1,0:T(8,128)(2,1)} %get-tuple-element.582.refs_1_, bf16[768,512]{1,0:T(8,128)(2,1)} %get-tuple-element.547.refs_2_, ...), custom_call_target="tpu_custom_call" | custom-call | flops 1 | bytes 1 | tf_op jit(solution)/shard_map/first_norm_backward/pallas_call | solution.py:558
  425.6 7.8 %projection_grads.3 = (bf16[16,3,32,512]{3,2,1,0:T(8,128)(2,1)}, bf16[16,3,32,512]{3,2,1,0:T(8,128)(2,1)}) custom-call(s32[9]{0:T(128)} %stack.86.info_ref, bf16[768,1024]{1,0:T(8,128)(2,1)} %get-tuple-element.518.refs_0_, bf16[768,512]{1,0:T(8,128)(2,1)} %get-tuple-element.582.refs_1_, bf16[768,512]{1,0:T(8,128)(2,1)} %get-tuple-element.583.refs_3_.refs_2_, ...), custom_call_target="tpu_custom_call" | custom-call | flops 1 | bytes 1 | tf_op jit(solution)/shard_map/projection_grads/pallas_call | solution.py:558
  490.1 7.1 %collective-permute-done.51.refs_4_ = bf16[1,3,32,512]{3,2,1,0:T(8,128)(2,1)S(1)} collective-permute-done((bf16[1,3,32,512]{3,2,1,0:T(8,128)(2,1)}, bf16[1,3,32,512]{3,2,1,0:T(8,128)(2,1)S(1)}, u32[]{:S(2)}, u32[]{:S(2)}) %collective-permute-start.51) | collective-permute-done | bytes 98336 | tf_op jit(solution)/shard_map/ppermute | solution.py:1004
  (265 shorter events, 194.2 us)
Async XLA Ops:
  0.7 38.8 %collective-permute-start.3 = (bf16[768,1024]{1,0:T(8,128)(2,1)}, bf16[768,1024]{1,0:T(8,128)(2,1)S(1)}, u32[]{:S(2)}, u32[]{:S(2)}) collective-permute-start(bf16[768,1024]{1,0:T(8,128)(2,1)} %bitcast.70), channel_id=1, source_target_pairs={{0,16},{1,17},{2,18},{3,19},{4,20},{5,21},{6,22},{7,23},{8,24},{9,... | collective-permute-start | bytes 4718600 | tf_op jit(solution)/shard_map/ppermute | solution.py:1256
  126.6 40.1 %collective-permute-start.7 = (bf16[16,4,32,512]{3,2,1,0:T(8,128)(2,1)}, bf16[16,4,32,512]{3,2,1,0:T(8,128)(2,1)S(1)}, u32[]{:S(2)}, u32[]{:S(2)}) collective-permute-start(bf16[16,4,32,512]{3,2,1,0:T(8,128)(2,1)} %get-tuple-element.379), channel_id=1, source_target_pairs={{0,1},{1,0},{2,3},{3,2},{4,5},{5,4},{6,7},{7,6},{8,9},{9,8},{10,11... | collective-permute-start | bytes 6291464 | tf_op jit(solution)/shard_map/ppermute | solution.py:1004
  126.8 39.9 %collective-permute-start.8 = (bf16[16,4,32,512]{3,2,1,0:T(8,128)(2,1)}, bf16[16,4,32,512]{3,2,1,0:T(8,128)(2,1)}, u32[]{:S(2)}, u32[]{:S(2)}) collective-permute-start(bf16[16,4,32,512]{3,2,1,0:T(8,128)(2,1)} %bitcast.96), channel_id=1, source_target_pairs={{0,1},{1,0},{2,3},{3,2},{4,5},{5,4},{6,7},{7,6},{8,9},{9,8},{10,11... | collective-permute-start | bytes 6291464 | tf_op jit(solution)/shard_map/ppermute | solution.py:1004
  172.4 27.4 %collective-permute-start.9 = (bf16[16,4,32,512]{3,2,1,0:T(8,128)(2,1)}, bf16[16,4,32,512]{3,2,1,0:T(8,128)(2,1)S(1)}, u32[]{:S(2)}, u32[]{:S(2)}) collective-permute-start(bf16[16,4,32,512]{3,2,1,0:T(8,128)(2,1)} %get-tuple-element.395), channel_id=1, source_target_pairs={{0,1},{1,0},{2,3},{3,2},{4,5},{5,4},{6,7},{7,6},{8,9},{9,8},{10,11... | collective-permute-start | bytes 6291464 | tf_op jit(solution)/shard_map/ppermute | solution.py:1004
  172.6 27.3 %collective-permute-start.10 = (bf16[16,4,32,512]{3,2,1,0:T(8,128)(2,1)}, bf16[16,4,32,512]{3,2,1,0:T(8,128)(2,1)}, u32[]{:S(2)}, u32[]{:S(2)}) collective-permute-start(bf16[16,4,32,512]{3,2,1,0:T(8,128)(2,1)} %bitcast.95), channel_id=1, source_target_pairs={{0,1},{1,0},{2,3},{3,2},{4,5},{5,4},{6,7},{7,6},{8,9},{9,8},{10,11... | collective-permute-start | bytes 6291464 | tf_op jit(solution)/shard_map/ppermute | solution.py:1004
  173.0 26.9 %collective-permute-start.11 = (bf16[16,2,32,512]{3,2,1,0:T(8,128)(2,1)}, bf16[16,2,32,512]{3,2,1,0:T(8,128)(2,1)S(1)}, u32[]{:S(2)}, u32[]{:S(2)}) collective-permute-start(bf16[16,2,32,512]{3,2,1,0:T(8,128)(2,1)} %get-tuple-element.397), channel_id=1, source_target_pairs={{0,1},{1,0},{2,3},{3,2},{4,5},{5,4},{6,7},{7,6},{8,9},{9,8},{10,11... | collective-permute-start | bytes 3145736 | tf_op jit(solution)/shard_map/ppermute | solution.py:1004
  173.2 45.7 %collective-permute-start.12 = (bf16[8,4,32,512]{3,2,1,0:T(8,128)(2,1)}, bf16[8,4,32,512]{3,2,1,0:T(8,128)(2,1)}, u32[]{:S(2)}, u32[]{:S(2)}) collective-permute-start(bf16[8,4,32,512]{3,2,1,0:T(8,128)(2,1)} %get-tuple-element.417), channel_id=1, source_target_pairs={{0,16},{16,0},{1,17},{17,1},{2,18},{18,2},{3,19},{19,3},{4,20},{20... | collective-permute-start | bytes 3145736 | tf_op jit(solution)/shard_map/ppermute | solution.py:1004
  186.6 32.3 %collective-permute-start.13 = (bf16[8,4,32,512]{3,2,1,0:T(8,128)(2,1)}, bf16[8,4,32,512]{3,2,1,0:T(8,128)(2,1)}, u32[]{:S(2)}, u32[]{:S(2)}) collective-permute-start(bf16[8,4,32,512]{3,2,1,0:T(8,128)(2,1)} %get-tuple-element.418), channel_id=1, source_target_pairs={{0,2},{1,3},{2,0},{3,1},{4,6},{5,7},{6,4},{7,5},{8,10},{9,11},{10,... | collective-permute-start | bytes 3145736 | tf_op jit(solution)/shard_map/ppermute | solution.py:1004
  206.5 50.5 %collective-permute-start.17 = (bf16[8,6,32,512]{3,2,1,0:T(8,128)(2,1)}, bf16[8,6,32,512]{3,2,1,0:T(8,128)(2,1)S(1)}, u32[]{:S(2)}, u32[]{:S(2)}) collective-permute-start(bf16[8,6,32,512]{3,2,1,0:T(8,128)(2,1)} %get-tuple-element.436), channel_id=1, source_target_pairs={{0,2},{1,3},{2,0},{3,1},{4,6},{5,7},{6,4},{7,5},{8,10},{9,11},{10,... | collective-permute-start | bytes 4718600 | tf_op jit(solution)/shard_map/ppermute | solution.py:1004
  207.0 49.9 %collective-permute-start.16 = (bf16[8,4,32,512]{3,2,1,0:T(8,128)(2,1)}, bf16[8,4,32,512]{3,2,1,0:T(8,128)(2,1)S(1)}, u32[]{:S(2)}, u32[]{:S(2)}) collective-permute-start(bf16[8,4,32,512]{3,2,1,0:T(8,128)(2,1)} %get-tuple-element.435), channel_id=1, source_target_pairs={{0,16},{16,0},{1,17},{17,1},{2,18},{18,2},{3,19},{19,3},{4,20},{20... | collective-permute-start | bytes 3145736 | tf_op jit(solution)/shard_map/ppermute | solution.py:1004
  223.1 33.8 %collective-permute-start.14 = (bf16[4,4,32,512]{3,2,1,0:T(8,128)(2,1)}, bf16[4,4,32,512]{3,2,1,0:T(8,128)(2,1)S(1)}, u32[]{:S(2)}, u32[]{:S(2)}) collective-permute-start(bf16[4,4,32,512]{3,2,1,0:T(8,128)(2,1)} %get-tuple-element.433), channel_id=1, source_target_pairs={{0,2},{1,3},{2,0},{3,1},{4,6},{5,7},{6,4},{7,5},{8,10},{9,11},{10,... | collective-permute-start | bytes 1572872 | tf_op jit(solution)/shard_map/ppermute | solution.py:1004
  224.7 32.3 %collective-permute-start.15 = (bf16[4,4,32,512]{3,2,1,0:T(8,128)(2,1)}, bf16[4,4,32,512]{3,2,1,0:T(8,128)(2,1)S(1)}, u32[]{:S(2)}, u32[]{:S(2)}) collective-permute-start(bf16[4,4,32,512]{3,2,1,0:T(8,128)(2,1)} %get-tuple-element.434), channel_id=1, source_target_pairs={{0,16},{16,0},{1,17},{17,1},{2,18},{18,2},{3,19},{19,3},{4,20},{20... | collective-permute-start | bytes 1572872 | tf_op jit(solution)/shard_map/ppermute | solution.py:1004
  263.9 20.3 %collective-permute-start.21 = (bf16[16,6,32,512]{3,2,1,0:T(8,128)(2,1)}, bf16[16,6,32,512]{3,2,1,0:T(8,128)(2,1)S(1)}, u32[]{:S(2)}, u32[]{:S(2)}) collective-permute-start(bf16[16,6,32,512]{3,2,1,0:T(8,128)(2,1)} %get-tuple-element.459), channel_id=1, source_target_pairs={{0,1},{1,0},{2,3},{3,2},{4,5},{5,4},{6,7},{7,6},{8,9},{9,8},{10,11... | collective-permute-start | bytes 9437192 | tf_op jit(solution)/shard_map/ppermute | solution.py:1004
  263.9 20.2 %collective-permute-start.22 = (bf16[16,4,32,512]{3,2,1,0:T(8,128)(2,1)}, bf16[16,4,32,512]{3,2,1,0:T(8,128)(2,1)S(1)}, u32[]{:S(2)}, u32[]{:S(2)}) collective-permute-start(bf16[16,4,32,512]{3,2,1,0:T(8,128)(2,1)} %get-tuple-element.460), channel_id=1, source_target_pairs={{0,1},{1,0},{2,3},{3,2},{4,5},{5,4},{6,7},{7,6},{8,9},{9,8},{10,11... | collective-permute-start | bytes 6291464 | tf_op jit(solution)/shard_map/ppermute | solution.py:1004
  264.4 19.7 %collective-permute-start.20 = (bf16[4,6,32,512]{3,2,1,0:T(8,128)(2,1)}, bf16[4,6,32,512]{3,2,1,0:T(8,128)(2,1)S(1)}, u32[]{:S(2)}, u32[]{:S(2)}) collective-permute-start(bf16[4,6,32,512]{3,2,1,0:T(8,128)(2,1)} %get-tuple-element.458), channel_id=1, source_target_pairs={{0,16},{16,0},{1,17},{17,1},{2,18},{18,2},{3,19},{19,3},{4,20},{20... | collective-permute-start | bytes 2359304 | tf_op jit(solution)/shard_map/ppermute | solution.py:1004
  294.7 35.8 %collective-permute-start.26 = (bf16[8,6,32,512]{3,2,1,0:T(8,128)(2,1)}, bf16[8,6,32,512]{3,2,1,0:T(8,128)(2,1)S(1)}, u32[]{:S(2)}, u32[]{:S(2)}) collective-permute-start(bf16[8,6,32,512]{3,2,1,0:T(8,128)(2,1)} %get-tuple-element.486), channel_id=1, source_target_pairs={{0,2},{1,3},{2,0},{3,1},{4,6},{5,7},{6,4},{7,5},{8,10},{9,11},{10,... | collective-permute-start | bytes 4718600 | tf_op jit(solution)/shard_map/ppermute | solution.py:1004
  296.3 24.2 %collective-permute-start.25 = (bf16[8,4,32,512]{3,2,1,0:T(8,128)(2,1)}, bf16[8,4,32,512]{3,2,1,0:T(8,128)(2,1)S(1)}, u32[]{:S(2)}, u32[]{:S(2)}) collective-permute-start(bf16[8,4,32,512]{3,2,1,0:T(8,128)(2,1)} %get-tuple-element.485), channel_id=1, source_target_pairs={{0,16},{16,0},{1,17},{17,1},{2,18},{18,2},{3,19},{19,3},{4,20},{20... | collective-permute-start | bytes 3145736 | tf_op jit(solution)/shard_map/ppermute | solution.py:1004
  296.6 22.6 %collective-permute-start.24 = (bf16[2,10,32,512]{3,2,1,0:T(8,128)(2,1)}, bf16[2,10,32,512]{3,2,1,0:T(8,128)(2,1)S(1)}, u32[]{:S(2)}, u32[]{:S(2)}) collective-permute-start(bf16[2,10,32,512]{3,2,1,0:T(8,128)(2,1)} %get-tuple-element.484), channel_id=1, source_target_pairs={{0,4},{1,5},{2,6},{3,7},{4,0},{5,1},{6,2},{7,3},{8,12},{9,13},{10,... | collective-permute-start | bytes 1966088 | tf_op jit(solution)/shard_map/ppermute | solution.py:1004
  298.2 21.0 %collective-permute-start.23 = (bf16[1,8,32,512]{3,2,1,0:T(8,128)(2,1)}, bf16[1,8,32,512]{3,2,1,0:T(8,128)(2,1)S(1)}, u32[]{:S(2)}, u32[]{:S(2)}) collective-permute-start(bf16[1,8,32,512]{3,2,1,0:T(8,128)(2,1)} %get-tuple-element.483), channel_id=1, source_target_pairs={{0,8},{1,9},{2,10},{3,11},{4,12},{5,13},{6,14},{7,15},{8,0},{9,1},... | collective-permute-start | bytes 786440 | tf_op jit(solution)/shard_map/ppermute | solution.py:1004
  337.6 20.8 %collective-permute-start.29 = (bf16[4,6,32,512]{3,2,1,0:T(8,128)(2,1)}, bf16[4,6,32,512]{3,2,1,0:T(8,128)(2,1)S(1)}, u32[]{:S(2)}, u32[]{:S(2)}) collective-permute-start(bf16[4,6,32,512]{3,2,1,0:T(8,128)(2,1)} %get-tuple-element.503), channel_id=1, source_target_pairs={{0,16},{16,0},{1,17},{17,1},{2,18},{18,2},{3,19},{19,3},{4,20},{20... | collective-permute-start | bytes 2359304 | tf_op jit(solution)/shard_map/ppermute | solution.py:1004
  342.1 47.4 %collective-permute-start.30 = (bf16[768,1024]{1,0:T(8,128)(2,1)}, bf16[768,1024]{1,0:T(8,128)(2,1)}, u32[]{:S(2)}, u32[]{:S(2)}) collective-permute-start(bf16[768,1024]{1,0:T(8,128)(2,1)} %get-tuple-element.529), channel_id=1, source_target_pairs={{16,0},{17,1},{18,2},{19,3},{20,4},{21,5},{22,6},{23,7},{24,8},{25... | collective-permute-start | bytes 4718600 | tf_op jit(solution)/shard_map/ppermute | solution.py:1366
  395.2 21.7 %collective-permute-start.34 = (bf16[8,2,32,512]{3,2,1,0:T(8,128)(2,1)}, bf16[8,2,32,512]{3,2,1,0:T(8,128)(2,1)S(1)}, u32[]{:S(2)}, u32[]{:S(2)}) collective-permute-start(bf16[8,2,32,512]{3,2,1,0:T(8,128)(2,1)} %get-tuple-element.557), channel_id=1, source_target_pairs={{0,2},{1,3},{2,0},{3,1},{4,6},{5,7},{6,4},{7,5},{8,10},{9,11},{10,... | collective-permute-start | bytes 1572872 | tf_op jit(solution)/shard_map/ppermute | solution.py:1004
  396.8 20.1 %collective-permute-start.35 = (bf16[8,1,32,512]{3,2,1,0:T(8,128)(2,1)}, bf16[8,1,32,512]{3,2,1,0:T(8,128)(2,1)S(1)}, u32[]{:S(2)}, u32[]{:S(2)}) collective-permute-start(bf16[8,1,32,512]{3,2,1,0:T(8,128)(2,1)} %get-tuple-element.558), channel_id=1, source_target_pairs={{0,16},{16,0},{1,17},{17,1},{2,18},{18,2},{3,19},{19,3},{4,20},{20... | collective-permute-start | bytes 786440 | tf_op jit(solution)/shard_map/ppermute | solution.py:1004
  397.6 19.3 %collective-permute-start.33 = (bf16[1,10,32,512]{3,2,1,0:T(8,128)(2,1)}, bf16[1,10,32,512]{3,2,1,0:T(8,128)(2,1)S(1)}, u32[]{:S(2)}, u32[]{:S(2)}) collective-permute-start(bf16[1,10,32,512]{3,2,1,0:T(8,128)(2,1)} %get-tuple-element.556), channel_id=1, source_target_pairs={{0,8},{1,9},{2,10},{3,11},{4,12},{5,13},{6,14},{7,15},{8,0},{9,1},... | collective-permute-start | bytes 983048 | tf_op jit(solution)/shard_map/ppermute | solution.py:1004
  (84 other events, 540.0 us)

commit v7 on v6

--- a/solution.py
+++ b/solution.py
@@ -1276,7 +1276,9 @@
     )
     query = gather.step(query)
     own_mixed, own_total = own_forward(query, own_keys, own_values)
-    lead_tokens, own_mixed = gather.step((lead_tokens, own_mixed))
+    small = (info, filled, cross_vectors, feed_vectors, output_vectors)
+    lead_tokens, own_mixed, small = gather.step((lead_tokens, own_mixed, small))
+    info, filled, cross_vectors, feed_vectors, output_vectors = small
     lead_keys, lead_values = norm_project(
         "lead_project", nothing, lead_tokens, [key_weight, value_weight],
         [(None, 1.0), (3, 1.0)], self_vectors, False,
@@ -1352,7 +1354,11 @@
     )
     self_args = (query, lead_keys, lead_values, self_mixed, self_total)
     own_args = (query, own_keys, own_values, self_mixed, self_total)
-    grad_self_out = advance(info, grad_self_out, [first, second], [third])
+    bias_rows = expand_bias_sums.reshape(owners, -1, fine)
+    bias_rows = jnp.transpose(bias_rows, (1, 0, 2)).reshape(-1, model_width)
+    grad_self_out, bias_rows = advance(
+        info, (grad_self_out, bias_rows), [first, second], [third]
+    )
     lead_low = lead_backward(*self_args, grad_self_out, trailing, 0, half_pairs)
     lead_low, grad_self_out = advance(info, (lead_low, grad_self_out), [first, second, third])
     lead_high = lead_backward(*self_args, grad_self_out, trailing, half_pairs, half_pairs)
@@ -1382,8 +1388,6 @@
         info, (first_sums, own_high, led_part), [third, fourth]
     )
     parts = projection_grads(info, hidden_one, *own_high, led_part, True, owners)
-    bias_rows = expand_bias_sums.reshape(owners, -1, fine)
-    bias_rows = jnp.transpose(bias_rows, (1, 0, 2)).reshape(-1, model_width)
     table = vector_table(feed_sums, bias_rows, probe_sums, paged[2], lead_sums, first_sums)
     table = scatter_rows(table, model_width, 0, 1)
     fifth = Sum(True, (parts[0], [Part(parts[1], i != 1, (i, half), i, 1) for i in range(3)]))

time: 507 us -> 499 us (0.984)
    unnamed x108 -> x106, local copies, waits for them, and re-layouts: 18.8 us -> 18.7 us
  transfers between devices with their start and end apart: 54 -> 54, of which waited for: 17 -> 16; matrix products, arithmetic and copies ran while one was open for 3% -> 3% of each run, Pallas kernels for 47% -> 47%
where the time goes in v7:
time: 499 us; the launch traced here: 492 us
  Pallas kernels  329 us (66%)
  starting transfers between devices  72.7 us (15%)
  waiting for transfers between devices  54.3 us (11%)
  local copies, waits for them, and re-layouts  27.6 us (6%)
  other arithmetic  6.32 us (1%)
    pallas_call x9, Pallas kernels, streamed(): pl.pallas_call(kernel, out_shape=[Shape(shape, kind) for shape, kind in o...  96 us
    pallas_call x2, Pallas kernels, feed_forward(): pl.pallas_call(body, out_shape=shapes + shared_shapes, grid_spec=pltpu.Pr...  72.3 us
    ppermute x52, starting transfers between devices, hop(): lax.ppermute(value, axis, [(i, i ^ flip) for i in range(lax.axis_size(axi...  66.5 us
    pallas_call x13, Pallas kernels, added_up(): pl.pallas_call(body, out_shape=[Shape(shape, kind) for shape, kind in sha...  55.9 us
    ppermute x52, waiting for transfers between devices, hop(): lax.ppermute(value, axis, [(i, i ^ flip) for i in range(lax.axis_size(axi...  52.9 us
    pallas_call x2, Pallas kernels, own_backward(): pl.pallas_call(body, out_shape=[Shape((rows, pairs * PAIR), bf16)] * 3, g...  25.5 us
    pallas_call x2, Pallas kernels, cross_backward(): pl.pallas_call(body, out_shape=[Shape((rows, pairs * PAIR), bf16)] + [Sha...  23.7 us
    unnamed x106, local copies, waits for them, and re-layouts  18.7 us
  transfers between devices with their start and end apart: 54, of which 16 were waited for; matrix products, arithmetic and copies ran while one was open for 3% of the time, Pallas kernels for 47%

profile of v7, /device:TPU:0, one launch (start us, length us, event | category | flops | bytes accessed | tf_op | source)
XLA Modules:
  0.0 492.4 jit_solution(13675069528927954955)
XLA Ops:
  10.7 9.4 %own_project.1 = (bf16[768,1024]{1,0:T(8,128)(2,1)}, bf16[768,1024]{1,0:T(8,128)(2,1)}, bf16[768,1024]{1,0:T(8,128)(2,1)}, bf16[768,1024]{1,0:T(8,128)(2,1)}) custom-call(s32[1]{0:T(128)} %constant.19.clone.1.info_ref, bf16[768,1024]{1,0:T(8,128)(2,1)} %bitcast.71, f32[8,1024]{1,0:T(8,128)} %select_maximum_fusion.7.refs_1_.refs_7_.refs_10_, ...), custom_call_target="tpu_custom_call" | custom-call | flops 1 | bytes 1 | tf_op jit(solution)/shard_map/own_project/pallas_call | solution.py:558
  27.4 14.0 %own_forward.1 = (bf16[768,1024]{1,0:T(8,128)(2,1)}, f32[8,2,768]{2,1,0:T(2,128)}) custom-call(bf16[768,1024]{1,0:T(8,128)(2,1)} %get-tuple-element.350.q_ref, bf16[768,1024]{1,0:T(8,128)(2,1)} %get-tuple-element.351.k_ref, bf16[768,1024]{1,0:T(8,128)(2,1)} %get-tuple-element.352.v_ref), custom_call_target="tpu_custom_call" | custom-call | flops 1 | bytes 1 | tf_op jit(solution)/shard_map/own_forward/pallas_call | solution.py:189
  42.5 6.9 %lead_project.1 = (bf16[768,1024]{1,0:T(8,128)(2,1)}, bf16[768,1024]{1,0:T(8,128)(2,1)}) custom-call(s32[1]{0:T(128)} %constant.19.clone.1.info_ref, bf16[768,1024]{1,0:T(8,128)(2,1)} %copy-done.17, f32[8,1024]{1,0:T(8,128)} %select_maximum_fusion.7.refs_1_.refs_7_.refs_10_, bf16[1024,1024]{1,0:T(8,128)(2,1)} %refs_7_.5, bf16[1024,1024]{1,0:T(8,128)(2,1)} %refs_8_.1), custom_call_target="tpu_custom_call" | custom-call | flops 1 | bytes 1 | tf_op jit(solution)/shard_map/lead_project/pallas_call | solution.py:558
  49.5 6.5 %lead_forward.1 = (bf16[768,1024]{1,0:T(8,128)(2,1)}, f32[8,2,768]{2,1,0:T(2,128)}) custom-call(s32[1]{0:T(128)} %bitcast.23.flag, bf16[768,1024]{1,0:T(8,128)(2,1)} %get-tuple-element.350.q_ref, bf16[768,1024]{1,0:T(8,128)(2,1)} %get-tuple-element.365.k_ref, bf16[768,1024]{1,0:T(8,128)(2,1)} %get-tuple-element.366.v_ref, ...), custom_call_target="tpu_custom_call" | custom-call | flops 1 | bytes 1 | tf_op jit(solution)/shard_map/lead_forward/pallas_call | solution.py:218
  56.8 8.5 %output_project.1 = (f32[768,1024]{1,0:T(8,128)}, bf16[768,1024]{1,0:T(8,128)(2,1)}) custom-call(s32[1]{0:T(128)} %constant.19.clone.1.info_ref, bf16[768,1024]{1,0:T(8,128)(2,1)} %get-tuple-element.373.refs_0_.refs_6_.out_ref, bf16[768,1024]{1,0:T(8,128)(2,1)} %bitcast.72, f32[8,1024]{1,0:T(8,128)} %get-tuple-element.374.refs_2_, ...), custom_call_target="tpu_custom_call" | custom-call | flops 1 | bytes 1 | tf_op jit(solution)/shard_map/output_project/pallas_call | solution.py:558
  67.0 6.8 %page_forward.1 = (bf16[512,1024]{1,0:T(8,128)(2,1)}, bf16[512,1024]{1,0:T(8,128)(2,1)}, bf16[512,1024]{1,0:T(8,128)(2,1)}) custom-call(s32[16]{0:T(128)S(1)} %shift-left_or_fusion.place_ref, bf16[32,32,1024]{2,1,0:T(8,128)(2,1)S(1)} %pad_maximum_fusion.blocks_ref, bf16[1024,1024]{1,0:T(8,128)(2,1)S(1)} %copy-done, bf16[1024,1024]{1,0:T(8,128)(2,1)} %refs_6_.2, ...), custom_call_target="tpu_custom_call" | custom-call | flops 1 | bytes 1 | tf_op jit(solution)/shard_map/page_forward/pallas_call | solution.py:906
  73.9 14.7 %cross_forward.1 = (bf16[768,1024]{1,0:T(8,128)(2,1)}, f32[8,2,768]{2,1,0:T(2,128)}) custom-call(s32[1]{0:T(128)} %bitcast.14.filled_ref, bf16[768,1024]{1,0:T(8,128)(2,1)} %get-tuple-element.379.q_ref, bf16[512,1024]{1,0:T(8,128)(2,1)} %get-tuple-element.381.k_ref, bf16[512,1024]{1,0:T(8,128)(2,1)} %get-tuple-element.382.v_ref), custom_call_target="tpu_custom_call" | custom-call | flops 1 | bytes 1 | tf_op jit(solution)/shard_map/cross_forward/pallas_call | solution.py:249
  88.6 32.8 %feed_forward.2 = (f32[768,1024]{1,0:T(8,128)}, f32[768,1024]{1,0:T(8,128)}, f32[768,1024]{1,0:T(8,128)}, bf16[2,8,4,32,512]{4,3,2,1,0:T(8,128)(2,1)}, bf16[2,8,...) custom-call(s32[9]{0:T(128)} %stack.91.info_ref, ...), custom_call_target="tpu_custom_call" | custom-call | flops 1 | bytes 1 | tf_op jit(solution)/shard_map/feed_forward/pallas_call | solution.py:499
  122.0 39.5 %feed_forward.3 = (bf16[768,1024]{1,0:T(8,128)(2,1)}, f32[768,1024]{1,0:T(8,128)}, bf16[768,1024]{1,0:T(8,128)(2,1)}, bf16[16,2,32,512]{3,2,1,0:T(8,128)(2,1)}, ...) custom-call(s32[9]{0:T(128)} %stack.91.info_ref, ...), custom_call_target="tpu_custom_call" | custom-call | flops 1 | bytes 1 | tf_op jit(solution)/shard_map/feed_forward/pallas_call | solution.py:499
  168.3 13.5 %collective-permute-start.12 = (bf16[8,4,32,512]{3,2,1,0:T(8,128)(2,1)}, bf16[8,4,32,512]{3,2,1,0:T(8,128)(2,1)}, u32[]{:S(2)}, u32[]{:S(2)}) collective-permute-start(bf16[8,4,32,512]{3,2,1,0:T(8,128)(2,1)} %get-tuple-element.438), channel_id=1, source_target_pairs={{0,16},{16,0},{1,17},{17,1},{2,18},{18,2},{3,19},{19,3},{4,20},{20... | collective-permute-start | bytes 3145736 | tf_op jit(solution)/shard_map/ppermute | solution.py:1004
  183.3 11.8 %cross_backward.2 = (bf16[768,512]{1,0:T(8,128)(2,1)}, bf16[512,512]{1,0:T(8,128)(2,1)}, bf16[512,512]{1,0:T(8,128)(2,1)}) custom-call(s32[1]{0:T(128)} %bitcast.14.filled_ref, bf16[768,1024]{1,0:T(8,128)(2,1)} %get-tuple-element.379.q_ref, bf16[512,1024]{1,0:T(8,128)(2,1)} %get-tuple-element.381.k_ref, bf16[512,1024]{1,0:T(8,128)(2,1)} %get-tuple-element.382.v_ref, ...), custom_call_target="tpu_custom_call" | custom-call | flops 1 | bytes 1 | tf_op jit(solution)/shard_map/cross_backward/pallas_call | solution.py:342
  202.3 11.9 %cross_backward.3 = (bf16[768,512]{1,0:T(8,128)(2,1)}, bf16[512,512]{1,0:T(8,128)(2,1)}, bf16[512,512]{1,0:T(8,128)(2,1)}) custom-call(s32[1]{0:T(128)} %bitcast.14.filled_ref, bf16[768,1024]{1,0:T(8,128)(2,1)} %get-tuple-element.379.q_ref, bf16[512,1024]{1,0:T(8,128)(2,1)} %get-tuple-element.381.k_ref, bf16[512,1024]{1,0:T(8,128)(2,1)} %get-tuple-element.382.v_ref, ...), custom_call_target="tpu_custom_call" | custom-call | flops 1 | bytes 1 | tf_op jit(solution)/shard_map/cross_backward/pallas_call | solution.py:342
  224.6 16.4 %probe_backward.1 = (f32[768,1024]{1,0:T(8,128)}, bf16[768,1024]{1,0:T(8,128)(2,1)}, bf16[16,4,32,512]{3,2,1,0:T(8,128)(2,1)}, bf16[16,4,32,512]{3,2,1,0:T(8,128)(2,1)}, f32[8,1024]{1,0:T(8,128)}) custom-call(s32[9]{0:T(128)} %stack.91.info_ref, bf16[768,512]{1,0:T(8,128)(2,1)} %get-tuple-element.450.refs_0_, bf16[768,512]{1,0:T(8,128)(2,1)} %get-tuple-element.451.refs_1_, ...), custom_call_target="tpu_custom_call" | custom-call | flops 1 | bytes 1 | tf_op jit(solution)/shard_map/probe_backward/pallas_call | solution.py:558
  241.1 10.4 %page_backward.1 = (bf16[16,6,32,512]{3,2,1,0:T(8,128)(2,1)}, bf16[16,6,32,512]{3,2,1,0:T(8,128)(2,1)}, f32[8,1024]{1,0:T(8,128)}) custom-call(s32[9]{0:T(128)} %stack.91.info_ref, bf16[512,512]{1,0:T(8,128)(2,1)} %get-tuple-element.470.refs_0_, bf16[512,512]{1,0:T(8,128)(2,1)} %get-tuple-element.471.refs_1_, bf16[512,512]{1,0:T(8,128)(2,1)} %get-tuple-element.472.refs_2_, ...), custom_call_target="tpu_custom_call" | custom-call | flops 1 | bytes 1 | tf_op jit(solution)/shard_map/page_backward/pallas_call | solution.py:558
  267.1 6.1 %collective-permute-done.18.refs_4_ = bf16[2,8,32,512]{3,2,1,0:T(8,128)(2,1)S(1)} collective-permute-done((bf16[2,8,32,512]{3,2,1,0:T(8,128)(2,1)}, bf16[2,8,32,512]{3,2,1,0:T(8,128)(2,1)S(1)}, u32[]{:S(2)}, u32[]{:S(2)}) %collective-permute-start.18) | collective-permute-done | bytes 524320 | tf_op jit(solution)/shard_map/ppermute | solution.py:1004
  281.9 7.5 %added_up.17 = (f32[1,8,32,512]{3,2,1,0:T(8,128)}, bf16[1,8,32,512]{3,2,1,0:T(8,128)(2,1)}, bf16[2,10,32,512]{3,2,1,0:T(8,128)(2,1)}, bf16[8,4,32,512]{3,2,1,0:T(8,128)(2,1)}, bf16[8,6,32,512]{3,2,1,0:T(8,128)(2,1)}) custom-call(s32[9]{0:T(128)} %stack.91.info_ref, bf16[16,4,32,512]{3,2,1,0:T(8,128)(2,1)} %get-tuple-element.403.refs_0_, ...), custom_call_target="tpu_custom_call" | custom-call | flops 1 | bytes 1 | tf_op jit(solution)/shard_map/added_up/pallas_call | solution.py:1117
  299.7 13.6 %lead_upstream.1 = (bf16[768,1024]{1,0:T(8,128)(2,1)}, bf16[1024,2048]{1,0:T(8,128)(2,1)}, f32[8,1024]{1,0:T(8,128)}) custom-call(s32[9]{0:T(128)} %stack.91.info_ref, bf16[768,512]{1,0:T(8,128)(2,1)} %get-tuple-element.501.refs_0_, bf16[768,512]{1,0:T(8,128)(2,1)} %get-tuple-element.503.refs_1_, bf16[768,512]{1,0:T(8,128)(2,1)} %get-tuple-element.504.refs_2_, ...), custom_call_target="tpu_custom_call" | custom-call | flops 1 | bytes 1 | tf_op jit(solution)/shard_map/lead_upstream/pallas_call | solution.py:558
  315.3 10.0 %collective-permute-done.26.refs_14_.refs_4_.refs_5_ = bf16[8,6,32,512]{3,2,1,0:T(8,128)(2,1)S(1)} collective-permute-done((bf16[8,6,32,512]{3,2,1,0:T(8,128)(2,1)}, bf16[8,6,32,512]{3,2,1,0:T(8,128)(2,1)S(1)}, u32[]{:S(2)}, u32[]{:S(2)}) %collective-permute-start.26) | collective-permute-done | bytes 1572896 | tf_op jit(solution)/shard_map/ppermute | solution.py:1004
  337.5 13.0 %own_backward.2 = (bf16[768,512]{1,0:T(8,128)(2,1)}, bf16[768,512]{1,0:T(8,128)(2,1)}, bf16[768,512]{1,0:T(8,128)(2,1)}) custom-call(bf16[768,1024]{1,0:T(8,128)(2,1)} %get-tuple-element.350.q_ref, bf16[768,1024]{1,0:T(8,128)(2,1)} %get-tuple-element.351.k_ref, bf16[768,1024]{1,0:T(8,128)(2,1)} %get-tuple-element.352.v_ref, ...), custom_call_target="tpu_custom_call" | custom-call | flops 1 | bytes 1 | tf_op jit(solution)/shard_map/own_backward/pallas_call | solution.py:312
  357.6 7.9 %projection_grads.2 = (bf16[16,3,32,512]{3,2,1,0:T(8,128)(2,1)}, bf16[16,3,32,512]{3,2,1,0:T(8,128)(2,1)}) custom-call(s32[9]{0:T(128)} %stack.91.info_ref, bf16[768,1024]{1,0:T(8,128)(2,1)} %get-tuple-element.543.refs_0_, bf16[768,512]{1,0:T(8,128)(2,1)} %get-tuple-element.570.refs_1_.refs_0_, bf16[768,512]{1,0:T(8,128)(2,1)} %get-tuple-element.572.refs_2_, ...), custom_call_target="tpu_custom_call" | custom-call | flops 1 | bytes 1 | tf_op jit(solution)/shard_map/projection_grads/pallas_call | solution.py:558
  367.3 12.6 %own_backward.3 = (bf16[768,512]{1,0:T(8,128)(2,1)}, bf16[768,512]{1,0:T(8,128)(2,1)}, bf16[768,512]{1,0:T(8,128)(2,1)}) custom-call(bf16[768,1024]{1,0:T(8,128)(2,1)} %get-tuple-element.350.q_ref, bf16[768,1024]{1,0:T(8,128)(2,1)} %get-tuple-element.351.k_ref, bf16[768,1024]{1,0:T(8,128)(2,1)} %get-tuple-element.352.v_ref, ...), custom_call_target="tpu_custom_call" | custom-call | flops 1 | bytes 1 | tf_op jit(solution)/shard_map/own_backward/pallas_call | solution.py:312
  393.5 14.9 %first_norm_backward.1 = (f32[768,1024]{1,0:T(8,128)}, f32[8,1024]{1,0:T(8,128)}) custom-call(s32[9]{0:T(128)} %stack.91.info_ref, bf16[768,512]{1,0:T(8,128)(2,1)} %get-tuple-element.570.refs_1_.refs_0_, bf16[768,512]{1,0:T(8,128)(2,1)} %get-tuple-element.606.refs_1_, bf16[768,512]{1,0:T(8,128)(2,1)} %get-tuple-element.572.refs_2_, ...), custom_call_target="tpu_custom_call" | custom-call | flops 1 | bytes 1 | tf_op jit(solution)/shard_map/first_norm_backward/pallas_call | solution.py:558
  417.2 7.8 %projection_grads.3 = (bf16[16,3,32,512]{3,2,1,0:T(8,128)(2,1)}, bf16[16,3,32,512]{3,2,1,0:T(8,128)(2,1)}) custom-call(s32[9]{0:T(128)} %stack.91.info_ref, bf16[768,1024]{1,0:T(8,128)(2,1)} %get-tuple-element.543.refs_0_, bf16[768,512]{1,0:T(8,128)(2,1)} %get-tuple-element.606.refs_1_, bf16[768,512]{1,0:T(8,128)(2,1)} %get-tuple-element.607.refs_3_.refs_2_, ...), custom_call_target="tpu_custom_call" | custom-call | flops 1 | bytes 1 | tf_op jit(solution)/shard_map/projection_grads/pallas_call | solution.py:558
  482.2 7.1 %collective-permute-done.51.refs_4_ = bf16[1,3,32,512]{3,2,1,0:T(8,128)(2,1)S(1)} collective-permute-done((bf16[1,3,32,512]{3,2,1,0:T(8,128)(2,1)}, bf16[1,3,32,512]{3,2,1,0:T(8,128)(2,1)S(1)}, u32[]{:S(2)}, u32[]{:S(2)}) %collective-permute-start.51) | collective-permute-done | bytes 98336 | tf_op jit(solution)/shard_map/ppermute | solution.py:1004
  (262 shorter events, 186.1 us)
Async XLA Ops:
  0.7 40.7 %collective-permute-start = (bf16[768,1024]{1,0:T(8,128)(2,1)}, bf16[768,1024]{1,0:T(8,128)(2,1)S(1)}, u32[]{:S(2)}, u32[]{:S(2)}) collective-permute-start(bf16[768,1024]{1,0:T(8,128)(2,1)} %bitcast.70), channel_id=1, source_target_pairs={{0,16},{1,17},{2,18},{3,19},{4,20},{5,21},{6,22},{7,23},{8,24},{9,... | collective-permute-start | bytes 4718600 | tf_op jit(solution)/shard_map/ppermute | solution.py:1256
  20.2 21.2 %collective-permute-start.4 = (bf16[4,32,1024]{2,1,0:T(8,128)(2,1)S(1)}, bf16[4,32,1024]{2,1,0:T(8,128)(2,1)S(1)}, u32[]{:S(2)}, u32[]{:S(2)}) collective-permute-start(bf16[4,32,1024]{2,1,0:T(8,128)(2,1)S(1)} %pad_maximum_fusion.4), channel_id=1, source_target_pairs={{0,8},{1,9},{2,10},{3,11},{4,12},{5,13},{6,14},{7,15},{8,0},{9,1},... | collective-permute-start | bytes 786440 | tf_op jit(solution)/shard_map/ppermute | solution.py:1004
  121.4 40.1 %collective-permute-start.7 = (bf16[16,4,32,512]{3,2,1,0:T(8,128)(2,1)}, bf16[16,4,32,512]{3,2,1,0:T(8,128)(2,1)S(1)}, u32[]{:S(2)}, u32[]{:S(2)}) collective-permute-start(bf16[16,4,32,512]{3,2,1,0:T(8,128)(2,1)} %get-tuple-element.400), channel_id=1, source_target_pairs={{0,1},{1,0},{2,3},{3,2},{4,5},{5,4},{6,7},{7,6},{8,9},{9,8},{10,11... | collective-permute-start | bytes 6291464 | tf_op jit(solution)/shard_map/ppermute | solution.py:1004
  122.0 39.6 %collective-permute-start.8 = (bf16[16,4,32,512]{3,2,1,0:T(8,128)(2,1)}, bf16[16,4,32,512]{3,2,1,0:T(8,128)(2,1)}, u32[]{:S(2)}, u32[]{:S(2)}) collective-permute-start(bf16[16,4,32,512]{3,2,1,0:T(8,128)(2,1)} %bitcast.96), channel_id=1, source_target_pairs={{0,1},{1,0},{2,3},{3,2},{4,5},{5,4},{6,7},{7,6},{8,9},{9,8},{10,11... | collective-permute-start | bytes 6291464 | tf_op jit(solution)/shard_map/ppermute | solution.py:1004
  167.3 27.9 %collective-permute-start.9 = (bf16[16,4,32,512]{3,2,1,0:T(8,128)(2,1)}, bf16[16,4,32,512]{3,2,1,0:T(8,128)(2,1)S(1)}, u32[]{:S(2)}, u32[]{:S(2)}) collective-permute-start(bf16[16,4,32,512]{3,2,1,0:T(8,128)(2,1)} %get-tuple-element.416), channel_id=1, source_target_pairs={{0,1},{1,0},{2,3},{3,2},{4,5},{5,4},{6,7},{7,6},{8,9},{9,8},{10,11... | collective-permute-start | bytes 6291464 | tf_op jit(solution)/shard_map/ppermute | solution.py:1004
  167.8 27.4 %collective-permute-start.10 = (bf16[16,4,32,512]{3,2,1,0:T(8,128)(2,1)}, bf16[16,4,32,512]{3,2,1,0:T(8,128)(2,1)}, u32[]{:S(2)}, u32[]{:S(2)}) collective-permute-start(bf16[16,4,32,512]{3,2,1,0:T(8,128)(2,1)} %bitcast.95), channel_id=1, source_target_pairs={{0,1},{1,0},{2,3},{3,2},{4,5},{5,4},{6,7},{7,6},{8,9},{9,8},{10,11... | collective-permute-start | bytes 6291464 | tf_op jit(solution)/shard_map/ppermute | solution.py:1004
  167.8 27.3 %collective-permute-start.11 = (bf16[16,2,32,512]{3,2,1,0:T(8,128)(2,1)}, bf16[16,2,32,512]{3,2,1,0:T(8,128)(2,1)S(1)}, u32[]{:S(2)}, u32[]{:S(2)}) collective-permute-start(bf16[16,2,32,512]{3,2,1,0:T(8,128)(2,1)} %get-tuple-element.418), channel_id=1, source_target_pairs={{0,1},{1,0},{2,3},{3,2},{4,5},{5,4},{6,7},{7,6},{8,9},{9,8},{10,11... | collective-permute-start | bytes 3145736 | tf_op jit(solution)/shard_map/ppermute | solution.py:1004
  168.3 45.9 %collective-permute-start.12 = (bf16[8,4,32,512]{3,2,1,0:T(8,128)(2,1)}, bf16[8,4,32,512]{3,2,1,0:T(8,128)(2,1)}, u32[]{:S(2)}, u32[]{:S(2)}) collective-permute-start(bf16[8,4,32,512]{3,2,1,0:T(8,128)(2,1)} %get-tuple-element.438), channel_id=1, source_target_pairs={{0,16},{16,0},{1,17},{17,1},{2,18},{18,2},{3,19},{19,3},{4,20},{20... | collective-permute-start | bytes 3145736 | tf_op jit(solution)/shard_map/ppermute | solution.py:1004
  181.8 32.4 %collective-permute-start.13 = (bf16[8,4,32,512]{3,2,1,0:T(8,128)(2,1)}, bf16[8,4,32,512]{3,2,1,0:T(8,128)(2,1)}, u32[]{:S(2)}, u32[]{:S(2)}) collective-permute-start(bf16[8,4,32,512]{3,2,1,0:T(8,128)(2,1)} %get-tuple-element.439), channel_id=1, source_target_pairs={{0,2},{1,3},{2,0},{3,1},{4,6},{5,7},{6,4},{7,5},{8,10},{9,11},{10,... | collective-permute-start | bytes 3145736 | tf_op jit(solution)/shard_map/ppermute | solution.py:1004
  201.7 50.1 %collective-permute-start.17 = (bf16[8,6,32,512]{3,2,1,0:T(8,128)(2,1)}, bf16[8,6,32,512]{3,2,1,0:T(8,128)(2,1)S(1)}, u32[]{:S(2)}, u32[]{:S(2)}) collective-permute-start(bf16[8,6,32,512]{3,2,1,0:T(8,128)(2,1)} %get-tuple-element.460), channel_id=1, source_target_pairs={{0,2},{1,3},{2,0},{3,1},{4,6},{5,7},{6,4},{7,5},{8,10},{9,11},{10,... | collective-permute-start | bytes 4718600 | tf_op jit(solution)/shard_map/ppermute | solution.py:1004
  202.3 49.6 %collective-permute-start.16 = (bf16[8,4,32,512]{3,2,1,0:T(8,128)(2,1)}, bf16[8,4,32,512]{3,2,1,0:T(8,128)(2,1)S(1)}, u32[]{:S(2)}, u32[]{:S(2)}) collective-permute-start(bf16[8,4,32,512]{3,2,1,0:T(8,128)(2,1)} %get-tuple-element.459), channel_id=1, source_target_pairs={{0,16},{16,0},{1,17},{17,1},{2,18},{18,2},{3,19},{19,3},{4,20},{20... | collective-permute-start | bytes 3145736 | tf_op jit(solution)/shard_map/ppermute | solution.py:1004
  218.4 33.4 %collective-permute-start.14 = (bf16[4,4,32,512]{3,2,1,0:T(8,128)(2,1)}, bf16[4,4,32,512]{3,2,1,0:T(8,128)(2,1)S(1)}, u32[]{:S(2)}, u32[]{:S(2)}) collective-permute-start(bf16[4,4,32,512]{3,2,1,0:T(8,128)(2,1)} %get-tuple-element.457), channel_id=1, source_target_pairs={{0,2},{1,3},{2,0},{3,1},{4,6},{5,7},{6,4},{7,5},{8,10},{9,11},{10,... | collective-permute-start | bytes 1572872 | tf_op jit(solution)/shard_map/ppermute | solution.py:1004
  220.0 31.9 %collective-permute-start.15 = (bf16[4,4,32,512]{3,2,1,0:T(8,128)(2,1)}, bf16[4,4,32,512]{3,2,1,0:T(8,128)(2,1)}, u32[]{:S(2)}, u32[]{:S(2)}) collective-permute-start(bf16[4,4,32,512]{3,2,1,0:T(8,128)(2,1)} %get-tuple-element.458), channel_id=1, source_target_pairs={{0,16},{16,0},{1,17},{17,1},{2,18},{18,2},{3,19},{19,3},{4,20},{20... | collective-permute-start | bytes 1572872 | tf_op jit(solution)/shard_map/ppermute | solution.py:1004
  258.6 20.3 %collective-permute-start.21 = (bf16[16,6,32,512]{3,2,1,0:T(8,128)(2,1)}, bf16[16,6,32,512]{3,2,1,0:T(8,128)(2,1)S(1)}, u32[]{:S(2)}, u32[]{:S(2)}) collective-permute-start(bf16[16,6,32,512]{3,2,1,0:T(8,128)(2,1)} %get-tuple-element.484), channel_id=1, source_target_pairs={{0,1},{1,0},{2,3},{3,2},{4,5},{5,4},{6,7},{7,6},{8,9},{9,8},{10,11... | collective-permute-start | bytes 9437192 | tf_op jit(solution)/shard_map/ppermute | solution.py:1004
  258.7 20.2 %collective-permute-start.22 = (bf16[16,4,32,512]{3,2,1,0:T(8,128)(2,1)}, bf16[16,4,32,512]{3,2,1,0:T(8,128)(2,1)S(1)}, u32[]{:S(2)}, u32[]{:S(2)}) collective-permute-start(bf16[16,4,32,512]{3,2,1,0:T(8,128)(2,1)} %get-tuple-element.485), channel_id=1, source_target_pairs={{0,1},{1,0},{2,3},{3,2},{4,5},{5,4},{6,7},{7,6},{8,9},{9,8},{10,11... | collective-permute-start | bytes 6291464 | tf_op jit(solution)/shard_map/ppermute | solution.py:1004
  259.2 19.7 %collective-permute-start.20 = (bf16[4,6,32,512]{3,2,1,0:T(8,128)(2,1)}, bf16[4,6,32,512]{3,2,1,0:T(8,128)(2,1)S(1)}, u32[]{:S(2)}, u32[]{:S(2)}) collective-permute-start(bf16[4,6,32,512]{3,2,1,0:T(8,128)(2,1)} %get-tuple-element.483), channel_id=1, source_target_pairs={{0,16},{16,0},{1,17},{17,1},{2,18},{18,2},{3,19},{19,3},{4,20},{20... | collective-permute-start | bytes 2359304 | tf_op jit(solution)/shard_map/ppermute | solution.py:1004
  289.5 35.8 %collective-permute-start.26 = (bf16[8,6,32,512]{3,2,1,0:T(8,128)(2,1)}, bf16[8,6,32,512]{3,2,1,0:T(8,128)(2,1)S(1)}, u32[]{:S(2)}, u32[]{:S(2)}) collective-permute-start(bf16[8,6,32,512]{3,2,1,0:T(8,128)(2,1)} %get-tuple-element.511), channel_id=1, source_target_pairs={{0,2},{1,3},{2,0},{3,1},{4,6},{5,7},{6,4},{7,5},{8,10},{9,11},{10,... | collective-permute-start | bytes 4718600 | tf_op jit(solution)/shard_map/ppermute | solution.py:1004
  291.1 24.2 %collective-permute-start.25 = (bf16[8,4,32,512]{3,2,1,0:T(8,128)(2,1)}, bf16[8,4,32,512]{3,2,1,0:T(8,128)(2,1)S(1)}, u32[]{:S(2)}, u32[]{:S(2)}) collective-permute-start(bf16[8,4,32,512]{3,2,1,0:T(8,128)(2,1)} %get-tuple-element.510), channel_id=1, source_target_pairs={{0,16},{16,0},{1,17},{17,1},{2,18},{18,2},{3,19},{19,3},{4,20},{20... | collective-permute-start | bytes 3145736 | tf_op jit(solution)/shard_map/ppermute | solution.py:1004
  291.3 22.0 %collective-permute-start.24 = (bf16[2,10,32,512]{3,2,1,0:T(8,128)(2,1)}, bf16[2,10,32,512]{3,2,1,0:T(8,128)(2,1)S(1)}, u32[]{:S(2)}, u32[]{:S(2)}) collective-permute-start(bf16[2,10,32,512]{3,2,1,0:T(8,128)(2,1)} %get-tuple-element.509), channel_id=1, source_target_pairs={{0,4},{1,5},{2,6},{3,7},{4,0},{5,1},{6,2},{7,3},{8,12},{9,13},{10,... | collective-permute-start | bytes 1966088 | tf_op jit(solution)/shard_map/ppermute | solution.py:1004
  292.9 20.4 %collective-permute-start.23 = (bf16[1,8,32,512]{3,2,1,0:T(8,128)(2,1)}, bf16[1,8,32,512]{3,2,1,0:T(8,128)(2,1)S(1)}, u32[]{:S(2)}, u32[]{:S(2)}) collective-permute-start(bf16[1,8,32,512]{3,2,1,0:T(8,128)(2,1)} %get-tuple-element.508), channel_id=1, source_target_pairs={{0,8},{1,9},{2,10},{3,11},{4,12},{5,13},{6,14},{7,15},{8,0},{9,1},... | collective-permute-start | bytes 786440 | tf_op jit(solution)/shard_map/ppermute | solution.py:1004
  332.3 20.8 %collective-permute-start.29 = (bf16[4,6,32,512]{3,2,1,0:T(8,128)(2,1)}, bf16[4,6,32,512]{3,2,1,0:T(8,128)(2,1)S(1)}, u32[]{:S(2)}, u32[]{:S(2)}) collective-permute-start(bf16[4,6,32,512]{3,2,1,0:T(8,128)(2,1)} %get-tuple-element.528), channel_id=1, source_target_pairs={{0,16},{16,0},{1,17},{17,1},{2,18},{18,2},{3,19},{19,3},{4,20},{20... | collective-permute-start | bytes 2359304 | tf_op jit(solution)/shard_map/ppermute | solution.py:1004
  336.2 48.0 %collective-permute-start.30 = (bf16[768,1024]{1,0:T(8,128)(2,1)}, bf16[768,1024]{1,0:T(8,128)(2,1)}, u32[]{:S(2)}, u32[]{:S(2)}) collective-permute-start(bf16[768,1024]{1,0:T(8,128)(2,1)} %get-tuple-element.554), channel_id=1, source_target_pairs={{16,0},{17,1},{18,2},{19,3},{20,4},{21,5},{22,6},{23,7},{24,8},{25... | collective-permute-start | bytes 4718600 | tf_op jit(solution)/shard_map/ppermute | solution.py:1372
  365.5 18.6 %collective-permute-start.32 = (bf16[16,3,32,512]{3,2,1,0:T(8,128)(2,1)}, bf16[16,3,32,512]{3,2,1,0:T(8,128)(2,1)S(1)}, u32[]{:S(2)}, u32[]{:S(2)}) collective-permute-start(bf16[16,3,32,512]{3,2,1,0:T(8,128)(2,1)} %get-tuple-element.556), channel_id=1, source_target_pairs={{0,1},{1,0},{2,3},{3,2},{4,5},{5,4},{6,7},{7,6},{8,9},{9,8},{10,11... | collective-permute-start | bytes 4718600 | tf_op jit(solution)/shard_map/ppermute | solution.py:1004
  390.0 18.5 %collective-permute-start.34 = (bf16[8,2,32,512]{3,2,1,0:T(8,128)(2,1)}, bf16[8,2,32,512]{3,2,1,0:T(8,128)(2,1)S(1)}, u32[]{:S(2)}, u32[]{:S(2)}) collective-permute-start(bf16[8,2,32,512]{3,2,1,0:T(8,128)(2,1)} %get-tuple-element.582), channel_id=1, source_target_pairs={{0,2},{1,3},{2,0},{3,1},{4,6},{5,7},{6,4},{7,5},{8,10},{9,11},{10,... | collective-permute-start | bytes 1572872 | tf_op jit(solution)/shard_map/ppermute | solution.py:1004
  (83 other events, 653.0 us)
